TPU v7x, 32 devices: a whole 2x2x4 slice. The times are simulated.
32 devices in a mesh: rep: 4 (over y, x), fsdp: 8 (over z, core).
Axes of the slice: x: 2, y: 2, z: 4, core: 2. Of those that a mesh axis runs over, the one named last changes fastest.
Arguments:
- tokens: bfloat16 [4, 4096, 1024], P('rep', 'fsdp'), may hold values from -6 to 6
- image_ids: int32 [4, 4096], P('rep', 'fsdp'), may hold values from 0 to 4, never falling along the last dimension, each value on 1 to 1024 neighbouring positions
- ln1_gain: bfloat16 [1024], P('fsdp'), may hold values from 0.099609375 to 1.8984375
- ln1_bias: bfloat16 [1024], P('fsdp'), may hold values from -3 to 3
- qkv_weight: bfloat16 [1024, 3072], P('fsdp'), may hold values from -0.1875 to 0.1875
- query_bias: bfloat16 [1024], P('fsdp'), may hold values from -3 to 3
- value_bias: bfloat16 [1024], P('fsdp'), may hold values from -3 to 3
- proj_weight: bfloat16 [1024, 1024], P('fsdp'), may hold values from -1.5 to 1.5
- proj_bias: bfloat16 [1024], P('fsdp'), may hold values from -3 to 3
- scale_attn: bfloat16 [1024], P('fsdp'), may hold values from 0.5 to 1.5
- ln2_gain: bfloat16 [1024], P('fsdp'), may hold values from 0.099609375 to 1.8984375
- ln2_bias: bfloat16 [1024], P('fsdp'), may hold values from -3 to 3
- fc1_weight: bfloat16 [1024, 4096], P('fsdp'), may hold values from -0.1875 to 0.1875
- fc1_bias: bfloat16 [4096], P('fsdp'), may hold values from -3 to 3
- fc2_weight: bfloat16 [4096, 1024], P('fsdp'), may hold values from -0.09375 to 0.09375
- fc2_bias: bfloat16 [1024], P('fsdp'), may hold values from -3 to 3
- scale_mlp: bfloat16 [1024], P('fsdp'), may hold values from 0.5 to 1.5
- cotangent: bfloat16 [4, 4096, 1024], P('rep', 'fsdp'), may hold values from -6 to 6
Outputs:
- output: bfloat16 [4, 4096, 1024], P('rep', 'fsdp')
- input_grad: float32 [4, 4096, 1024], P('rep', 'fsdp')
- grad_ln1_gain: float32 [1024], P('fsdp')
- grad_ln1_bias: float32 [1024], P('fsdp')
- grad_qkv_weight: float32 [1024, 3072], P('fsdp')
- grad_query_bias: float32 [1024], P('fsdp')
- grad_value_bias: float32 [1024], P('fsdp')
- grad_proj_weight: float32 [1024, 1024], P('fsdp')
- grad_proj_bias: float32 [1024], P('fsdp')
- grad_scale_attn: float32 [1024], P('fsdp')
- grad_ln2_gain: float32 [1024], P('fsdp')
- grad_ln2_bias: float32 [1024], P('fsdp')
- grad_fc1_weight: float32 [1024, 4096], P('fsdp')
- grad_fc1_bias: float32 [4096], P('fsdp')
- grad_fc2_weight: float32 [4096, 1024], P('fsdp')
- grad_fc2_bias: float32 [1024], P('fsdp')
- grad_scale_mlp: float32 [1024], P('fsdp')
Inputs may be any that keep to these rules, and one draw needn't show every extreme that they name: `image_ids`: within each replica group the image numbers never fall along the tokens, every number from 0 up is used, and each image holds 1 to 1024 tokens, one of them exactly 1024.
All inputs are finite; a program needn't handle non-finite values.
Results may differ from a plain program's by a relative error of at most 0.012.
The roundings to bfloat16 on the way count: a program that leaves them out, or rounds other values in their place, can miss the bound.
Values may be sent and summed in bfloat16 or wider, within the bound.
No kernel may reach another device: no remote copies, remote signals or barrier semaphores. Data moves between devices by JAX's collectives and lax.ppermute only.
A program may use at most 256 MiB of HBM per device.

v0:
```python
import math

import jax
import jax.numpy as jnp
from jax import lax
from jax.sharding import PartitionSpec as P

D = 1024
HEADS = 16
HEAD_DIM = 64


EPSILON = 1e-06
MASKED = -1e30
NEIGHBOURS = (-2, -1, 1, 2)


def from_behind(shard, axis, by):
    size = lax.axis_size(axis)
    pairs = [(i, i + by) for i in range(size) if 0 <= i + by < size]
    return lax.ppermute(shard, axis, pairs)


def layer_norm(features, gain_vec, bias_vec):
    row_mean = jnp.mean(features, axis=-1, keepdims=True)
    centred = features - row_mean
    variance = jnp.mean(centred * centred, axis=-1, keepdims=True)
    inverse = lax.rsqrt(variance + EPSILON)
    normal = centred * inverse
    return (normal * gain_vec + bias_vec, normal, inverse)


def norm_back(gradient, normal, inverse, gain_vec):
    scaled = gradient * gain_vec
    mean_first = jnp.mean(scaled, axis=-1, keepdims=True)
    mean_second = jnp.mean(scaled * normal, axis=-1, keepdims=True)
    return inverse * (scaled - mean_first - normal * mean_second)


def gelu_pair(values):
    cumulative = 0.5 * (1.0 + lax.erf(values * 2.0 ** (-0.5)))
    density = jnp.exp(-0.5 * values * values) * (2.0 * math.pi) ** (-0.5)
    return (values * cumulative, cumulative + values * density)


def split_heads(matrix):
    return matrix.reshape(matrix.shape[0], HEADS, HEAD_DIM)


def masked_scores(query_heads, key_rows, query_tag, key_tag):
    scores = jnp.einsum(
        "qhd,khd->hqk", query_heads, split_heads(key_rows), preferred_element_type=jnp.float32
    ) * HEAD_DIM ** (-0.5)
    same_image = query_tag[:, None] == key_tag[None, :]
    return jnp.where(same_image[None], scores, MASKED)


def touches(own_tag, other_tag):
    return jnp.logical_and(other_tag[0] <= own_tag[-1], other_tag[-1] >= own_tag[0])


def on_device(
    tokens,
    image_ids,
    ln1_gain,
    ln1_bias,
    qkv_weight,
    query_bias,
    value_bias,
    proj_weight,
    proj_bias,
    scale_attn,
    ln2_gain,
    ln2_bias,
    fc1_weight,
    fc1_bias,
    fc2_weight,
    fc2_bias,
    scale_mlp,
    cotangent,
):
    (
        attn_gain,
        attn_shift,
        qkv_matrix,
        query_shift,
        value_shift,
        proj_matrix,
        proj_shift,
        attn_scale,
        mlp_gain,
        mlp_shift,
        fc1_matrix,
        fc1_shift,
        fc2_matrix,
        fc2_shift,
        mlp_scale,
    ) = (
        lax.all_gather(ln1_gain, "fsdp", axis=0, tiled=True),
        lax.all_gather(ln1_bias, "fsdp", axis=0, tiled=True),
        lax.all_gather(qkv_weight, "fsdp", axis=0, tiled=True),
        lax.all_gather(query_bias, "fsdp", axis=0, tiled=True),
        lax.all_gather(value_bias, "fsdp", axis=0, tiled=True),
        lax.all_gather(proj_weight, "fsdp", axis=0, tiled=True),
        lax.all_gather(proj_bias, "fsdp", axis=0, tiled=True),
        lax.all_gather(scale_attn, "fsdp", axis=0, tiled=True),
        lax.all_gather(ln2_gain, "fsdp", axis=0, tiled=True),
        lax.all_gather(ln2_bias, "fsdp", axis=0, tiled=True),
        lax.all_gather(fc1_weight, "fsdp", axis=0, tiled=True),
        lax.all_gather(fc1_bias, "fsdp", axis=0, tiled=True),
        lax.all_gather(fc2_weight, "fsdp", axis=0, tiled=True),
        lax.all_gather(fc2_bias, "fsdp", axis=0, tiled=True),
        lax.all_gather(scale_mlp, "fsdp", axis=0, tiled=True),
    )
    features = tokens[0].astype(jnp.float32)
    image_tag = (image_ids[0] + 1).astype(jnp.bfloat16)
    token_count = features.shape[0]
    attn_input, attn_normal, attn_inverse = layer_norm(
        features, attn_gain.astype(jnp.float32), attn_shift.astype(jnp.float32)
    )
    attn_input = attn_input.astype(jnp.bfloat16)
    qkv_full = jnp.dot(attn_input, qkv_matrix, preferred_element_type=jnp.float32)
    queries = (qkv_full[:, :D] + query_shift.astype(jnp.float32)).astype(jnp.bfloat16)
    key_rows = qkv_full[:, D : 2 * D].astype(jnp.bfloat16)
    value_rows = (qkv_full[:, 2 * D :] + value_shift.astype(jnp.float32)).astype(jnp.bfloat16)
    query_heads = split_heads(queries)
    own_piece = (key_rows, value_rows, image_tag)
    remote = [
        from_behind((key_rows, value_rows, image_tag), "fsdp", distance) for distance in NEIGHBOURS
    ]

    def add_stats(current, neighbour):
        row_max, row_sum = current
        scores = masked_scores(query_heads, neighbour[0], image_tag, neighbour[2])
        new_max = jnp.maximum(row_max, jnp.max(scores, axis=-1))
        row_sum = row_sum * jnp.exp(row_max - new_max) + jnp.sum(
            jnp.exp(scores - new_max[..., None]), axis=-1
        )
        return (new_max, row_sum)

    own_scores = masked_scores(query_heads, key_rows, image_tag, image_tag)
    own_max = jnp.max(own_scores, axis=-1)
    current = (own_max, jnp.sum(jnp.exp(own_scores - own_max[..., None]), axis=-1))
    for neighbour in remote:
        current = lax.cond(
            touches(image_tag, neighbour[2]),
            add_stats,
            lambda kept, unused: kept,
            current,
            neighbour,
        )
    log_total = current[0] + jnp.log(current[1])

    def add_context(context_sum, neighbour):
        scores = masked_scores(query_heads, neighbour[0], image_tag, neighbour[2])
        attn_probs = jnp.exp(scores - log_total[..., None]).astype(jnp.bfloat16)
        return context_sum + jnp.einsum(
            "hqk,khd->qhd",
            attn_probs,
            split_heads(neighbour[1]),
            preferred_element_type=jnp.float32,
        )

    context_sum = add_context(jnp.zeros((token_count, HEADS, HEAD_DIM), jnp.float32), own_piece)
    for neighbour in remote:
        context_sum = lax.cond(
            touches(image_tag, neighbour[2]),
            add_context,
            lambda kept, unused: kept,
            context_sum,
            neighbour,
        )
    context = context_sum.reshape(token_count, D).astype(jnp.bfloat16)
    attn_out = jnp.dot(
        context, proj_matrix, preferred_element_type=jnp.float32
    ) + proj_shift.astype(jnp.float32)
    resid = features + attn_scale.astype(jnp.float32) * attn_out
    mlp_input, mlp_normal, mlp_inverse = layer_norm(
        resid, mlp_gain.astype(jnp.float32), mlp_shift.astype(jnp.float32)
    )
    mlp_input = mlp_input.astype(jnp.bfloat16)
    pre_act = jnp.dot(mlp_input, fc1_matrix, preferred_element_type=jnp.float32) + fc1_shift.astype(
        jnp.float32
    )
    activated, slope = gelu_pair(pre_act)
    activated = activated.astype(jnp.bfloat16)
    mlp_out = jnp.dot(activated, fc2_matrix, preferred_element_type=jnp.float32) + fc2_shift.astype(
        jnp.float32
    )
    output_rows = (resid + mlp_scale.astype(jnp.float32) * mlp_out).astype(jnp.bfloat16)
    (
        attn_gain,
        attn_shift,
        qkv_matrix,
        query_shift,
        value_shift,
        proj_matrix,
        proj_shift,
        attn_scale,
        mlp_gain,
        mlp_shift,
        fc1_matrix,
        fc1_shift,
        fc2_matrix,
        fc2_shift,
        mlp_scale,
    ) = (
        lax.all_gather(ln1_gain, "fsdp", axis=0, tiled=True),
        lax.all_gather(ln1_bias, "fsdp", axis=0, tiled=True),
        lax.all_gather(qkv_weight, "fsdp", axis=0, tiled=True),
        lax.all_gather(query_bias, "fsdp", axis=0, tiled=True),
        lax.all_gather(value_bias, "fsdp", axis=0, tiled=True),
        lax.all_gather(proj_weight, "fsdp", axis=0, tiled=True),
        lax.all_gather(proj_bias, "fsdp", axis=0, tiled=True),
        lax.all_gather(scale_attn, "fsdp", axis=0, tiled=True),
        lax.all_gather(ln2_gain, "fsdp", axis=0, tiled=True),
        lax.all_gather(ln2_bias, "fsdp", axis=0, tiled=True),
        lax.all_gather(fc1_weight, "fsdp", axis=0, tiled=True),
        lax.all_gather(fc1_bias, "fsdp", axis=0, tiled=True),
        lax.all_gather(fc2_weight, "fsdp", axis=0, tiled=True),
        lax.all_gather(fc2_bias, "fsdp", axis=0, tiled=True),
        lax.all_gather(scale_mlp, "fsdp", axis=0, tiled=True),
    )
    factor = 1.0 / math.sqrt(token_count * lax.axis_size("fsdp") * lax.axis_size("rep"))
    out_grad = cotangent[0].astype(jnp.float32)
    mlp_grad_full = out_grad * mlp_scale.astype(jnp.float32)
    mlp_grad = mlp_grad_full.astype(jnp.bfloat16)
    pre_grad_full = (
        jnp.einsum("te,fe->tf", mlp_grad, fc2_matrix, preferred_element_type=jnp.float32) * slope
    )
    pre_grad = pre_grad_full.astype(jnp.bfloat16)
    mlp_in_grad = jnp.einsum("tf,df->td", pre_grad, fc1_matrix, preferred_element_type=jnp.float32)
    resid_grad = out_grad + norm_back(
        mlp_in_grad, mlp_normal, mlp_inverse, mlp_gain.astype(jnp.float32)
    )
    mlp_terms = (
        jnp.sum(mlp_in_grad * mlp_normal, axis=0) * factor,
        jnp.sum(mlp_in_grad, axis=0) * factor,
        jnp.einsum("td,tf->df", mlp_input, pre_grad, preferred_element_type=jnp.float32) * factor,
        jnp.sum(pre_grad_full, axis=0) * factor,
        jnp.einsum("tf,te->fe", activated, mlp_grad, preferred_element_type=jnp.float32) * factor,
        jnp.sum(mlp_grad_full, axis=0) * factor,
        jnp.sum(out_grad * mlp_out, axis=0) * factor,
    )
    attn_grad_full = resid_grad * attn_scale.astype(jnp.float32)
    attn_grad = attn_grad_full.astype(jnp.bfloat16)
    context_grad = jnp.einsum(
        "te,de->td", attn_grad, proj_matrix, preferred_element_type=jnp.float32
    ).astype(jnp.bfloat16)
    row_delta = jnp.sum(
        split_heads(context_grad.astype(jnp.float32) * context.astype(jnp.float32)), axis=-1
    ).T
    grad_heads = split_heads(context_grad)
    score_scale = HEAD_DIM ** (-0.5)

    def piece_grads(neighbour):
        scores = masked_scores(query_heads, neighbour[0], image_tag, neighbour[2])
        exact_probs = jnp.exp(scores - log_total[..., None])
        prob_grad = jnp.einsum(
            "qhd,khd->hqk",
            grad_heads,
            split_heads(neighbour[1]),
            preferred_element_type=jnp.float32,
        )
        score_grad = (exact_probs * (prob_grad - row_delta[..., None]) * score_scale).astype(
            jnp.bfloat16
        )
        query_part = jnp.einsum(
            "hqk,khd->qhd",
            score_grad,
            split_heads(neighbour[0]),
            preferred_element_type=jnp.float32,
        )
        key_part = jnp.einsum(
            "hqk,qhd->khd", score_grad, query_heads, preferred_element_type=jnp.float32
        )
        value_part = jnp.einsum(
            "hqk,qhd->khd",
            exact_probs.astype(jnp.bfloat16),
            grad_heads,
            preferred_element_type=jnp.float32,
        )
        return (query_part, key_part.reshape(-1, D), value_part.reshape(-1, D))

    query_grad, key_grad, value_grad = piece_grads(own_piece)
    nothing = (
        jnp.zeros((token_count, HEADS, HEAD_DIM), jnp.float32),
        jnp.zeros((token_count, D), jnp.float32),
        jnp.zeros((token_count, D), jnp.float32),
    )
    for distance, neighbour in zip(NEIGHBOURS, remote):
        query_part, key_part, value_part = lax.cond(
            touches(image_tag, neighbour[2]), piece_grads, lambda unused: nothing, neighbour
        )
        query_grad = query_grad + query_part
        key_back, value_back = (
            from_behind(key_part.astype(jnp.bfloat16), "fsdp", -distance).astype(key_part.dtype),
            from_behind(value_part.astype(jnp.bfloat16), "fsdp", -distance).astype(
                value_part.dtype
            ),
        )
        key_grad = key_grad + key_back
        value_grad = value_grad + value_back
    query_grad = query_grad.reshape(token_count, D)
    qkv_grad = jnp.concatenate([query_grad, key_grad, value_grad], axis=1).astype(jnp.bfloat16)
    attn_in_grad = jnp.einsum("tf,df->td", qkv_grad, qkv_matrix, preferred_element_type=jnp.float32)
    input_rows = resid_grad + norm_back(
        attn_in_grad, attn_normal, attn_inverse, attn_gain.astype(jnp.float32)
    )
    attn_terms = (
        jnp.sum(attn_in_grad * attn_normal, axis=0) * factor,
        jnp.sum(attn_in_grad, axis=0) * factor,
        jnp.einsum("td,tf->df", attn_input, qkv_grad, preferred_element_type=jnp.float32) * factor,
        jnp.sum(query_grad, axis=0) * factor,
        jnp.sum(value_grad, axis=0) * factor,
        jnp.einsum("td,te->de", context, attn_grad, preferred_element_type=jnp.float32) * factor,
        jnp.sum(attn_grad_full, axis=0) * factor,
        jnp.sum(resid_grad * attn_out, axis=0) * factor,
    )
    owned = (
        lax.psum_scatter(attn_terms[0], "fsdp", scatter_dimension=0, tiled=True),
        lax.psum_scatter(attn_terms[1], "fsdp", scatter_dimension=0, tiled=True),
        lax.psum_scatter(attn_terms[2], "fsdp", scatter_dimension=0, tiled=True),
        lax.psum_scatter(attn_terms[3], "fsdp", scatter_dimension=0, tiled=True),
        lax.psum_scatter(attn_terms[4], "fsdp", scatter_dimension=0, tiled=True),
        lax.psum_scatter(attn_terms[5], "fsdp", scatter_dimension=0, tiled=True),
        lax.psum_scatter(attn_terms[6], "fsdp", scatter_dimension=0, tiled=True),
        lax.psum_scatter(attn_terms[7], "fsdp", scatter_dimension=0, tiled=True),
        lax.psum_scatter(mlp_terms[0], "fsdp", scatter_dimension=0, tiled=True),
        lax.psum_scatter(mlp_terms[1], "fsdp", scatter_dimension=0, tiled=True),
        lax.psum_scatter(mlp_terms[2], "fsdp", scatter_dimension=0, tiled=True),
        lax.psum_scatter(mlp_terms[3], "fsdp", scatter_dimension=0, tiled=True),
        lax.psum_scatter(mlp_terms[4], "fsdp", scatter_dimension=0, tiled=True),
        lax.psum_scatter(mlp_terms[5], "fsdp", scatter_dimension=0, tiled=True),
        lax.psum_scatter(mlp_terms[6], "fsdp", scatter_dimension=0, tiled=True),
    )
    (
        grad_attn_gain,
        grad_attn_shift,
        grad_qkv_matrix,
        grad_query_shift,
        grad_value_shift,
        grad_proj_matrix,
        grad_proj_shift,
        grad_attn_scale,
        grad_mlp_gain,
        grad_mlp_shift,
        grad_fc1_matrix,
        grad_fc1_shift,
        grad_fc2_matrix,
        grad_fc2_shift,
        grad_mlp_scale,
    ) = lax.psum(
        (
            owned[0],
            owned[1],
            owned[2],
            owned[3],
            owned[4],
            owned[5],
            owned[6],
            owned[7],
            owned[8],
            owned[9],
            owned[10],
            owned[11],
            owned[12],
            owned[13],
            owned[14],
        ),
        "rep",
    )
    return (
        output_rows[None],
        input_rows[None],
        grad_attn_gain,
        grad_attn_shift,
        grad_qkv_matrix,
        grad_query_shift,
        grad_value_shift,
        grad_proj_matrix,
        grad_proj_shift,
        grad_attn_scale,
        grad_mlp_gain,
        grad_mlp_shift,
        grad_fc1_matrix,
        grad_fc1_shift,
        grad_fc2_matrix,
        grad_fc2_shift,
        grad_mlp_scale,
    )


def solution(mesh):
    placed = (
        P("rep", "fsdp", None),
        P("rep", "fsdp"),
        P("fsdp"),
        P("fsdp"),
        P("fsdp", None),
        P("fsdp"),
        P("fsdp"),
        P("fsdp", None),
        P("fsdp"),
        P("fsdp"),
        P("fsdp"),
        P("fsdp"),
        P("fsdp", None),
        P("fsdp"),
        P("fsdp", None),
        P("fsdp"),
        P("fsdp"),
        P("rep", "fsdp", None),
    )
    return jax.shard_map(
        on_device,
        mesh=mesh,
        in_specs=placed,
        out_specs=(
            P("rep", "fsdp", None),
            P("rep", "fsdp", None),
            P("fsdp"),
            P("fsdp"),
            P("fsdp", None),
            P("fsdp"),
            P("fsdp"),
            P("fsdp", None),
            P("fsdp"),
            P("fsdp"),
            P("fsdp"),
            P("fsdp"),
            P("fsdp", None),
            P("fsdp"),
            P("fsdp", None),
            P("fsdp"),
            P("fsdp"),
        ),
        check_vma=False,
    )
```

profile of v0, /device:TPU:0, one launch (start us, length us, event | category | flops | bytes accessed | tf_op | source)
XLA Modules:
  0.0 1335.7 jit_solution(5482529630284199184)
XLA Ops:
  19.8 16.4 %all-gather.10 = bf16[8,1,128]{2,1,0:T(2,128)(2,1)S(1)} all-gather(bf16[1,1,128]{2,1,0:T(2,128)(2,1)} %bitcast.354), channel_id=1, replica_groups=mesh['rep'=4,'fsdp'=8] {'fsdp'}, dimensions={0}, use_global_device_ids=true | all-gather | bytes 2304 | tf_op jit(solution)/shard_map/all_gather | solution.py:112
  36.7 9.3 all-gather.6
  46.1 10.6 all-gather.5
  57.2 9.2 all-gather
  66.5 11.2 all-gather.2
  77.7 8.9 all-gather.1
  86.6 10.5 all-gather.4
  97.1 9.5 all-gather.3
  106.6 9.7 all-gather.7
  117.0 13.3 all-gather.9
  135.0 9.3 all-gather.8
  157.7 6.1 fusion.97
  189.6 7.4 fusion.41
  197.0 9.2 exponential_reduce_fusion.4
  210.3 61.5 %collective-permute-start.10 = (bf16[512,1024]{1,0:T(8,128)(2,1)}, bf16[512,1024]{1,0:T(8,128)(2,1)}, u32[]{:S(2)}, u32[]{:S(2)}) collective-permute-start(bf16[512,1024]{1,0:T(8,128)(2,1)} %get-tuple-element.668), channel_id=1, source_target_pairs={{0,1},{1,2},{2,3},{3,4},{4,5},{5,6},{6,7},{8,9},{9,10},{10,11},{11... | collective-permute-start | bytes 3145736 | tf_op jit(solution)/shard_map/ppermute | solution.py:21
  271.8 20.1 %conditional.13 = ((f32[16,512]{1,0:T(8,128)S(1)}, f32[16,512]{1,0:T(8,128)S(1)})) conditional(s32[]{:T(128)} %bitcast.51, (f32[16,512]{1,0:T(8,128)S(1)}, f32[16,512]{1,0:T(8,128)S(1)}) %get-tuple-element.761, (bf16[512]{0:T(512)(128)(2,1)S(1)}, bf16[512]{0:T(512)(128)(2,1)S(1)}, bf16[512,1024]{1,0:T(8,128)(2,1)}, ...), branch_computations={%region_8.9_spmd, %region_9.12_spmd} | conditional | flops 566509568 | bytes 38963224 | solution.py:145
  274.2 8.4 fusion.1
  282.7 9.2 exponential_reduce_fusion.1
  294.4 8.8 conditional.15
  303.2 11.6 convolution_bitcast_fusion.4
  314.9 12.8 conditional.17
  318.1 9.5 bitcast_add_fusion.1
  335.8 11.2 multiply_convert_fusion.5
  346.9 11.7 fusion.111
  358.6 11.8 multiply_reduce_fusion
  370.5 10.1 fusion.66
  409.5 44.3 %conditional.21 = (f32[512,16,64]{0,2,1:T(8,128)}, bf16[512,1024]{0,1:T(8,128)(2,1)}, bf16[512,1024]{0,1:T(8,128)(2,1)}) conditional(s32[]{:T(128)} %bitcast.51, () %tuple.120, (bf16[512]{0:T(512)(128)(2,1)S(1)}, bf16[512]{0:T(512)(128)(2,1)S(1)}, bf16[512,1024]{1,0:T(8,128)(2,1)}, bf16[512,16,64]{0,2,1:T(8,128)(2,1)S(1)}, ...), branch_computations={%region_35.36_spmd, %region_36.37_spmd} | conditional | flops 2730754048 | bytes 96307248 | solution.py:292
  416.7 8.1 fusion.114
  427.4 10.5 multiply_convert_fusion.1
  444.3 9.5 fusion.23
  453.8 9.5 collective-permute-start.17
  467.4 50.1 %collective-permute-start.16 = (bf16[512,1024]{0,1:T(8,128)(2,1)}, bf16[512,1024]{0,1:T(8,128)(2,1)}, u32[]{:S(2)}, u32[]{:S(2)}) collective-permute-start(bf16[512,1024]{0,1:T(8,128)(2,1)} %get-tuple-element.353), channel_id=1, source_target_pairs={{0,2},{1,3},{2,4},{3,5},{4,6},{5,7},{8,10},{9,11},{10,12},{11,13},... | collective-permute-start | bytes 3145736 | tf_op jit(solution)/shard_map/ppermute | solution.py:21
  518.8 14.2 %multiply_convert_fusion.4 = bf16[16,512,512]{1,2,0:T(8,128)(2,1)} fusion(f32[16,512,512]{1,2,0:T(8,128)} %get-tuple-element.684, bf16[512,16,64]{0,2,1:T(8,128)(2,1)} %bitcast.309, bf16[512,16,64]{0,2,1:T(8,128)(2,1)} %bitcast.304, f32[16,512]{1,0:T(8,128)} %bitcast.327, f32[16,512]{1,0:T(8,128)} %copy-done.24, pred[512,512]{0,1:T(8,128)(4,1)} %copy-done.10), kind=kOutput, calls=%fused_computation.80 | convolution fusion | flops 566231040 | bytes 27590656 | tf_op jit(solution)/shard_map/qhd,khd->hqk/dot_general | solution.py:259
  533.1 6.7 fusion.120
  539.8 6.4 fusion.86
  547.8 14.2 %collective-permute-start.13 = (bf16[512,1024]{0,1:T(8,128)(2,1)}, bf16[512,1024]{0,1:T(8,128)(2,1)S(1)}, u32[]{:S(2)}, u32[]{:S(2)}) collective-permute-start(bf16[512,1024]{0,1:T(8,128)(2,1)} %get-tuple-element.350), channel_id=1, source_target_pairs={{0,1},{1,2},{2,3},{3,4},{4,5},{5,6},{6,7},{8,9},{9,10},{10,11},{11... | collective-permute-start | bytes 3145736 | tf_op jit(solution)/shard_map/ppermute | solution.py:21
  562.0 39.7 %collective-permute-start.12 = (bf16[512,1024]{0,1:T(8,128)(2,1)}, bf16[512,1024]{0,1:T(8,128)(2,1)S(1)}, u32[]{:S(2)}, u32[]{:S(2)}) collective-permute-start(bf16[512,1024]{0,1:T(8,128)(2,1)} %get-tuple-element.349), channel_id=1, source_target_pairs={{0,2},{1,3},{2,4},{3,5},{4,6},{5,7},{8,10},{9,11},{10,12},{11,13},... | collective-permute-start | bytes 3145736 | tf_op jit(solution)/shard_map/ppermute | solution.py:21
  612.0 13.3 collective-permute-done.12
  628.4 9.6 convolution_multiply_fusion.1
  639.7 10.5 convolution_multiply_fusion
  651.4 10.4 broadcast_multiply_fusion
  661.9 179.0 %reduce-scatter.5.cloned.1.call-done = f32[128,3072]{1,0:T(8,128)} async-done(((f32[1024,3072]{1,0:T(8,128)}), f32[128,3072]{1,0:T(8,128)}) %reduce-scatter.5.cloned.1.call-update) | async-done | bytes 1572880 | tf_op jit(solution)/shard_map/reduce_scatter | solution.py:323
  841.0 169.0 %reduce-scatter.9.cloned.1.call-done = f32[128,4096]{1,0:T(8,128)} async-done(((f32[1024,4096]{1,0:T(8,128)}), f32[128,4096]{1,0:T(8,128)}) %reduce-scatter.9.cloned.1.call-update) | async-done | bytes 2097168 | tf_op jit(solution)/shard_map/reduce_scatter | solution.py:331
  1010.0 169.0 %reduce-scatter.11.cloned.1.call-done = f32[512,1024]{1,0:T(8,128)} async-done(((f32[4096,1024]{1,0:T(8,128)}), f32[512,1024]{1,0:T(8,128)}) %reduce-scatter.11.cloned.1.call-update) | async-done | bytes 2097168 | tf_op jit(solution)/shard_map/reduce_scatter | solution.py:333
  1181.1 9.2 fusion.64
  1190.3 26.4 %all-reduce.11 = (f32[1024]{0:T(1024)S(1)}, f32[1024]{0:T(1024)S(1)}, f32[1024]{0:T(1024)S(1)}, f32[1024]{0:T(1024)S(1)}, f32[1024]{0:T(1024)S(1)}, /*index=5*/f...) all-reduce(f32[1024]{0:T(1024)S(1)} %broadcast_multiply_fusion.11, ...), channel_id=2, replica_groups=mesh['rep'=4,'fsdp'=8] {'fsdp'}, use_global_device_ids=true, to_apply=%region_44.45.clone | all-reduce | flops 14336 | bytes 114688
  1217.6 10.8 all-reduce.12
  1232.2 87.6 %all-reduce.16.cloned.1.call-done = (f32[128,3072]{1,0:T(8,128)}, f32[128,1024]{1,0:T(8,128)}, f32[128,4096]{1,0:T(8,128)}, f32[512,1024]{1,0:T(8,128)}) async-done(((f32[128,3072]{1,0:T(8,128)}, f32[128,1024]{1,0:T(8,128)}, f32[128,4096]{1,0:T(8,128)}, f32[512,1024]{1,0:T(8,128)}), (f32[128,3072]{1,0:T(8,128)}, f32[128,1024]{1,0:T(8,128)}, f32[128,4096]{1,0:T(8,128)}, ...) | async-done | bytes 6291472 | tf_op jit(solution)/shard_map/psum | solution.py:353
  (287 shorter events, 156.1 us)
Async XLA Ops:
  7.2 150.5 %all-gather.16.cloned.1.call-start = ((), (), s32[]{:S(2)}) async-start(), calls=%async_computation.4 | async-start | bytes 7077888 | tf_op jit(solution)/shard_map/all_gather | solution.py:101
  7.9 321.8 %all-gather.18.cloned.1.call-start = ((), (), s32[]{:S(2)}) async-start(), calls=%async_computation.5 | async-start | bytes 2359296 | tf_op jit(solution)/shard_map/all_gather | solution.py:104
  8.7 327.1 %all-gather.20.cloned.1.call-start = ((), (), s32[]{:S(2)}) async-start(), calls=%async_computation.6 | async-start | bytes 9437184 | tf_op jit(solution)/shard_map/all_gather | solution.py:109
  9.4 337.5 %all-gather.22.cloned.1.call-start = ((), (), s32[]{:S(2)}) async-start(), calls=%async_computation.7 | async-start | bytes 9437184 | tf_op jit(solution)/shard_map/all_gather | solution.py:111
  10.0 651.9 %reduce-scatter.7.cloned.1.call-start = ((), (), s32[]{:S(2)}) async-start(), calls=%async_computation.9 | async-start | bytes 4718592 | tf_op jit(solution)/shard_map/reduce_scatter | solution.py:326
  10.7 134.1 %collective-permute-start = (bf16[512]{0:T(512)(128)(2,1)S(1)}, bf16[512]{0:T(512)(128)(2,1)S(1)}, u32[]{:S(2)}, u32[]{:S(2)}) collective-permute-start(bf16[512]{0:T(512)(128)(2,1)S(1)} %fusion.95), channel_id=1, source_target_pairs={{0,2},{1,3},{2,4},{3,5},{4,6},{5,7},{8,10},{9,11},{10,12},{11,13},... | collective-permute-start | bytes 3080 | tf_op jit(solution)/shard_map/ppermute | solution.py:21
  15.7 129.7 %collective-permute-start.1 = (bf16[512]{0:T(512)(128)(2,1)S(1)}, bf16[512]{0:T(512)(128)(2,1)S(1)}, u32[]{:S(2)}, u32[]{:S(2)}) collective-permute-start(bf16[512]{0:T(512)(128)(2,1)S(1)} %fusion.95), channel_id=1, source_target_pairs={{0,1},{1,2},{2,3},{3,4},{4,5},{5,6},{6,7},{8,9},{9,10},{10,11},{11... | collective-permute-start | bytes 3080 | tf_op jit(solution)/shard_map/ppermute | solution.py:21
  17.2 128.9 %collective-permute-start.2 = (bf16[512]{0:T(512)(128)(2,1)S(1)}, bf16[512]{0:T(512)(128)(2,1)S(1)}, u32[]{:S(2)}, u32[]{:S(2)}) collective-permute-start(bf16[512]{0:T(512)(128)(2,1)S(1)} %fusion.95), channel_id=1, source_target_pairs={{1,0},{2,1},{3,2},{4,3},{5,4},{6,5},{7,6},{9,8},{10,9},{11,10},{12... | collective-permute-start | bytes 3080 | tf_op jit(solution)/shard_map/ppermute | solution.py:21
  18.5 136.0 %collective-permute-start.3 = (bf16[512]{0:T(512)(128)(2,1)S(1)}, bf16[512]{0:T(512)(128)(2,1)S(1)}, u32[]{:S(2)}, u32[]{:S(2)}) collective-permute-start(bf16[512]{0:T(512)(128)(2,1)S(1)} %fusion.95), channel_id=1, source_target_pairs={{2,0},{3,1},{4,2},{5,3},{6,4},{7,5},{10,8},{11,9},{12,10},{13,11},... | collective-permute-start | bytes 3080 | tf_op jit(solution)/shard_map/ppermute | solution.py:21
  46.1 324.3 %copy-start.36 = (f32[8,1,128]{2,1,0:T(1,128)}, f32[8,1,128]{2,1,0:T(1,128)S(1)}, u32[]{:S(2)}) copy-start(f32[8,1,128]{2,1,0:T(1,128)S(1)} %convert_element_type.301) | copy-start | bytes 12292
  77.7 86.1 %copy-start.38 = (f32[8,1,128]{2,1,0:T(1,128)}, f32[8,1,128]{2,1,0:T(1,128)S(1)}, u32[]{:S(2)}) copy-start(f32[8,1,128]{2,1,0:T(1,128)S(1)} %convert_element_type.297) | copy-start | bytes 12292
  86.6 77.2 %copy-start.29 = (f32[8,1,128]{2,1,0:T(1,128)}, f32[8,1,128]{2,1,0:T(1,128)S(1)}, u32[]{:S(2)}) copy-start(f32[8,1,128]{2,1,0:T(1,128)S(1)} %convert_element_type.296) | copy-start | bytes 12292
  116.3 254.1 %copy-start.40 = (f32[8,1,128]{2,1,0:T(1,128)}, f32[8,1,128]{2,1,0:T(1,128)S(1)}, u32[]{:S(2)}) copy-start(f32[8,1,128]{2,1,0:T(1,128)S(1)} %convert_element_type.302) | copy-start | bytes 12292
  134.9 168.2 %copy-start.10 = (pred[512,512]{0,1:T(8,128)(4,1)}, pred[512,512]{0,1:T(8,128)(4,1)S(1)}, u32[]{:S(2)}) copy-start(pred[512,512]{0,1:T(8,128)(4,1)S(1)} %broadcast_compare_fusion.12) | copy-start | bytes 786436
  154.4 160.4 %copy-start.27 = (bf16[512]{0:T(512)(128)(2,1)}, bf16[512]{0:T(512)(128)(2,1)S(1)}, u32[]{:S(2)}) copy-start(bf16[512]{0:T(512)(128)(2,1)S(1)} %collective-permute-done.3) | copy-start | bytes 3076
  169.1 39.7 %collective-permute-start.4 = (bf16[512,1024]{1,0:T(8,128)(2,1)}, bf16[512,1024]{1,0:T(8,128)(2,1)S(1)}, u32[]{:S(2)}, u32[]{:S(2)}) collective-permute-start(bf16[512,1024]{1,0:T(8,128)(2,1)} %slice.111), channel_id=1, source_target_pairs={{2,0},{3,1},{4,2},{5,3},{6,4},{7,5},{10,8},{11,9},{12,10},{13,11},... | collective-permute-start | bytes 3145736 | tf_op jit(solution)/shard_map/ppermute | solution.py:21
  170.4 39.9 %collective-permute-start.5 = (bf16[512,1024]{1,0:T(8,128)(2,1)}, bf16[512,1024]{1,0:T(8,128)(2,1)}, u32[]{:S(2)}, u32[]{:S(2)}) collective-permute-start(bf16[512,1024]{1,0:T(8,128)(2,1)} %slice.111), channel_id=1, source_target_pairs={{1,0},{2,1},{3,2},{4,3},{5,4},{6,5},{7,6},{9,8},{10,9},{11,10},{12... | collective-permute-start | bytes 3145736 | tf_op jit(solution)/shard_map/ppermute | solution.py:21
  171.7 120.2 %collective-permute-start.6 = (bf16[512,1024]{1,0:T(8,128)(2,1)}, bf16[512,1024]{1,0:T(8,128)(2,1)}, u32[]{:S(2)}, u32[]{:S(2)}) collective-permute-start(bf16[512,1024]{1,0:T(8,128)(2,1)} %slice.111), channel_id=1, source_target_pairs={{0,1},{1,2},{2,3},{3,4},{4,5},{5,6},{6,7},{8,9},{9,10},{10,11},{11... | collective-permute-start | bytes 3145736 | tf_op jit(solution)/shard_map/ppermute | solution.py:21
  175.7 118.7 %collective-permute-start.7 = (bf16[512,1024]{1,0:T(8,128)(2,1)}, bf16[512,1024]{1,0:T(8,128)(2,1)}, u32[]{:S(2)}, u32[]{:S(2)}) collective-permute-start(bf16[512,1024]{1,0:T(8,128)(2,1)} %slice.111), channel_id=1, source_target_pairs={{0,2},{1,3},{2,4},{3,5},{4,6},{5,7},{8,10},{9,11},{10,12},{11,13},... | collective-permute-start | bytes 3145736 | tf_op jit(solution)/shard_map/ppermute | solution.py:21
  186.8 128.1 %collective-permute-start.8 = (bf16[512,1024]{1,0:T(8,128)(2,1)}, bf16[512,1024]{1,0:T(8,128)(2,1)}, u32[]{:S(2)}, u32[]{:S(2)}) collective-permute-start(bf16[512,1024]{1,0:T(8,128)(2,1)} %get-tuple-element.668), channel_id=1, source_target_pairs={{2,0},{3,1},{4,2},{5,3},{6,4},{7,5},{10,8},{11,9},{12,10},{13,11},... | collective-permute-start | bytes 3145736 | tf_op jit(solution)/shard_map/ppermute | solution.py:21
  208.8 106.0 %copy-start.2 = (bf16[512,1024]{1,0:T(8,128)(2,1)}, bf16[512,1024]{1,0:T(8,128)(2,1)S(1)}, u32[]{:S(2)}) copy-start(bf16[512,1024]{1,0:T(8,128)(2,1)S(1)} %collective-permute-done.4) | copy-start | bytes 3145732
  208.8 106.1 %collective-permute-start.9 = (bf16[512,1024]{1,0:T(8,128)(2,1)}, bf16[512,1024]{1,0:T(8,128)(2,1)}, u32[]{:S(2)}, u32[]{:S(2)}) collective-permute-start(bf16[512,1024]{1,0:T(8,128)(2,1)} %get-tuple-element.668), channel_id=1, source_target_pairs={{1,0},{2,1},{3,2},{4,3},{5,4},{6,5},{7,6},{9,8},{10,9},{11,10},{12... | collective-permute-start | bytes 3145736 | tf_op jit(solution)/shard_map/ppermute | solution.py:21
  210.3 117.4 %collective-permute-start.10 = (bf16[512,1024]{1,0:T(8,128)(2,1)}, bf16[512,1024]{1,0:T(8,128)(2,1)}, u32[]{:S(2)}, u32[]{:S(2)}) collective-permute-start(bf16[512,1024]{1,0:T(8,128)(2,1)} %get-tuple-element.668), channel_id=1, source_target_pairs={{0,1},{1,2},{2,3},{3,4},{4,5},{5,6},{6,7},{8,9},{9,10},{10,11},{11... | collective-permute-start | bytes 3145736 | tf_op jit(solution)/shard_map/ppermute | solution.py:21
  291.9 35.9 %collective-permute-start.11 = (bf16[512,1024]{1,0:T(8,128)(2,1)}, bf16[512,1024]{1,0:T(8,128)(2,1)}, u32[]{:S(2)}, u32[]{:S(2)}) collective-permute-start(bf16[512,1024]{1,0:T(8,128)(2,1)} %get-tuple-element.668), channel_id=1, source_target_pairs={{0,2},{1,3},{2,4},{3,5},{4,6},{5,7},{8,10},{9,11},{10,12},{11,13},... | collective-permute-start | bytes 3145736 | tf_op jit(solution)/shard_map/ppermute | solution.py:21
  303.1 160.2 %copy-start.24 = (f32[16,512]{1,0:T(8,128)}, f32[16,512]{1,0:T(8,128)S(1)}, u32[]{:S(2)}) copy-start(f32[16,512]{1,0:T(8,128)S(1)} %log_add_fusion) | copy-start | bytes 98308
  385.1 455.8 %reduce-scatter.5.cloned.1.call-start = ((), (), s32[]{:S(2)}) async-start(), calls=%async_computation.8 | async-start | bytes 14155776 | tf_op jit(solution)/shard_map/reduce_scatter | solution.py:323
  398.0 65.4 %copy-start.23 = (f32[512,16]{0,1:T(8,128)}, f32[512,16]{0,1:T(8,128)S(1)}, u32[]{:S(2)}) copy-start(f32[512,16]{0,1:T(8,128)S(1)} %bitcast_reduce_fusion) | copy-start | bytes 98308
  402.2 144.0 %collective-permute-start.19 = (bf16[512,1024]{0,1:T(8,128)(2,1)}, bf16[512,1024]{0,1:T(8,128)(2,1)}, u32[]{:S(2)}, u32[]{:S(2)}) collective-permute-start(bf16[512,1024]{0,1:T(8,128)(2,1)} %get-tuple-element.356), channel_id=1, source_target_pairs={{2,0},{3,1},{4,2},{5,3},{6,4},{7,5},{10,8},{11,9},{12,10},{13,11},... | collective-permute-start | bytes 3145736 | tf_op jit(solution)/shard_map/ppermute | solution.py:21
  408.2 139.6 %collective-permute-start.18 = (bf16[512,1024]{0,1:T(8,128)(2,1)}, bf16[512,1024]{0,1:T(8,128)(2,1)}, u32[]{:S(2)}, u32[]{:S(2)}) collective-permute-start(bf16[512,1024]{0,1:T(8,128)(2,1)} %get-tuple-element.355), channel_id=1, source_target_pairs={{1,0},{2,1},{3,2},{4,3},{5,4},{6,5},{7,6},{9,8},{10,9},{11,10},{12... | collective-permute-start | bytes 3145736 | tf_op jit(solution)/shard_map/ppermute | solution.py:21
  409.5 53.9 %copy-start.3 = (bf16[512,1024]{1,0:T(8,128)(2,1)S(1)}, bf16[512,1024]{1,0:T(8,128)(2,1)}, u32[]{:S(2)}) copy-start(bf16[512,1024]{1,0:T(8,128)(2,1)} %copy-done.2) | copy-start | bytes 3145732
  453.8 108.2 %collective-permute-start.17 = (bf16[512,1024]{0,1:T(8,128)(2,1)}, bf16[512,1024]{0,1:T(8,128)(2,1)}, u32[]{:S(2)}, u32[]{:S(2)}) collective-permute-start(bf16[512,1024]{0,1:T(8,128)(2,1)} %get-tuple-element.354), channel_id=1, source_target_pairs={{0,1},{1,2},{2,3},{3,4},{4,5},{5,6},{6,7},{8,9},{9,10},{10,11},{11... | collective-permute-start | bytes 3145736 | tf_op jit(solution)/shard_map/ppermute | solution.py:21
  467.4 141.6 %collective-permute-start.16 = (bf16[512,1024]{0,1:T(8,128)(2,1)}, bf16[512,1024]{0,1:T(8,128)(2,1)}, u32[]{:S(2)}, u32[]{:S(2)}) collective-permute-start(bf16[512,1024]{0,1:T(8,128)(2,1)} %get-tuple-element.353), channel_id=1, source_target_pairs={{0,2},{1,3},{2,4},{3,5},{4,6},{5,7},{8,10},{9,11},{10,12},{11,13},... | collective-permute-start | bytes 3145736 | tf_op jit(solution)/shard_map/ppermute | solution.py:21
  517.5 94.5 %collective-permute-start.15 = (bf16[512,1024]{0,1:T(8,128)(2,1)}, bf16[512,1024]{0,1:T(8,128)(2,1)}, u32[]{:S(2)}, u32[]{:S(2)}) collective-permute-start(bf16[512,1024]{0,1:T(8,128)(2,1)} %get-tuple-element.352), channel_id=1, source_target_pairs={{2,0},{3,1},{4,2},{5,3},{6,4},{7,5},{10,8},{11,9},{12,10},{13,11},... | collective-permute-start | bytes 3145736 | tf_op jit(solution)/shard_map/ppermute | solution.py:21
  546.2 60.1 %copy-start = (bf16[16,512,512]{1,2,0:T(8,128)(2,1)S(1)}, bf16[16,512,512]{1,2,0:T(8,128)(2,1)}, u32[]{:S(2)}) copy-start(bf16[16,512,512]{1,2,0:T(8,128)(2,1)} %multiply_convert_fusion.4) | copy-start | bytes 25165828
  546.2 65.8 %collective-permute-start.14 = (bf16[512,1024]{0,1:T(8,128)(2,1)}, bf16[512,1024]{0,1:T(8,128)(2,1)S(1)}, u32[]{:S(2)}, u32[]{:S(2)}) collective-permute-start(bf16[512,1024]{0,1:T(8,128)(2,1)} %get-tuple-element.351), channel_id=1, source_target_pairs={{1,0},{2,1},{3,2},{4,3},{5,4},{6,5},{7,6},{9,8},{10,9},{11,10},{12... | collective-permute-start | bytes 3145736 | tf_op jit(solution)/shard_map/ppermute | solution.py:21
  547.8 64.2 %collective-permute-start.13 = (bf16[512,1024]{0,1:T(8,128)(2,1)}, bf16[512,1024]{0,1:T(8,128)(2,1)S(1)}, u32[]{:S(2)}, u32[]{:S(2)}) collective-permute-start(bf16[512,1024]{0,1:T(8,128)(2,1)} %get-tuple-element.350), channel_id=1, source_target_pairs={{0,1},{1,2},{2,3},{3,4},{4,5},{5,6},{6,7},{8,9},{9,10},{10,11},{11... | collective-permute-start | bytes 3145736 | tf_op jit(solution)/shard_map/ppermute | solution.py:21
  562.0 63.3 %collective-permute-start.12 = (bf16[512,1024]{0,1:T(8,128)(2,1)}, bf16[512,1024]{0,1:T(8,128)(2,1)S(1)}, u32[]{:S(2)}, u32[]{:S(2)}) collective-permute-start(bf16[512,1024]{0,1:T(8,128)(2,1)} %get-tuple-element.349), channel_id=1, source_target_pairs={{0,2},{1,3},{2,4},{3,5},{4,6},{5,7},{8,10},{9,11},{10,12},{11,13},... | collective-permute-start | bytes 3145736 | tf_op jit(solution)/shard_map/ppermute | solution.py:21
  638.1 371.9 %reduce-scatter.9.cloned.1.call-start = ((), (), s32[]{:S(2)}) async-start(), calls=%async_computation.10 | async-start | bytes 18874368 | tf_op jit(solution)/shard_map/reduce_scatter | solution.py:331
  650.2 528.8 %reduce-scatter.11.cloned.1.call-start = ((), (), s32[]{:S(2)}) async-start(), calls=%async_computation.11 | async-start | bytes 18874368 | tf_op jit(solution)/shard_map/reduce_scatter | solution.py:333
  661.8 517.3 %copy-start.57 = (u32[32]{0:T(128)S(1)}, u32[32]{0:T(128)}, u32[]{:S(2)}) copy-start(u32[32]{0:T(128)} %constant.120) | copy-start | bytes 388
  661.8 519.2 %copy-start.49 = (f32[1024]{0:T(1024)S(1)}, f32[1024]{0:T(1024)}, u32[]{:S(2)}) copy-start(f32[1024]{0:T(1024)} %get-tuple-element.670) | copy-start | bytes 12292
  661.8 519.2 %copy-start.48 = (f32[1024]{0:T(1024)S(1)}, f32[1024]{0:T(1024)}, u32[]{:S(2)}) copy-start(f32[1024]{0:T(1024)} %get-tuple-element.671) | copy-start | bytes 12292
  661.8 519.2 %copy-start.47 = (f32[1024]{0:T(1024)S(1)}, f32[1024]{0:T(1024)}, u32[]{:S(2)}) copy-start(f32[1024]{0:T(1024)} %get-tuple-element.625) | copy-start | bytes 12292
  661.8 519.3 %copy-start.46 = (f32[1024]{0:T(1024)S(1)}, f32[1024]{0:T(1024)}, u32[]{:S(2)}) copy-start(f32[1024]{0:T(1024)} %get-tuple-element.624) | copy-start | bytes 12292
  661.8 519.3 %copy-start.50 = (f32[1024]{0:T(1024)S(1)}, f32[1024]{0:T(1024)}, u32[]{:S(2)}) copy-start(f32[1024]{0:T(1024)} %get-tuple-element.614) | copy-start | bytes 12292
  661.8 519.3 %copy-start.51 = (f32[1024]{0:T(1024)S(1)}, f32[1024]{0:T(1024)}, u32[]{:S(2)}) copy-start(f32[1024]{0:T(1024)} %get-tuple-element.620) | copy-start | bytes 12292
  661.8 519.3 %copy-start.31 = (f32[4096]{0:T(1024)S(1)}, f32[4096]{0:T(1024)}, u32[]{:S(2)}) copy-start(f32[4096]{0:T(1024)} %get-tuple-element.690) | copy-start | bytes 49156
  661.9 657.9 %all-reduce.16.cloned.1.call-start = ((), (), s32[]{:S(2)}) async-start(), calls=%async_computation.12 | async-start | bytes 12582912 | tf_op jit(solution)/shard_map/psum | solution.py:353
  (42 other events, 575.5 us)
Sparse Core Ops, SparseCore 0:
  9.6 67.5 all-gather.15
  78.8 27.8 all-gather.17
  108.3 88.4 all-gather.19
  198.2 110.0 all-gather.21
  385.3 124.0 reduce-scatter.6
  638.2 202.6 reduce-scatter.4
  843.3 166.6 reduce-scatter.8
  1012.4 166.6 reduce-scatter.10
  1182.8 136.9 all-reduce.15
where the time goes:
time: 1350 us; the launch traced here: 1340 us
  waiting for transfers between devices  623 us (46%)
  starting transfers between devices  206 us (15%)
  matrix products  203 us (15%)
  blocking collectives  155 us (11%)
  local copies, waits for them, and re-layouts  54.5 us (4%)
  other arithmetic  50 us (4%)
  between operations  26.9 us (2%)
  loops' own time  16.9 us (1%)
    ppermute x20, starting transfers between devices, from_behind(): return lax.ppermute(shard, axis, pairs)  205 us
    reduce_scatter x1, waiting for transfers between devices, on_device(): lax.psum_scatter(attn_terms[2], 'fsdp', scatter_dimension=0, tiled=True)  179 us
    reduce_scatter x1, waiting for transfers between devices, on_device(): lax.psum_scatter(mlp_terms[4], 'fsdp', scatter_dimension=0, tiled=True)  169 us
    reduce_scatter x1, waiting for transfers between devices, on_device(): lax.psum_scatter(mlp_terms[2], 'fsdp', scatter_dimension=0, tiled=True)  169 us
    psum x1, waiting for transfers between devices, on_device(): lax.psum((owned[0], owned[1], owned[2], owned[3], owned[4], owned[5], own...  87.6 us
  transfers between devices with their start and end apart: 29, of which 6 were waited for; matrix products, arithmetic and copies ran while one was open for 19% of the time, Pallas kernels for 0%

commit v1 on v0

v1 whole, which is shorter than its diff:
```python
import functools
import math

import jax
import jax.numpy as jnp
from jax import lax
from jax.experimental import pallas as pl
from jax.experimental.pallas import tpu as pltpu
from jax.sharding import PartitionSpec as P

D = 1024
HEADS = 16
HEAD_DIM = 64
LANES = 128

EPSILON = 1e-06
MASKED = -1e30
BLOCK = 256

f32 = jnp.float32
bf16 = jnp.bfloat16


def normalize(features):
    row_mean = jnp.mean(features, axis=-1, keepdims=True)
    centred = features - row_mean
    variance = jnp.mean(centred * centred, axis=-1, keepdims=True)
    inverse = lax.rsqrt(variance + EPSILON)
    return centred * inverse, inverse


def norm_back(gradient, normal, inverse, gain_vec):
    scaled = gradient * gain_vec
    mean_first = jnp.mean(scaled, axis=-1, keepdims=True)
    mean_second = jnp.mean(scaled * normal, axis=-1, keepdims=True)
    return inverse * (scaled - mean_first - normal * mean_second)


def gelu_pair(values):
    cumulative = 0.5 * (1.0 + lax.erf(values * 2.0 ** (-0.5)))
    density = jnp.exp(-0.5 * values * values) * (2.0 * math.pi) ** (-0.5)
    return (values * cumulative, cumulative + values * density)


def dot(a, b):
    return jnp.dot(a, b, preferred_element_type=f32)


def dot_nt(a, b):
    return lax.dot_general(a, b, (((1,), (1,)), ((), ())), preferred_element_type=f32)


def dot_tn(a, b):
    return lax.dot_general(a, b, (((0,), (0,)), ((), ())), preferred_element_type=f32)


def swap_cores(value):
    size = lax.axis_size("fsdp")
    return lax.ppermute(value, "fsdp", [(i, i ^ 1) for i in range(size)])


def along_z(value, by):
    size = lax.axis_size("fsdp")
    return lax.ppermute(value, "fsdp", [(i, (i + 2 * by) % size) for i in range(size)])


def from_chip(value, by):
    size = lax.axis_size("fsdp")
    pairs = [(i, i + 2 * by) for i in range(size) if 0 <= i + 2 * by < size]
    return lax.ppermute(value, "fsdp", pairs)


def across_rep(value, bit):
    size = lax.axis_size("rep")
    return lax.ppermute(value, "rep", [(i, i ^ (1 << bit)) for i in range(size)])


def pick(value, index, axis):
    return lax.dynamic_index_in_dim(value, index, axis, keepdims=False)


def rep_bits():
    return lax.axis_size("rep").bit_length() - 1


def spread_over_rep(value, order):
    stacked, offsets = value[None], [0]
    for step, bit in enumerate(order):
        received = across_rep(stacked, bit)
        further = [o ^ (1 << bit) for o in offsets]
        if step + 1 < len(order):
            stacked, offsets = jnp.concatenate([stacked, received]), offsets + further
        else:
            return [(stacked, offsets), (received, further)]
    return [(stacked, offsets)]


def assemble_kernel(plan, index_ref, *refs):
    count = len(plan)
    sources, target, held, in_sems, out_sems = refs[:count], refs[count], refs[count + 1], refs[count + 2], refs[count + 3]
    here, rank = index_ref[0], index_ref[1]
    depth = target.shape[0]
    half = target.shape[2] // 2
    rows = target.shape[2]
    width = sources[0].shape[-1]
    waits = [[] for _ in range(depth)]
    number = 0
    for which, (colour, offsets) in enumerate(plan):
        lo = colour * half
        for m, offset in enumerate(offsets):
            for k in range(depth):
                place = lax.rem(here - k + depth, depth)
                copy = pltpu.make_async_copy(
                    sources[which].at[m, k],
                    held.at[place, rank ^ offset, pl.ds(lo, half)],
                    in_sems.at[number],
                )
                copy.start()
                waits[k].append(copy)
                number += 1
    outs = []
    ranks = target.shape[1]
    for k in range(depth):
        place = lax.rem(here - k + depth, depth)
        for copy in waits[k]:
            copy.wait()
        for i in range(ranks):
            out = pltpu.make_async_copy(held.at[place, i], target.at[place, i], out_sems.at[k, i])
            out.start()
            outs.append(out)
    for out in outs:
        out.wait()


def gather_group(own, here, rank):
    depth, ranks = lax.axis_size("fsdp") // 2, lax.axis_size("rep")
    pieces = [own] + [along_z(own, k) for k in range(1, depth)]
    rows, cols = own.shape
    half = rows // 2
    order = list(range(rep_bits()))
    upper = spread_over_rep(jnp.stack([p[:half] for p in pieces]), order)
    lower = spread_over_rep(jnp.stack([p[half:] for p in pieces]), order[::-1])
    sources, plan = [], []
    for colour, parts in enumerate((upper, lower)):
        for array, offsets in parts:
            sources.append(array)
            plan.append((colour, offsets))
    total = 2 * ranks * depth
    return pl.pallas_call(
        functools.partial(assemble_kernel, plan),
        out_shape=jax.ShapeDtypeStruct((depth, ranks, rows, cols), own.dtype),
        grid_spec=pltpu.PrefetchScalarGridSpec(
            num_scalar_prefetch=1,
            grid=(1,),
            in_specs=[pl.BlockSpec(memory_space=pl.ANY)] * len(sources),
            out_specs=pl.BlockSpec(memory_space=pl.ANY),
            scratch_shapes=[
                pltpu.VMEM((depth, ranks, rows, cols), own.dtype),
                pltpu.SemaphoreType.DMA((total,)),
                pltpu.SemaphoreType.DMA((depth, ranks)),
            ],
        ),
        compiler_params=pltpu.CompilerParams(vmem_limit_bytes=16 << 20),
        cost_estimate=pl.CostEstimate(
            flops=0, transcendentals=0, bytes_accessed=2 * depth * ranks * rows * cols * own.dtype.itemsize
        ),
        name="assemble",
    )(jnp.stack([here, rank]).astype(jnp.int32), *sources)


def merge_columns(gathered):
    depth, ranks, rows, cols = gathered.shape
    return jnp.concatenate(
        [gathered[:, i].reshape(depth * rows, cols) for i in range(ranks)], axis=1
    )


def reduce_group(grads, here, rank, orders):
    depth, ranks = lax.axis_size("fsdp") // 2, lax.axis_size("rep")
    width = grads.shape[1] // ranks
    rows = grads.shape[0] // depth
    shaped = grads.reshape(depth, rows, grads.shape[1])
    share = rows // len(orders)
    reduced = []
    for colour, order in enumerate(orders):
        block = lambda o: lax.dynamic_slice(
            shaped, (0, colour * share, (rank ^ o) * width), (depth, share, width)
        )
        held = {o: block(o) for o in range(ranks)}
        for bit in order:
            flip = 1 << bit
            kept = [o for o in held if not o & flip]
            received = across_rep(jnp.stack([held[o ^ flip] for o in kept]), bit)
            held = {
                o: (held[o].astype(f32) + received[i].astype(f32)).astype(bf16)
                for i, o in enumerate(kept)
            }
        reduced.append(held[0])
    reduced = reduced[0] if len(reduced) == 1 else jnp.concatenate(reduced, axis=1)
    total = pick(reduced, here, 0).astype(f32)
    for k in range(1, depth):
        sent = pick(reduced, lax.rem(here + k, depth), 0)
        total = total + along_z(sent, k).astype(f32)
    return total


def share_over_rep(mine, rank):
    stacked = mine[None]
    offsets = [0]
    for bit in range(rep_bits()):
        received = across_rep(stacked, bit)
        stacked = jnp.concatenate([stacked, received])
        offsets = offsets + [o ^ (1 << bit) for o in offsets]
    blocks = [pick(stacked, rank ^ i, 0) for i in range(lax.axis_size("rep"))]
    return jnp.concatenate(blocks, axis=1)


def spread_lanes(tags, width):
    return jnp.concatenate([tags] * (width // LANES), axis=1)


def project_kernel(need_ref, n_ref, w_ref, b_ref, q_ref, k_ref, v_ref):
    row = pl.program_id(0)
    wide = q_ref.shape[1]

    @pl.when(need_ref[row] > 0)
    def _():
        n = n_ref[...]
        for i, ref in enumerate((q_ref, k_ref, v_ref)):
            out = dot(n, w_ref[:, i * wide : (i + 1) * wide]) + b_ref[0:1, i * wide : (i + 1) * wide]
            if i == 0:
                out = out.astype(bf16).astype(f32) * HEAD_DIM ** (-0.5)
            ref[...] = out.astype(bf16)

    @pl.when(need_ref[row] == 0)
    def _():
        for ref in (q_ref, k_ref, v_ref):
            ref[...] = jnp.zeros_like(ref)


def project(need, normed, weight, bias, wide):
    rows = normed.shape[0]
    return pl.pallas_call(
        project_kernel,
        out_shape=[jax.ShapeDtypeStruct((rows, wide), bf16)] * 3,
        grid_spec=pltpu.PrefetchScalarGridSpec(
            num_scalar_prefetch=1,
            grid=(rows // BLOCK,),
            in_specs=[
                pl.BlockSpec((BLOCK, D), lambda i, s: (i, 0)),
                pl.BlockSpec(weight.shape, lambda i, s: (0, 0)),
                pl.BlockSpec((8, 3 * wide), lambda i, s: (0, 0)),
            ],
            out_specs=[pl.BlockSpec((BLOCK, wide), lambda i, s: (i, 0))] * 3,
        ),
        compiler_params=pltpu.CompilerParams(vmem_limit_bytes=32 << 20),
        cost_estimate=pl.CostEstimate(
            flops=2 * rows * D * 3 * wide, transcendentals=0, bytes_accessed=rows * D * 6
        ),
        name="project",
    )(need, normed, weight, bias)


def attend_kernel(lo_ref, hi_ref, q_ref, k_ref, v_ref, qt_ref, kt_ref, o_ref, lse_ref):
    i = pl.program_id(1)
    first = lax.broadcasted_iota(jnp.int32, (1, LANES), 1) < HEAD_DIM
    q = q_ref[...]
    zero = jnp.zeros_like(q)
    heads = (jnp.where(first, q, zero), jnp.where(first, zero, q))
    q_tags = spread_lanes(qt_ref[...], BLOCK)

    def step(j, carry):
        at = pl.multiple_of(j * BLOCK, BLOCK)
        k = k_ref[pl.ds(at, BLOCK), :]
        v = v_ref[pl.ds(at, BLOCK), :]
        same = q_tags == kt_ref[:, pl.ds(at, BLOCK)]
        acc = carry[4]
        stats, scales, parts = [], [], []
        for h in range(2):
            old_max, old_sum = carry[2 * h], carry[2 * h + 1]
            s = jnp.where(same, dot_nt(heads[h], k), MASKED)
            new_max = jnp.maximum(old_max, jnp.max(s, axis=1, keepdims=True))
            scale = jnp.exp(old_max - new_max)
            p = jnp.exp(s - new_max)
            stats += [new_max, old_sum * scale + jnp.sum(p, axis=1, keepdims=True)]
            vz = jnp.zeros_like(v)
            vh = jnp.where(first, v, vz) if h == 0 else jnp.where(first, vz, v)
            parts.append(dot(p.astype(bf16), vh))
            scales.append(scale)
        acc = acc * jnp.where(first, scales[0], scales[1]) + parts[0] + parts[1]
        return (*stats, acc)

    low = jnp.full((BLOCK, 1), MASKED, f32)
    none = jnp.zeros((BLOCK, 1), f32)
    ma, la, mb, lb, acc = lax.fori_loop(
        lo_ref[i], hi_ref[i], step, (low, none, low, none, jnp.zeros((BLOCK, LANES), f32))
    )
    o_ref[...] = (acc / jnp.where(first, la, lb)).astype(bf16)
    lse_ref[0] = jnp.where(first, ma + jnp.log(la), mb + jnp.log(lb))


def attend(lo, hi, q, k, v, tag_cols, tag_row, own_rows):
    window, wide = q.shape
    pairs = wide // LANES
    skip = (window - own_rows) // 2 // BLOCK
    blocks = own_rows // BLOCK
    return pl.pallas_call(
        attend_kernel,
        out_shape=[
            jax.ShapeDtypeStruct((own_rows, wide), bf16),
            jax.ShapeDtypeStruct((pairs, own_rows, LANES), f32),
        ],
        grid_spec=pltpu.PrefetchScalarGridSpec(
            num_scalar_prefetch=2,
            grid=(pairs, blocks),
            in_specs=[
                pl.BlockSpec((BLOCK, LANES), lambda p, i, a, b: (i + skip, p)),
                pl.BlockSpec((window, LANES), lambda p, i, a, b: (0, p)),
                pl.BlockSpec((window, LANES), lambda p, i, a, b: (0, p)),
                pl.BlockSpec((BLOCK, LANES), lambda p, i, a, b: (i + skip, 0)),
                pl.BlockSpec((1, window), lambda p, i, a, b: (0, 0)),
            ],
            out_specs=[
                pl.BlockSpec((BLOCK, LANES), lambda p, i, a, b: (i, p)),
                pl.BlockSpec((1, BLOCK, LANES), lambda p, i, a, b: (p, i, 0)),
            ],
        ),
        compiler_params=pltpu.CompilerParams(vmem_limit_bytes=32 << 20),
        cost_estimate=pl.CostEstimate(
            flops=4 * own_rows * own_rows * 4 * wide,
            transcendentals=own_rows * own_rows * 8,
            bytes_accessed=window * wide * 4,
        ),
        name="attend",
    )(lo, hi, q, k, v, tag_cols, tag_row)


def attend_back_kernel(
    start, stop, lo_ref, hi_ref, q_ref, k_ref, v_ref, g_ref, tc_ref, tr_ref, lse_ref, delta_ref,
    dq_ref, dk_ref, dv_ref, sum_ref, dk_acc, dv_acc, dq_acc,
):
    first = lax.broadcasted_iota(jnp.int32, (1, LANES), 1) < HEAD_DIM
    dk_acc[...] = jnp.zeros_like(dk_acc)
    dv_acc[...] = jnp.zeros_like(dv_acc)
    sum_ref[...] = jnp.zeros_like(sum_ref)

    def split(value):
        zero = jnp.zeros_like(value)
        return jnp.where(first, value, zero), jnp.where(first, zero, value)

    def query_block(i, carry):
        at_q = pl.multiple_of(i * BLOCK, BLOCK)
        own_q = jnp.logical_and(i >= start, i < stop)
        lo = jnp.where(own_q, lo_ref[i], jnp.maximum(lo_ref[i], start))
        hi = jnp.where(own_q, hi_ref[i], jnp.minimum(hi_ref[i], stop))

        @pl.when(own_q)
        def _():
            dq_acc[...] = jnp.zeros_like(dq_acc)

        def key_block(j, carry):
            at_k = pl.multiple_of(j * BLOCK, BLOCK)
            k = k_ref[pl.ds(at_k, BLOCK), :]
            v = v_ref[pl.ds(at_k, BLOCK), :]
            qs = split(q_ref[pl.ds(at_q, BLOCK), :])
            gs = split(g_ref[pl.ds(at_q, BLOCK), :])
            same = spread_lanes(tc_ref[pl.ds(at_k, BLOCK), :], BLOCK) == tr_ref[:, pl.ds(at_q, BLOCK)]
            ps, ds = [], []
            for h in range(2):
                s = dot_nt(k, qs[h])
                p = jnp.where(same, jnp.exp(s - lse_ref[0, h : h + 1, pl.ds(at_q, BLOCK)]), 0.0)
                dp = dot_nt(v, gs[h])
                d = p * (dp - delta_ref[0, h : h + 1, pl.ds(at_q, BLOCK)])
                ps.append(p.astype(bf16))
                ds.append(d.astype(bf16))

            @pl.when(jnp.logical_and(j >= start, j < stop))
            def _():
                at = pl.multiple_of((j - start) * BLOCK, BLOCK)
                dv_acc[pl.ds(at, BLOCK), :] += dot(ps[0], gs[0]) + dot(ps[1], gs[1])
                dk_acc[pl.ds(at, BLOCK), :] += dot(ds[0], qs[0]) + dot(ds[1], qs[1])

            @pl.when(own_q)
            def _():
                ks = split(k)
                dq_acc[...] += dot_tn(ds[0], ks[0]) + dot_tn(ds[1], ks[1])

            return carry

        lax.fori_loop(lo, hi, key_block, 0)

        @pl.when(own_q)
        def _():
            at = pl.multiple_of((i - start) * BLOCK, BLOCK)
            dq = dq_acc[...] * HEAD_DIM ** (-0.5)
            dq_ref[pl.ds(at, BLOCK), :] = dq.astype(bf16)
            sum_ref[0, 0:1, :] += jnp.sum(dq, axis=0, keepdims=True)

        return carry

    lax.fori_loop(0, q_ref.shape[0] // BLOCK, query_block, 0)
    dk_ref[...] = dk_acc[...].astype(bf16)
    dv_ref[...] = dv_acc[...].astype(bf16)
    sum_ref[0, 1:2, :] = jnp.sum(dv_acc[...], axis=0, keepdims=True)


def attend_back(lo, hi, q, k, v, g, tag_cols, tag_row, lse, delta, own_rows):
    window, wide = q.shape
    pairs = wide // LANES
    start = (window - own_rows) // 2 // BLOCK
    stop = start + own_rows // BLOCK
    whole = lambda: pl.BlockSpec((window, LANES), lambda p, a, b: (0, p))
    own = lambda: pl.BlockSpec((own_rows, LANES), lambda p, a, b: (0, p))
    stat = lambda: pl.BlockSpec((1, 2, window), lambda p, a, b: (p, 0, 0))
    return pl.pallas_call(
        functools.partial(attend_back_kernel, start, stop),
        out_shape=[jax.ShapeDtypeStruct((own_rows, wide), bf16)] * 3
        + [jax.ShapeDtypeStruct((pairs, 8, LANES), f32)],
        grid_spec=pltpu.PrefetchScalarGridSpec(
            num_scalar_prefetch=2,
            grid=(pairs,),
            in_specs=[
                whole(), whole(), whole(), whole(),
                pl.BlockSpec((window, LANES), lambda p, a, b: (0, 0)),
                pl.BlockSpec((1, window), lambda p, a, b: (0, 0)),
                stat(), stat(),
            ],
            out_specs=[own(), own(), own(), pl.BlockSpec((1, 8, LANES), lambda p, a, b: (p, 0, 0))],
            scratch_shapes=[
                pltpu.VMEM((own_rows, LANES), f32),
                pltpu.VMEM((own_rows, LANES), f32),
                pltpu.VMEM((BLOCK, LANES), f32),
            ],
        ),
        compiler_params=pltpu.CompilerParams(vmem_limit_bytes=40 << 20),
        cost_estimate=pl.CostEstimate(
            flops=10 * own_rows * own_rows * 4 * wide,
            transcendentals=own_rows * own_rows * 8,
            bytes_accessed=window * wide * 8,
        ),
        name="attend_back",
    )(lo, hi, q, k, v, g, tag_cols, tag_row, lse, delta)


def on_device(
    tokens, image_ids, ln1_gain, ln1_bias, qkv_weight, query_bias, value_bias, proj_weight,
    proj_bias, scale_attn, ln2_gain, ln2_bias, fc1_weight, fc1_bias, fc2_weight, fc2_bias,
    scale_mlp, cotangent,
):
    devices = lax.axis_size("fsdp")
    depth, ranks = devices // 2, lax.axis_size("rep")
    place = lax.axis_index("fsdp")
    rank = lax.axis_index("rep")
    here, core = place // 2, place % 2
    count = tokens.shape[1]
    chip = 2 * count
    head_rows = D // devices
    ff = fc1_weight.shape[1]
    unit_rows = ff // devices
    half_heads = D // 2

    def in_order(own, other, axis=0):
        return jnp.where(
            core == 0,
            jnp.concatenate([own, other], axis=axis),
            jnp.concatenate([other, own], axis=axis),
        )

    def mine(value):
        return lax.dynamic_slice_in_dim(value, core * count, count, 0)

    def others(value):
        return lax.dynamic_slice_in_dim(value, (1 - core) * count, count, 0)

    qkv_split = qkv_weight.reshape(head_rows, 3 * depth, 2, head_rows)
    fc1_split = fc1_weight.reshape(head_rows, depth, 2, unit_rows)

    def of_core(index):
        return jnp.concatenate(
            [
                pick(qkv_split, index, 2).reshape(head_rows, 3 * half_heads),
                pick(fc1_split, index, 2).reshape(head_rows, ff // 2),
            ],
            axis=1,
        )

    paired = in_order(of_core(core), swap_cores(of_core(1 - core)))
    proj_packed = jnp.concatenate([proj_weight[:, :half_heads], proj_weight[:, half_heads:]], axis=0)
    group1 = jnp.concatenate([paired[:, : 3 * half_heads], proj_packed], axis=1)
    group2 = paired[:, 3 * half_heads :]
    group3 = fc2_weight

    def own_columns(group):
        width = group.shape[1] // ranks
        return lax.dynamic_slice_in_dim(group, rank * width, width, 1)

    tok = tokens[0]
    behind, ahead = from_chip(tok, 1), from_chip(tok, -1)
    tok_other = swap_cores(jnp.concatenate([tok, behind, ahead, cotangent[0]]))
    cot_other = tok_other[3 * count :]
    window_tokens = jnp.concatenate(
        [
            in_order(behind, tok_other[count : 2 * count]),
            in_order(tok, tok_other[:count]),
            in_order(ahead, tok_other[2 * count : 3 * count]),
        ]
    )
    window = window_tokens.shape[0]

    small = (
        ln1_gain, ln1_bias, query_bias, value_bias, proj_bias, scale_attn, ln2_gain, ln2_bias,
        fc2_bias, scale_mlp, fc1_bias, (image_ids[0] + 1).astype(bf16),
    )
    sizes = [v.shape[0] for v in small]
    gathered = lax.all_gather(jnp.concatenate(small), "fsdp", axis=0)
    vectors, offset = [], 0
    for size in sizes:
        vectors.append(gathered[:, offset : offset + size].reshape(-1).astype(f32))
        offset += size
    (
        attn_gain, attn_shift, query_shift, value_shift, proj_shift, attn_scale, mlp_gain,
        mlp_shift, fc2_shift, mlp_scale, fc1_shift, all_tags,
    ) = vectors
    core_part = lambda vec: pick(vec.reshape(depth, 2, -1), core, 1).reshape(-1)
    query_shift, value_shift, fc1_shift = map(core_part, (query_shift, value_shift, fc1_shift))

    padded = jnp.concatenate(
        [jnp.zeros((chip,), f32), all_tags, jnp.full((chip,), 1e6, f32)]
    )
    tags = lax.dynamic_slice(padded, (here * chip,), (window,))
    firsts, lasts = tags[::BLOCK], tags[BLOCK - 1 :: BLOCK]
    real = firsts * (1e6 - firsts) > 0
    below = jnp.sum((tags[None, :] < firsts[:, None]).astype(jnp.int32), axis=1)
    upto = jnp.sum((tags[None, :] <= lasts[:, None]).astype(jnp.int32), axis=1)
    blocks = window // BLOCK
    block_lo = jnp.where(real, below // BLOCK, 0)
    block_hi = jnp.where(real, (upto + BLOCK - 1) // BLOCK, 0)
    own_lo, own_hi = chip // BLOCK, 2 * chip // BLOCK
    numbers = jnp.arange(blocks)
    need = jnp.logical_and(numbers >= block_lo[own_lo], numbers < block_hi[own_hi - 1])
    tag_cols = jnp.broadcast_to(tags[:, None], (window, LANES))
    tag_row = tags[None, :]

    normal_window, _ = normalize(window_tokens.astype(f32))
    normed1 = (normal_window * attn_gain + attn_shift).astype(bf16)

    full1 = merge_columns(gather_group(own_columns(group1), here, rank))
    full2 = merge_columns(gather_group(own_columns(group2), here, rank))
    full3 = merge_columns(gather_group(own_columns(group3), here, rank))
    qkv_matrix = full1[:, : 3 * half_heads]
    proj_matrix = (
        full1[:, 3 * half_heads :]
        .reshape(depth, 2, head_rows, half_heads)
        .transpose(0, 2, 1, 3)
        .reshape(half_heads, D)
    )
    fc1_matrix, fc2_matrix = full2, full3

    shifts = jnp.broadcast_to(
        jnp.concatenate([query_shift, jnp.zeros_like(query_shift), value_shift])[None],
        (8, 3 * half_heads),
    )
    queries, keys, values = project(
        need.astype(jnp.int32), normed1, qkv_matrix, shifts, half_heads
    )
    context, lse = attend(
        block_lo[own_lo:own_hi], block_hi[own_lo:own_hi], queries, keys, values, tag_cols, tag_row, chip
    )
    local_heads = half_heads // HEAD_DIM
    lse_rows = lse[:, :, ::HEAD_DIM].transpose(0, 2, 1).reshape(local_heads, chip)

    features = tok.astype(f32)
    sent = swap_cores(dot(others(context), proj_matrix))
    attn_out = dot(mine(context), proj_matrix) + sent + proj_shift
    resid = features + attn_scale * attn_out
    mlp_normal, mlp_inverse = normalize(resid)
    mlp_input = (mlp_normal * mlp_gain + mlp_shift).astype(bf16)
    mlp_input = jnp.concatenate([mlp_input, swap_cores(mlp_input)])
    pre_act = dot(mlp_input, fc1_matrix) + fc1_shift
    activated, slope = gelu_pair(pre_act)
    activated = activated.astype(bf16)

    out_grad = cotangent[0].astype(f32)
    mlp_grad_full = out_grad * mlp_scale
    mlp_grad = (jnp.concatenate([cotangent[0], cot_other]).astype(f32) * mlp_scale).astype(bf16)
    sent = swap_cores(dot(activated[count:], fc2_matrix))
    mlp_out = dot(activated[:count], fc2_matrix) + sent + fc2_shift
    output_rows = (resid + mlp_scale * mlp_out).astype(bf16)

    fc2_grad = dot_tn(activated, mlp_grad).astype(bf16)
    fc2_total = reduce_group(fc2_grad, here, rank, [list(range(rep_bits()))])

    pre_grad_full = dot_nt(mlp_grad, fc2_matrix) * slope
    pre_grad = pre_grad_full.astype(bf16)
    fc1_grad = dot_tn(mlp_input, pre_grad).astype(bf16)
    fc1_total = reduce_group(fc1_grad, here, rank, [list(range(rep_bits()))[::-1]])

    sent = swap_cores(dot_nt(pre_grad[count:], fc1_matrix))
    mlp_in_grad = dot_nt(pre_grad[:count], fc1_matrix) + sent
    resid_grad = out_grad + norm_back(mlp_in_grad, mlp_normal, mlp_inverse, mlp_gain)
    attn_grad_full = resid_grad * attn_scale
    attn_grad = attn_grad_full.astype(bf16)
    attn_grad = in_order(attn_grad, swap_cores(attn_grad))
    context_grad = dot_nt(attn_grad, proj_matrix).astype(bf16)
    row_delta = jnp.sum(
        (context_grad.astype(f32) * context.astype(f32)).reshape(chip, local_heads, HEAD_DIM), axis=-1
    ).T
    stats = jnp.concatenate([lse_rows, row_delta])
    grad_window = jnp.concatenate([from_chip(context_grad, 1), context_grad, from_chip(context_grad, -1)])
    stat_window = jnp.concatenate([from_chip(stats, 1), stats, from_chip(stats, -1)], axis=1)
    by_pair = lambda s: s.reshape(local_heads // 2, 2, window)

    query_grad, key_grad, value_grad, sums = attend_back(
        block_lo, block_hi, queries, keys, values, grad_window, tag_cols, tag_row,
        by_pair(stat_window[:local_heads]), by_pair(stat_window[local_heads:]), chip,
    )
    qkv_grad = jnp.concatenate([query_grad, key_grad, value_grad], axis=1)
    qkv_w_grad = dot_tn(normed1[chip : 2 * chip], qkv_grad).astype(bf16)
    proj_grad = dot_tn(context, attn_grad).astype(bf16)
    proj_grad = (
        proj_grad.reshape(depth, head_rows, 2, half_heads)
        .transpose(0, 2, 1, 3)
        .reshape(D, half_heads)
    )
    group1_total = reduce_group(
        jnp.concatenate([qkv_w_grad, proj_grad], axis=1), here, rank,
        [list(range(rep_bits())), list(range(rep_bits()))[::-1]],
    )

    sent = swap_cores(dot_nt(others(qkv_grad), qkv_matrix))
    attn_in_grad = dot_nt(mine(qkv_grad), qkv_matrix) + sent
    attn_normal, attn_inverse = normalize(features)
    input_rows = resid_grad + norm_back(attn_in_grad, attn_normal, attn_inverse, attn_gain)

    factor = 1.0 / math.sqrt(count * devices * ranks)

    def on_core(part):
        part = part.reshape(depth, 1, -1)
        zero = jnp.zeros_like(part)
        return jnp.where(
            core == 0,
            jnp.concatenate([part, zero], axis=1),
            jnp.concatenate([zero, part], axis=1),
        ).reshape(-1)

    columns = lambda value: jnp.sum(value, axis=0)
    partial = jnp.concatenate(
        [
            v.reshape(devices, -1)
            for v in (
                columns(attn_in_grad * attn_normal), columns(attn_in_grad),
                on_core(sums[:, 0]), on_core(sums[:, 1]),
                columns(attn_grad_full), columns(resid_grad * attn_out),
                columns(mlp_in_grad * mlp_normal), columns(mlp_in_grad),
                columns(mlp_grad_full), columns(out_grad * mlp_out),
                on_core(columns(pre_grad_full)),
            )
        ],
        axis=1,
    )
    totals = pick(lax.psum(partial, ("rep", "fsdp")), place, 0) * factor
    small_grads, offset = [], 0
    for size in sizes[:-1]:
        small_grads.append(totals[offset : offset + size])
        offset += size
    (
        grad_attn_gain, grad_attn_shift, grad_query_shift, grad_value_shift, grad_proj_shift,
        grad_attn_scale, grad_mlp_gain, grad_mlp_shift, grad_fc2_shift, grad_mlp_scale, grad_fc1_shift,
    ) = small_grads

    def finish(total):
        return share_over_rep(total.astype(bf16), rank)

    fc2_full = finish(fc2_total).astype(f32) * factor
    fc1_full = finish(fc1_total)
    first_full = finish(group1_total)
    rows_of = lambda value, index: lax.dynamic_slice_in_dim(value, index * head_rows, head_rows, 0)
    both = jnp.concatenate([first_full[:, : 3 * half_heads], fc1_full], axis=1)
    own_part, other_part = rows_of(both, core), swap_cores(rows_of(both, 1 - core))

    def interleave(own, other, blocks):
        own = own.reshape(head_rows, blocks, 1, -1)
        other = other.reshape(head_rows, blocks, 1, -1)
        joined = in_order(own, other, axis=2)
        return joined.reshape(head_rows, -1).astype(f32) * factor

    grad_qkv = interleave(own_part[:, : 3 * half_heads], other_part[:, : 3 * half_heads], 3 * depth)
    grad_fc1 = interleave(own_part[:, 3 * half_heads :], other_part[:, 3 * half_heads :], depth)
    proj_part = first_full[:, 3 * half_heads :]
    grad_proj = jnp.concatenate([proj_part[:head_rows], proj_part[head_rows:]], axis=1).astype(f32) * factor

    return (
        output_rows[None],
        input_rows[None],
        grad_attn_gain,
        grad_attn_shift,
        grad_qkv,
        grad_query_shift,
        grad_value_shift,
        grad_proj,
        grad_proj_shift,
        grad_attn_scale,
        grad_mlp_gain,
        grad_mlp_shift,
        grad_fc1,
        grad_fc1_shift,
        fc2_full,
        grad_fc2_shift,
        grad_mlp_scale,
    )


def solution(mesh):
    rows = P("fsdp", None)
    vec = P("fsdp")
    tok = P("rep", "fsdp", None)
    return jax.shard_map(
        on_device,
        mesh=mesh,
        in_specs=(
            tok, P("rep", "fsdp"), vec, vec, rows, vec, vec, rows, vec, vec, vec, vec, rows, vec,
            rows, vec, vec, tok,
        ),
        out_specs=(
            tok, tok, vec, vec, rows, vec, vec, rows, vec, vec, vec, vec, rows, vec, rows, vec, vec,
        ),
        check_vma=False,
    )
```

time: 1350 us -> 832 us (0.62)
  waiting for transfers between devices: 623 us -> 209 us
  Pallas kernels: 0 us -> 171 us
  matrix products: 203 us -> 79.5 us
  blocking collectives: 155 us -> 62.1 us
  starting transfers between devices: 206 us -> 122 us
  local copies, waits for them, and re-layouts: 54.5 us -> 98.1 us
  other arithmetic: 50 us -> 81.1 us
  between operations: 26.9 us -> 3.17 us
  loops' own time: 16.9 us -> 0 us
    reduce_scatter x4 -> x0, waiting for transfers between devices: 517 us -> none  [the longest x1 179 us: on_device(): lax.psum_scatter(attn_terms[2], 'fsdp', scatter_dimension=0, tiled=True)]
    ppermute x20 -> x59, waiting for transfers between devices: 16 us -> 209 us  [the longest x26 120 us: across_rep(): return lax.ppermute(value, 'rep', [(i, i ^ 1 << bit) for i in range(size)])]
    pallas_call x0 -> x6, Pallas kernels: none -> 171 us  [the longest x1 80.8 us: attend_back(): pl.pallas_call(functools.partial(attend_back_kernel, start, stop), out_sh...]
    dot_general x25 -> x15, matrix products: 203 us -> 79.5 us  [the longest x6 29.7 us: dot_nt(): lax.dot_general(a, b, (((1,), (1,)), ((), ())), preferred_element_type=f32)]
    all_gather x11 -> x1, blocking collectives: 118 us -> 20.5 us  [on_device(): gathered = lax.all_gather(jnp.concatenate(small), 'fsdp', axis=0)]
    psum x1 -> x0, waiting for transfers between devices: 87.6 us -> none  [on_device(): lax.psum((owned[0], owned[1], owned[2], owned[3], owned[4], owned[5], own...]
    ppermute x20 -> x59, starting transfers between devices: 205 us -> 122 us  [the longest x18 73.5 us: along_z(): lax.ppermute(value, 'fsdp', [(i, (i + 2 * by) % size) for i in range(size)])]
    psum x1, blocking collectives: 10.8 us -> 41.6 us  [on_device(): totals = pick(lax.psum(partial, ('rep', 'fsdp')), place, 0) * factor]
  transfers between devices with their start and end apart: 29 -> 59, of which waited for: 6 -> 22; matrix products, arithmetic and copies ran while one was open for 19% -> 25% of each run, Pallas kernels for 0% -> 21%
where the time goes in v1:
time: 832 us; the launch traced here: 826 us
  waiting for transfers between devices  209 us (25%)
  Pallas kernels  171 us (21%)
  starting transfers between devices  122 us (15%)
  local copies, waits for them, and re-layouts  98.1 us (12%)
  other arithmetic  81.1 us (10%)
  matrix products  79.5 us (10%)
  blocking collectives  62.1 us (7%)
    ppermute x26, waiting for transfers between devices, across_rep(): return lax.ppermute(value, 'rep', [(i, i ^ 1 << bit) for i in range(size)])  120 us
    ppermute x18, waiting for transfers between devices, along_z(): lax.ppermute(value, 'fsdp', [(i, (i + 2 * by) % size) for i in range(size)])  83.8 us
    pallas_call x1, Pallas kernels, attend_back(): pl.pallas_call(functools.partial(attend_back_kernel, start, stop), out_sh...  80.8 us
    ppermute x18, starting transfers between devices, along_z(): lax.ppermute(value, 'fsdp', [(i, (i + 2 * by) % size) for i in range(size)])  73.5 us
    pallas_call x1, Pallas kernels, attend(): pl.pallas_call(attend_kernel, out_shape=[jax.ShapeDtypeStruct((own_rows,...  65.3 us
    psum x1, blocking collectives, on_device(): totals = pick(lax.psum(partial, ('rep', 'fsdp')), place, 0) * factor  41.6 us
    unnamed x216, local copies, waits for them, and re-layouts  35 us
    dot_general x6, matrix products, dot_nt(): lax.dot_general(a, b, (((1,), (1,)), ((), ())), preferred_element_type=f32)  29.7 us
  transfers between devices with their start and end apart: 59, of which 22 were waited for; matrix products, arithmetic and copies ran while one was open for 25% of the time, Pallas kernels for 21%

profile of v1, /device:TPU:0, one launch (start us, length us, event | category | flops | bytes accessed | tf_op | source)
XLA Modules:
  0.0 825.8 jit_solution(1199892806641711279)
XLA Ops:
  2.0 5.7 collective-permute-start
  14.6 7.2 dynamic-slice_reduce_fusion.1
  36.1 20.5 %all-gather.1 = bf16[8,1,2304]{2,1,0:T(2,128)(2,1)S(1)} all-gather(bf16[1,1,2304]{2,1,0:T(2,128)(2,1)S(1)} %reshape.394), channel_id=2, replica_groups=mesh['rep'=4,'fsdp'=8] {'fsdp'}, dimensions={0}, use_global_device_ids=true | all-gather | bytes 41472 | tf_op jit(solution)/shard_map/all_gather | solution.py:515
  65.8 3.8 pad_maximum_fusion.1
  69.9 6.9 maximum_select_fusion.4
  78.4 8.7 %collective-permute-done.6 = bf16[256,512]{1,0:T(8,128)(2,1)S(1)} collective-permute-done((bf16[256,512]{1,0:T(8,128)(2,1)S(1)}, bf16[256,512]{1,0:T(8,128)(2,1)S(1)}, u32[]{:S(2)}, u32[]{:S(2)}) %collective-permute-start.6) | collective-permute-done | bytes 262176 | tf_op jit(solution)/shard_map/ppermute | solution.py:64
  87.1 14.4 %collective-permute-done.5 = bf16[256,512]{1,0:T(8,128)(2,1)S(1)} collective-permute-done((bf16[256,512]{1,0:T(8,128)(2,1)S(1)}, bf16[256,512]{1,0:T(8,128)(2,1)S(1)}, u32[]{:S(2)}, u32[]{:S(2)}) %collective-permute-start.5) | collective-permute-done | bytes 262176 | tf_op jit(solution)/shard_map/ppermute | solution.py:64
  105.1 10.0 %collective-permute-done.7 = bf16[1,4,128,512]{3,2,1,0:T(8,128)(2,1)S(1)} collective-permute-done((bf16[1,4,128,512]{3,2,1,0:T(8,128)(2,1)S(1)}, bf16[1,4,128,512]{3,2,1,0:T(8,128)(2,1)S(1)}, u32[]{:S(2)}, u32[]{:S(2)}) %collective-permute-start.7) | collective-permute-done | bytes 524320 | tf_op jit(solution)/shard_map/ppermute | solution.py:75
  124.0 5.5 collective-permute-done.20
  132.5 6.5 collective-permute-done.8.refs_1_
  140.6 6.6 assemble.3
  156.8 4.6 convert_reduce_fusion
  161.4 5.1 fusion.2
  166.5 6.9 fusion.5.n_ref
  173.5 8.9 %project.1 = (bf16[3072,512]{1,0:T(8,128)(2,1)S(1)}, bf16[3072,512]{1,0:T(8,128)(2,1)S(1)}, bf16[3072,512]{1,0:T(8,128)(2,1)S(1)}) custom-call(s32[12]{0:T(128)S(1)} %and_convert_fusion.need_ref, bf16[3072,1024]{1,0:T(8,128)(2,1)S(1)} %fusion.5.n_ref, bf16[1024,1536]{1,0:T(8,128)(2,1)S(1)} %pad_maximum_fusion.4.w_ref, f32[8,1536]{1,0:T(8,128)S(1)} %broadcast_in_dim.42.b_ref), custom_call_target="tpu_custom_call" | custom-call | flops 9663676416 | bytes 18874368 | tf_op jit(solution)/shard_map/project/pallas_call | solution.py:243
  183.0 65.3 %attend.1 = (bf16[1024,512]{1,0:T(8,128)(2,1)S(1)}, f32[4,1024,128]{2,1,0:T(8,128)S(1)}) custom-call(s32[4]{0:T(128)S(1)} %slice.336.lo_ref, s32[4]{0:T(128)S(1)} %slice.338.hi_ref, bf16[3072,512]{1,0:T(8,128)(2,1)S(1)} %get-tuple-element.26.q_ref, bf16[3072,512]{1,0:T(8,128)(2,1)S(1)} %get-tuple-element.27.k_ref, ...), custom_call_target="tpu_custom_call" | custom-call | flops 8589934592 | bytes 6291456 | tf_op jit(solution)/shard_map/attend/pallas_call | solution.py:307
  253.0 15.6 %collective-permute-start.14 = (bf16[256,512]{1,0:T(8,128)(2,1)S(1)}, bf16[256,512]{1,0:T(8,128)(2,1)S(1)}, u32[]{:S(2)}, u32[]{:S(2)}) collective-permute-start(bf16[256,512]{1,0:T(8,128)(2,1)S(1)} %constant_dynamic-slice_fusion.12), channel_id=1, source_target_pairs={{0,4},{1,5},{2,6},{3,7},{4,0},{5,1},{6,2},{7,3},{8,12},{9,13},{10,... | collective-permute-start | bytes 786440 | tf_op jit(solution)/shard_map/ppermute | solution.py:64
  268.8 17.8 %collective-permute-done.14 = bf16[256,512]{1,0:T(8,128)(2,1)S(1)} collective-permute-done((bf16[256,512]{1,0:T(8,128)(2,1)S(1)}, bf16[256,512]{1,0:T(8,128)(2,1)S(1)}, u32[]{:S(2)}, u32[]{:S(2)}) %collective-permute-start.14) | collective-permute-done | bytes 262176 | tf_op jit(solution)/shard_map/ppermute | solution.py:64
  294.1 8.5 %collective-permute-done.16 = bf16[1,4,128,512]{3,2,1,0:T(8,128)(2,1)} collective-permute-done((bf16[1,4,128,512]{3,2,1,0:T(8,128)(2,1)}, bf16[1,4,128,512]{3,2,1,0:T(8,128)(2,1)}, u32[]{:S(2)}, u32[]{:S(2)}) %collective-permute-start.16) | collective-permute-done | bytes 524320 | tf_op jit(solution)/shard_map/ppermute | solution.py:75
  308.3 4.0 fusion.124
  315.0 12.3 %collective-permute-done.24.refs_1_ = bf16[2,4,256,256]{3,2,1,0:T(8,128)(2,1)} collective-permute-done((bf16[2,4,256,256]{3,2,1,0:T(8,128)(2,1)S(1)}, bf16[2,4,256,256]{3,2,1,0:T(8,128)(2,1)}, u32[]{:S(2)}, u32[]{:S(2)}) %collective-permute-start.24) | collective-permute-done | bytes 1048608 | tf_op jit(solution)/shard_map/ppermute | solution.py:75
  327.3 5.2 assemble.5
  332.9 15.5 %collective-permute-done.17.refs_1_ = bf16[2,4,128,512]{3,2,1,0:T(8,128)(2,1)} collective-permute-done((bf16[2,4,128,512]{3,2,1,0:T(8,128)(2,1)S(1)}, bf16[2,4,128,512]{3,2,1,0:T(8,128)(2,1)}, u32[]{:S(2)}, u32[]{:S(2)}) %collective-permute-start.17) | collective-permute-done | bytes 1048608 | tf_op jit(solution)/shard_map/ppermute | solution.py:75
  348.4 4.5 assemble.4
  353.2 10.1 %multiply_convert_fusion = (bf16[1024,2048]{1,0:T(8,128)(2,1)}, f32[1024,2048]{1,0:T(8,128)}) fusion(f32[2048]{0:T(1024)S(1)} %bitcast.445, bf16[1024,512]{1,0:T(8,128)(2,1)S(1)} %bitcast.424, bf16[1024,512]{1,0:T(8,128)(2,1)S(1)} %bitcast.427, bf16[1024,512]{1,0:T(8,128)(2,1)S(1)} %bitcast.430, bf16[1024,512]{1,0:T(8,128)(2,1)S(1)} %bitcast.421, ...), kind=kOutput, calls=%fused_computation.22 | convolution fusion | flops 4328521728 | bytes 18882560 | tf_op jit(solution)/shard_map/dot_general | solution.py:46
  363.3 9.9 %fusion.125 = (f32[2048]{0:T(1024)S(1)}, bf16[1024,2048]{1,0:T(8,128)(2,1)S(1)}) fusion(f32[1024,2048]{1,0:T(8,128)} %get-tuple-element.218, f32[2048]{0:T(1024)S(1)} %bitcast.446, bf16[2048,256]{1,0:T(8,128)(2,1)S(1)} %bitcast.412, bf16[2048,256]{1,0:T(8,128)(2,1)S(1)} %bitcast.415, bf16[2048,256]{1,0:T(8,128)(2,1)S(1)} %bitcast.418, ...), kind=kOutput, calls=%fused_computation.378 | convolution fusion | flops 4343199744 | bytes 18894848 | tf_op jit(solution)/shard_map/dot_general | solution.py:50
  379.3 7.4 convolution_convert_fusion.2
  386.8 8.7 %convolution_convert_fusion.1 = bf16[2048,1024]{1,0:T(8,128)(2,1)S(1)} fusion(bf16[1024,2048]{1,0:T(8,128)(2,1)} %get-tuple-element.217, bf16[512,1024]{1,0:T(8,128)(2,1)S(1)} %copy-done.59, bf16[512,1024]{1,0:T(8,128)(2,1)S(1)} %bitcast.408, f32[1024]{0:T(1024)S(1)} %copy-done.78), kind=kOutput, calls=%fused_computation.38 | convolution fusion | flops 4303355904 | bytes 10489856 | tf_op jit(solution)/shard_map/dot_general | solution.py:54
  401.7 4.5 multiply_reduce_fusion
  406.3 5.9 fusion.24
  414.6 9.0 %slice.399 = f32[4,1024,2]{2,1,0:T(8,128)} slice(f32[4,1024,128]{2,1,0:T(8,128)S(1)} %copy-done.2), slice={[0:4:1], [0:1024:1], [0:128:64]} | slice | bytes 65536 | tf_op jit(solution)/shard_map/slice | solution.py:570
  426.0 20.0 %collective-permute-done.44 = bf16[2,4,256,512]{3,2,1,0:T(8,128)(2,1)} collective-permute-done((bf16[2,4,256,512]{3,2,1,0:T(8,128)(2,1)}, bf16[2,4,256,512]{3,2,1,0:T(8,128)(2,1)}, u32[]{:S(2)}, u32[]{:S(2)}) %collective-permute-start.44) | collective-permute-done | bytes 2097184 | tf_op jit(solution)/shard_map/ppermute | solution.py:75
  453.9 4.6 convert_multiply_fusion.4
  459.8 5.5 collective-permute-start.30
  474.4 4.5 collective-permute-start.32
  489.5 9.3 %collective-permute-start.46 = (bf16[256,512]{1,0:T(8,128)(2,1)S(1)}, bf16[256,512]{1,0:T(8,128)(2,1)S(1)}, u32[]{:S(2)}, u32[]{:S(2)}) collective-permute-start(bf16[256,512]{1,0:T(8,128)(2,1)S(1)} %get-tuple-element.150), channel_id=1, source_target_pairs={{0,2},{1,3},{2,4},{3,5},{4,6},{5,7},{6,0},{7,1},{8,10},{9,11},{10,... | collective-permute-start | bytes 786440 | tf_op jit(solution)/shard_map/ppermute | solution.py:64
  499.5 14.2 %collective-permute-done.47 = bf16[256,512]{1,0:T(8,128)(2,1)S(1)} collective-permute-done((bf16[256,512]{1,0:T(8,128)(2,1)S(1)}, bf16[256,512]{1,0:T(8,128)(2,1)S(1)}, u32[]{:S(2)}, u32[]{:S(2)}) %collective-permute-start.47) | collective-permute-done | bytes 262176 | tf_op jit(solution)/shard_map/ppermute | solution.py:64
  513.7 9.7 %collective-permute-start.54 = (bf16[512,256]{1,0:T(8,128)(2,1)S(1)}, bf16[512,256]{1,0:T(8,128)(2,1)}, u32[]{:S(2)}, u32[]{:S(2)}) collective-permute-start(bf16[512,256]{1,0:T(8,128)(2,1)S(1)} %get-tuple-element.141), channel_id=1, source_target_pairs={{0,2},{1,3},{2,4},{3,5},{4,6},{5,7},{6,0},{7,1},{8,10},{9,11},{10,... | collective-permute-start | bytes 786440 | tf_op jit(solution)/shard_map/ppermute | solution.py:64
  536.2 80.8 %attend_back.1 = (bf16[1024,512]{1,0:T(8,128)(2,1)S(1)}, bf16[1024,512]{1,0:T(8,128)(2,1)S(1)}, bf16[1024,512]{1,0:T(8,128)(2,1)S(1)}, f32[4,8,128]{2,1,0:T(8,128)S(1)}) custom-call(s32[12]{0:T(128)S(1)} %copy-done.11, s32[12]{0:T(128)S(1)} %copy-done.9, bf16[3072,512]{1,0:T(8,128)(2,1)S(1)} %copy-done.13, bf16[3072,512]{1,0:T(8,128)(2,1)S(1)} %copy-done.15, ...), custom_call_target="tpu_custom_call" | custom-call | flops 21474836480 | bytes 12582912 | tf_op jit(solution)/shard_map/attend_back/pallas_call | solution.py:415
  622.1 5.5 convolution_convert_fusion
  635.1 31.0 %collective-permute-done.50 = bf16[2,256,512]{2,1,0:T(8,128)(2,1)S(1)} collective-permute-done((bf16[2,256,512]{2,1,0:T(8,128)(2,1)S(1)}, bf16[2,256,512]{2,1,0:T(8,128)(2,1)S(1)}, u32[]{:S(2)}, u32[]{:S(2)}) %collective-permute-start.50) | collective-permute-done | bytes 524320 | tf_op jit(solution)/shard_map/ppermute | solution.py:75
  684.0 5.2 fusion.21
  689.2 7.2 collective-permute-done.36
  697.9 5.3 collective-permute-start.41
  703.1 24.0 %collective-permute-start.40 = (bf16[256,512]{1,0:T(8,128)(2,1)S(1)}, bf16[256,512]{1,0:T(8,128)(2,1)S(1)}, u32[]{:S(2)}, u32[]{:S(2)}) collective-permute-start(bf16[256,512]{1,0:T(8,128)(2,1)S(1)} %get-tuple-element.157), channel_id=1, source_target_pairs={{0,4},{1,5},{2,6},{3,7},{4,0},{5,1},{6,2},{7,3},{8,12},{9,13},{10,... | collective-permute-start | bytes 786440 | tf_op jit(solution)/shard_map/ppermute | solution.py:64
  730.2 18.6 %collective-permute-done.40 = bf16[256,512]{1,0:T(8,128)(2,1)S(1)} collective-permute-done((bf16[256,512]{1,0:T(8,128)(2,1)S(1)}, bf16[256,512]{1,0:T(8,128)(2,1)S(1)}, u32[]{:S(2)}, u32[]{:S(2)}) %collective-permute-start.40) | collective-permute-done | bytes 262176 | tf_op jit(solution)/shard_map/ppermute | solution.py:64
  749.0 6.3 collective-permute-done.42
  756.9 41.6 %psum.7 = f32[8,1792]{1,0:T(8,128)S(1)} all-reduce(f32[8,1792]{1,0:T(8,128)S(1)} %constant_dynamic-update-slice_fusion.3), channel_id=1, replica_groups=mesh['rep'=4,'fsdp'=8] {'rep','fsdp'}, use_global_device_ids=true, to_apply=%region_22.23 | all-reduce | flops 14336 | bytes 114688 | tf_op jit(solution)/shard_map/psum | solution.py:661
  (471 shorter events, 203.8 us)
Async XLA Ops:
  0.7 65.0 %collective-permute-start.1 = (bf16[512,1024]{1,0:T(8,128)(2,1)}, bf16[512,1024]{1,0:T(8,128)(2,1)S(1)}, u32[]{:S(2)}, u32[]{:S(2)}) collective-permute-start(bf16[512,1024]{1,0:T(8,128)(2,1)} %bitcast.367), channel_id=1, source_target_pairs={{2,0},{3,1},{4,2},{5,3},{6,4},{7,5},{10,8},{11,9},{12,10},{13,11},... | collective-permute-start | bytes 3145736 | tf_op jit(solution)/shard_map/ppermute | solution.py:70
  2.0 63.8 %collective-permute-start = (bf16[512,1024]{1,0:T(8,128)(2,1)}, bf16[512,1024]{1,0:T(8,128)(2,1)S(1)}, u32[]{:S(2)}, u32[]{:S(2)}) collective-permute-start(bf16[512,1024]{1,0:T(8,128)(2,1)} %bitcast.368), channel_id=1, source_target_pairs={{0,2},{1,3},{2,4},{3,5},{4,6},{5,7},{8,10},{9,11},{10,12},{11,13},... | collective-permute-start | bytes 3145736 | tf_op jit(solution)/shard_map/ppermute | solution.py:70
  9.3 111.9 %collective-permute-start.22 = (bf16[512,256]{1,0:T(8,128)(2,1)}, bf16[512,256]{1,0:T(8,128)(2,1)}, u32[]{:S(2)}, u32[]{:S(2)}) collective-permute-start(bf16[512,256]{1,0:T(8,128)(2,1)} %constant_dynamic-slice_fusion.10), channel_id=1, source_target_pairs={{0,6},{1,7},{2,0},{3,1},{4,2},{5,3},{6,4},{7,5},{8,14},{9,15},{10,... | collective-permute-start | bytes 786440 | tf_op jit(solution)/shard_map/ppermute | solution.py:64
  11.1 111.9 %collective-permute-start.21 = (bf16[512,256]{1,0:T(8,128)(2,1)}, bf16[512,256]{1,0:T(8,128)(2,1)}, u32[]{:S(2)}, u32[]{:S(2)}) collective-permute-start(bf16[512,256]{1,0:T(8,128)(2,1)} %constant_dynamic-slice_fusion.10), channel_id=1, source_target_pairs={{0,4},{1,5},{2,6},{3,7},{4,0},{5,1},{6,2},{7,3},{8,12},{9,13},{10,... | collective-permute-start | bytes 786440 | tf_op jit(solution)/shard_map/ppermute | solution.py:64
  28.4 41.5 %collective-permute-start.3 = (bf16[128,3584]{1,0:T(8,128)(2,1)}, bf16[128,3584]{1,0:T(8,128)(2,1)}, u32[]{:S(2)}, u32[]{:S(2)}) collective-permute-start(bf16[128,3584]{1,0:T(8,128)(2,1)} %pad_maximum_fusion.22), channel_id=1, source_target_pairs={{0,1},{1,0},{2,3},{3,2},{4,5},{5,4},{6,7},{7,6},{8,9},{9,8},{10,11... | collective-permute-start | bytes 2752520 | tf_op jit(solution)/shard_map/ppermute | solution.py:59
  69.6 79.7 %collective-permute-start.2 = (bf16[2048,1024]{1,0:T(8,128)(2,1)}, bf16[2048,1024]{1,0:T(8,128)(2,1)}, u32[]{:S(2)}, u32[]{:S(2)}) collective-permute-start(bf16[2048,1024]{1,0:T(8,128)(2,1)} %pad_maximum_fusion.1), channel_id=1, source_target_pairs={{0,1},{1,0},{2,3},{3,2},{4,5},{5,4},{6,7},{7,6},{8,9},{9,8},{10,11... | collective-permute-start | bytes 12582920 | tf_op jit(solution)/shard_map/ppermute | solution.py:59
  77.7 23.8 %collective-permute-start.5 = (bf16[256,512]{1,0:T(8,128)(2,1)S(1)}, bf16[256,512]{1,0:T(8,128)(2,1)S(1)}, u32[]{:S(2)}, u32[]{:S(2)}) collective-permute-start(bf16[256,512]{1,0:T(8,128)(2,1)S(1)} %fusion.91), channel_id=1, source_target_pairs={{0,4},{1,5},{2,6},{3,7},{4,0},{5,1},{6,2},{7,3},{8,12},{9,13},{10,... | collective-permute-start | bytes 786440 | tf_op jit(solution)/shard_map/ppermute | solution.py:64
  115.2 23.9 %collective-permute-start.8 = (bf16[2,4,128,512]{3,2,1,0:T(8,128)(2,1)S(1)}, bf16[2,4,128,512]{3,2,1,0:T(8,128)(2,1)S(1)}, u32[]{:S(2)}, u32[]{:S(2)}) collective-permute-start(bf16[2,4,128,512]{3,2,1,0:T(8,128)(2,1)S(1)} %pad_maximum_fusion.11.refs_0_), channel_id=1, source_target_pairs={{0,16},{8,24},{16,0},{24,8},{1,17},{9,25},{17,1},{25,9},{2,18},{10... | collective-permute-start | bytes 3145736 | tf_op jit(solution)/shard_map/ppermute | solution.py:75
  116.9 23.7 %collective-permute-start.10 = (bf16[2,4,128,512]{3,2,1,0:T(8,128)(2,1)S(1)}, bf16[2,4,128,512]{3,2,1,0:T(8,128)(2,1)}, u32[]{:S(2)}, u32[]{:S(2)}) collective-permute-start(bf16[2,4,128,512]{3,2,1,0:T(8,128)(2,1)S(1)} %pad_maximum_fusion.12.refs_2_), channel_id=1, source_target_pairs={{0,8},{8,0},{16,24},{24,16},{1,9},{9,1},{17,25},{25,17},{2,10},{10... | collective-permute-start | bytes 3145736 | tf_op jit(solution)/shard_map/ppermute | solution.py:75
  130.9 137.8 %collective-permute-start.15 = (bf16[256,512]{1,0:T(8,128)(2,1)S(1)}, bf16[256,512]{1,0:T(8,128)(2,1)S(1)}, u32[]{:S(2)}, u32[]{:S(2)}) collective-permute-start(bf16[256,512]{1,0:T(8,128)(2,1)S(1)} %constant_dynamic-slice_fusion.12), channel_id=1, source_target_pairs={{0,6},{1,7},{2,0},{3,1},{4,2},{5,3},{6,4},{7,5},{8,14},{9,15},{10,... | collective-permute-start | bytes 786440 | tf_op jit(solution)/shard_map/ppermute | solution.py:64
  250.7 57.5 %collective-permute-start.11 = (f32[512,1024]{1,0:T(8,128)}, f32[512,1024]{1,0:T(8,128)}, u32[]{:S(2)}, u32[]{:S(2)}) collective-permute-start(f32[512,1024]{1,0:T(8,128)} %fusion.81), channel_id=1, source_target_pairs={{0,1},{1,0},{2,3},{3,2},{4,5},{5,4},{6,7},{7,6},{8,9},{9,8},{10,11... | collective-permute-start | bytes 6291464 | tf_op jit(solution)/shard_map/ppermute | solution.py:59
  250.8 39.5 %collective-permute-start.23 = (bf16[1,4,256,256]{3,2,1,0:T(8,128)(2,1)S(1)}, bf16[1,4,256,256]{3,2,1,0:T(8,128)(2,1)S(1)}, u32[]{:S(2)}, u32[]{:S(2)}) collective-permute-start(bf16[1,4,256,256]{3,2,1,0:T(8,128)(2,1)S(1)} %maximum_bitcast_fusion.4), channel_id=1, source_target_pairs={{0,8},{8,0},{16,24},{24,16},{1,9},{9,1},{17,25},{25,17},{2,10},{10... | collective-permute-start | bytes 1572872 | tf_op jit(solution)/shard_map/ppermute | solution.py:75
  252.4 39.6 %collective-permute-start.25 = (bf16[1,4,256,256]{3,2,1,0:T(8,128)(2,1)S(1)}, bf16[1,4,256,256]{3,2,1,0:T(8,128)(2,1)}, u32[]{:S(2)}, u32[]{:S(2)}) collective-permute-start(bf16[1,4,256,256]{3,2,1,0:T(8,128)(2,1)S(1)} %maximum_bitcast_fusion.5), channel_id=1, source_target_pairs={{0,16},{8,24},{16,0},{24,8},{1,17},{9,25},{17,1},{25,9},{2,18},{10... | collective-permute-start | bytes 1572872 | tf_op jit(solution)/shard_map/ppermute | solution.py:75
  253.0 33.6 %collective-permute-start.14 = (bf16[256,512]{1,0:T(8,128)(2,1)S(1)}, bf16[256,512]{1,0:T(8,128)(2,1)S(1)}, u32[]{:S(2)}, u32[]{:S(2)}) collective-permute-start(bf16[256,512]{1,0:T(8,128)(2,1)S(1)} %constant_dynamic-slice_fusion.12), channel_id=1, source_target_pairs={{0,4},{1,5},{2,6},{3,7},{4,0},{5,1},{6,2},{7,3},{8,12},{9,13},{10,... | collective-permute-start | bytes 786440 | tf_op jit(solution)/shard_map/ppermute | solution.py:64
  268.7 17.9 %collective-permute-start.13 = (bf16[256,512]{1,0:T(8,128)(2,1)S(1)}, bf16[256,512]{1,0:T(8,128)(2,1)S(1)}, u32[]{:S(2)}, u32[]{:S(2)}) collective-permute-start(bf16[256,512]{1,0:T(8,128)(2,1)S(1)} %constant_dynamic-slice_fusion.12), channel_id=1, source_target_pairs={{0,2},{1,3},{2,4},{3,5},{4,6},{5,7},{6,0},{7,1},{8,10},{9,11},{10,... | collective-permute-start | bytes 786440 | tf_op jit(solution)/shard_map/ppermute | solution.py:64
  289.7 15.9 %collective-permute-start.18 = (bf16[1,4,128,512]{3,2,1,0:T(8,128)(2,1)}, bf16[1,4,128,512]{3,2,1,0:T(8,128)(2,1)}, u32[]{:S(2)}, u32[]{:S(2)}) collective-permute-start(bf16[1,4,128,512]{3,2,1,0:T(8,128)(2,1)} %maximum_bitcast_fusion.3), channel_id=1, source_target_pairs={{0,16},{8,24},{16,0},{24,8},{1,17},{9,25},{17,1},{25,9},{2,18},{10... | collective-permute-start | bytes 1572872 | tf_op jit(solution)/shard_map/ppermute | solution.py:75
  290.5 36.8 %collective-permute-start.24 = (bf16[2,4,256,256]{3,2,1,0:T(8,128)(2,1)S(1)}, bf16[2,4,256,256]{3,2,1,0:T(8,128)(2,1)}, u32[]{:S(2)}, u32[]{:S(2)}) collective-permute-start(bf16[2,4,256,256]{3,2,1,0:T(8,128)(2,1)S(1)} %pad_maximum_fusion.15.refs_0_), channel_id=1, source_target_pairs={{0,16},{8,24},{16,0},{24,8},{1,17},{9,25},{17,1},{25,9},{2,18},{10... | collective-permute-start | bytes 3145736 | tf_op jit(solution)/shard_map/ppermute | solution.py:75
  293.1 34.2 %collective-permute-start.26 = (bf16[2,4,256,256]{3,2,1,0:T(8,128)(2,1)S(1)}, bf16[2,4,256,256]{3,2,1,0:T(8,128)(2,1)}, u32[]{:S(2)}, u32[]{:S(2)}) collective-permute-start(bf16[2,4,256,256]{3,2,1,0:T(8,128)(2,1)S(1)} %pad_maximum_fusion.16.refs_2_), channel_id=1, source_target_pairs={{0,8},{8,0},{16,24},{24,16},{1,9},{9,1},{17,25},{25,17},{2,10},{10... | collective-permute-start | bytes 3145736 | tf_op jit(solution)/shard_map/ppermute | solution.py:75
  303.9 44.5 %collective-permute-start.17 = (bf16[2,4,128,512]{3,2,1,0:T(8,128)(2,1)S(1)}, bf16[2,4,128,512]{3,2,1,0:T(8,128)(2,1)}, u32[]{:S(2)}, u32[]{:S(2)}) collective-permute-start(bf16[2,4,128,512]{3,2,1,0:T(8,128)(2,1)S(1)} %pad_maximum_fusion.13.refs_0_), channel_id=1, source_target_pairs={{0,16},{8,24},{16,0},{24,8},{1,17},{9,25},{17,1},{25,9},{2,18},{10... | collective-permute-start | bytes 3145736 | tf_op jit(solution)/shard_map/ppermute | solution.py:75
  307.9 40.5 %collective-permute-start.19 = (bf16[2,4,128,512]{3,2,1,0:T(8,128)(2,1)}, bf16[2,4,128,512]{3,2,1,0:T(8,128)(2,1)}, u32[]{:S(2)}, u32[]{:S(2)}) collective-permute-start(bf16[2,4,128,512]{3,2,1,0:T(8,128)(2,1)} %pad_maximum_fusion.14.refs_2_), channel_id=1, source_target_pairs={{0,8},{8,0},{16,24},{24,16},{1,9},{9,1},{17,25},{25,17},{2,10},{10... | collective-permute-start | bytes 3145736 | tf_op jit(solution)/shard_map/ppermute | solution.py:75
  315.0 38.2 %collective-permute-start.12 = (bf16[512,1024]{1,0:T(8,128)(2,1)}, bf16[512,1024]{1,0:T(8,128)(2,1)}, u32[]{:S(2)}, u32[]{:S(2)}) collective-permute-start(bf16[512,1024]{1,0:T(8,128)(2,1)} %add_convert_fusion.1), channel_id=1, source_target_pairs={{0,1},{1,0},{2,3},{3,2},{4,5},{5,4},{6,7},{7,6},{8,9},{9,8},{10,11... | collective-permute-start | bytes 3145736 | tf_op jit(solution)/shard_map/ppermute | solution.py:59
  375.6 26.1 %collective-permute-start.28 = (f32[512,1024]{1,0:T(8,128)S(1)}, f32[512,1024]{1,0:T(8,128)S(1)}, u32[]{:S(2)}, u32[]{:S(2)}) collective-permute-start(f32[512,1024]{1,0:T(8,128)S(1)} %fusion.26), channel_id=1, source_target_pairs={{0,1},{1,0},{2,3},{3,2},{4,5},{5,4},{6,7},{7,6},{8,9},{9,8},{10,11... | collective-permute-start | bytes 6291464 | tf_op jit(solution)/shard_map/ppermute | solution.py:59
  379.2 27.0 %collective-permute-start.27 = (f32[512,1024]{1,0:T(8,128)S(1)}, f32[512,1024]{1,0:T(8,128)S(1)}, u32[]{:S(2)}, u32[]{:S(2)}) collective-permute-start(f32[512,1024]{1,0:T(8,128)S(1)} %fusion.30), channel_id=1, source_target_pairs={{0,1},{1,0},{2,3},{3,2},{4,5},{5,4},{6,7},{7,6},{8,9},{9,8},{10,11... | collective-permute-start | bytes 6291464 | tf_op jit(solution)/shard_map/ppermute | solution.py:59
  397.6 48.4 %collective-permute-start.44 = (bf16[2,4,256,512]{3,2,1,0:T(8,128)(2,1)}, bf16[2,4,256,512]{3,2,1,0:T(8,128)(2,1)}, u32[]{:S(2)}, u32[]{:S(2)}) collective-permute-start(bf16[2,4,256,512]{3,2,1,0:T(8,128)(2,1)} %pad_maximum_fusion.7), channel_id=1, source_target_pairs={{0,16},{8,24},{16,0},{24,8},{1,17},{9,25},{17,1},{25,9},{2,18},{10... | collective-permute-start | bytes 6291464 | tf_op jit(solution)/shard_map/ppermute | solution.py:75
  400.0 49.4 %collective-permute-start.52 = (bf16[2,4,512,256]{3,2,1,0:T(8,128)(2,1)}, bf16[2,4,512,256]{3,2,1,0:T(8,128)(2,1)}, u32[]{:S(2)}, u32[]{:S(2)}) collective-permute-start(bf16[2,4,512,256]{3,2,1,0:T(8,128)(2,1)} %pad_maximum_fusion.8), channel_id=1, source_target_pairs={{0,8},{8,0},{16,24},{24,16},{1,9},{9,1},{17,25},{25,17},{2,10},{10... | collective-permute-start | bytes 6291464 | tf_op jit(solution)/shard_map/ppermute | solution.py:75
  413.8 40.0 %collective-permute-start.29 = (bf16[512,1024]{1,0:T(8,128)(2,1)S(1)}, bf16[512,1024]{1,0:T(8,128)(2,1)}, u32[]{:S(2)}, u32[]{:S(2)}) collective-permute-start(bf16[512,1024]{1,0:T(8,128)(2,1)S(1)} %multiply_convert_fusion.2), channel_id=1, source_target_pairs={{0,1},{1,0},{2,3},{3,2},{4,5},{5,4},{6,7},{7,6},{8,9},{9,8},{10,11... | collective-permute-start | bytes 3145736 | tf_op jit(solution)/shard_map/ppermute | solution.py:59
  448.7 25.6 %collective-permute-start.45 = (bf16[1,4,256,512]{3,2,1,0:T(8,128)(2,1)}, bf16[1,4,256,512]{3,2,1,0:T(8,128)(2,1)}, u32[]{:S(2)}, u32[]{:S(2)}) collective-permute-start(bf16[1,4,256,512]{3,2,1,0:T(8,128)(2,1)} %fusion.54), channel_id=1, source_target_pairs={{0,8},{8,0},{16,24},{24,16},{1,9},{9,1},{17,25},{25,17},{2,10},{10... | collective-permute-start | bytes 3145736 | tf_op jit(solution)/shard_map/ppermute | solution.py:75
  452.2 29.1 %collective-permute-start.53 = (bf16[1,4,512,256]{3,2,1,0:T(8,128)(2,1)}, bf16[1,4,512,256]{3,2,1,0:T(8,128)(2,1)}, u32[]{:S(2)}, u32[]{:S(2)}) collective-permute-start(bf16[1,4,512,256]{3,2,1,0:T(8,128)(2,1)} %fusion.55), channel_id=1, source_target_pairs={{0,16},{8,24},{16,0},{24,8},{1,17},{9,25},{17,1},{25,9},{2,18},{10... | collective-permute-start | bytes 3145736 | tf_op jit(solution)/shard_map/ppermute | solution.py:75
  458.5 72.2 %collective-permute-start.31 = (bf16[1024,512]{1,0:T(8,128)(2,1)}, bf16[1024,512]{1,0:T(8,128)(2,1)}, u32[]{:S(2)}, u32[]{:S(2)}) collective-permute-start(bf16[1024,512]{1,0:T(8,128)(2,1)} %get-tuple-element.222), channel_id=1, source_target_pairs={{2,0},{3,1},{4,2},{5,3},{6,4},{7,5},{10,8},{11,9},{12,10},{13,11},... | collective-permute-start | bytes 3145736 | tf_op jit(solution)/shard_map/ppermute | solution.py:70
  459.8 70.9 %collective-permute-start.30 = (bf16[1024,512]{1,0:T(8,128)(2,1)}, bf16[1024,512]{1,0:T(8,128)(2,1)}, u32[]{:S(2)}, u32[]{:S(2)}) collective-permute-start(bf16[1024,512]{1,0:T(8,128)(2,1)} %get-tuple-element.222), channel_id=1, source_target_pairs={{0,2},{1,3},{2,4},{3,5},{4,6},{5,7},{8,10},{9,11},{10,12},{11,13},... | collective-permute-start | bytes 3145736 | tf_op jit(solution)/shard_map/ppermute | solution.py:70
  467.5 20.6 %collective-permute-start.33 = (f32[16,1024]{1,0:T(8,128)S(1)}, f32[16,1024]{1,0:T(8,128)S(1)}, u32[]{:S(2)}, u32[]{:S(2)}) collective-permute-start(f32[16,1024]{1,0:T(8,128)S(1)} %pad_maximum_fusion.27), channel_id=1, source_target_pairs={{2,0},{3,1},{4,2},{5,3},{6,4},{7,5},{10,8},{11,9},{12,10},{13,11},... | collective-permute-start | bytes 196616 | tf_op jit(solution)/shard_map/ppermute | solution.py:70
  481.3 17.5 %collective-permute-start.48 = (bf16[256,512]{1,0:T(8,128)(2,1)S(1)}, bf16[256,512]{1,0:T(8,128)(2,1)S(1)}, u32[]{:S(2)}, u32[]{:S(2)}) collective-permute-start(bf16[256,512]{1,0:T(8,128)(2,1)S(1)} %get-tuple-element.151), channel_id=1, source_target_pairs={{0,6},{1,7},{2,0},{3,1},{4,2},{5,3},{6,4},{7,5},{8,14},{9,15},{10,... | collective-permute-start | bytes 786440 | tf_op jit(solution)/shard_map/ppermute | solution.py:64
  488.1 25.6 %collective-permute-start.47 = (bf16[256,512]{1,0:T(8,128)(2,1)S(1)}, bf16[256,512]{1,0:T(8,128)(2,1)S(1)}, u32[]{:S(2)}, u32[]{:S(2)}) collective-permute-start(bf16[256,512]{1,0:T(8,128)(2,1)S(1)} %get-tuple-element.152), channel_id=1, source_target_pairs={{0,4},{1,5},{2,6},{3,7},{4,0},{5,1},{6,2},{7,3},{8,12},{9,13},{10,... | collective-permute-start | bytes 786440 | tf_op jit(solution)/shard_map/ppermute | solution.py:64
  489.5 24.2 %collective-permute-start.46 = (bf16[256,512]{1,0:T(8,128)(2,1)S(1)}, bf16[256,512]{1,0:T(8,128)(2,1)S(1)}, u32[]{:S(2)}, u32[]{:S(2)}) collective-permute-start(bf16[256,512]{1,0:T(8,128)(2,1)S(1)} %get-tuple-element.150), channel_id=1, source_target_pairs={{0,2},{1,3},{2,4},{3,5},{4,6},{5,7},{6,0},{7,1},{8,10},{9,11},{10,... | collective-permute-start | bytes 786440 | tf_op jit(solution)/shard_map/ppermute | solution.py:64
  498.8 26.2 %collective-permute-start.56 = (bf16[512,256]{1,0:T(8,128)(2,1)}, bf16[512,256]{1,0:T(8,128)(2,1)S(1)}, u32[]{:S(2)}, u32[]{:S(2)}) collective-permute-start(bf16[512,256]{1,0:T(8,128)(2,1)} %get-tuple-element.142), channel_id=1, source_target_pairs={{0,6},{1,7},{2,0},{3,1},{4,2},{5,3},{6,4},{7,5},{8,14},{9,15},{10,... | collective-permute-start | bytes 786440 | tf_op jit(solution)/shard_map/ppermute | solution.py:64
  513.7 15.4 %collective-permute-start.55 = (bf16[512,256]{1,0:T(8,128)(2,1)S(1)}, bf16[512,256]{1,0:T(8,128)(2,1)}, u32[]{:S(2)}, u32[]{:S(2)}) collective-permute-start(bf16[512,256]{1,0:T(8,128)(2,1)S(1)} %get-tuple-element.143), channel_id=1, source_target_pairs={{0,4},{1,5},{2,6},{3,7},{4,0},{5,1},{6,2},{7,3},{8,12},{9,13},{10,... | collective-permute-start | bytes 786440 | tf_op jit(solution)/shard_map/ppermute | solution.py:64
  513.7 15.3 %collective-permute-start.54 = (bf16[512,256]{1,0:T(8,128)(2,1)S(1)}, bf16[512,256]{1,0:T(8,128)(2,1)}, u32[]{:S(2)}, u32[]{:S(2)}) collective-permute-start(bf16[512,256]{1,0:T(8,128)(2,1)S(1)} %get-tuple-element.141), channel_id=1, source_target_pairs={{0,2},{1,3},{2,4},{3,5},{4,6},{5,7},{6,0},{7,1},{8,10},{9,11},{10,... | collective-permute-start | bytes 786440 | tf_op jit(solution)/shard_map/ppermute | solution.py:64
  525.0 103.8 %collective-permute-start.49 = (bf16[1,256,512]{2,1,0:T(8,128)(2,1)S(1)}, bf16[1,256,512]{2,1,0:T(8,128)(2,1)S(1)}, u32[]{:S(2)}, u32[]{:S(2)}) collective-permute-start(bf16[1,256,512]{2,1,0:T(8,128)(2,1)S(1)} %fusion.89), channel_id=1, source_target_pairs={{0,8},{8,0},{16,24},{24,16},{1,9},{9,1},{17,25},{25,17},{2,10},{10... | collective-permute-start | bytes 786440 | tf_op jit(solution)/shard_map/ppermute | solution.py:75
  530.3 100.6 %collective-permute-start.57 = (bf16[1,512,256]{2,1,0:T(8,128)(2,1)S(1)}, bf16[1,512,256]{2,1,0:T(8,128)(2,1)S(1)}, u32[]{:S(2)}, u32[]{:S(2)}) collective-permute-start(bf16[1,512,256]{2,1,0:T(8,128)(2,1)S(1)} %fusion.90), channel_id=1, source_target_pairs={{0,8},{8,0},{16,24},{24,16},{1,9},{9,1},{17,25},{25,17},{2,10},{10... | collective-permute-start | bytes 786440 | tf_op jit(solution)/shard_map/ppermute | solution.py:75
  627.5 56.4 %collective-permute-start.34 = (f32[512,1024]{1,0:T(8,128)}, f32[512,1024]{1,0:T(8,128)}, u32[]{:S(2)}, u32[]{:S(2)}) collective-permute-start(f32[512,1024]{1,0:T(8,128)} %fusion.40), channel_id=1, source_target_pairs={{0,1},{1,0},{2,3},{3,2},{4,5},{5,4},{6,7},{7,6},{8,9},{9,8},{10,11... | collective-permute-start | bytes 6291464 | tf_op jit(solution)/shard_map/ppermute | solution.py:59
  628.8 37.4 %collective-permute-start.37 = (bf16[2,4,128,512]{3,2,1,0:T(8,128)(2,1)S(1)}, bf16[2,4,128,512]{3,2,1,0:T(8,128)(2,1)S(1)}, u32[]{:S(2)}, u32[]{:S(2)}) collective-permute-start(bf16[2,4,128,512]{3,2,1,0:T(8,128)(2,1)S(1)} %pad_maximum_fusion.18), channel_id=1, source_target_pairs={{0,16},{8,24},{16,0},{24,8},{1,17},{9,25},{17,1},{25,9},{2,18},{10... | collective-permute-start | bytes 3145736 | tf_op jit(solution)/shard_map/ppermute | solution.py:75
  628.9 37.2 %collective-permute-start.50 = (bf16[2,256,512]{2,1,0:T(8,128)(2,1)S(1)}, bf16[2,256,512]{2,1,0:T(8,128)(2,1)S(1)}, u32[]{:S(2)}, u32[]{:S(2)}) collective-permute-start(bf16[2,256,512]{2,1,0:T(8,128)(2,1)S(1)} %pad_maximum_fusion.24), channel_id=1, source_target_pairs={{0,16},{8,24},{16,0},{24,8},{1,17},{9,25},{17,1},{25,9},{2,18},{10... | collective-permute-start | bytes 1572872 | tf_op jit(solution)/shard_map/ppermute | solution.py:75
  631.8 45.1 %collective-permute-start.58 = (bf16[2,512,256]{2,1,0:T(8,128)(2,1)}, bf16[2,512,256]{2,1,0:T(8,128)(2,1)}, u32[]{:S(2)}, u32[]{:S(2)}) collective-permute-start(bf16[2,512,256]{2,1,0:T(8,128)(2,1)} %pad_maximum_fusion.25), channel_id=1, source_target_pairs={{0,16},{8,24},{16,0},{24,8},{1,17},{9,25},{17,1},{25,9},{2,18},{10... | collective-permute-start | bytes 1572872 | tf_op jit(solution)/shard_map/ppermute | solution.py:75
  632.9 47.0 %collective-permute-start.35 = (bf16[2,4,128,512]{3,2,1,0:T(8,128)(2,1)}, bf16[2,4,128,512]{3,2,1,0:T(8,128)(2,1)}, u32[]{:S(2)}, u32[]{:S(2)}) collective-permute-start(bf16[2,4,128,512]{3,2,1,0:T(8,128)(2,1)} %pad_maximum_fusion.17), channel_id=1, source_target_pairs={{0,8},{8,0},{16,24},{24,16},{1,9},{9,1},{17,25},{25,17},{2,10},{10... | collective-permute-start | bytes 3145736 | tf_op jit(solution)/shard_map/ppermute | solution.py:75
  697.9 32.3 %collective-permute-start.41 = (bf16[256,512]{1,0:T(8,128)(2,1)S(1)}, bf16[256,512]{1,0:T(8,128)(2,1)S(1)}, u32[]{:S(2)}, u32[]{:S(2)}) collective-permute-start(bf16[256,512]{1,0:T(8,128)(2,1)S(1)} %get-tuple-element.158), channel_id=1, source_target_pairs={{0,6},{1,7},{2,0},{3,1},{4,2},{5,3},{6,4},{7,5},{8,14},{9,15},{10,... | collective-permute-start | bytes 786440 | tf_op jit(solution)/shard_map/ppermute | solution.py:64
  703.1 45.6 %collective-permute-start.40 = (bf16[256,512]{1,0:T(8,128)(2,1)S(1)}, bf16[256,512]{1,0:T(8,128)(2,1)S(1)}, u32[]{:S(2)}, u32[]{:S(2)}) collective-permute-start(bf16[256,512]{1,0:T(8,128)(2,1)S(1)} %get-tuple-element.157), channel_id=1, source_target_pairs={{0,4},{1,5},{2,6},{3,7},{4,0},{5,1},{6,2},{7,3},{8,12},{9,13},{10,... | collective-permute-start | bytes 786440 | tf_op jit(solution)/shard_map/ppermute | solution.py:64
  727.1 21.6 %collective-permute-start.39 = (bf16[256,512]{1,0:T(8,128)(2,1)S(1)}, bf16[256,512]{1,0:T(8,128)(2,1)S(1)}, u32[]{:S(2)}, u32[]{:S(2)}) collective-permute-start(bf16[256,512]{1,0:T(8,128)(2,1)S(1)} %get-tuple-element.156), channel_id=1, source_target_pairs={{0,2},{1,3},{2,4},{3,5},{4,6},{5,7},{6,0},{7,1},{8,10},{9,11},{10,... | collective-permute-start | bytes 786440 | tf_op jit(solution)/shard_map/ppermute | solution.py:64
  755.4 43.7 %collective-permute-start.43 = (bf16[2,256,512]{2,1,0:T(8,128)(2,1)S(1)}, bf16[2,256,512]{2,1,0:T(8,128)(2,1)S(1)}, u32[]{:S(2)}, u32[]{:S(2)}) collective-permute-start(bf16[2,256,512]{2,1,0:T(8,128)(2,1)S(1)} %pad_maximum_fusion.23), channel_id=1, source_target_pairs={{0,16},{8,24},{16,0},{24,8},{1,17},{9,25},{17,1},{25,9},{2,18},{10... | collective-permute-start | bytes 1572872 | tf_op jit(solution)/shard_map/ppermute | solution.py:75
  (101 other events, 1309.4 us)

commit v2 on v1

v2 whole, which is shorter than its diff:
```python
import functools
import math

import jax
import jax.numpy as jnp
from jax import lax
from jax.experimental import pallas as pl
from jax.experimental.pallas import tpu as pltpu
from jax.sharding import PartitionSpec as P

D = 1024
HEADS = 16
HEAD_DIM = 64
LANES = 128

EPSILON = 1e-06
MASKED = -1e30
BLOCK = 256

f32 = jnp.float32
bf16 = jnp.bfloat16


def normalize(features):
    row_mean = jnp.mean(features, axis=-1, keepdims=True)
    centred = features - row_mean
    variance = jnp.mean(centred * centred, axis=-1, keepdims=True)
    inverse = lax.rsqrt(variance + EPSILON)
    return centred * inverse, inverse


def norm_back(gradient, normal, inverse, gain_vec):
    scaled = gradient * gain_vec
    mean_first = jnp.mean(scaled, axis=-1, keepdims=True)
    mean_second = jnp.mean(scaled * normal, axis=-1, keepdims=True)
    return inverse * (scaled - mean_first - normal * mean_second)


def gelu_pair(values):
    cumulative = 0.5 * (1.0 + lax.erf(values * 2.0 ** (-0.5)))
    density = jnp.exp(-0.5 * values * values) * (2.0 * math.pi) ** (-0.5)
    return (values * cumulative, cumulative + values * density)


def dot(a, b):
    return jnp.dot(a, b, preferred_element_type=f32)


def dot_nt(a, b):
    return lax.dot_general(a, b, (((1,), (1,)), ((), ())), preferred_element_type=f32)


def dot_tn(a, b):
    return lax.dot_general(a, b, (((0,), (0,)), ((), ())), preferred_element_type=f32)


def swap_cores(value):
    size = lax.axis_size("fsdp")
    return lax.ppermute(value, "fsdp", [(i, i ^ 1) for i in range(size)])


def along_z(value, by):
    size = lax.axis_size("fsdp")
    return lax.ppermute(value, "fsdp", [(i, (i + 2 * by) % size) for i in range(size)])


def from_chip(value, by):
    size = lax.axis_size("fsdp")
    pairs = [(i, i + 2 * by) for i in range(size) if 0 <= i + 2 * by < size]
    return lax.ppermute(value, "fsdp", pairs)


def across_rep(value, bit):
    size = lax.axis_size("rep")
    return lax.ppermute(value, "rep", [(i, i ^ (1 << bit)) for i in range(size)])


def pick(value, index, axis):
    return lax.dynamic_index_in_dim(value, index, axis, keepdims=False)


def rep_bits():
    return lax.axis_size("rep").bit_length() - 1


def tie(*values):
    return lax.optimization_barrier(values)


def fetch_z(own):
    return [own] + [along_z(own, k) for k in range(1, lax.axis_size("fsdp") // 2)]


class Gather:
    def __init__(self, pieces, rows, name):
        self.rows, self.cols, self.name = rows, pieces[0].shape[1], name
        half = rows // 2
        bits = list(range(rep_bits()))
        self.orders = [bits, bits[::-1]]
        self.parts = [
            [(jnp.stack([p[:half] for p in pieces])[None], [0])],
            [(jnp.stack([p[half:rows] for p in pieces])[None], [0])],
        ]
        self.at = 0

    def send(self, *values):
        whole = [
            (ps[0][0] if len(ps) == 1 else jnp.concatenate([a for a, _ in ps]), [o for _, os in ps for o in os])
            for ps in self.parts
        ]
        values, arrays = lax.optimization_barrier((values, [a for a, _ in whole]))
        self.parts = []
        for array, (_, offsets), order in zip(arrays, whole, self.orders):
            flip = 1 << order[self.at]
            received = across_rep(array, order[self.at])
            self.parts.append([(array, offsets), (received, [o ^ flip for o in offsets])])
        self.at += 1
        return values[0] if len(values) == 1 else values

    def arrive(self, value):
        value, arrays = lax.optimization_barrier((value, [a for ps in self.parts for a, _ in ps]))
        self.parts = [[(arrays.pop(0), o) for _, o in ps] for ps in self.parts]
        return value

    def assemble(self, here, rank, tail_rows=0):
        depth, ranks = lax.axis_size("fsdp") // 2, lax.axis_size("rep")
        sources, plan = [], []
        for number, parts in enumerate(self.parts):
            for array, offsets in parts:
                sources.append(array)
                plan.append((number, offsets))
        dtype = sources[0].dtype
        shape = (depth * self.rows, ranks * self.cols)
        shapes = [jax.ShapeDtypeStruct(shape, dtype)]
        if tail_rows:
            tail = shape[1] // 4
            shapes = [
                jax.ShapeDtypeStruct((shape[0], shape[1] - tail), dtype),
                jax.ShapeDtypeStruct((depth * tail_rows, 2 * tail), dtype),
            ]
        out = pl.pallas_call(
            functools.partial(assemble_kernel, plan, depth, self.rows, self.cols, tail_rows),
            out_shape=shapes,
            grid_spec=pltpu.PrefetchScalarGridSpec(
                num_scalar_prefetch=1,
                grid=(1,),
                in_specs=[pl.BlockSpec(memory_space=pl.ANY)] * len(sources),
                out_specs=[pl.BlockSpec(memory_space=pl.ANY)] * len(shapes),
                scratch_shapes=[
                    pltpu.VMEM(shape, dtype),
                    pltpu.SemaphoreType.DMA((2 * ranks * depth,)),
                    pltpu.SemaphoreType.DMA((3 * depth,)),
                ],
            ),
            compiler_params=pltpu.CompilerParams(vmem_limit_bytes=16 << 20),
            cost_estimate=pl.CostEstimate(
                flops=0, transcendentals=0, bytes_accessed=2 * shape[0] * shape[1] * dtype.itemsize
            ),
            name=self.name,
        )(jnp.stack([here, rank]).astype(jnp.int32), *sources)
        return out if tail_rows else out[0]


def assemble_kernel(plan, depth, rows, cols, tail_rows, index_ref, *refs):
    count = len(plan)
    sources = refs[:count]
    targets = refs[count : count + (2 if tail_rows else 1)]
    held, in_sems, out_sems = refs[-3:]
    here, rank = index_ref[0], index_ref[1]
    half = rows // 2
    waits = [[] for _ in range(depth)]
    number = 0
    for k in range(depth):
        place = lax.rem(here - k + depth, depth)
        for which, (colour, offsets) in enumerate(plan):
            for m, offset in enumerate(offsets):
                at_row = pl.multiple_of(place * rows + colour * half, half)
                at_col = pl.multiple_of((rank ^ offset) * cols, cols)
                copy = pltpu.make_async_copy(
                    sources[which].at[m, k],
                    held.at[pl.ds(at_row, half), pl.ds(at_col, cols)],
                    in_sems.at[number],
                )
                copy.start()
                waits[k].append(copy)
                number += 1
    outs = []
    main = targets[0].shape[1]
    for k in range(depth):
        place = lax.rem(here - k + depth, depth)
        for copy in waits[k]:
            copy.wait()
        base = pl.multiple_of(place * rows, rows)
        band = pl.ds(base, rows)
        out = pltpu.make_async_copy(held.at[band, pl.ds(0, main)], targets[0].at[band], out_sems.at[3 * k])
        out.start()
        outs.append(out)
        if tail_rows:
            wide = targets[1].shape[1] // 2
            for side in range(2):
                out = pltpu.make_async_copy(
                    held.at[pl.ds(base + side * tail_rows, tail_rows), pl.ds(main, wide)],
                    targets[1].at[
                        pl.ds(pl.multiple_of(place * tail_rows, tail_rows), tail_rows),
                        pl.ds(side * wide, wide),
                    ],
                    out_sems.at[3 * k + 1 + side],
                )
                out.start()
                outs.append(out)
    for out in outs:
        out.wait()


def halves(ranks, bit, held):
    flip = 1 << bit
    kept = [o for o in held if not o & flip]
    return kept, [o ^ flip for o in kept]


def relative_blocks(grads, rank, orders):
    depth, ranks = lax.axis_size("fsdp") // 2, lax.axis_size("rep")
    width = grads.shape[1] // ranks
    rows = grads.shape[0] // depth
    shaped = grads.reshape(depth, rows, grads.shape[1])
    share = rows // len(orders)
    first = []
    for n, order in enumerate(orders):
        block = lambda o: lax.dynamic_slice(
            shaped, (0, n * share, (rank ^ o) * width), (depth, share, width)
        )
        kept, given = halves(ranks, order[0], list(range(ranks)))
        first.append((jnp.stack([block(o) for o in kept]), jnp.stack([block(o) for o in given])))
    return first


class Reduce:
    def __init__(self, first, here, orders):
        self.here, self.orders, self.at = here, orders, 0
        ranks = lax.axis_size("rep")
        self.held = []
        for (keep, give), order in zip(first, orders):
            kept, given = halves(ranks, order[0], list(range(ranks)))
            self.held.append((kept, keep, give))

    def send(self, *values):
        values, gives = lax.optimization_barrier((values, [give for _, _, give in self.held]))
        self.received = [across_rep(g, order[self.at]) for g, order in zip(gives, self.orders)]
        self.at += 1
        return values[0] if len(values) == 1 else values

    def arrive(self, *values):
        values, received = lax.optimization_barrier((values, self.received))
        held = []
        for (kept, keep, _), got, order in zip(self.held, received, self.orders):
            total = (keep.astype(f32) + got.astype(f32)).astype(bf16)
            if self.at < len(order):
                stay, leave = halves(None, order[self.at], kept)
                take = lambda os: jnp.stack([total[kept.index(o)] for o in os])
                held.append((stay, take(stay), take(leave)))
            else:
                held.append((kept, total[0], None))
        self.held = held
        return values[0] if len(values) == 1 else values

    def send_z(self, *values):
        depth = lax.axis_size("fsdp") // 2
        parts = [keep for _, keep, _ in self.held]
        whole = parts[0] if len(parts) == 1 else jnp.concatenate(parts, axis=1)
        pieces = [pick(whole, lax.rem(self.here + k, depth), 0) for k in range(depth)]
        values, pieces = lax.optimization_barrier((values, pieces))
        self.pieces = [pieces[0]] + [along_z(p, k) for k, p in enumerate(pieces) if k]
        return values[0] if len(values) == 1 else values

    def arrive_z(self, *values):
        values, pieces = lax.optimization_barrier((values, self.pieces))
        total = pieces[0].astype(f32)
        for piece in pieces[1:]:
            total = total + piece.astype(f32)
        self.total = total
        return values[0] if len(values) == 1 else values


def rep_blocks(stacked, offsets, rank):
    blocks = []
    for i in range(len(offsets)):
        block = stacked[0]
        for entry, offset in enumerate(offsets):
            block = jnp.where((rank ^ offset) == i, stacked[entry], block)
        blocks.append(block)
    return jnp.concatenate(blocks, axis=1)


def whole_specs(arrays):
    return [pl.BlockSpec(a.shape, lambda *_, n=len(a.shape): (0,) * n) for a in arrays]


def slot_lists(sizes):
    slots = []
    for number, size in enumerate(sizes):
        for start in range(0, size, LANES):
            slots.append((number, start, min(LANES, size - start)))
    return slots


def pack_kernel(slots, *refs):
    *sources, out_ref, held = refs
    per_row = held.shape[1] // LANES
    held[...] = jnp.zeros_like(held)
    for slot, (number, start, size) in enumerate(slots):
        row, at = slot // per_row, slot % per_row * LANES
        held[row : row + 1, at : at + size] = sources[number][:, start : start + size].astype(f32)
    out_ref[...] = held[...].astype(out_ref.dtype)


def pack_small(vectors, width, slots):
    shape = (32 * LANES // width, width)
    vectors = [v.reshape(1, -1) for v in vectors]
    return pl.pallas_call(
        functools.partial(pack_kernel, slots),
        out_shape=jax.ShapeDtypeStruct(shape, bf16),
        scratch_shapes=[pltpu.VMEM(shape, f32)],
        name="pack_small",
    )(*vectors)


def unpack_kernel(slots, depth, index_ref, *refs):
    pieces, (vec_ref, unit_ref, tag_ref) = refs[:depth], refs[depth:]
    here, core = index_ref[0], index_ref[1]
    rows, width = pieces[0].shape
    per_row = width // LANES
    single = sum(1 for number, _, _ in slots if number < 10)
    vec_ref[...] = jnp.zeros_like(vec_ref)
    for k in range(depth):
        place = lax.rem(here - k + depth, depth)
        values = pieces[k][...].astype(f32)

        def part(side, slot, size):
            row, at = side * (rows // 2) + slot // per_row, slot % per_row * LANES
            return values[row : row + 1, at : at + size]

        for slot, (number, start, size) in enumerate(slots):
            own, other = part(0, slot, size), part(1, slot, size)
            first = jnp.where(core == 0, own, other)
            second = jnp.where(core == 0, other, own)
            if number < 10:
                at = pl.multiple_of(place * 2 * size, 2 * size)
                vec_ref[number : number + 1, pl.ds(at, 2 * size)] = jnp.concatenate([first, second], axis=1)
            elif number == 10:
                wide = unit_ref.shape[1] // depth
                unit_ref[0:1, pl.ds(pl.multiple_of(place * wide + start, LANES), LANES)] = own
            else:
                wide = tag_ref.shape[1] // depth
                at = pl.multiple_of(place * wide + start, LANES)
                tag_ref[0:1, pl.ds(at, LANES)] = first
                tag_ref[0:1, pl.ds(pl.multiple_of(at + wide // 2, LANES), LANES)] = second


def unpack_small(pieces, slots, rows, here, core, units, group_tokens):
    depth = len(pieces)
    extra, width = pieces[0].shape[0] - rows, pieces[0].shape[1]
    shapes = [(16, D), (1, units), (1, group_tokens)]
    return pl.pallas_call(
        functools.partial(unpack_kernel, slots, depth),
        out_shape=[jax.ShapeDtypeStruct(s, f32) for s in shapes],
        grid_spec=pltpu.PrefetchScalarGridSpec(
            num_scalar_prefetch=1,
            grid=(1,),
            in_specs=[pl.BlockSpec((extra, width), lambda i, a: (rows // extra, 0))] * depth,
            out_specs=[pl.BlockSpec(s, lambda i, a: (0, 0)) for s in shapes],
        ),
        name="unpack_small",
    )(jnp.stack([here, core]).astype(jnp.int32), *pieces)


def pack_grads_kernel(depth, sizes, index_ref, *refs):
    *sources, out_ref = refs
    core = index_ref[0]
    out_ref[...] = jnp.zeros_like(out_ref)
    for z in range(depth):
        for c in range(2):
            row = 16 * c
            for source, (size, of_core) in zip(sources, sizes):
                for start in range(0, size, LANES):
                    lanes = min(LANES, size - start)
                    at = (z if of_core else 2 * z + c) * size + start
                    value = source[0:1, at : at + lanes]
                    if of_core:
                        value = jnp.where(core == c, value, 0.0)
                    out_ref[z, row : row + 1, 0:lanes] = value
                    row += 1


def pack_grads(vectors, sizes, core, depth):
    return pl.pallas_call(
        functools.partial(pack_grads_kernel, depth, sizes),
        out_shape=jax.ShapeDtypeStruct((depth, 32, LANES), f32),
        grid_spec=pltpu.PrefetchScalarGridSpec(
            num_scalar_prefetch=1,
            grid=(1,),
            in_specs=whole_specs(vectors),
            out_specs=pl.BlockSpec((depth, 32, LANES), lambda i, a: (0, 0, 0)),
        ),
        name="pack_grads",
    )(core.reshape(1).astype(jnp.int32), *vectors)


def proj_grad_kernel(head_rows, c_ref, g_ref, out_ref):
    wide = out_ref.shape[1]
    for side in range(2):
        grad = dot_tn(c_ref[...], g_ref[:, side * wide : (side + 1) * wide]).astype(bf16)
        for z in range(grad.shape[0] // head_rows):
            at = (2 * z + side) * head_rows
            out_ref[at : at + head_rows, :] = grad[z * head_rows : (z + 1) * head_rows]


def packed_proj_grad(context, attn_grad, head_rows):
    wide = D // 2
    return pl.pallas_call(
        functools.partial(proj_grad_kernel, head_rows),
        out_shape=jax.ShapeDtypeStruct((D, wide), bf16),
        compiler_params=pltpu.CompilerParams(vmem_limit_bytes=32 << 20),
        cost_estimate=pl.CostEstimate(flops=2 * context.shape[0] * D * wide, transcendentals=0, bytes_accessed=6 << 20),
        name="proj_grad",
    )(context, attn_grad)


def qkv_grad_kernel(orders, ranks, depth, per, index_ref, n_ref, *refs):
    grads, p_ref = refs[: 3 * per], refs[3 * per]
    outs, held = refs[3 * per + 1 : -1], refs[-1]
    rank = index_ref[0]
    normed = n_ref[...]
    for number in range(3):
        pieces = [g[...] for g in grads[number * per : (number + 1) * per]]
        wide = per * LANES
        joined = pieces[0] if per == 1 else jnp.concatenate(pieces, axis=1)
        held[:, number * wide : (number + 1) * wide] = dot_tn(normed, joined).astype(bf16)
    held[:, 3 * per * LANES :] = p_ref[...]
    width = held.shape[1] // ranks
    rows = held.shape[0] // depth
    share = rows // len(orders)
    for n, order in enumerate(orders):
        for which, offsets in enumerate(halves(ranks, order[0], list(range(ranks)))):
            for i, o in enumerate(offsets):
                cols = pl.ds(pl.multiple_of((rank ^ o) * width, width), width)
                for z in range(depth):
                    at = z * rows + n * share
                    outs[2 * n + which][i, z] = held[at : at + share, cols]


def qkv_grad_blocks(normed, grads, proj_packed, part, parts, rank, orders):
    depth, ranks = lax.axis_size("fsdp") // 2, lax.axis_size("rep")
    per = len(grads) // 3
    cols = 4 * per * LANES
    block = (ranks // 2, depth, D // depth // len(orders), cols // ranks)
    tokens = normed.shape[0] // 3
    outs = pl.pallas_call(
        functools.partial(qkv_grad_kernel, orders, ranks, depth, per),
        out_shape=[jax.ShapeDtypeStruct(block, bf16)] * (2 * len(orders)),
        grid_spec=pltpu.PrefetchScalarGridSpec(
            num_scalar_prefetch=1,
            grid=(1,),
            in_specs=[pl.BlockSpec((tokens, D), lambda i, a: (1, 0))]
            + whole_specs(grads)
            + [pl.BlockSpec((D, per * LANES), lambda i, a: (0, part))],
            out_specs=[pl.BlockSpec(block, lambda i, a: (0, 0, 0, 0))] * (2 * len(orders)),
            scratch_shapes=[pltpu.VMEM((D, cols), bf16)],
        ),
        compiler_params=pltpu.CompilerParams(vmem_limit_bytes=40 << 20),
        cost_estimate=pl.CostEstimate(flops=2 * tokens * D * cols, transcendentals=0, bytes_accessed=8 << 20),
        name="qkv_grad",
    )(rank.reshape(1).astype(jnp.int32), normed, *grads, proj_packed)
    return [(outs[2 * n], outs[2 * n + 1]) for n in range(len(orders))]


def spread_lanes(tags, width):
    return jnp.concatenate([tags] * (width // LANES), axis=1)


def project_kernel(need_ref, n_ref, w_ref, b_ref, q_ref, k_ref, v_ref):
    row = pl.program_id(0)
    wide = q_ref.shape[1]

    @pl.when(need_ref[row] > 0)
    def _():
        n = n_ref[...]
        for i, ref in enumerate((q_ref, k_ref, v_ref)):
            out = dot(n, w_ref[:, i * wide : (i + 1) * wide]) + b_ref[0:1, i * wide : (i + 1) * wide]
            if i == 0:
                out = out.astype(bf16).astype(f32) * HEAD_DIM ** (-0.5)
            ref[...] = out.astype(bf16)

    @pl.when(need_ref[row] == 0)
    def _():
        for ref in (q_ref, k_ref, v_ref):
            ref[...] = jnp.zeros_like(ref)


def project(need, normed, weight, bias, wide):
    rows = normed.shape[0]
    return pl.pallas_call(
        project_kernel,
        out_shape=[jax.ShapeDtypeStruct((rows, wide), bf16)] * 3,
        grid_spec=pltpu.PrefetchScalarGridSpec(
            num_scalar_prefetch=1,
            grid=(rows // BLOCK,),
            in_specs=[
                pl.BlockSpec((BLOCK, D), lambda i, s: (i, 0)),
                pl.BlockSpec(weight.shape, lambda i, s: (0, 0)),
                pl.BlockSpec((1, 3 * wide), lambda i, s: (0, 0)),
            ],
            out_specs=[pl.BlockSpec((BLOCK, wide), lambda i, s: (i, 0))] * 3,
        ),
        compiler_params=pltpu.CompilerParams(vmem_limit_bytes=32 << 20),
        cost_estimate=pl.CostEstimate(
            flops=2 * rows * D * 3 * wide, transcendentals=0, bytes_accessed=rows * D * 6
        ),
        name="project",
    )(need, normed, weight, bias)


def norm_kernel(need_ref, info_ref, *refs):
    *sources, vec_ref, out_ref = refs
    row = pl.program_id(0)
    side = (row // info_ref[1]) % 2
    chip = row // (2 * info_ref[1])

    @pl.when(need_ref[row] > 0)
    def _():
        picked = jnp.where(chip == 0, sources[0][...], jnp.where(chip == 1, sources[2][...], sources[4][...]))
        theirs = jnp.where(chip == 0, sources[1][...], jnp.where(chip == 1, sources[3][...], sources[5][...]))
        picked = jnp.where(side == info_ref[0], picked, theirs)
        normal, _ = normalize(picked.astype(f32))
        out_ref[...] = (normal * vec_ref[0:1, :] + vec_ref[1:2, :]).astype(bf16)

    @pl.when(need_ref[row] == 0)
    def _():
        out_ref[...] = jnp.zeros_like(out_ref)


def norm_window(need, info, sources, vecs, window, count):
    per = count // BLOCK

    def spec(chip):
        def index(i, a, b):
            inside = jnp.clip(i - 2 * per * chip, 0, 2 * per - 1)
            return (inside % per, 0)

        return pl.BlockSpec((BLOCK, D), index)

    return pl.pallas_call(
        norm_kernel,
        out_shape=jax.ShapeDtypeStruct((window, D), bf16),
        grid_spec=pltpu.PrefetchScalarGridSpec(
            num_scalar_prefetch=2,
            grid=(window // BLOCK,),
            in_specs=[spec(i // 2) for i in range(6)] + [pl.BlockSpec(vecs.shape, lambda i, a, b: (0, 0))],
            out_specs=pl.BlockSpec((BLOCK, D), lambda i, a, b: (i, 0)),
        ),
        compiler_params=pltpu.CompilerParams(vmem_limit_bytes=24 << 20),
        cost_estimate=pl.CostEstimate(flops=window * D * 10, transcendentals=0, bytes_accessed=30 << 20),
        name="norm_window",
    )(need, info, *sources, vecs)


def attend_kernel(lo_ref, hi_ref, first_ref, last_ref, q_ref, k_ref, v_ref, qt_ref, kt_ref, o_ref, lse_ref, s_ref, m_ref):
    i = pl.program_id(0)
    left = lax.broadcasted_iota(jnp.int32, (1, LANES), 1) < HEAD_DIM
    lo, hi = lo_ref[i], hi_ref[i]
    base = (first_ref.shape[0] - pl.num_programs(0)) // 2
    q = q_ref[...]
    zero = jnp.zeros_like(q)
    heads = (jnp.where(left, q, zero), jnp.where(left, zero, q))
    m_ref[...] = jnp.full_like(m_ref, MASKED)
    one_image = first_ref[base + i] == last_ref[base + i]
    folds = BLOCK // LANES

    def fold(value, combine):
        parts = [value[:, n * LANES : (n + 1) * LANES] for n in range(folds)]
        return functools.reduce(combine, parts)

    def scores(j, carry):
        at = pl.multiple_of(j * BLOCK, BLOCK)
        k = k_ref[pl.ds(at, BLOCK), :]
        inside = one_image & (first_ref[j] == first_ref[base + i]) & (last_ref[j] == first_ref[base + i])

        @pl.when(inside)
        def _():
            for h in range(2):
                s = dot_nt(heads[h], k)
                s_ref[h, j] = s
                m_ref[h] = jnp.maximum(m_ref[h], fold(s, jnp.maximum))

        @pl.when(jnp.logical_not(inside))
        def _():
            same = spread_lanes(qt_ref[...], BLOCK) == kt_ref[:, pl.ds(at, BLOCK)]
            for h in range(2):
                s = jnp.where(same, dot_nt(heads[h], k), MASKED)
                s_ref[h, j] = s
                m_ref[h] = jnp.maximum(m_ref[h], fold(s, jnp.maximum))

        return carry

    lax.fori_loop(lo, hi, scores, 0)
    tops = [jnp.max(m_ref[h], axis=1, keepdims=True) for h in range(2)]
    m_ref[...] = jnp.zeros_like(m_ref)

    def powers(j, carry):
        for h in range(2):
            e = jnp.exp(s_ref[h, j] - tops[h])
            s_ref[h, j] = e
            m_ref[h] += fold(e, jnp.add)
        return carry

    lax.fori_loop(lo, hi, powers, 0)
    sums = [jnp.sum(m_ref[h], axis=1, keepdims=True) for h in range(2)]
    shares = [1.0 / s for s in sums]
    m_ref[...] = jnp.zeros_like(m_ref)

    def mix(j, carry):
        at = pl.multiple_of(j * BLOCK, BLOCK)
        v = v_ref[pl.ds(at, BLOCK), :]
        for h in range(2):
            m_ref[h] += dot((s_ref[h, j] * shares[h]).astype(bf16), v)
        return carry

    lax.fori_loop(lo, hi, mix, 0)
    o_ref[...] = jnp.where(left, m_ref[0], m_ref[1]).astype(bf16)
    for h in range(2):
        lse = jnp.broadcast_to(tops[h] + jnp.log(sums[h]), (BLOCK, LANES))
        lse_ref[0, h : h + 1, :] = lse.T[0:1, :]


def attend(lo, hi, firsts, lasts, q, k, v, tag_cols, tag_row, own_rows, pair):
    window = q.shape[0]
    blocks = own_rows // BLOCK
    skip = (window - own_rows) // 2 // BLOCK
    return pl.pallas_call(
        attend_kernel,
        out_shape=[
            jax.ShapeDtypeStruct((own_rows, LANES), bf16),
            jax.ShapeDtypeStruct((1, 2, own_rows), f32),
        ],
        grid_spec=pltpu.PrefetchScalarGridSpec(
            num_scalar_prefetch=4,
            grid=(blocks,),
            in_specs=[
                pl.BlockSpec((BLOCK, LANES), lambda i, *_: (i + skip, pair)),
                pl.BlockSpec((window, LANES), lambda i, *_: (0, pair)),
                pl.BlockSpec((window, LANES), lambda i, *_: (0, pair)),
                pl.BlockSpec((BLOCK, LANES), lambda i, *_: (i + skip, 0)),
                pl.BlockSpec((1, window), lambda i, *_: (0, 0)),
            ],
            out_specs=[
                pl.BlockSpec((BLOCK, LANES), lambda i, *_: (i, 0)),
                pl.BlockSpec((1, 2, BLOCK), lambda i, *_: (0, 0, i)),
            ],
            scratch_shapes=[
                pltpu.VMEM((2, window // BLOCK, BLOCK, BLOCK), f32),
                pltpu.VMEM((2, BLOCK, LANES), f32),
            ],
        ),
        compiler_params=pltpu.CompilerParams(vmem_limit_bytes=32 << 20),
        cost_estimate=pl.CostEstimate(
            flops=90 * own_rows * own_rows * LANES,
            transcendentals=own_rows * own_rows * 2,
            bytes_accessed=window * LANES * 6,
        ),
        name="attend",
    )(lo, hi, firsts, lasts, q, k, v, tag_cols, tag_row)


def attend_back_kernel(
    start, stop, lo_ref, hi_ref, q_ref, k_ref, v_ref, g_ref, tc_ref, tr_ref, lse_ref, delta_ref,
    dq_ref, dk_ref, dv_ref, sum_ref, dk_acc, dv_acc, dq_acc,
):
    first = lax.broadcasted_iota(jnp.int32, (1, LANES), 1) < HEAD_DIM
    dk_acc[...] = jnp.zeros_like(dk_acc)
    dv_acc[...] = jnp.zeros_like(dv_acc)
    sum_ref[...] = jnp.zeros_like(sum_ref)

    def split(value):
        zero = jnp.zeros_like(value)
        return jnp.where(first, value, zero), jnp.where(first, zero, value)

    def query_block(i, carry):
        at_q = pl.multiple_of(i * BLOCK, BLOCK)
        own_q = jnp.logical_and(i >= start, i < stop)
        lo = jnp.where(own_q, lo_ref[i], jnp.maximum(lo_ref[i], start))
        hi = jnp.where(own_q, hi_ref[i], jnp.minimum(hi_ref[i], stop))

        @pl.when(own_q)
        def _():
            dq_acc[...] = jnp.zeros_like(dq_acc)

        def key_block(j, carry):
            at_k = pl.multiple_of(j * BLOCK, BLOCK)
            k = k_ref[pl.ds(at_k, BLOCK), :]
            v = v_ref[pl.ds(at_k, BLOCK), :]
            qs = split(q_ref[pl.ds(at_q, BLOCK), :])
            gs = split(g_ref[pl.ds(at_q, BLOCK), :])
            same = spread_lanes(tc_ref[pl.ds(at_k, BLOCK), :], BLOCK) == tr_ref[:, pl.ds(at_q, BLOCK)]
            ps, ds = [], []
            for h in range(2):
                s = dot_nt(k, qs[h])
                p = jnp.where(same, jnp.exp(s - lse_ref[0, h : h + 1, pl.ds(at_q, BLOCK)]), 0.0)
                dp = dot_nt(v, gs[h])
                d = p * (dp - delta_ref[0, h : h + 1, pl.ds(at_q, BLOCK)])
                ps.append(p.astype(bf16))
                ds.append(d.astype(bf16))

            @pl.when(jnp.logical_and(j >= start, j < stop))
            def _():
                at = pl.multiple_of((j - start) * BLOCK, BLOCK)
                dv_acc[pl.ds(at, BLOCK), :] += dot(ps[0], gs[0]) + dot(ps[1], gs[1])
                dk_acc[pl.ds(at, BLOCK), :] += dot(ds[0], qs[0]) + dot(ds[1], qs[1])

            @pl.when(own_q)
            def _():
                ks = split(k)
                dq_acc[...] += dot_tn(ds[0], ks[0]) + dot_tn(ds[1], ks[1])

            return carry

        lax.fori_loop(lo, hi, key_block, 0)

        @pl.when(own_q)
        def _():
            at = pl.multiple_of((i - start) * BLOCK, BLOCK)
            dq = dq_acc[...] * HEAD_DIM ** (-0.5)
            dq_ref[pl.ds(at, BLOCK), :] = dq.astype(bf16)
            sum_ref[0, 0:1, :] += jnp.sum(dq, axis=0, keepdims=True)

        return carry

    lax.fori_loop(0, q_ref.shape[0] // BLOCK, query_block, 0)
    dk_ref[...] = dk_acc[...].astype(bf16)
    dv_ref[...] = dv_acc[...].astype(bf16)
    sum_ref[0, 1:2, :] = jnp.sum(dv_acc[...], axis=0, keepdims=True)


def attend_back(lo, hi, q, k, v, g, tag_cols, tag_row, lse, delta, own_rows, pair):
    window = q.shape[0]
    pairs, wide = 1, LANES
    start = (window - own_rows) // 2 // BLOCK
    stop = start + own_rows // BLOCK
    whole = lambda: pl.BlockSpec((window, LANES), lambda p, a, b: (0, pair))
    own = lambda: pl.BlockSpec((own_rows, LANES), lambda p, a, b: (0, p))
    stat = lambda: pl.BlockSpec((1, 2, window), lambda p, a, b: (pair, 0, 0))
    return pl.pallas_call(
        functools.partial(attend_back_kernel, start, stop),
        out_shape=[jax.ShapeDtypeStruct((own_rows, wide), bf16)] * 3
        + [jax.ShapeDtypeStruct((pairs, 8, LANES), f32)],
        grid_spec=pltpu.PrefetchScalarGridSpec(
            num_scalar_prefetch=2,
            grid=(pairs,),
            in_specs=[
                whole(), whole(), whole(), whole(),
                pl.BlockSpec((window, LANES), lambda p, a, b: (0, 0)),
                pl.BlockSpec((1, window), lambda p, a, b: (0, 0)),
                stat(), stat(),
            ],
            out_specs=[own(), own(), own(), pl.BlockSpec((1, 8, LANES), lambda p, a, b: (p, 0, 0))],
            scratch_shapes=[
                pltpu.VMEM((own_rows, LANES), f32),
                pltpu.VMEM((own_rows, LANES), f32),
                pltpu.VMEM((BLOCK, LANES), f32),
            ],
        ),
        compiler_params=pltpu.CompilerParams(vmem_limit_bytes=40 << 20),
        cost_estimate=pl.CostEstimate(
            flops=180 * own_rows * own_rows * LANES,
            transcendentals=own_rows * own_rows * 2,
            bytes_accessed=window * wide * 8,
        ),
        name="attend_back",
    )(lo, hi, q, k, v, g, tag_cols, tag_row, lse, delta)


def on_device(
    tokens, image_ids, ln1_gain, ln1_bias, qkv_weight, query_bias, value_bias, proj_weight,
    proj_bias, scale_attn, ln2_gain, ln2_bias, fc1_weight, fc1_bias, fc2_weight, fc2_bias,
    scale_mlp, cotangent,
):
    devices = lax.axis_size("fsdp")
    depth, ranks = devices // 2, lax.axis_size("rep")
    place = lax.axis_index("fsdp")
    rank = lax.axis_index("rep")
    here, core = place // 2, place % 2
    count = tokens.shape[1]
    chip = 2 * count
    head_rows = D // devices
    ff = fc1_weight.shape[1]
    unit_rows = ff // devices
    half_heads = D // 2
    local_heads = half_heads // HEAD_DIM
    pairs = half_heads // LANES
    bits = list(range(rep_bits()))

    def in_order(own, other, axis=0):
        return jnp.where(
            core == 0,
            jnp.concatenate([own, other], axis=axis),
            jnp.concatenate([other, own], axis=axis),
        )

    def mine(value):
        return lax.dynamic_slice_in_dim(value, core * count, count, 0)

    def others(value):
        return lax.dynamic_slice_in_dim(value, (1 - core) * count, count, 0)

    def every_other(value, width, start):
        cuts = range(start * width, value.shape[1], 2 * width)
        return jnp.concatenate([value[:, c : c + width] for c in cuts], axis=1)

    even = jnp.concatenate(
        [every_other(qkv_weight, head_rows, 0), every_other(fc1_weight, unit_rows, 0)], axis=1
    )
    odd = jnp.concatenate(
        [every_other(qkv_weight, head_rows, 1), every_other(fc1_weight, unit_rows, 1)], axis=1
    )
    kept, given = jnp.where(core == 0, even, odd), jnp.where(core == 0, odd, even)
    small = (
        ln1_gain, ln1_bias, query_bias, value_bias, proj_bias, scale_attn, ln2_gain, ln2_bias,
        fc2_bias, scale_mlp, fc1_bias, (image_ids[0] + 1).astype(bf16),
    )
    sizes = [v.shape[0] for v in small]
    slots = slot_lists(sizes)
    width = 2 * D // ranks
    small = pack_small(small, width, slots)
    paired = in_order(kept, swap_cores(given))
    small_other = swap_cores(small)
    proj_packed = jnp.concatenate([proj_weight[:, :half_heads], proj_weight[:, half_heads:]], axis=0)
    group1 = jnp.concatenate([paired[:, : 3 * half_heads], proj_packed], axis=1)
    group2 = paired[:, 3 * half_heads :]

    def own_columns(group):
        width = group.shape[1] // ranks
        return lax.dynamic_slice_in_dim(group, rank * width, width, 1)

    own1, own2, own3 = own_columns(group1), own_columns(group2), own_columns(fc2_weight)
    rows1, rows3 = own1.shape[0], own3.shape[0]
    tok_other = swap_cores(tokens[0])
    cot_other = swap_cores(cotangent[0])
    own1 = jnp.concatenate([own1, small, small_other])
    own1, own2, own3, tok, cot, tok_other, cot_other = tie(
        own1, own2, own3, tokens[0], cotangent[0], tok_other, cot_other
    )
    pieces1 = fetch_z(own1)
    tok, pieces1[1] = tie(tok, pieces1[1])
    behind, ahead = from_chip(tok, 1), from_chip(tok, -1)
    own2, *pieces1 = tie(own2, *pieces1)
    gather1 = Gather(pieces1, rows1, "gather1")
    own2, behind, ahead = gather1.send(own2, behind, ahead)
    behind_other, ahead_other = swap_cores(behind), swap_cores(ahead)
    pieces2 = fetch_z(own2)

    vec_rows, fc1_shift, all_tags = unpack_small(
        pieces1, slots, rows1, here, core, ff // 2, devices * count
    )
    vector = lambda i: vec_rows[i : i + 1]
    (
        attn_gain, attn_shift, query_shift, value_shift, proj_shift, attn_scale, mlp_gain,
        mlp_shift, fc2_shift, mlp_scale,
    ) = map(vector, range(10))
    core_part = lambda vec: jnp.where(
        core == 0, every_other(vec, head_rows, 0), every_other(vec, head_rows, 1)
    )

    window = 3 * chip
    padded = jnp.concatenate(
        [jnp.zeros((1, chip), f32), all_tags, jnp.full((1, chip), 1e6, f32)], axis=1
    )
    tag_row = lax.dynamic_slice(padded, (0, here * chip), (1, window))
    tags = tag_row.reshape(window)
    firsts, lasts = tags[::BLOCK], tags[BLOCK - 1 :: BLOCK]
    real = firsts * (1e6 - firsts) > 0
    below = jnp.sum((tag_row < firsts[:, None]).astype(jnp.int32), axis=1)
    upto = jnp.sum((tag_row <= lasts[:, None]).astype(jnp.int32), axis=1)
    blocks = window // BLOCK
    block_lo = jnp.where(real, below // BLOCK, 0)
    block_hi = jnp.where(real, (upto + BLOCK - 1) // BLOCK, 0)
    own_lo, own_hi = chip // BLOCK, 2 * chip // BLOCK
    numbers = jnp.arange(blocks)
    need = jnp.logical_and(numbers >= block_lo[own_lo], numbers < block_hi[own_hi - 1]).astype(jnp.int32)
    firsts, lasts = firsts.astype(jnp.int32), lasts.astype(jnp.int32)
    tag_cols = jnp.broadcast_to(tags[:, None], (window, LANES))

    info = jnp.stack([core, jnp.int32(count // BLOCK)]).astype(jnp.int32)
    normed1 = norm_window(
        need, info, (behind, behind_other, tok, tok_other, ahead, ahead_other), vec_rows, window, count
    )

    normed1 = gather1.arrive(normed1)
    normed1, own3 = gather1.send(normed1, own3)
    for _ in bits[2:]:
        normed1 = gather1.arrive(normed1)
        normed1 = gather1.send(normed1)
    normed1, *pieces2 = tie(normed1, *pieces2)
    gather2 = Gather(pieces2, rows1, "gather2")
    normed1, own3 = gather2.send(normed1, own3)
    pieces3 = fetch_z(own3)
    normed1 = gather1.arrive(normed1)
    qkv_matrix, proj_matrix = gather1.assemble(here, rank, head_rows)

    shifts = jnp.concatenate(
        [core_part(query_shift), jnp.zeros((1, half_heads), f32), core_part(value_shift)], axis=1
    )
    queries, keys, values = project(need, normed1, qkv_matrix, shifts, half_heads)

    contexts, lses = [], []
    los = block_lo[own_lo:own_hi]
    los, queries = tie(los, queries)
    for pair in range(pairs):
        if pair == 1:
            los = gather2.arrive(los)
            los, *pieces3 = tie(los, *pieces3)
            gather3 = Gather(pieces3, rows3, "gather3")
            los = gather2.send(los)
            los = gather3.send(los)
        if pair == 3:
            los = gather2.arrive(los)
            los = gather3.arrive(los)
            for _ in bits[2:]:
                los = gather2.send(los)
                los = gather2.arrive(los)
            los = gather3.send(los)
        context, lse = attend(
            los, block_hi[own_lo:own_hi], firsts, lasts, queries, keys, values, tag_cols,
            tag_row, chip, pair,
        )
        los, context = tie(los, context)
        contexts.append(context)
        lses.append(lse)
    context = jnp.concatenate(contexts, axis=1)
    lse_rows = jnp.concatenate(lses).reshape(local_heads, chip)
    fc1_matrix = gather2.assemble(here, rank)

    features = tok.astype(f32)
    sent = swap_cores(dot(others(context), proj_matrix))
    attn_out = dot(mine(context), proj_matrix) + sent + proj_shift
    resid = features + attn_scale * attn_out
    mlp_normal, mlp_inverse = normalize(resid)
    mlp_input = (mlp_normal * mlp_gain + mlp_shift).astype(bf16)
    mlp_input = jnp.concatenate([mlp_input, swap_cores(mlp_input)])
    pre_act = dot(mlp_input, fc1_matrix) + fc1_shift
    activated, slope = gelu_pair(pre_act)
    activated = activated.astype(bf16)

    out_grad = cot.astype(f32)
    mlp_grad_full = out_grad * mlp_scale
    mlp_grad = (jnp.concatenate([cot, cot_other]).astype(f32) * mlp_scale).astype(bf16)

    activated = gather3.arrive(activated)
    for _ in bits[2:]:
        activated = gather3.send(activated)
        activated = gather3.arrive(activated)
    fc2_matrix = gather3.assemble(here, rank)
    fc2_grad = dot_tn(activated, mlp_grad).astype(bf16)
    reduce3 = Reduce(relative_blocks(fc2_grad, rank, [bits]), here, [bits])
    activated, fc2_matrix = reduce3.send(activated, fc2_matrix)
    sent = swap_cores(dot(activated[count:], fc2_matrix))
    mlp_out = dot(activated[:count], fc2_matrix) + sent + fc2_shift
    output_rows = (resid + mlp_scale * mlp_out).astype(bf16)
    pre_grad_full = dot_nt(mlp_grad, fc2_matrix) * slope
    pre_grad = pre_grad_full.astype(bf16)
    fc1_bias_part = jnp.sum(pre_grad_full, axis=0, keepdims=True)

    fc1_grad = dot_tn(mlp_input, pre_grad).astype(bf16)
    reduce2 = Reduce(relative_blocks(fc1_grad, rank, [bits[::-1]]), here, [bits[::-1]])
    pre_grad = reduce2.send(pre_grad)
    sent = swap_cores(dot_nt(pre_grad[count:], fc1_matrix))
    mlp_in_grad = dot_nt(pre_grad[:count], fc1_matrix) + sent
    resid_grad = out_grad + norm_back(mlp_in_grad, mlp_normal, mlp_inverse, mlp_gain)
    attn_grad_full = resid_grad * attn_scale
    attn_grad = attn_grad_full.astype(bf16)
    attn_grad = in_order(attn_grad, swap_cores(attn_grad))
    context_grad = dot_nt(attn_grad, proj_matrix).astype(bf16)
    head_of = (
        lax.broadcasted_iota(jnp.int32, (local_heads, half_heads), 1) // HEAD_DIM
        == lax.broadcasted_iota(jnp.int32, (local_heads, half_heads), 0)
    ).astype(f32)
    row_delta = lax.dot_general(
        head_of, context_grad.astype(f32) * context.astype(f32), (((1,), (1,)), ((), ())),
        precision=lax.Precision.HIGHEST, preferred_element_type=f32,
    )
    stats = jnp.concatenate([lse_rows, row_delta])
    grads_behind, grads_ahead = from_chip(context_grad, 1), from_chip(context_grad, -1)
    stats_behind, stats_ahead = from_chip(stats, 1), from_chip(stats, -1)
    proj_grad = packed_proj_grad(context, attn_grad, head_rows)
    grad_window = jnp.concatenate([grads_behind, context_grad, grads_ahead])
    stat_window = jnp.concatenate([stats_behind, stats, stats_ahead], axis=1)
    by_pair = lambda s: s.reshape(pairs, 2, window)
    lse_window, delta_window = by_pair(stat_window[:local_heads]), by_pair(stat_window[local_heads:])

    half_pairs = pairs // 2
    half_width = half_heads // 2
    both = [bits, bits[::-1]]

    def first_group(parts, number):
        grads = [g for kind in zip(*parts) for g in kind]
        return Reduce(
            qkv_grad_blocks(normed1, grads, proj_grad, number, 2, rank, both), here, both
        )

    parts, sums = [], []
    lo, delta_window = tie(block_lo, delta_window)
    for pair in range(pairs):
        if pair == 0:
            lo = reduce3.arrive(lo)
            for _ in bits[2:]:
                lo = reduce3.arrive(reduce3.send(lo))
            lo = reduce3.send(lo)
        if pair == 1:
            lo = reduce3.arrive(lo)
            lo = reduce3.send_z(lo)
            lo = reduce2.arrive(lo)
            for _ in bits[2:]:
                lo = reduce2.arrive(reduce2.send(lo))
            lo = reduce2.send(lo)
        if pair == 2:
            lo = reduce2.arrive(lo)
            lo = reduce2.send_z(lo)
            reduce1a = first_group(parts, 0)
            lo = reduce1a.send(lo)
        if pair == 3:
            lo = reduce3.arrive_z(lo)
            lo = reduce2.arrive_z(lo)
            fc2_part = reduce3.total.astype(bf16)
            fc1_part = reduce2.total.astype(bf16)
            split = fc2_part.shape[0] // fc1_part.shape[0]
            mlp_part = jnp.concatenate([fc1_part, *jnp.split(fc2_part, split)], axis=1)[None]
            mlp_offsets = [0]
            lo, mlp_part = tie(lo, mlp_part)
            mlp_more = across_rep(mlp_part, 0)
            lo = reduce1a.arrive(lo)
            for _ in bits[2:]:
                lo = reduce1a.arrive(reduce1a.send(lo))
            lo = reduce1a.send(lo)
        *grads, total = attend_back(
            lo, block_hi, queries, keys, values, grad_window, tag_cols, tag_row, lse_window,
            delta_window, chip, pair,
        )
        lo, *grads = tie(lo, *grads)
        parts.append(grads)
        sums.append(total[0])

    reduce1b = first_group(parts[half_pairs:], 1)
    lo = reduce1b.send(lo)
    every = [jnp.concatenate(p, axis=1) for p in zip(*parts)]
    every[0], mlp_more, lo = tie(every[0], mlp_more, lo)
    for later in bits[1:] + [None]:
        mlp_part = jnp.concatenate([mlp_part, mlp_more])
        flip = 1 << (len(mlp_offsets).bit_length() - 1)
        mlp_offsets = mlp_offsets + [o ^ flip for o in mlp_offsets]
        if later is not None:
            mlp_more = across_rep(mlp_part, later)
    reduce1a.arrive(lo)
    every[0] = reduce1a.send_z(every[0])

    factor = 1.0 / math.sqrt(count * devices * ranks)
    qkv_grad = jnp.concatenate(every, axis=1)
    sent = swap_cores(dot_nt(others(qkv_grad), qkv_matrix))
    attn_in_grad = dot_nt(mine(qkv_grad), qkv_matrix) + sent
    for _ in bits[1:]:
        attn_in_grad = reduce1b.arrive(attn_in_grad)
        attn_in_grad = reduce1b.send(attn_in_grad)
    attn_normal, attn_inverse = normalize(features)
    input_rows = resid_grad + norm_back(attn_in_grad, attn_normal, attn_inverse, attn_gain)

    columns = lambda value: jnp.sum(value, axis=0, keepdims=True)
    vectors = (
        columns(attn_in_grad * attn_normal), columns(attn_in_grad),
        jnp.concatenate([s[0:1] for s in sums], axis=1), jnp.concatenate([s[1:2] for s in sums], axis=1),
        columns(attn_grad_full), columns(resid_grad * attn_out),
        columns(mlp_in_grad * mlp_normal), columns(mlp_in_grad),
        columns(mlp_grad_full), columns(out_grad * mlp_out), fc1_bias_part,
    )
    of_core = [number in (2, 3, 10) for number in range(11)]
    partial = pack_grads(vectors, list(zip(sizes, of_core)), core, depth)
    partial = reduce1b.arrive(partial)
    partial = reduce1b.send_z(partial)

    vec_total = pick(partial, here, 0)
    for k in range(1, depth):
        vec_total = vec_total + along_z(pick(partial, lax.rem(here + k, depth), 0), k)
    reduce1a.arrive_z(lo)
    vec_total = reduce1b.arrive_z(vec_total)
    first_part = jnp.concatenate([reduce1a.total, reduce1b.total], axis=1).astype(bf16)[None]
    first_offsets = [0]
    for bit in bits:
        received = across_rep(first_part, bit)
        vec_total = vec_total + across_rep(vec_total, bit)
        first_part = jnp.concatenate([first_part, received])
        first_offsets = first_offsets + [o ^ (1 << bit) for o in first_offsets]
    vec_half = vec_total.reshape(2, 16, LANES)
    totals = (pick(vec_half, core, 0) + swap_cores(pick(vec_half, 1 - core, 0))) * factor

    mlp_cols = fc1_part.shape[1]
    fc1_full = rep_blocks(mlp_part[:, :, :mlp_cols], mlp_offsets, rank)
    fc2_width = fc2_part.shape[1]
    grad_fc2 = jnp.concatenate(
        [
            rep_blocks(
                mlp_part[:, :, mlp_cols + n * fc2_width : mlp_cols + (n + 1) * fc2_width], mlp_offsets, rank
            )
            for n in range(split)
        ]
    ).astype(f32) * factor
    vec_width = D // ranks
    first_a = rep_blocks(first_part[:, :, :vec_width], first_offsets, rank)
    first_b = rep_blocks(first_part[:, :, vec_width:], first_offsets, rank)

    def rows_of(value, index):
        return lax.dynamic_slice_in_dim(value, index * head_rows, head_rows, 0)

    def interleave(own, other, width):
        cuts = range(0, own.shape[1], width)
        zipped = lambda a, b: jnp.concatenate(
            [v[:, c : c + width] for c in cuts for v in (a, b)], axis=1
        )
        return jnp.where(core == 0, zipped(own, other), zipped(other, own)).astype(f32) * factor

    fc1_other = swap_cores(rows_of(fc1_full, 1 - core))
    grad_fc1 = interleave(rows_of(fc1_full, core), fc1_other, unit_rows)
    qkv_full = jnp.concatenate(
        [
            part[:, n * half_width : (n + 1) * half_width]
            for n in range(3)
            for part in (first_a, first_b)
        ],
        axis=1,
    )
    grad_qkv = interleave(rows_of(qkv_full, core), swap_cores(rows_of(qkv_full, 1 - core)), head_rows)
    proj_part = jnp.concatenate([first_a[:, 3 * half_width :], first_b[:, 3 * half_width :]], axis=1)
    grad_proj = jnp.concatenate([proj_part[:head_rows], proj_part[head_rows:]], axis=1).astype(f32) * factor

    small_grads = [totals[i, : sizes[i]] for i in range(10)]
    lines = -(-sizes[10] // LANES)
    small_grads.append(totals[10 : 10 + lines].reshape(-1))
    (
        grad_attn_gain, grad_attn_shift, grad_query_shift, grad_value_shift, grad_proj_shift,
        grad_attn_scale, grad_mlp_gain, grad_mlp_shift, grad_fc2_shift, grad_mlp_scale, grad_fc1_shift,
    ) = small_grads

    return (
        output_rows[None],
        input_rows[None],
        grad_attn_gain,
        grad_attn_shift,
        grad_qkv,
        grad_query_shift,
        grad_value_shift,
        grad_proj,
        grad_proj_shift,
        grad_attn_scale,
        grad_mlp_gain,
        grad_mlp_shift,
        grad_fc1,
        grad_fc1_shift,
        grad_fc2,
        grad_fc2_shift,
        grad_mlp_scale,
    )


def solution(mesh):
    rows = P("fsdp", None)
    vec = P("fsdp")
    tok = P("rep", "fsdp", None)
    return jax.shard_map(
        on_device,
        mesh=mesh,
        in_specs=(
            tok, P("rep", "fsdp"), vec, vec, rows, vec, vec, rows, vec, vec, vec, vec, rows, vec,
            rows, vec, vec, tok,
        ),
        out_specs=(
            tok, tok, vec, vec, rows, vec, vec, rows, vec, vec, vec, vec, rows, vec, rows, vec, vec,
        ),
        check_vma=False,
    )
```

time: 832 us -> 658 us (0.79)
  waiting for transfers between devices: 209 us -> 140 us
  blocking collectives: 62.1 us -> 0 us
  starting transfers between devices: 122 us -> 173 us
  local copies, waits for them, and re-layouts: 98.1 us -> 58.1 us
  other arithmetic: 81.1 us -> 56.6 us
  matrix products: 79.5 us -> 64.4 us
  Pallas kernels: 171 us -> 156 us
    ppermute x18 -> x24, waiting for transfers between devices: 83.8 us -> 19.4 us  [along_z(): lax.ppermute(value, 'fsdp', [(i, (i + 2 * by) % size) for i in range(size)])]
    psum x1 -> x0, blocking collectives: 41.6 us -> none  [on_device(): totals = pick(lax.psum(partial, ('rep', 'fsdp')), place, 0) * factor]
    ppermute x26 -> x30, starting transfers between devices: 28 us -> 50.7 us  [across_rep(): return lax.ppermute(value, 'rep', [(i, i ^ 1 << bit) for i in range(size)])]
    dynamic_slice x13 -> x2, local copies, waits for them, and re-layouts: 21.1 us -> 0.09 us  [rows_of(): return lax.dynamic_slice_in_dim(value, index * head_rows, head_rows, 0)]
    all_gather x1 -> x0, blocking collectives: 20.5 us -> none  [on_device(): gathered = lax.all_gather(jnp.concatenate(small), 'fsdp', axis=0)]
    ppermute x6, starting transfers between devices: 19.6 us -> 38.1 us  [from_chip(): return lax.ppermute(value, 'fsdp', pairs)]
    ppermute x26 -> x30, waiting for transfers between devices: 120 us -> 101 us  [across_rep(): return lax.ppermute(value, 'rep', [(i, i ^ 1 << bit) for i in range(size)])]
    pallas_call x1 -> x4, Pallas kernels: 65.3 us -> 50.1 us  [attend(): pl.pallas_call(attend_kernel, out_shape=[jax.ShapeDtypeStruct((own_rows,...]
  transfers between devices with their start and end apart: 59 -> 75, of which waited for: 22 -> 29; matrix products, arithmetic and copies ran while one was open for 25% -> 12% of each run, Pallas kernels for 21% -> 20%
where the time goes in v2:
time: 658 us; the launch traced here: 651 us
  starting transfers between devices  173 us (26%)
  Pallas kernels  156 us (24%)
  waiting for transfers between devices  140 us (21%)
  matrix products  64.4 us (10%)
  local copies, waits for them, and re-layouts  58.1 us (9%)
  other arithmetic  56.6 us (9%)
    ppermute x30, waiting for transfers between devices, across_rep(): return lax.ppermute(value, 'rep', [(i, i ^ 1 << bit) for i in range(size)])  101 us
    ppermute x24, starting transfers between devices, along_z(): lax.ppermute(value, 'fsdp', [(i, (i + 2 * by) % size) for i in range(size)])  81.1 us
    pallas_call x4, Pallas kernels, attend_back(): pl.pallas_call(functools.partial(attend_back_kernel, start, stop), out_sh...  75.9 us
    ppermute x30, starting transfers between devices, across_rep(): return lax.ppermute(value, 'rep', [(i, i ^ 1 << bit) for i in range(size)])  50.7 us
    pallas_call x4, Pallas kernels, attend(): pl.pallas_call(attend_kernel, out_shape=[jax.ShapeDtypeStruct((own_rows,...  50.1 us
    ppermute x6, starting transfers between devices, from_chip(): return lax.ppermute(value, 'fsdp', pairs)  38.1 us
    unnamed x197, local copies, waits for them, and re-layouts  36.7 us
    dot_general x6, matrix products, dot_nt(): lax.dot_general(a, b, (((1,), (1,)), ((), ())), preferred_element_type=f32)  24.3 us
  transfers between devices with their start and end apart: 75, of which 29 were waited for; matrix products, arithmetic and copies ran while one was open for 12% of the time, Pallas kernels for 20%

profile of v2, /device:TPU:0, one launch (start us, length us, event | category | flops | bytes accessed | tf_op | source)
XLA Modules:
  0.0 650.6 jit_solution(17909017234851372007)
XLA Ops:
  43.5 5.1 collective-permute-done.4.refs_1_
  48.6 12.3 %collective-permute-start.7 = (bf16[512,1024]{1,0:T(8,128)(2,1)S(1)}, bf16[512,1024]{1,0:T(8,128)(2,1)S(1)}, u32[]{:S(2)}, u32[]{:S(2)}) collective-permute-start(bf16[512,1024]{1,0:T(8,128)(2,1)S(1)} %bitcast.281), channel_id=1, source_target_pairs={{0,2},{1,3},{2,4},{3,5},{4,6},{5,7},{8,10},{9,11},{10,12},{11,13},... | collective-permute-start | bytes 3145736 | tf_op jit(solution)/shard_map/ppermute | solution.py:70
  71.2 8.3 %collective-permute-done.7.refs_0_ = bf16[512,1024]{1,0:T(8,128)(2,1)S(1)} collective-permute-done((bf16[512,1024]{1,0:T(8,128)(2,1)S(1)}, bf16[512,1024]{1,0:T(8,128)(2,1)S(1)}, u32[]{:S(2)}, u32[]{:S(2)}) %collective-permute-start.7) | collective-permute-done | bytes 1048608 | tf_op jit(solution)/shard_map/ppermute | solution.py:70
  88.8 6.7 %collective-permute-start.13 = (bf16[256,512]{1,0:T(8,128)(2,1)S(1)}, bf16[256,512]{1,0:T(8,128)(2,1)S(1)}, u32[]{:S(2)}, u32[]{:S(2)}) collective-permute-start(bf16[256,512]{1,0:T(8,128)(2,1)S(1)} %copy-done.52), channel_id=1, source_target_pairs={{0,2},{1,3},{2,4},{3,5},{4,6},{5,7},{6,0},{7,1},{8,10},{9,11},{10,... | collective-permute-start | bytes 786440 | tf_op jit(solution)/shard_map/ppermute | solution.py:64
  98.4 6.7 %norm_window.1.n_ref = bf16[3072,1024]{1,0:T(8,128)(2,1)S(1)} custom-call(s32[12]{0:T(128)S(1)} %and_convert_fusion.need_ref, s32[2]{0:T(128)S(1)} %pad_add_fusion.1.info_ref, bf16[512,1024]{1,0:T(8,128)(2,1)S(1)} %collective-permute-done.7.refs_0_, bf16[512,1024]{1,0:T(8,128)(2,1)S(1)} %collective-permute-done.9.refs_1_, bf16[512,1024]{1,0:T(8,128)(2,1)S(1)} %bitcast.283, ...), custom_call_target="tpu_custom_call" | custom-call | flops 31457280 | bytes 31457280 | tf_op jit(solution)/shard_map/norm_window/pallas_call | solution.py:551
  105.4 5.7 collective-permute-done.14
  113.2 6.2 collective-permute-start.20
  119.5 3.4 collective-permute-start.21
  123.0 13.1 %collective-permute-done.16.refs_1_ = bf16[2,4,128,512]{3,2,1,0:T(8,128)(2,1)S(1)} collective-permute-done((bf16[2,4,128,512]{3,2,1,0:T(8,128)(2,1)S(1)}, bf16[2,4,128,512]{3,2,1,0:T(8,128)(2,1)S(1)}, u32[]{:S(2)}, u32[]{:S(2)}) %collective-permute-start.16) | collective-permute-done | bytes 1048608 | tf_op jit(solution)/shard_map/ppermute | solution.py:75
  140.2 7.0 %project.1 = (bf16[3072,512]{1,0:T(8,128)(2,1)S(1)}, bf16[3072,512]{1,0:T(8,128)(2,1)S(1)}, bf16[3072,512]{1,0:T(8,128)(2,1)S(1)}) custom-call(s32[12]{0:T(128)S(1)} %and_convert_fusion.need_ref, bf16[3072,1024]{1,0:T(8,128)(2,1)S(1)} %norm_window.1.n_ref, bf16[1024,1536]{1,0:T(8,128)(2,1)S(1)} %get-tuple-element.283.w_ref, f32[1,1536]{1,0:T(1,128)S(1)} %fusion.89.b_ref), custom_call_target="tpu_custom_call" | custom-call | flops 9663676416 | bytes 18874368 | tf_op jit(solution)/shard_map/project/pallas_call | solution.py:501
  147.7 12.5 %attend.4 = (bf16[1024,128]{1,0:T(8,128)(2,1)S(1)}, f32[1,2,1024]{2,1,0:T(2,128)S(1)}) custom-call(s32[4]{0:T(128)S(1)} %slice.776.lo_ref, s32[4]{0:T(128)S(1)} %slice.812.hi_ref, s32[12]{0:T(128)S(1)} %convert_element_type.249.first_ref, s32[12]{0:T(128)S(1)} %convert_element_type.250.last_ref, bf16[3072,512]{1,0:T(8,128)(2,1)S(1)} %get-tuple-element.286.q_ref, ...), custom_call_target="tpu_custom_call" | custom-call | flops 12079595520 | bytes 2359296 | tf_op jit(solution)/shard_map/attend/pallas_call | solution.py:638
  160.8 12.5 %attend.5 = (bf16[1024,128]{1,0:T(8,128)(2,1)S(1)}, f32[1,2,1024]{2,1,0:T(2,128)S(1)}) custom-call(s32[4]{0:T(128)S(1)} %slice.776.lo_ref, s32[4]{0:T(128)S(1)} %slice.812.hi_ref, s32[12]{0:T(128)S(1)} %convert_element_type.249.first_ref, s32[12]{0:T(128)S(1)} %convert_element_type.250.last_ref, bf16[3072,512]{1,0:T(8,128)(2,1)S(1)} %get-tuple-element.286.q_ref, ...), custom_call_target="tpu_custom_call" | custom-call | flops 12079595520 | bytes 2359296 | tf_op jit(solution)/shard_map/attend/pallas_call | solution.py:638
  173.4 4.7 collective-permute-start.24
  180.0 12.5 %attend.6 = (bf16[1024,128]{1,0:T(8,128)(2,1)S(1)}, f32[1,2,1024]{2,1,0:T(2,128)S(1)}) custom-call(s32[4]{0:T(128)S(1)} %slice.776.lo_ref, s32[4]{0:T(128)S(1)} %slice.812.hi_ref, s32[12]{0:T(128)S(1)} %convert_element_type.249.first_ref, s32[12]{0:T(128)S(1)} %convert_element_type.250.last_ref, bf16[3072,512]{1,0:T(8,128)(2,1)S(1)} %get-tuple-element.286.q_ref, ...), custom_call_target="tpu_custom_call" | custom-call | flops 12079595520 | bytes 2359296 | tf_op jit(solution)/shard_map/attend/pallas_call | solution.py:638
  192.8 6.6 %collective-permute-done.23.refs_1_ = bf16[2,4,128,512]{3,2,1,0:T(8,128)(2,1)S(1)} collective-permute-done((bf16[2,4,128,512]{3,2,1,0:T(8,128)(2,1)S(1)}, bf16[2,4,128,512]{3,2,1,0:T(8,128)(2,1)S(1)}, u32[]{:S(2)}, u32[]{:S(2)}) %collective-permute-start.23) | collective-permute-done | bytes 1048608 | tf_op jit(solution)/shard_map/ppermute | solution.py:75
  202.1 8.1 %collective-permute-done.25 = bf16[1,4,256,256]{3,2,1,0:T(8,128)(2,1)S(1)} collective-permute-done((bf16[1,4,256,256]{3,2,1,0:T(8,128)(2,1)S(1)}, bf16[1,4,256,256]{3,2,1,0:T(8,128)(2,1)S(1)}, u32[]{:S(2)}, u32[]{:S(2)}) %collective-permute-start.25) | collective-permute-done | bytes 524320 | tf_op jit(solution)/shard_map/ppermute | solution.py:75
  212.4 12.5 %attend.7 = (bf16[1024,128]{1,0:T(8,128)(2,1)S(1)}, f32[1,2,1024]{2,1,0:T(2,128)S(1)}) custom-call(s32[4]{0:T(128)S(1)} %slice.776.lo_ref, s32[4]{0:T(128)S(1)} %slice.812.hi_ref, s32[12]{0:T(128)S(1)} %convert_element_type.249.first_ref, s32[12]{0:T(128)S(1)} %convert_element_type.250.last_ref, bf16[3072,512]{1,0:T(8,128)(2,1)S(1)} %get-tuple-element.286.q_ref, ...), custom_call_target="tpu_custom_call" | custom-call | flops 12079595520 | bytes 2359296 | tf_op jit(solution)/shard_map/attend/pallas_call | solution.py:638
  227.9 3.7 collective-permute-done.27
  231.5 4.3 fusion.97
  237.7 3.4 collective-permute-start.30
  245.4 9.2 %multiply_convert_fusion = (bf16[1024,2048]{1,0:T(8,128)(2,1)S(1)}, f32[1024,2048]{1,0:T(8,128)}) fusion(f32[2048]{0:T(1024)S(1)} %bitcast.335, bf16[1024,2048]{1,0:T(8,128)(2,1)S(1)} %gather2.1, bf16[512,1024]{1,0:T(8,128)(2,1)} %collective-permute-done.28, bf16[512,1024]{1,0:T(8,128)(2,1)} %add_convert_fusion.5), kind=kOutput, calls=%fused_computation.6 | convolution fusion | flops 4311744512 | bytes 18882560 | tf_op jit(solution)/shard_map/dot_general | solution.py:46
  254.6 8.7 %collective-permute-done.29.refs_1_ = bf16[2,4,256,256]{3,2,1,0:T(8,128)(2,1)S(1)} collective-permute-done((bf16[2,4,256,256]{3,2,1,0:T(8,128)(2,1)}, bf16[2,4,256,256]{3,2,1,0:T(8,128)(2,1)S(1)}, u32[]{:S(2)}, u32[]{:S(2)}) %collective-permute-start.29) | collective-permute-done | bytes 1048608 | tf_op jit(solution)/shard_map/ppermute | solution.py:75
  264.7 6.1 convolution_convert_fusion.1
  276.9 10.7 %fusion.98 = (f32[2048]{0:T(1024)}, bf16[1024,2048]{1,0:T(8,128)(2,1)S(1)}) fusion(f32[1024,2048]{1,0:T(8,128)} %get-tuple-element.689, f32[2048]{0:T(1024)S(1)} %bitcast.336, bf16[2048,1024]{1,0:T(8,128)(2,1)S(1)} %gather3.1, bf16[512,1024]{1,0:T(8,128)(2,1)} %collective-permute-done.3, bf16[512,1024]{1,0:T(8,128)(2,1)S(1)} %bitcast.333, ...), kind=kOutput, calls=%fused_computation.427 | convolution fusion | flops 4326422528 | bytes 18894848 | tf_op jit(solution)/shard_map/dot_general | solution.py:50
  287.6 8.4 %convolution_convert_fusion = bf16[1024,2048]{1,0:T(8,128)(2,1)S(1)} fusion(bf16[1024,2048]{1,0:T(8,128)(2,1)S(1)} %get-tuple-element.343, bf16[512,1024]{1,0:T(8,128)(2,1)} %collective-permute-done.28, bf16[512,1024]{1,0:T(8,128)(2,1)} %add_convert_fusion.5), kind=kOutput, calls=%fused_computation.11 | convolution fusion | flops 4301258752 | bytes 10485760 | tf_op jit(solution)/shard_map/dot_general | solution.py:54
  305.9 5.3 multiply_reduce_fusion
  311.3 5.3 fusion.18
  328.8 16.4 %collective-permute-start.34 = (f32[16,1024]{1,0:T(8,128)S(1)}, f32[16,1024]{1,0:T(8,128)S(1)}, u32[]{:S(2)}, u32[]{:S(2)}) collective-permute-start(f32[16,1024]{1,0:T(8,128)S(1)} %pad_maximum_fusion.20), channel_id=1, source_target_pairs={{0,2},{1,3},{2,4},{3,5},{4,6},{5,7},{8,10},{9,11},{10,12},{11,13},... | collective-permute-start | bytes 196616 | tf_op jit(solution)/shard_map/ppermute | solution.py:70
  347.8 5.5 collective-permute-start.37
  353.4 13.3 %collective-permute-done.36 = bf16[2,4,512,256]{3,2,1,0:T(8,128)(2,1)} collective-permute-done((bf16[2,4,512,256]{3,2,1,0:T(8,128)(2,1)}, bf16[2,4,512,256]{3,2,1,0:T(8,128)(2,1)}, u32[]{:S(2)}, u32[]{:S(2)}) %collective-permute-start.36) | collective-permute-done | bytes 2097184 | tf_op jit(solution)/shard_map/ppermute | solution.py:75
  374.8 3.2 pad_maximum_fusion.g_ref
  381.8 19.0 %attend_back.4 = (bf16[1024,128]{1,0:T(8,128)(2,1)S(1)}, bf16[1024,128]{1,0:T(8,128)(2,1)S(1)}, bf16[1024,128]{1,0:T(8,128)(2,1)S(1)}, f32[1,8,128]{2,1,0:T(8,128)S(1)}) custom-call(s32[12]{0:T(128)S(1)} %copy-done.19, s32[12]{0:T(128)S(1)} %copy-done.21, bf16[3072,512]{1,0:T(8,128)(2,1)S(1)} %copy-done.25, bf16[3072,512]{1,0:T(8,128)(2,1)S(1)} %copy-done.29, ...), custom_call_target="tpu_custom_call" | custom-call | flops 24159191040 | bytes 3145728 | tf_op jit(solution)/shard_map/attend_back/pallas_call | solution.py:750
  402.3 3.7 add_convert_fusion
  408.4 4.1 collective-permute-start.41
  412.6 19.0 %attend_back.5 = (bf16[1024,128]{1,0:T(8,128)(2,1)S(1)}, bf16[1024,128]{1,0:T(8,128)(2,1)S(1)}, bf16[1024,128]{1,0:T(8,128)(2,1)S(1)}, f32[1,8,128]{2,1,0:T(8,128)S(1)}) custom-call(s32[12]{0:T(128)S(1)} %copy-done.19, s32[12]{0:T(128)S(1)} %copy-done.21, bf16[3072,512]{1,0:T(8,128)(2,1)S(1)} %copy-done.26, bf16[3072,512]{1,0:T(8,128)(2,1)S(1)} %copy-done.30, ...), custom_call_target="tpu_custom_call" | custom-call | flops 24159191040 | bytes 3145728 | tf_op jit(solution)/shard_map/attend_back/pallas_call | solution.py:750
  431.5 12.9 %collective-permute-start.42 = (bf16[512,256]{1,0:T(8,128)(2,1)S(1)}, bf16[512,256]{1,0:T(8,128)(2,1)S(1)}, u32[]{:S(2)}, u32[]{:S(2)}) collective-permute-start(bf16[512,256]{1,0:T(8,128)(2,1)S(1)} %get-tuple-element.389), channel_id=1, source_target_pairs={{0,2},{1,3},{2,4},{3,5},{4,6},{5,7},{6,0},{7,1},{8,10},{9,11},{10,... | collective-permute-start | bytes 786440 | tf_op jit(solution)/shard_map/ppermute | solution.py:64
  444.4 7.2 %collective-permute-start.43 = (bf16[512,256]{1,0:T(8,128)(2,1)S(1)}, bf16[512,256]{1,0:T(8,128)(2,1)}, u32[]{:S(2)}, u32[]{:S(2)}) collective-permute-start(bf16[512,256]{1,0:T(8,128)(2,1)S(1)} %get-tuple-element.390), channel_id=1, source_target_pairs={{0,4},{1,5},{2,6},{3,7},{4,0},{5,1},{6,2},{7,3},{8,12},{9,13},{10,... | collective-permute-start | bytes 786440 | tf_op jit(solution)/shard_map/ppermute | solution.py:64
  459.8 19.0 %attend_back.6 = (bf16[1024,128]{1,0:T(8,128)(2,1)S(1)}, bf16[1024,128]{1,0:T(8,128)(2,1)S(1)}, bf16[1024,128]{1,0:T(8,128)(2,1)S(1)}, f32[1,8,128]{2,1,0:T(8,128)S(1)}) custom-call(s32[12]{0:T(128)S(1)} %copy-done.19, s32[12]{0:T(128)S(1)} %copy-done.21, bf16[3072,512]{1,0:T(8,128)(2,1)S(1)} %copy-done.27, bf16[3072,512]{1,0:T(8,128)(2,1)S(1)} %copy-done.30, ...), custom_call_target="tpu_custom_call" | custom-call | flops 24159191040 | bytes 3145728 | tf_op jit(solution)/shard_map/attend_back/pallas_call | solution.py:750
  478.9 5.1 collective-permute-start.46
  488.2 9.1 %collective-permute-start.49 = (bf16[2,4,128,256]{3,2,1,0:T(8,128)(2,1)S(1)}, bf16[2,4,128,256]{3,2,1,0:T(8,128)(2,1)S(1)}, u32[]{:S(2)}, u32[]{:S(2)}) collective-permute-start(bf16[2,4,128,256]{3,2,1,0:T(8,128)(2,1)S(1)} %get-tuple-element.408), channel_id=1, source_target_pairs={{0,16},{8,24},{16,0},{24,8},{1,17},{9,25},{17,1},{25,9},{2,18},{10... | collective-permute-start | bytes 1572872 | tf_op jit(solution)/shard_map/ppermute | solution.py:75
  501.9 5.2 collective-permute-done.49
  508.3 19.0 %attend_back.7 = (bf16[1024,128]{1,0:T(8,128)(2,1)S(1)}, bf16[1024,128]{1,0:T(8,128)(2,1)S(1)}, bf16[1024,128]{1,0:T(8,128)(2,1)S(1)}, f32[1,8,128]{2,1,0:T(8,128)S(1)}) custom-call(s32[12]{0:T(128)S(1)} %copy-done.19, s32[12]{0:T(128)S(1)} %copy-done.21, bf16[3072,512]{1,0:T(8,128)(2,1)S(1)} %copy-done.27, bf16[3072,512]{1,0:T(8,128)(2,1)S(1)} %copy-done.30, ...), custom_call_target="tpu_custom_call" | custom-call | flops 24159191040 | bytes 3145728 | tf_op jit(solution)/shard_map/attend_back/pallas_call | solution.py:750
  529.5 4.6 collective-permute-start.52
  535.9 5.4 collective-permute-done.52
  541.9 13.0 %collective-permute-start.67 = (bf16[256,256]{1,0:T(8,128)(2,1)S(1)}, bf16[256,256]{1,0:T(8,128)(2,1)S(1)}, u32[]{:S(2)}, u32[]{:S(2)}) collective-permute-start(bf16[256,256]{1,0:T(8,128)(2,1)S(1)} %get-tuple-element.459), channel_id=1, source_target_pairs={{0,2},{1,3},{2,4},{3,5},{4,6},{5,7},{6,0},{7,1},{8,10},{9,11},{10,... | collective-permute-start | bytes 393224 | tf_op jit(solution)/shard_map/ppermute | solution.py:64
  563.2 20.0 %collective-permute-done.73 = bf16[2,256,1024]{2,1,0:T(8,128)(2,1)S(1)} collective-permute-done((bf16[2,256,1024]{2,1,0:T(8,128)(2,1)S(1)}, bf16[2,256,1024]{2,1,0:T(8,128)(2,1)S(1)}, u32[]{:S(2)}, u32[]{:S(2)}) %collective-permute-start.73) | collective-permute-done | bytes 1048608 | tf_op jit(solution)/shard_map/ppermute | solution.py:75
  619.6 3.7 collective-permute-done.62
  635.8 10.1 %collective-permute-done.71 = bf16[2,256,512]{2,1,0:T(8,128)(2,1)S(1)} collective-permute-done((bf16[2,256,512]{2,1,0:T(8,128)(2,1)S(1)}, bf16[2,256,512]{2,1,0:T(8,128)(2,1)S(1)}, u32[]{:S(2)}, u32[]{:S(2)}) %collective-permute-start.71) | collective-permute-done | bytes 524320 | tf_op jit(solution)/shard_map/ppermute | solution.py:75
  (497 shorter events, 220.1 us)
Async XLA Ops:
  35.8 12.8 %collective-permute-start.4 = (bf16[272,512]{1,0:T(8,128)(2,1)S(1)}, bf16[272,512]{1,0:T(8,128)(2,1)}, u32[]{:S(2)}, u32[]{:S(2)}) collective-permute-start(bf16[272,512]{1,0:T(8,128)(2,1)S(1)} %pad_maximum_fusion.16.refs_0_), channel_id=1, source_target_pairs={{0,2},{1,3},{2,4},{3,5},{4,6},{5,7},{6,0},{7,1},{8,10},{9,11},{10,... | collective-permute-start | bytes 835592 | tf_op jit(solution)/shard_map/ppermute | solution.py:64
  38.8 23.4 %collective-permute-start.5 = (bf16[272,512]{1,0:T(8,128)(2,1)S(1)}, bf16[272,512]{1,0:T(8,128)(2,1)}, u32[]{:S(2)}, u32[]{:S(2)}) collective-permute-start(bf16[272,512]{1,0:T(8,128)(2,1)S(1)} %pad_maximum_fusion.16.refs_0_), channel_id=1, source_target_pairs={{0,4},{1,5},{2,6},{3,7},{4,0},{5,1},{6,2},{7,3},{8,12},{9,13},{10,... | collective-permute-start | bytes 835592 | tf_op jit(solution)/shard_map/ppermute | solution.py:64
  41.4 20.9 %collective-permute-start.6 = (bf16[272,512]{1,0:T(8,128)(2,1)S(1)}, bf16[272,512]{1,0:T(8,128)(2,1)}, u32[]{:S(2)}, u32[]{:S(2)}) collective-permute-start(bf16[272,512]{1,0:T(8,128)(2,1)S(1)} %pad_maximum_fusion.16.refs_0_), channel_id=1, source_target_pairs={{0,6},{1,7},{2,0},{3,1},{4,2},{5,3},{6,4},{7,5},{8,14},{9,15},{10,... | collective-permute-start | bytes 835592 | tf_op jit(solution)/shard_map/ppermute | solution.py:64
  48.6 30.9 %collective-permute-start.7 = (bf16[512,1024]{1,0:T(8,128)(2,1)S(1)}, bf16[512,1024]{1,0:T(8,128)(2,1)S(1)}, u32[]{:S(2)}, u32[]{:S(2)}) collective-permute-start(bf16[512,1024]{1,0:T(8,128)(2,1)S(1)} %bitcast.281), channel_id=1, source_target_pairs={{0,2},{1,3},{2,4},{3,5},{4,6},{5,7},{8,10},{9,11},{10,12},{11,13},... | collective-permute-start | bytes 3145736 | tf_op jit(solution)/shard_map/ppermute | solution.py:70
  60.9 21.3 %collective-permute-start.8 = (bf16[512,1024]{1,0:T(8,128)(2,1)S(1)}, bf16[512,1024]{1,0:T(8,128)(2,1)}, u32[]{:S(2)}, u32[]{:S(2)}) collective-permute-start(bf16[512,1024]{1,0:T(8,128)(2,1)S(1)} %bitcast.282), channel_id=1, source_target_pairs={{2,0},{3,1},{4,2},{5,3},{6,4},{7,5},{10,8},{11,9},{12,10},{13,11},... | collective-permute-start | bytes 3145736 | tf_op jit(solution)/shard_map/ppermute | solution.py:70
  82.2 13.2 %collective-permute-start.9 = (bf16[512,1024]{1,0:T(8,128)(2,1)S(1)}, bf16[512,1024]{1,0:T(8,128)(2,1)S(1)}, u32[]{:S(2)}, u32[]{:S(2)}) collective-permute-start(bf16[512,1024]{1,0:T(8,128)(2,1)S(1)} %collective-permute-done.7.refs_0_), channel_id=1, source_target_pairs={{0,1},{1,0},{2,3},{3,2},{4,5},{5,4},{6,7},{7,6},{8,9},{9,8},{10,11... | collective-permute-start | bytes 3145736 | tf_op jit(solution)/shard_map/ppermute | solution.py:59
  82.2 13.3 %collective-permute-start.10 = (bf16[512,1024]{1,0:T(8,128)(2,1)}, bf16[512,1024]{1,0:T(8,128)(2,1)S(1)}, u32[]{:S(2)}, u32[]{:S(2)}) collective-permute-start(bf16[512,1024]{1,0:T(8,128)(2,1)} %collective-permute-done.8.refs_4_), channel_id=1, source_target_pairs={{0,1},{1,0},{2,3},{3,2},{4,5},{5,4},{6,7},{7,6},{8,9},{9,8},{10,11... | collective-permute-start | bytes 3145736 | tf_op jit(solution)/shard_map/ppermute | solution.py:59
  84.4 20.8 %collective-permute-start.11 = (bf16[1,4,128,512]{3,2,1,0:T(8,128)(2,1)S(1)}, bf16[1,4,128,512]{3,2,1,0:T(8,128)(2,1)S(1)}, u32[]{:S(2)}, u32[]{:S(2)}) collective-permute-start(bf16[1,4,128,512]{3,2,1,0:T(8,128)(2,1)S(1)} %maximum_bitcast_fusion), channel_id=1, source_target_pairs={{0,8},{8,0},{16,24},{24,16},{1,9},{9,1},{17,25},{25,17},{2,10},{10... | collective-permute-start | bytes 1572872 | tf_op jit(solution)/shard_map/ppermute | solution.py:75
  85.9 19.3 %collective-permute-start.12 = (bf16[1,4,128,512]{3,2,1,0:T(8,128)(2,1)S(1)}, bf16[1,4,128,512]{3,2,1,0:T(8,128)(2,1)S(1)}, u32[]{:S(2)}, u32[]{:S(2)}) collective-permute-start(bf16[1,4,128,512]{3,2,1,0:T(8,128)(2,1)S(1)} %maximum_bitcast_fusion.1), channel_id=1, source_target_pairs={{0,16},{8,24},{16,0},{24,8},{1,17},{9,25},{17,1},{25,9},{2,18},{10... | collective-permute-start | bytes 1572872 | tf_op jit(solution)/shard_map/ppermute | solution.py:75
  88.8 16.6 %collective-permute-start.13 = (bf16[256,512]{1,0:T(8,128)(2,1)S(1)}, bf16[256,512]{1,0:T(8,128)(2,1)S(1)}, u32[]{:S(2)}, u32[]{:S(2)}) collective-permute-start(bf16[256,512]{1,0:T(8,128)(2,1)S(1)} %copy-done.52), channel_id=1, source_target_pairs={{0,2},{1,3},{2,4},{3,5},{4,6},{5,7},{6,0},{7,1},{8,10},{9,11},{10,... | collective-permute-start | bytes 786440 | tf_op jit(solution)/shard_map/ppermute | solution.py:64
  95.5 15.6 %collective-permute-start.14 = (bf16[256,512]{1,0:T(8,128)(2,1)S(1)}, bf16[256,512]{1,0:T(8,128)(2,1)S(1)}, u32[]{:S(2)}, u32[]{:S(2)}) collective-permute-start(bf16[256,512]{1,0:T(8,128)(2,1)S(1)} %copy-done.52), channel_id=1, source_target_pairs={{0,4},{1,5},{2,6},{3,7},{4,0},{5,1},{6,2},{7,3},{8,12},{9,13},{10,... | collective-permute-start | bytes 786440 | tf_op jit(solution)/shard_map/ppermute | solution.py:64
  95.6 16.3 %collective-permute-start.15 = (bf16[256,512]{1,0:T(8,128)(2,1)S(1)}, bf16[256,512]{1,0:T(8,128)(2,1)S(1)}, u32[]{:S(2)}, u32[]{:S(2)}) collective-permute-start(bf16[256,512]{1,0:T(8,128)(2,1)S(1)} %copy-done.52), channel_id=1, source_target_pairs={{0,6},{1,7},{2,0},{3,1},{4,2},{5,3},{6,4},{7,5},{8,14},{9,15},{10,... | collective-permute-start | bytes 786440 | tf_op jit(solution)/shard_map/ppermute | solution.py:64
  111.9 24.2 %collective-permute-start.16 = (bf16[2,4,128,512]{3,2,1,0:T(8,128)(2,1)S(1)}, bf16[2,4,128,512]{3,2,1,0:T(8,128)(2,1)S(1)}, u32[]{:S(2)}, u32[]{:S(2)}) collective-permute-start(bf16[2,4,128,512]{3,2,1,0:T(8,128)(2,1)S(1)} %pad_maximum_fusion.6.refs_0_), channel_id=1, source_target_pairs={{0,16},{8,24},{16,0},{24,8},{1,17},{9,25},{17,1},{25,9},{2,18},{10... | collective-permute-start | bytes 3145736 | tf_op jit(solution)/shard_map/ppermute | solution.py:75
  112.4 24.2 %collective-permute-start.17 = (bf16[2,4,128,512]{3,2,1,0:T(8,128)(2,1)S(1)}, bf16[2,4,128,512]{3,2,1,0:T(8,128)(2,1)S(1)}, u32[]{:S(2)}, u32[]{:S(2)}) collective-permute-start(bf16[2,4,128,512]{3,2,1,0:T(8,128)(2,1)S(1)} %pad_maximum_fusion.7.refs_2_), channel_id=1, source_target_pairs={{0,8},{8,0},{16,24},{24,16},{1,9},{9,1},{17,25},{25,17},{2,10},{10... | collective-permute-start | bytes 3145736 | tf_op jit(solution)/shard_map/ppermute | solution.py:75
  113.2 47.0 %collective-permute-start.20 = (bf16[512,256]{1,0:T(8,128)(2,1)S(1)}, bf16[512,256]{1,0:T(8,128)(2,1)S(1)}, u32[]{:S(2)}, u32[]{:S(2)}) collective-permute-start(bf16[512,256]{1,0:T(8,128)(2,1)S(1)} %copy-done.50), channel_id=1, source_target_pairs={{0,2},{1,3},{2,4},{3,5},{4,6},{5,7},{6,0},{7,1},{8,10},{9,11},{10,... | collective-permute-start | bytes 786440 | tf_op jit(solution)/shard_map/ppermute | solution.py:64
  119.5 40.8 %collective-permute-start.21 = (bf16[512,256]{1,0:T(8,128)(2,1)S(1)}, bf16[512,256]{1,0:T(8,128)(2,1)S(1)}, u32[]{:S(2)}, u32[]{:S(2)}) collective-permute-start(bf16[512,256]{1,0:T(8,128)(2,1)S(1)} %copy-done.50), channel_id=1, source_target_pairs={{0,4},{1,5},{2,6},{3,7},{4,0},{5,1},{6,2},{7,3},{8,12},{9,13},{10,... | collective-permute-start | bytes 786440 | tf_op jit(solution)/shard_map/ppermute | solution.py:64
  122.8 37.4 %collective-permute-start.22 = (bf16[512,256]{1,0:T(8,128)(2,1)S(1)}, bf16[512,256]{1,0:T(8,128)(2,1)S(1)}, u32[]{:S(2)}, u32[]{:S(2)}) collective-permute-start(bf16[512,256]{1,0:T(8,128)(2,1)S(1)} %copy-done.50), channel_id=1, source_target_pairs={{0,6},{1,7},{2,0},{3,1},{4,2},{5,3},{6,4},{7,5},{8,14},{9,15},{10,... | collective-permute-start | bytes 786440 | tf_op jit(solution)/shard_map/ppermute | solution.py:64
  136.1 24.2 %collective-permute-start.18 = (bf16[1,4,128,512]{3,2,1,0:T(8,128)(2,1)S(1)}, bf16[1,4,128,512]{3,2,1,0:T(8,128)(2,1)S(1)}, u32[]{:S(2)}, u32[]{:S(2)}) collective-permute-start(bf16[1,4,128,512]{3,2,1,0:T(8,128)(2,1)S(1)} %maximum_bitcast_fusion.2), channel_id=1, source_target_pairs={{0,8},{8,0},{16,24},{24,16},{1,9},{9,1},{17,25},{25,17},{2,10},{10... | collective-permute-start | bytes 1572872 | tf_op jit(solution)/shard_map/ppermute | solution.py:75
  136.6 23.6 %collective-permute-start.19 = (bf16[1,4,128,512]{3,2,1,0:T(8,128)(2,1)S(1)}, bf16[1,4,128,512]{3,2,1,0:T(8,128)(2,1)S(1)}, u32[]{:S(2)}, u32[]{:S(2)}) collective-permute-start(bf16[1,4,128,512]{3,2,1,0:T(8,128)(2,1)S(1)} %maximum_bitcast_fusion.3), channel_id=1, source_target_pairs={{0,16},{8,24},{16,0},{24,8},{1,17},{9,25},{17,1},{25,9},{2,18},{10... | collective-permute-start | bytes 1572872 | tf_op jit(solution)/shard_map/ppermute | solution.py:75
  173.3 26.1 %collective-permute-start.23 = (bf16[2,4,128,512]{3,2,1,0:T(8,128)(2,1)S(1)}, bf16[2,4,128,512]{3,2,1,0:T(8,128)(2,1)S(1)}, u32[]{:S(2)}, u32[]{:S(2)}) collective-permute-start(bf16[2,4,128,512]{3,2,1,0:T(8,128)(2,1)S(1)} %pad_maximum_fusion.8.refs_0_), channel_id=1, source_target_pairs={{0,16},{8,24},{16,0},{24,8},{1,17},{9,25},{17,1},{25,9},{2,18},{10... | collective-permute-start | bytes 3145736 | tf_op jit(solution)/shard_map/ppermute | solution.py:75
  173.4 28.7 %collective-permute-start.24 = (bf16[2,4,128,512]{3,2,1,0:T(8,128)(2,1)S(1)}, bf16[2,4,128,512]{3,2,1,0:T(8,128)(2,1)S(1)}, u32[]{:S(2)}, u32[]{:S(2)}) collective-permute-start(bf16[2,4,128,512]{3,2,1,0:T(8,128)(2,1)S(1)} %pad_maximum_fusion.9.refs_2_), channel_id=1, source_target_pairs={{0,8},{8,0},{16,24},{24,16},{1,9},{9,1},{17,25},{25,17},{2,10},{10... | collective-permute-start | bytes 3145736 | tf_op jit(solution)/shard_map/ppermute | solution.py:75
  178.1 32.1 %collective-permute-start.25 = (bf16[1,4,256,256]{3,2,1,0:T(8,128)(2,1)S(1)}, bf16[1,4,256,256]{3,2,1,0:T(8,128)(2,1)S(1)}, u32[]{:S(2)}, u32[]{:S(2)}) collective-permute-start(bf16[1,4,256,256]{3,2,1,0:T(8,128)(2,1)S(1)} %maximum_bitcast_fusion.4), channel_id=1, source_target_pairs={{0,8},{8,0},{16,24},{24,16},{1,9},{9,1},{17,25},{25,17},{2,10},{10... | collective-permute-start | bytes 1572872 | tf_op jit(solution)/shard_map/ppermute | solution.py:75
  178.2 32.0 %collective-permute-start.26 = (bf16[1,4,256,256]{3,2,1,0:T(8,128)(2,1)S(1)}, bf16[1,4,256,256]{3,2,1,0:T(8,128)(2,1)S(1)}, u32[]{:S(2)}, u32[]{:S(2)}) collective-permute-start(bf16[1,4,256,256]{3,2,1,0:T(8,128)(2,1)S(1)} %maximum_bitcast_fusion.5), channel_id=1, source_target_pairs={{0,16},{8,24},{16,0},{24,8},{1,17},{9,25},{17,1},{25,9},{2,18},{10... | collective-permute-start | bytes 1572872 | tf_op jit(solution)/shard_map/ppermute | solution.py:75
  237.7 25.7 %collective-permute-start.29 = (bf16[2,4,256,256]{3,2,1,0:T(8,128)(2,1)}, bf16[2,4,256,256]{3,2,1,0:T(8,128)(2,1)S(1)}, u32[]{:S(2)}, u32[]{:S(2)}) collective-permute-start(bf16[2,4,256,256]{3,2,1,0:T(8,128)(2,1)} %pad_maximum_fusion.10.refs_0_), channel_id=1, source_target_pairs={{0,16},{8,24},{16,0},{24,8},{1,17},{9,25},{17,1},{25,9},{2,18},{10... | collective-permute-start | bytes 3145736 | tf_op jit(solution)/shard_map/ppermute | solution.py:75
  237.7 27.0 %collective-permute-start.30 = (bf16[2,4,256,256]{3,2,1,0:T(8,128)(2,1)}, bf16[2,4,256,256]{3,2,1,0:T(8,128)(2,1)S(1)}, u32[]{:S(2)}, u32[]{:S(2)}) collective-permute-start(bf16[2,4,256,256]{3,2,1,0:T(8,128)(2,1)} %pad_maximum_fusion.11.refs_2_), channel_id=1, source_target_pairs={{0,8},{8,0},{16,24},{24,16},{1,9},{9,1},{17,25},{25,17},{2,10},{10... | collective-permute-start | bytes 3145736 | tf_op jit(solution)/shard_map/ppermute | solution.py:75
  318.5 48.3 %collective-permute-start.36 = (bf16[2,4,512,256]{3,2,1,0:T(8,128)(2,1)}, bf16[2,4,512,256]{3,2,1,0:T(8,128)(2,1)}, u32[]{:S(2)}, u32[]{:S(2)}) collective-permute-start(bf16[2,4,512,256]{3,2,1,0:T(8,128)(2,1)} %pad_maximum_fusion.2), channel_id=1, source_target_pairs={{0,8},{8,0},{16,24},{24,16},{1,9},{9,1},{17,25},{25,17},{2,10},{10... | collective-permute-start | bytes 6291464 | tf_op jit(solution)/shard_map/ppermute | solution.py:75
  320.3 80.9 %collective-permute-start.40 = (bf16[2,4,256,512]{3,2,1,0:T(8,128)(2,1)}, bf16[2,4,256,512]{3,2,1,0:T(8,128)(2,1)}, u32[]{:S(2)}, u32[]{:S(2)}) collective-permute-start(bf16[2,4,256,512]{3,2,1,0:T(8,128)(2,1)} %pad_maximum_fusion.3), channel_id=1, source_target_pairs={{0,16},{8,24},{16,0},{24,8},{1,17},{9,25},{17,1},{25,9},{2,18},{10... | collective-permute-start | bytes 6291464 | tf_op jit(solution)/shard_map/ppermute | solution.py:75
  327.5 20.3 %collective-permute-start.35 = (f32[16,1024]{1,0:T(8,128)S(1)}, f32[16,1024]{1,0:T(8,128)S(1)}, u32[]{:S(2)}, u32[]{:S(2)}) collective-permute-start(f32[16,1024]{1,0:T(8,128)S(1)} %pad_maximum_fusion.20), channel_id=1, source_target_pairs={{2,0},{3,1},{4,2},{5,3},{6,4},{7,5},{10,8},{11,9},{12,10},{13,11},... | collective-permute-start | bytes 196616 | tf_op jit(solution)/shard_map/ppermute | solution.py:70
  328.8 24.5 %collective-permute-start.34 = (f32[16,1024]{1,0:T(8,128)S(1)}, f32[16,1024]{1,0:T(8,128)S(1)}, u32[]{:S(2)}, u32[]{:S(2)}) collective-permute-start(f32[16,1024]{1,0:T(8,128)S(1)} %pad_maximum_fusion.20), channel_id=1, source_target_pairs={{0,2},{1,3},{2,4},{3,5},{4,6},{5,7},{8,10},{9,11},{10,12},{11,13},... | collective-permute-start | bytes 196616 | tf_op jit(solution)/shard_map/ppermute | solution.py:70
  345.2 27.2 %collective-permute-start.38 = (bf16[1024,512]{1,0:T(8,128)(2,1)}, bf16[1024,512]{1,0:T(8,128)(2,1)}, u32[]{:S(2)}, u32[]{:S(2)}) collective-permute-start(bf16[1024,512]{1,0:T(8,128)(2,1)} %convolution_convert_fusion.2), channel_id=1, source_target_pairs={{2,0},{3,1},{4,2},{5,3},{6,4},{7,5},{10,8},{11,9},{12,10},{13,11},... | collective-permute-start | bytes 3145736 | tf_op jit(solution)/shard_map/ppermute | solution.py:70
  347.8 27.0 %collective-permute-start.37 = (bf16[1024,512]{1,0:T(8,128)(2,1)}, bf16[1024,512]{1,0:T(8,128)(2,1)}, u32[]{:S(2)}, u32[]{:S(2)}) collective-permute-start(bf16[1024,512]{1,0:T(8,128)(2,1)} %convolution_convert_fusion.2), channel_id=1, source_target_pairs={{0,2},{1,3},{2,4},{3,5},{4,6},{5,7},{8,10},{9,11},{10,12},{11,13},... | collective-permute-start | bytes 3145736 | tf_op jit(solution)/shard_map/ppermute | solution.py:70
  370.8 29.9 %collective-permute-start.39 = (bf16[1,4,512,256]{3,2,1,0:T(8,128)(2,1)S(1)}, bf16[1,4,512,256]{3,2,1,0:T(8,128)(2,1)S(1)}, u32[]{:S(2)}, u32[]{:S(2)}) collective-permute-start(bf16[1,4,512,256]{3,2,1,0:T(8,128)(2,1)S(1)} %slice.927), channel_id=1, source_target_pairs={{0,16},{8,24},{16,0},{24,8},{1,17},{9,25},{17,1},{25,9},{2,18},{10... | collective-permute-start | bytes 3145736 | tf_op jit(solution)/shard_map/ppermute | solution.py:75
  408.4 48.5 %collective-permute-start.41 = (bf16[1,4,256,512]{3,2,1,0:T(8,128)(2,1)}, bf16[1,4,256,512]{3,2,1,0:T(8,128)(2,1)}, u32[]{:S(2)}, u32[]{:S(2)}) collective-permute-start(bf16[1,4,256,512]{3,2,1,0:T(8,128)(2,1)} %slice.930), channel_id=1, source_target_pairs={{0,8},{8,0},{16,24},{24,16},{1,9},{9,1},{17,25},{25,17},{2,10},{10... | collective-permute-start | bytes 3145736 | tf_op jit(solution)/shard_map/ppermute | solution.py:75
  431.5 47.3 %collective-permute-start.42 = (bf16[512,256]{1,0:T(8,128)(2,1)S(1)}, bf16[512,256]{1,0:T(8,128)(2,1)S(1)}, u32[]{:S(2)}, u32[]{:S(2)}) collective-permute-start(bf16[512,256]{1,0:T(8,128)(2,1)S(1)} %get-tuple-element.389), channel_id=1, source_target_pairs={{0,2},{1,3},{2,4},{3,5},{4,6},{5,7},{6,0},{7,1},{8,10},{9,11},{10,... | collective-permute-start | bytes 786440 | tf_op jit(solution)/shard_map/ppermute | solution.py:64
  444.4 34.4 %collective-permute-start.43 = (bf16[512,256]{1,0:T(8,128)(2,1)S(1)}, bf16[512,256]{1,0:T(8,128)(2,1)}, u32[]{:S(2)}, u32[]{:S(2)}) collective-permute-start(bf16[512,256]{1,0:T(8,128)(2,1)S(1)} %get-tuple-element.390), channel_id=1, source_target_pairs={{0,4},{1,5},{2,6},{3,7},{4,0},{5,1},{6,2},{7,3},{8,12},{9,13},{10,... | collective-permute-start | bytes 786440 | tf_op jit(solution)/shard_map/ppermute | solution.py:64
  451.7 27.2 %collective-permute-start.44 = (bf16[512,256]{1,0:T(8,128)(2,1)S(1)}, bf16[512,256]{1,0:T(8,128)(2,1)}, u32[]{:S(2)}, u32[]{:S(2)}) collective-permute-start(bf16[512,256]{1,0:T(8,128)(2,1)S(1)} %get-tuple-element.391), channel_id=1, source_target_pairs={{0,6},{1,7},{2,0},{3,1},{4,2},{5,3},{6,4},{7,5},{8,14},{9,15},{10,... | collective-permute-start | bytes 786440 | tf_op jit(solution)/shard_map/ppermute | solution.py:64
  478.8 18.4 %collective-permute-start.45 = (bf16[256,512]{1,0:T(8,128)(2,1)}, bf16[256,512]{1,0:T(8,128)(2,1)S(1)}, u32[]{:S(2)}, u32[]{:S(2)}) collective-permute-start(bf16[256,512]{1,0:T(8,128)(2,1)} %get-tuple-element.394), channel_id=1, source_target_pairs={{0,2},{1,3},{2,4},{3,5},{4,6},{5,7},{6,0},{7,1},{8,10},{9,11},{10,... | collective-permute-start | bytes 786440 | tf_op jit(solution)/shard_map/ppermute | solution.py:64
  478.9 20.2 %collective-permute-start.46 = (bf16[256,512]{1,0:T(8,128)(2,1)}, bf16[256,512]{1,0:T(8,128)(2,1)S(1)}, u32[]{:S(2)}, u32[]{:S(2)}) collective-permute-start(bf16[256,512]{1,0:T(8,128)(2,1)} %get-tuple-element.395), channel_id=1, source_target_pairs={{0,4},{1,5},{2,6},{3,7},{4,0},{5,1},{6,2},{7,3},{8,12},{9,13},{10,... | collective-permute-start | bytes 786440 | tf_op jit(solution)/shard_map/ppermute | solution.py:64
  484.0 15.1 %collective-permute-start.47 = (bf16[256,512]{1,0:T(8,128)(2,1)}, bf16[256,512]{1,0:T(8,128)(2,1)S(1)}, u32[]{:S(2)}, u32[]{:S(2)}) collective-permute-start(bf16[256,512]{1,0:T(8,128)(2,1)} %get-tuple-element.396), channel_id=1, source_target_pairs={{0,6},{1,7},{2,0},{3,1},{4,2},{5,3},{6,4},{7,5},{8,14},{9,15},{10,... | collective-permute-start | bytes 786440 | tf_op jit(solution)/shard_map/ppermute | solution.py:64
  488.1 13.8 %collective-permute-start.48 = (bf16[2,4,128,256]{3,2,1,0:T(8,128)(2,1)S(1)}, bf16[2,4,128,256]{3,2,1,0:T(8,128)(2,1)S(1)}, u32[]{:S(2)}, u32[]{:S(2)}) collective-permute-start(bf16[2,4,128,256]{3,2,1,0:T(8,128)(2,1)S(1)} %get-tuple-element.407), channel_id=1, source_target_pairs={{0,8},{8,0},{16,24},{24,16},{1,9},{9,1},{17,25},{25,17},{2,10},{10... | collective-permute-start | bytes 1572872 | tf_op jit(solution)/shard_map/ppermute | solution.py:75
  488.2 19.0 %collective-permute-start.49 = (bf16[2,4,128,256]{3,2,1,0:T(8,128)(2,1)S(1)}, bf16[2,4,128,256]{3,2,1,0:T(8,128)(2,1)S(1)}, u32[]{:S(2)}, u32[]{:S(2)}) collective-permute-start(bf16[2,4,128,256]{3,2,1,0:T(8,128)(2,1)S(1)} %get-tuple-element.408), channel_id=1, source_target_pairs={{0,16},{8,24},{16,0},{24,8},{1,17},{9,25},{17,1},{25,9},{2,18},{10... | collective-permute-start | bytes 1572872 | tf_op jit(solution)/shard_map/ppermute | solution.py:75
  500.1 35.3 %collective-permute-start.50 = (bf16[1,256,1024]{2,1,0:T(8,128)(2,1)}, bf16[1,256,1024]{2,1,0:T(8,128)(2,1)}, u32[]{:S(2)}, u32[]{:S(2)}) collective-permute-start(bf16[1,256,1024]{2,1,0:T(8,128)(2,1)} %maximum_bitcast_fusion.6), channel_id=1, source_target_pairs={{0,8},{8,0},{16,24},{24,16},{1,9},{9,1},{17,25},{25,17},{2,10},{10... | collective-permute-start | bytes 1572872 | tf_op jit(solution)/shard_map/ppermute | solution.py:75
  534.1 60.3 %collective-permute-start.54 = (bf16[2,4,128,256]{3,2,1,0:T(8,128)(2,1)S(1)}, bf16[2,4,128,256]{3,2,1,0:T(8,128)(2,1)S(1)}, u32[]{:S(2)}, u32[]{:S(2)}) collective-permute-start(bf16[2,4,128,256]{3,2,1,0:T(8,128)(2,1)S(1)} %get-tuple-element.435), channel_id=1, source_target_pairs={{0,8},{8,0},{16,24},{24,16},{1,9},{9,1},{17,25},{25,17},{2,10},{10... | collective-permute-start | bytes 1572872 | tf_op jit(solution)/shard_map/ppermute | solution.py:75
  541.9 19.2 %collective-permute-start.67 = (bf16[256,256]{1,0:T(8,128)(2,1)S(1)}, bf16[256,256]{1,0:T(8,128)(2,1)S(1)}, u32[]{:S(2)}, u32[]{:S(2)}) collective-permute-start(bf16[256,256]{1,0:T(8,128)(2,1)S(1)} %get-tuple-element.459), channel_id=1, source_target_pairs={{0,2},{1,3},{2,4},{3,5},{4,6},{5,7},{6,0},{7,1},{8,10},{9,11},{10,... | collective-permute-start | bytes 393224 | tf_op jit(solution)/shard_map/ppermute | solution.py:64
  558.9 24.3 %collective-permute-start.73 = (bf16[2,256,1024]{2,1,0:T(8,128)(2,1)S(1)}, bf16[2,256,1024]{2,1,0:T(8,128)(2,1)S(1)}, u32[]{:S(2)}, u32[]{:S(2)}) collective-permute-start(bf16[2,256,1024]{2,1,0:T(8,128)(2,1)S(1)} %pad_maximum_fusion.13), channel_id=1, source_target_pairs={{0,16},{8,24},{16,0},{24,8},{1,17},{9,25},{17,1},{25,9},{2,18},{10... | collective-permute-start | bytes 3145736 | tf_op jit(solution)/shard_map/ppermute | solution.py:75
  561.1 33.3 %collective-permute-start.55 = (bf16[2,4,128,256]{3,2,1,0:T(8,128)(2,1)S(1)}, bf16[2,4,128,256]{3,2,1,0:T(8,128)(2,1)S(1)}, u32[]{:S(2)}, u32[]{:S(2)}) collective-permute-start(bf16[2,4,128,256]{3,2,1,0:T(8,128)(2,1)S(1)} %get-tuple-element.436), channel_id=1, source_target_pairs={{0,16},{8,24},{16,0},{24,8},{1,17},{9,25},{17,1},{25,9},{2,18},{10... | collective-permute-start | bytes 1572872 | tf_op jit(solution)/shard_map/ppermute | solution.py:75
  563.1 29.5 %collective-permute-start.53 = (f32[512,1024]{1,0:T(8,128)S(1)}, f32[512,1024]{1,0:T(8,128)S(1)}, u32[]{:S(2)}, u32[]{:S(2)}) collective-permute-start(f32[512,1024]{1,0:T(8,128)S(1)} %fusion.31), channel_id=1, source_target_pairs={{0,1},{1,0},{2,3},{3,2},{4,5},{5,4},{6,7},{7,6},{8,9},{9,8},{10,11... | collective-permute-start | bytes 6291464 | tf_op jit(solution)/shard_map/ppermute | solution.py:59
  633.1 12.7 %collective-permute-start.71 = (bf16[2,256,512]{2,1,0:T(8,128)(2,1)S(1)}, bf16[2,256,512]{2,1,0:T(8,128)(2,1)S(1)}, u32[]{:S(2)}, u32[]{:S(2)}) collective-permute-start(bf16[2,256,512]{2,1,0:T(8,128)(2,1)S(1)} %pad_maximum_fusion.15), channel_id=1, source_target_pairs={{0,16},{8,24},{16,0},{24,8},{1,17},{9,25},{17,1},{25,9},{2,18},{10... | collective-permute-start | bytes 1572872 | tf_op jit(solution)/shard_map/ppermute | solution.py:75
  (94 other events, 1139.7 us)

commit v3 on v2

--- a/solution.py
+++ b/solution.py
@@ -17,6 +17,8 @@
 MASKED = -1e30
 BLOCK = 256
 
+SHORT = pl.CostEstimate(flops=1, transcendentals=0, bytes_accessed=1)
+
 f32 = jnp.float32
 bf16 = jnp.bfloat16
 
@@ -85,6 +87,14 @@
 
 def tie(*values):
     return lax.optimization_barrier(values)
+
+
+def settle(value, *fields):
+    held = [getattr(o, name) for o, name in fields]
+    value, held = lax.optimization_barrier((value, held))
+    for (o, name), new in zip(fields, held):
+        setattr(o, name, new)
+    return value
 
 
 def fetch_z(own):
@@ -153,9 +163,7 @@
                 ],
             ),
             compiler_params=pltpu.CompilerParams(vmem_limit_bytes=16 << 20),
-            cost_estimate=pl.CostEstimate(
-                flops=0, transcendentals=0, bytes_accessed=2 * shape[0] * shape[1] * dtype.itemsize
-            ),
+            cost_estimate=SHORT,
             name=self.name,
         )(jnp.stack([here, rank]).astype(jnp.int32), *sources)
         return out if tail_rows else out[0]
@@ -281,6 +289,32 @@
         return values[0] if len(values) == 1 else values
 
 
+class Spread:
+    def __init__(self, value):
+        bits = list(range(rep_bits()))
+        self.orders = [bits, bits[::-1]]
+        half = value.shape[0] // 2
+        self.arrays = [value[:half][None], value[half:][None]]
+        self.offsets = [[0], [0]]
+        self.at = 0
+
+    def send(self, *values):
+        values, arrays = lax.optimization_barrier((values, self.arrays))
+        self.arrays = []
+        for n, (array, order) in enumerate(zip(arrays, self.orders)):
+            flip = 1 << order[self.at]
+            received = across_rep(array, order[self.at])
+            self.arrays.append(jnp.concatenate([array, received]))
+            self.offsets[n] = self.offsets[n] + [o ^ flip for o in self.offsets[n]]
+        self.at += 1
+        return values[0] if len(values) == 1 else values
+
+    def blocks(self, rank, start, size):
+        return jnp.concatenate(
+            [rep_blocks(a[:, :, start : start + size], o, rank) for a, o in zip(self.arrays, self.offsets)]
+        )
+
+
 def rep_blocks(stacked, offsets, rank):
     blocks = []
     for i in range(len(offsets)):
@@ -289,6 +323,73 @@
             block = jnp.where((rank ^ offset) == i, stacked[entry], block)
         blocks.append(block)
     return jnp.concatenate(blocks, axis=1)
+
+
+def share_kernel(widths, index_ref, qkv_ref, proj_ref, fc1_ref, keep_ref, give_ref, sems):
+    rank, core = index_ref[0], index_ref[1]
+    wide1, wide2, block, unit, half = widths
+    is_proj = rank * wide1 >= 3 * half
+
+    def copies(second):
+        made = []
+        for out, (ref, which) in enumerate(((keep_ref, core), (give_ref, 1 - core))):
+            for c in range(wide1 // block):
+                col = rank * wide1 + c * block
+                if second:
+                    source, at = proj_ref, which * half + col - 3 * half
+                else:
+                    source, at = qkv_ref, 2 * col + which * block
+                made.append((source, at, block, ref, c * block))
+        return made
+
+    def run(plan, first):
+        started = []
+        for n, (source, at, size, ref, to) in enumerate(plan):
+            copy = pltpu.make_async_copy(
+                source.at[:, pl.ds(pl.multiple_of(at, LANES), size)], ref.at[:, pl.ds(to, size)], sems.at[first + n]
+            )
+            copy.start()
+            started.append(copy)
+        return started
+
+    col = rank * wide2
+    plan2 = []
+    for ref, which in ((keep_ref, core), (give_ref, 1 - core)):
+        at = col + (lax.div(col, unit) + which) * unit
+        plan2.append((fc1_ref, at, wide2, ref, wide1))
+    second = run(plan2, 0)
+
+    @pl.when(is_proj)
+    def _():
+        for copy in run(copies(True), 2):
+            copy.wait()
+
+    @pl.when(jnp.logical_not(is_proj))
+    def _():
+        for copy in run(copies(False), 2):
+            copy.wait()
+
+    for copy in second:
+        copy.wait()
+
+
+def weight_share(rank, core, qkv_weight, proj_weight, fc1_weight, ranks, block, unit):
+    rows = qkv_weight.shape[0]
+    wide1, wide2 = 2 * D // ranks, fc1_weight.shape[1] // 2 // ranks
+    out = jax.ShapeDtypeStruct((rows, wide1 + wide2), bf16)
+    return pl.pallas_call(
+        functools.partial(share_kernel, (wide1, wide2, block, unit, D // 2)),
+        out_shape=[out, out],
+        grid_spec=pltpu.PrefetchScalarGridSpec(
+            num_scalar_prefetch=1,
+            grid=(1,),
+            in_specs=[pl.BlockSpec(memory_space=pl.ANY)] * 3,
+            out_specs=[pl.BlockSpec(out.shape, lambda i, a: (0, 0))] * 2,
+            scratch_shapes=[pltpu.SemaphoreType.DMA((2 + 2 * (wide1 // block),))],
+        ),
+        cost_estimate=SHORT,
+        name="weight_share",
+    )(jnp.stack([rank, core]).astype(jnp.int32), qkv_weight, proj_weight, fc1_weight)
 
 
 def whole_specs(arrays):
@@ -405,6 +506,169 @@
     )(core.reshape(1).astype(jnp.int32), *vectors)
 
 
+def grad_blocks_kernel(orders, ranks, index_ref, a_ref, b_ref, *refs):
+    outs, held = refs[:-1], refs[-1]
+    rank = index_ref[0]
+    held[...] = dot_tn(a_ref[...], b_ref[...]).astype(bf16)
+    width = held.shape[1] // ranks
+    share = held.shape[0] // len(orders)
+    for n, order in enumerate(orders):
+        for which, offsets in enumerate(halves(ranks, order[0], list(range(ranks)))):
+            for i, o in enumerate(offsets):
+                cols = pl.ds(pl.multiple_of((rank ^ o) * width, width), width)
+                outs[2 * n + which][i, 0] = held[n * share : (n + 1) * share, cols]
+
+
+def grad_blocks(a, b, rank, orders, name):
+    depth, ranks = lax.axis_size("fsdp") // 2, lax.axis_size("rep")
+    tokens, rows, cols = a.shape[0], a.shape[1] // depth, b.shape[1]
+    if cols // ranks % LANES:
+        return relative_blocks(dot_tn(a, b).astype(bf16), rank, orders)
+    block = (ranks // 2, depth, rows // len(orders), cols // ranks)
+    outs = pl.pallas_call(
+        functools.partial(grad_blocks_kernel, orders, ranks),
+        out_shape=[jax.ShapeDtypeStruct(block, bf16)] * (2 * len(orders)),
+        grid_spec=pltpu.PrefetchScalarGridSpec(
+            num_scalar_prefetch=1,
+            grid=(depth,),
+            in_specs=[
+                pl.BlockSpec((tokens, rows), lambda i, s: (0, i)),
+                pl.BlockSpec((tokens, cols), lambda i, s: (0, 0)),
+            ],
+            out_specs=[pl.BlockSpec((block[0], 1) + block[2:], lambda i, s: (0, i, 0, 0))] * (2 * len(orders)),
+            scratch_shapes=[pltpu.VMEM((rows, cols), bf16)],
+        ),
+        compiler_params=pltpu.CompilerParams(vmem_limit_bytes=40 << 20),
+        cost_estimate=SHORT,
+        name=name,
+    )(rank.reshape(1).astype(jnp.int32), a, b)
+    return [(outs[2 * n], outs[2 * n + 1]) for n in range(len(orders))]
+
+
+def pre_grad_kernel(g_ref, w_ref, slope_ref, out_ref, sum_ref):
+    grad = dot_nt(g_ref[...], w_ref[...]) * slope_ref[...]
+    out_ref[...] = grad.astype(bf16)
+    sum_ref[...] = jnp.sum(grad, axis=0, keepdims=True)
+
+
+def pre_grads(mlp_grad, fc2_matrix, slope):
+    tokens, units = slope.shape
+    tile = 256
+    return pl.pallas_call(
+        pre_grad_kernel,
+        out_shape=[jax.ShapeDtypeStruct((tokens, units), bf16), jax.ShapeDtypeStruct((1, units), f32)],
+        grid=(units // tile,),
+        in_specs=[
+            pl.BlockSpec((tokens, D), lambda i: (0, 0)),
+            pl.BlockSpec((tile, D), lambda i: (i, 0)),
+            pl.BlockSpec((tokens, tile), lambda i: (0, i)),
+        ],
+        out_specs=[pl.BlockSpec((tokens, tile), lambda i: (0, i)), pl.BlockSpec((1, tile), lambda i: (0, i))],
+        compiler_params=pltpu.CompilerParams(vmem_limit_bytes=40 << 20),
+        cost_estimate=SHORT,
+        name="pre_grad",
+    )(mlp_grad, fc2_matrix, slope)
+
+
+def product_kernel(multiply, half_ref, first_ref, second_ref, w_ref, out1_ref, out2_ref):
+    out1_ref[...] = multiply(first_ref[...], w_ref[...])
+    out2_ref[...] = multiply(second_ref[...], w_ref[...])
+
+
+def product(a, weight, multiply, half, name):
+    rows, tile = a.shape[0] // 2, 128
+    count = rows // tile
+    out = pl.BlockSpec((tile, D), lambda i, h: (i, 0))
+    return pl.pallas_call(
+        functools.partial(product_kernel, multiply),
+        out_shape=[jax.ShapeDtypeStruct((rows, D), f32)] * 2,
+        grid_spec=pltpu.PrefetchScalarGridSpec(
+            num_scalar_prefetch=1,
+            grid=(count,),
+            in_specs=[
+                pl.BlockSpec((tile, a.shape[1]), lambda i, h: (i + h[0] * count, 0)),
+                pl.BlockSpec((tile, a.shape[1]), lambda i, h: (i + (1 - h[0]) * count, 0)),
+                pl.BlockSpec(weight.shape, lambda i, h: (0, 0)),
+            ],
+            out_specs=[out, out],
+        ),
+        compiler_params=pltpu.CompilerParams(vmem_limit_bytes=32 << 20),
+        cost_estimate=SHORT,
+        name=name,
+    )(jnp.asarray(half, jnp.int32).reshape(1), a, a, weight)
+
+
+def finish_kernel(
+    own1_ref, sent1_ref, tok_ref, grad_ref, own2_ref, sent2_ref, resid_ref, cot_ref, vec_ref,
+    in_grad_ref, out_ref, sum_ref,
+):
+    grad = own1_ref[...] + sent1_ref[...]
+    normal, inverse = normalize(tok_ref[...].astype(f32))
+    in_grad_ref[...] = grad_ref[...] + norm_back(grad, normal, inverse, vec_ref[0:1, :])
+    mlp = own2_ref[...] + sent2_ref[...] + vec_ref[8:9, :]
+    out_ref[...] = (resid_ref[...] + vec_ref[9:10, :] * mlp).astype(bf16)
+    out_grad = cot_ref[...].astype(f32)
+
+    @pl.when(pl.program_id(0) == 0)
+    def _():
+        sum_ref[...] = jnp.zeros_like(sum_ref)
+
+    for row, value in enumerate((grad * normal, grad, out_grad * vec_ref[9:10, :], out_grad * mlp)):
+        sum_ref[row : row + 1, :] += jnp.sum(value, axis=0, keepdims=True)
+
+
+def finish(own1, sent1, tok, resid_grad, own2, sent2, resid, cot, vecs):
+    rows, tile = own1.shape[0], 64
+    part = pl.BlockSpec((tile, D), lambda i: (i, 0))
+    return pl.pallas_call(
+        finish_kernel,
+        out_shape=[
+            jax.ShapeDtypeStruct((rows, D), f32), jax.ShapeDtypeStruct((rows, D), bf16),
+            jax.ShapeDtypeStruct((8, D), f32),
+        ],
+        grid=(rows // tile,),
+        in_specs=[part] * 8 + [pl.BlockSpec(vecs.shape, lambda i: (0, 0))],
+        out_specs=[part, part, pl.BlockSpec((8, D), lambda i: (0, 0))],
+        compiler_params=pltpu.CompilerParams(vmem_limit_bytes=24 << 20),
+        cost_estimate=SHORT,
+        name="finish",
+    )(own1, sent1, tok, resid_grad, own2, sent2, resid, cot, vecs)
+
+
+def norm_grad_kernel(own_ref, sent_ref, resid_ref, cot_ref, attn_ref, vec_ref, grad_ref, scaled_ref, sum_ref):
+    grad = own_ref[...] + sent_ref[...]
+    normal, inverse = normalize(resid_ref[...])
+    resid_grad = cot_ref[...].astype(f32) + norm_back(grad, normal, inverse, vec_ref[6:7, :])
+    scaled = resid_grad * vec_ref[5:6, :]
+    grad_ref[...] = resid_grad
+    scaled_ref[...] = scaled.astype(bf16)
+
+    @pl.when(pl.program_id(0) == 0)
+    def _():
+        sum_ref[...] = jnp.zeros_like(sum_ref)
+
+    for row, value in enumerate((grad * normal, grad, scaled, resid_grad * attn_ref[...])):
+        sum_ref[row : row + 1, :] += jnp.sum(value, axis=0, keepdims=True)
+
+
+def norm_grads(own, sent, resid, cot, attn_out, vecs):
+    rows, tile = own.shape[0], 64
+    part = pl.BlockSpec((tile, D), lambda i: (i, 0))
+    return pl.pallas_call(
+        norm_grad_kernel,
+        out_shape=[
+            jax.ShapeDtypeStruct((rows, D), f32), jax.ShapeDtypeStruct((rows, D), bf16),
+            jax.ShapeDtypeStruct((8, D), f32),
+        ],
+        grid=(rows // tile,),
+        in_specs=[part] * 5 + [pl.BlockSpec(vecs.shape, lambda i: (0, 0))],
+        out_specs=[part, part, pl.BlockSpec((8, D), lambda i: (0, 0))],
+        compiler_params=pltpu.CompilerParams(vmem_limit_bytes=24 << 20),
+        cost_estimate=SHORT,
+        name="norm_grad",
+    )(own, sent, resid, cot, attn_out, vecs)
+
+
 def proj_grad_kernel(head_rows, c_ref, g_ref, out_ref):
     wide = out_ref.shape[1]
     for side in range(2):
@@ -420,7 +684,7 @@
         functools.partial(proj_grad_kernel, head_rows),
         out_shape=jax.ShapeDtypeStruct((D, wide), bf16),
         compiler_params=pltpu.CompilerParams(vmem_limit_bytes=32 << 20),
-        cost_estimate=pl.CostEstimate(flops=2 * context.shape[0] * D * wide, transcendentals=0, bytes_accessed=6 << 20),
+        cost_estimate=SHORT,
         name="proj_grad",
     )(context, attn_grad)
 
@@ -467,7 +731,7 @@
             scratch_shapes=[pltpu.VMEM((D, cols), bf16)],
         ),
         compiler_params=pltpu.CompilerParams(vmem_limit_bytes=40 << 20),
-        cost_estimate=pl.CostEstimate(flops=2 * tokens * D * cols, transcendentals=0, bytes_accessed=8 << 20),
+        cost_estimate=SHORT,
         name="qkv_grad",
     )(rank.reshape(1).astype(jnp.int32), normed, *grads, proj_packed)
     return [(outs[2 * n], outs[2 * n + 1]) for n in range(len(orders))]
@@ -512,9 +776,7 @@
             out_specs=[pl.BlockSpec((BLOCK, wide), lambda i, s: (i, 0))] * 3,
         ),
         compiler_params=pltpu.CompilerParams(vmem_limit_bytes=32 << 20),
-        cost_estimate=pl.CostEstimate(
-            flops=2 * rows * D * 3 * wide, transcendentals=0, bytes_accessed=rows * D * 6
-        ),
+        cost_estimate=SHORT,
         name="project",
     )(need, normed, weight, bias)
 
@@ -558,7 +820,7 @@
             out_specs=pl.BlockSpec((BLOCK, D), lambda i, a, b: (i, 0)),
         ),
         compiler_params=pltpu.CompilerParams(vmem_limit_bytes=24 << 20),
-        cost_estimate=pl.CostEstimate(flops=window * D * 10, transcendentals=0, bytes_accessed=30 << 20),
+        cost_estimate=SHORT,
         name="norm_window",
     )(need, info, *sources, vecs)
 
@@ -661,11 +923,7 @@
             ],
         ),
         compiler_params=pltpu.CompilerParams(vmem_limit_bytes=32 << 20),
-        cost_estimate=pl.CostEstimate(
-            flops=90 * own_rows * own_rows * LANES,
-            transcendentals=own_rows * own_rows * 2,
-            bytes_accessed=window * LANES * 6,
-        ),
+        cost_estimate=SHORT,
         name="attend",
     )(lo, hi, firsts, lasts, q, k, v, tag_cols, tag_row)
 
@@ -742,6 +1000,7 @@
 def attend_back(lo, hi, q, k, v, g, tag_cols, tag_row, lse, delta, own_rows, pair):
     window = q.shape[0]
     pairs, wide = 1, LANES
+    grad_pair = pair % (g.shape[1] // LANES)
     start = (window - own_rows) // 2 // BLOCK
     stop = start + own_rows // BLOCK
     whole = lambda: pl.BlockSpec((window, LANES), lambda p, a, b: (0, pair))
@@ -755,7 +1014,8 @@
             num_scalar_prefetch=2,
             grid=(pairs,),
             in_specs=[
-                whole(), whole(), whole(), whole(),
+                whole(), whole(), whole(),
+                pl.BlockSpec((window, LANES), lambda p, a, b: (0, grad_pair)),
                 pl.BlockSpec((window, LANES), lambda p, a, b: (0, 0)),
                 pl.BlockSpec((1, window), lambda p, a, b: (0, 0)),
                 stat(), stat(),
@@ -768,11 +1028,7 @@
             ],
         ),
         compiler_params=pltpu.CompilerParams(vmem_limit_bytes=40 << 20),
-        cost_estimate=pl.CostEstimate(
-            flops=180 * own_rows * own_rows * LANES,
-            transcendentals=own_rows * own_rows * 2,
-            bytes_accessed=window * wide * 8,
-        ),
+        cost_estimate=SHORT,
         name="attend_back",
     )(lo, hi, q, k, v, g, tag_cols, tag_row, lse, delta)
 
@@ -814,13 +1070,35 @@
         cuts = range(start * width, value.shape[1], 2 * width)
         return jnp.concatenate([value[:, c : c + width] for c in cuts], axis=1)
 
-    even = jnp.concatenate(
-        [every_other(qkv_weight, head_rows, 0), every_other(fc1_weight, unit_rows, 0)], axis=1
-    )
-    odd = jnp.concatenate(
-        [every_other(qkv_weight, head_rows, 1), every_other(fc1_weight, unit_rows, 1)], axis=1
-    )
-    kept, given = jnp.where(core == 0, even, odd), jnp.where(core == 0, odd, even)
+    def all_share(which):
+        pick_cols = lambda v, w: jnp.where(which == 0, every_other(v, w, 0), every_other(v, w, 1))
+        heads = lax.dynamic_slice_in_dim(
+            jnp.concatenate(
+                [
+                    pick_cols(qkv_weight, head_rows),
+                    lax.dynamic_slice_in_dim(proj_weight, which * half_heads, half_heads, 1),
+                ],
+                axis=1,
+            ),
+            rank * (2 * D // ranks), 2 * D // ranks, 1,
+        )
+        units = lax.dynamic_slice_in_dim(
+            pick_cols(fc1_weight, unit_rows), rank * (ff // 2 // ranks), ff // 2 // ranks, 1
+        )
+        return jnp.concatenate([heads, units], axis=1)
+
+    if head_rows % LANES:
+        kept, given = all_share(core), all_share(1 - core)
+    else:
+        kept, given = weight_share(
+            rank, core, qkv_weight, proj_weight, fc1_weight, ranks, head_rows, unit_rows
+        )
+    wide1 = 2 * D // ranks
+    got = swap_cores(given)
+    is_proj = rank * wide1 >= 3 * half_heads
+    own1 = in_order(kept[:, :wide1], jnp.where(is_proj, given[:, :wide1], got[:, :wide1]))
+    own2 = in_order(kept[:, wide1:], got[:, wide1:])
+    own3 = lax.dynamic_slice_in_dim(fc2_weight, rank * (D // ranks), D // ranks, 1)
     small = (
         ln1_gain, ln1_bias, query_bias, value_bias, proj_bias, scale_attn, ln2_gain, ln2_bias,
         fc2_bias, scale_mlp, fc1_bias, (image_ids[0] + 1).astype(bf16),
@@ -829,32 +1107,21 @@
     slots = slot_lists(sizes)
     width = 2 * D // ranks
     small = pack_small(small, width, slots)
-    paired = in_order(kept, swap_cores(given))
     small_other = swap_cores(small)
-    proj_packed = jnp.concatenate([proj_weight[:, :half_heads], proj_weight[:, half_heads:]], axis=0)
-    group1 = jnp.concatenate([paired[:, : 3 * half_heads], proj_packed], axis=1)
-    group2 = paired[:, 3 * half_heads :]
-
-    def own_columns(group):
-        width = group.shape[1] // ranks
-        return lax.dynamic_slice_in_dim(group, rank * width, width, 1)
-
-    own1, own2, own3 = own_columns(group1), own_columns(group2), own_columns(fc2_weight)
     rows1, rows3 = own1.shape[0], own3.shape[0]
-    tok_other = swap_cores(tokens[0])
-    cot_other = swap_cores(cotangent[0])
+    tok, cot = tokens[0], cotangent[0]
+    tok_other = swap_cores(tok)
+    cot_other = swap_cores(cot)
     own1 = jnp.concatenate([own1, small, small_other])
-    own1, own2, own3, tok, cot, tok_other, cot_other = tie(
-        own1, own2, own3, tokens[0], cotangent[0], tok_other, cot_other
-    )
+    own1, own2, own3, tok = tie(own1, own2, own3, tok)
     pieces1 = fetch_z(own1)
     tok, pieces1[1] = tie(tok, pieces1[1])
     behind, ahead = from_chip(tok, 1), from_chip(tok, -1)
-    own2, *pieces1 = tie(own2, *pieces1)
     gather1 = Gather(pieces1, rows1, "gather1")
-    own2, behind, ahead = gather1.send(own2, behind, ahead)
+    gather1.send()
     behind_other, ahead_other = swap_cores(behind), swap_cores(ahead)
-    pieces2 = fetch_z(own2)
+    for _ in bits[1:]:
+        gather1.send()
 
     vec_rows, fc1_shift, all_tags = unpack_small(
         pieces1, slots, rows1, here, core, ff // 2, devices * count
@@ -892,15 +1159,8 @@
         need, info, (behind, behind_other, tok, tok_other, ahead, ahead_other), vec_rows, window, count
     )
 
-    normed1 = gather1.arrive(normed1)
-    normed1, own3 = gather1.send(normed1, own3)
-    for _ in bits[2:]:
-        normed1 = gather1.arrive(normed1)
-        normed1 = gather1.send(normed1)
-    normed1, *pieces2 = tie(normed1, *pieces2)
-    gather2 = Gather(pieces2, rows1, "gather2")
-    normed1, own3 = gather2.send(normed1, own3)
-    pieces3 = fetch_z(own3)
+    normed1, own2 = tie(normed1, own2)
+    pieces2 = fetch_z(own2)
     normed1 = gather1.arrive(normed1)
     qkv_matrix, proj_matrix = gather1.assemble(here, rank, head_rows)
 
@@ -914,17 +1174,19 @@
     los, queries = tie(los, queries)
     for pair in range(pairs):
         if pair == 1:
+            los, own3, *pieces2 = tie(los, own3, *pieces2)
+            gather2 = Gather(pieces2, rows1, "gather2")
+            los = gather2.send(los)
+            pieces3 = fetch_z(own3)
+        if pair == 2:
             los = gather2.arrive(los)
+            los = gather2.send(los)
+        if pair == 3:
+            los = gather2.arrive(los)
+            for _ in bits[2:]:
+                los = gather2.arrive(gather2.send(los))
             los, *pieces3 = tie(los, *pieces3)
             gather3 = Gather(pieces3, rows3, "gather3")
-            los = gather2.send(los)
-            los = gather3.send(los)
-        if pair == 3:
-            los = gather2.arrive(los)
-            los = gather3.arrive(los)
-            for _ in bits[2:]:
-                los = gather2.send(los)
-                los = gather2.arrive(los)
             los = gather3.send(los)
         context, lse = attend(
             los, block_hi[own_lo:own_hi], firsts, lasts, queries, keys, values, tag_cols,
@@ -935,6 +1197,8 @@
         lses.append(lse)
     context = jnp.concatenate(contexts, axis=1)
     lse_rows = jnp.concatenate(lses).reshape(local_heads, chip)
+    context = gather3.arrive(context)
+    context = gather3.send(context)
     fc1_matrix = gather2.assemble(here, rank)
 
     features = tok.astype(f32)
@@ -952,29 +1216,23 @@
     mlp_grad_full = out_grad * mlp_scale
     mlp_grad = (jnp.concatenate([cot, cot_other]).astype(f32) * mlp_scale).astype(bf16)
 
+    both = [bits, bits[::-1]]
     activated = gather3.arrive(activated)
     for _ in bits[2:]:
-        activated = gather3.send(activated)
-        activated = gather3.arrive(activated)
+        activated = gather3.arrive(gather3.send(activated))
+    reduce3 = Reduce(grad_blocks(activated, mlp_grad, rank, both, "fc2_grad"), here, both)
+    mlp_grad = reduce3.send(mlp_grad)
     fc2_matrix = gather3.assemble(here, rank)
-    fc2_grad = dot_tn(activated, mlp_grad).astype(bf16)
-    reduce3 = Reduce(relative_blocks(fc2_grad, rank, [bits]), here, [bits])
-    activated, fc2_matrix = reduce3.send(activated, fc2_matrix)
-    sent = swap_cores(dot(activated[count:], fc2_matrix))
-    mlp_out = dot(activated[:count], fc2_matrix) + sent + fc2_shift
-    output_rows = (resid + mlp_scale * mlp_out).astype(bf16)
-    pre_grad_full = dot_nt(mlp_grad, fc2_matrix) * slope
-    pre_grad = pre_grad_full.astype(bf16)
-    fc1_bias_part = jnp.sum(pre_grad_full, axis=0, keepdims=True)
-
-    fc1_grad = dot_tn(mlp_input, pre_grad).astype(bf16)
-    reduce2 = Reduce(relative_blocks(fc1_grad, rank, [bits[::-1]]), here, [bits[::-1]])
-    pre_grad = reduce2.send(pre_grad)
-    sent = swap_cores(dot_nt(pre_grad[count:], fc1_matrix))
-    mlp_in_grad = dot_nt(pre_grad[:count], fc1_matrix) + sent
-    resid_grad = out_grad + norm_back(mlp_in_grad, mlp_normal, mlp_inverse, mlp_gain)
-    attn_grad_full = resid_grad * attn_scale
-    attn_grad = attn_grad_full.astype(bf16)
+    pre_grad, fc1_bias_part = pre_grads(mlp_grad, fc2_matrix, slope)
+    reduce2 = Reduce(grad_blocks(mlp_input, pre_grad, rank, both, "fc1_grad"), here, both)
+    pre_grad, _ = tie(pre_grad, [give for _, _, give in reduce2.held])
+    own, given = product(pre_grad, fc1_matrix, dot_nt, 0, "mlp_in_grad")
+    own, given = reduce3.arrive(own, given)
+    for _ in bits[2:]:
+        own, given = reduce3.arrive(*reduce3.send(own, given))
+    own, given = reduce3.send(own, given)
+    sent = swap_cores(given)
+    resid_grad, attn_grad, norm_sums = norm_grads(own, sent, resid, cot, attn_out, vec_rows)
     attn_grad = in_order(attn_grad, swap_cores(attn_grad))
     context_grad = dot_nt(attn_grad, proj_matrix).astype(bf16)
     head_of = (
@@ -986,17 +1244,18 @@
         precision=lax.Precision.HIGHEST, preferred_element_type=f32,
     )
     stats = jnp.concatenate([lse_rows, row_delta])
-    grads_behind, grads_ahead = from_chip(context_grad, 1), from_chip(context_grad, -1)
+    context_grad, activated, attn_grad = tie(context_grad, activated, attn_grad)
+    chunk = half_heads // 2
+    chunks = [context_grad[:, :chunk], context_grad[:, chunk:]]
+    grads_behind, grads_ahead = zip(*[(from_chip(c, 1), from_chip(c, -1)) for c in chunks])
     stats_behind, stats_ahead = from_chip(stats, 1), from_chip(stats, -1)
     proj_grad = packed_proj_grad(context, attn_grad, head_rows)
-    grad_window = jnp.concatenate([grads_behind, context_grad, grads_ahead])
     stat_window = jnp.concatenate([stats_behind, stats, stats_ahead], axis=1)
     by_pair = lambda s: s.reshape(pairs, 2, window)
     lse_window, delta_window = by_pair(stat_window[:local_heads]), by_pair(stat_window[local_heads:])
 
     half_pairs = pairs // 2
     half_width = half_heads // 2
-    both = [bits, bits[::-1]]
 
     def first_group(parts, number):
         grads = [g for kind in zip(*parts) for g in kind]
@@ -1005,77 +1264,76 @@
         )
 
     parts, sums = [], []
-    lo, delta_window = tie(block_lo, delta_window)
+    first, delta_window, lo = settle(
+        ((grads_behind[0], grads_ahead[0]), delta_window, block_lo), (reduce3, "received")
+    )
+    sides = [first, *list(zip(grads_behind, grads_ahead))[1:]]
+    grad_windows = [jnp.concatenate([b, c, a]) for c, (b, a) in zip(chunks, sides)]
     for pair in range(pairs):
         if pair == 0:
             lo = reduce3.arrive(lo)
-            for _ in bits[2:]:
-                lo = reduce3.arrive(reduce3.send(lo))
-            lo = reduce3.send(lo)
+            lo = reduce2.send(lo)
         if pair == 1:
-            lo = reduce3.arrive(lo)
+            lo = reduce2.arrive(lo)
             lo = reduce3.send_z(lo)
-            lo = reduce2.arrive(lo)
             for _ in bits[2:]:
                 lo = reduce2.arrive(reduce2.send(lo))
             lo = reduce2.send(lo)
         if pair == 2:
+            lo = settle(lo, (reduce2, "received"), (reduce3, "pieces"))
             lo = reduce2.arrive(lo)
             lo = reduce2.send_z(lo)
             reduce1a = first_group(parts, 0)
             lo = reduce1a.send(lo)
         if pair == 3:
+            lo = settle(lo, (reduce2, "pieces"), (reduce1a, "received"))
             lo = reduce3.arrive_z(lo)
             lo = reduce2.arrive_z(lo)
             fc2_part = reduce3.total.astype(bf16)
             fc1_part = reduce2.total.astype(bf16)
             split = fc2_part.shape[0] // fc1_part.shape[0]
-            mlp_part = jnp.concatenate([fc1_part, *jnp.split(fc2_part, split)], axis=1)[None]
-            mlp_offsets = [0]
-            lo, mlp_part = tie(lo, mlp_part)
-            mlp_more = across_rep(mlp_part, 0)
+            mlp_spread = Spread(jnp.concatenate([fc1_part, *jnp.split(fc2_part, split)], axis=1))
+            lo = mlp_spread.send(lo)
             lo = reduce1a.arrive(lo)
             for _ in bits[2:]:
                 lo = reduce1a.arrive(reduce1a.send(lo))
             lo = reduce1a.send(lo)
         *grads, total = attend_back(
-            lo, block_hi, queries, keys, values, grad_window, tag_cols, tag_row, lse_window,
+            lo, block_hi, queries, keys, values, grad_windows[pair * 2 // pairs], tag_cols, tag_row, lse_window,
             delta_window, chip, pair,
         )
         lo, *grads = tie(lo, *grads)
         parts.append(grads)
         sums.append(total[0])
 
+    parts[-1], activated = settle((parts[-1], activated), (mlp_spread, "arrays"))
+    parts[-1] = reduce1a.arrive(parts[-1])
+    parts[-1] = reduce1a.send_z(parts[-1])
     reduce1b = first_group(parts[half_pairs:], 1)
-    lo = reduce1b.send(lo)
+    parts[-1], activated = reduce1b.send(parts[-1], activated)
     every = [jnp.concatenate(p, axis=1) for p in zip(*parts)]
-    every[0], mlp_more, lo = tie(every[0], mlp_more, lo)
-    for later in bits[1:] + [None]:
-        mlp_part = jnp.concatenate([mlp_part, mlp_more])
-        flip = 1 << (len(mlp_offsets).bit_length() - 1)
-        mlp_offsets = mlp_offsets + [o ^ flip for o in mlp_offsets]
-        if later is not None:
-            mlp_more = across_rep(mlp_part, later)
-    reduce1a.arrive(lo)
-    every[0] = reduce1a.send_z(every[0])
 
     factor = 1.0 / math.sqrt(count * devices * ranks)
-    qkv_grad = jnp.concatenate(every, axis=1)
-    sent = swap_cores(dot_nt(others(qkv_grad), qkv_matrix))
-    attn_in_grad = dot_nt(mine(qkv_grad), qkv_matrix) + sent
+    in_own, in_given = product(
+        jnp.concatenate(every, axis=1), qkv_matrix, dot_nt, core, "attn_in_grad"
+    )
+    out_own, out_given = product(activated, fc2_matrix, dot, 0, "mlp_out")
+    tail = (in_own, in_given, out_own, out_given)
+    tail = settle(tail, (reduce1b, "received"), (reduce1a, "pieces"))
     for _ in bits[1:]:
-        attn_in_grad = reduce1b.arrive(attn_in_grad)
-        attn_in_grad = reduce1b.send(attn_in_grad)
-    attn_normal, attn_inverse = normalize(features)
-    input_rows = resid_grad + norm_back(attn_in_grad, attn_normal, attn_inverse, attn_gain)
-
-    columns = lambda value: jnp.sum(value, axis=0, keepdims=True)
+        tail = reduce1b.arrive(tail)
+        tail = reduce1b.send(tail)
+        tail = mlp_spread.send(tail)
+    in_own, in_given, out_own, out_given = tail
+    input_rows, output_rows, end_sums = finish(
+        in_own, swap_cores(in_given), tok, resid_grad, out_own, swap_cores(out_given), resid, cot, vec_rows
+    )
+
     vectors = (
-        columns(attn_in_grad * attn_normal), columns(attn_in_grad),
+        end_sums[0:1], end_sums[1:2],
         jnp.concatenate([s[0:1] for s in sums], axis=1), jnp.concatenate([s[1:2] for s in sums], axis=1),
-        columns(attn_grad_full), columns(resid_grad * attn_out),
-        columns(mlp_in_grad * mlp_normal), columns(mlp_in_grad),
-        columns(mlp_grad_full), columns(out_grad * mlp_out), fc1_bias_part,
+        norm_sums[2:3], norm_sums[3:4], norm_sums[0:1], norm_sums[1:2],
+        end_sums[2:3], end_sums[3:4], fc1_bias_part,
     )
     of_core = [number in (2, 3, 10) for number in range(11)]
     partial = pack_grads(vectors, list(zip(sizes, of_core)), core, depth)
@@ -1085,32 +1343,25 @@
     vec_total = pick(partial, here, 0)
     for k in range(1, depth):
         vec_total = vec_total + along_z(pick(partial, lax.rem(here + k, depth), 0), k)
-    reduce1a.arrive_z(lo)
+    reduce1a.arrive_z()
     vec_total = reduce1b.arrive_z(vec_total)
-    first_part = jnp.concatenate([reduce1a.total, reduce1b.total], axis=1).astype(bf16)[None]
-    first_offsets = [0]
+    vec_total = settle(vec_total, (mlp_spread, "arrays"))
+    first_spread = Spread(jnp.concatenate([reduce1a.total, reduce1b.total], axis=1).astype(bf16))
     for bit in bits:
-        received = across_rep(first_part, bit)
+        first_spread.send()
         vec_total = vec_total + across_rep(vec_total, bit)
-        first_part = jnp.concatenate([first_part, received])
-        first_offsets = first_offsets + [o ^ (1 << bit) for o in first_offsets]
     vec_half = vec_total.reshape(2, 16, LANES)
     totals = (pick(vec_half, core, 0) + swap_cores(pick(vec_half, 1 - core, 0))) * factor
 
     mlp_cols = fc1_part.shape[1]
-    fc1_full = rep_blocks(mlp_part[:, :, :mlp_cols], mlp_offsets, rank)
+    fc1_full = mlp_spread.blocks(rank, 0, mlp_cols)
     fc2_width = fc2_part.shape[1]
     grad_fc2 = jnp.concatenate(
-        [
-            rep_blocks(
-                mlp_part[:, :, mlp_cols + n * fc2_width : mlp_cols + (n + 1) * fc2_width], mlp_offsets, rank
-            )
-            for n in range(split)
-        ]
+        [mlp_spread.blocks(rank, mlp_cols + n * fc2_width, fc2_width) for n in range(split)]
     ).astype(f32) * factor
     vec_width = D // ranks
-    first_a = rep_blocks(first_part[:, :, :vec_width], first_offsets, rank)
-    first_b = rep_blocks(first_part[:, :, vec_width:], first_offsets, rank)
+    first_a = first_spread.blocks(rank, 0, vec_width)
+    first_b = first_spread.blocks(rank, vec_width, vec_width)
 
     def rows_of(value, index):
         return lax.dynamic_slice_in_dim(value, index * head_rows, head_rows, 0)

time: 658 us -> 630 us (0.957)
  Pallas kernels: 156 us -> 227 us
  waiting for transfers between devices: 140 us -> 88.8 us
  matrix products: 64.4 us -> 19.7 us
  starting transfers between devices: 173 us -> 160 us
  other arithmetic: 56.6 us -> 69.6 us
  local copies, waits for them, and re-layouts: 58.1 us -> 50.1 us
    pallas_call x0 -> x9, Pallas kernels: none -> 67.3 us  [the longest x3 26.8 us: product(): pl.pallas_call(functools.partial(product_kernel, multiply), out_shape=[ja...]
    ppermute x30 -> x38, waiting for transfers between devices: 101 us -> 37.1 us  [across_rep(): return lax.ppermute(value, 'rep', [(i, i ^ 1 << bit) for i in range(size)])]
    dot_general x6 -> x1, matrix products: 24.3 us -> 1.28 us  [dot_nt(): lax.dot_general(a, b, (((1,), (1,)), ((), ())), preferred_element_type=f32)]
    ppermute x6 -> x8, waiting for transfers between devices: 13.5 us -> 30.9 us  [from_chip(): return lax.ppermute(value, 'fsdp', pairs)]
    dot_general x2 -> x0, matrix products: 14.5 us -> none  [dot_tn(): lax.dot_general(a, b, (((0,), (0,)), ((), ())), preferred_element_type=f32)]
    ppermute x24, starting transfers between devices: 81.1 us -> 69.3 us  [along_z(): lax.ppermute(value, 'fsdp', [(i, (i + 2 * by) % size) for i in range(size)])]
    mul x1, other arithmetic: 1.6 us -> 9.36 us  [on_device(): jnp.concatenate([mlp_spread.blocks(rank, mlp_cols + n * fc2_width, fc2_wi...]
    ppermute x24, waiting for transfers between devices: 19.4 us -> 12.4 us  [along_z(): lax.ppermute(value, 'fsdp', [(i, (i + 2 * by) % size) for i in range(size)])]
  transfers between devices with their start and end apart: 75 -> 85, of which waited for: 29 -> 18; matrix products, arithmetic and copies ran while one was open for 12% -> 13% of each run, Pallas kernels for 20% -> 34%
where the time goes in v3:
time: 630 us; the launch traced here: 619 us
  Pallas kernels  227 us (36%)
  starting transfers between devices  160 us (25%)
  waiting for transfers between devices  88.8 us (14%)
  other arithmetic  69.6 us (11%)
  local copies, waits for them, and re-layouts  50.1 us (8%)
  matrix products  19.7 us (3%)
    pallas_call x4, Pallas kernels, attend_back(): pl.pallas_call(functools.partial(attend_back_kernel, start, stop), out_sh...  76.7 us
    ppermute x24, starting transfers between devices, along_z(): lax.ppermute(value, 'fsdp', [(i, (i + 2 * by) % size) for i in range(size)])  69.3 us
    pallas_call x4, Pallas kernels, attend(): pl.pallas_call(attend_kernel, out_shape=[jax.ShapeDtypeStruct((own_rows,...  52.3 us
    ppermute x38, starting transfers between devices, across_rep(): return lax.ppermute(value, 'rep', [(i, i ^ 1 << bit) for i in range(size)])  48.3 us
    ppermute x8, starting transfers between devices, from_chip(): return lax.ppermute(value, 'fsdp', pairs)  40 us
    ppermute x38, waiting for transfers between devices, across_rep(): return lax.ppermute(value, 'rep', [(i, i ^ 1 << bit) for i in range(size)])  37.1 us
    unnamed x301, local copies, waits for them, and re-layouts  32.9 us
    ppermute x8, waiting for transfers between devices, from_chip(): return lax.ppermute(value, 'fsdp', pairs)  30.9 us
  transfers between devices with their start and end apart: 85, of which 18 were waited for; matrix products, arithmetic and copies ran while one was open for 13% of the time, Pallas kernels for 34%

profile of v3, /device:TPU:0, one launch (start us, length us, event | category | flops | bytes accessed | tf_op | source)
XLA Modules:
  0.0 619.3 jit_solution(1271870121203975670)
XLA Ops:
  17.7 5.8 collective-permute-done.3.refs_1_
  24.8 13.9 %collective-permute-start.6 = (bf16[512,1024]{1,0:T(8,128)(2,1)S(1)}, bf16[512,1024]{1,0:T(8,128)(2,1)}, u32[]{:S(2)}, u32[]{:S(2)}) collective-permute-start(bf16[512,1024]{1,0:T(8,128)(2,1)S(1)} %bitcast.293), channel_id=1, source_target_pairs={{0,2},{1,3},{2,4},{3,5},{4,6},{5,7},{8,10},{9,11},{10,12},{11,13},... | collective-permute-start | bytes 3145736 | tf_op jit(solution)/shard_map/ppermute | solution.py:72
  49.7 7.3 %collective-permute-done.9.refs_4_ = bf16[512,1024]{1,0:T(8,128)(2,1)S(1)} collective-permute-done((bf16[512,1024]{1,0:T(8,128)(2,1)S(1)}, bf16[512,1024]{1,0:T(8,128)(2,1)S(1)}, u32[]{:S(2)}, u32[]{:S(2)}) %collective-permute-start.9) | collective-permute-done | bytes 1048608 | tf_op jit(solution)/shard_map/ppermute | solution.py:72
  66.1 7.0 %norm_window.1.n_ref = bf16[3072,1024]{1,0:T(8,128)(2,1)S(1)} custom-call(s32[12]{0:T(128)S(1)} %and_convert_fusion.need_ref, s32[2]{0:T(128)S(1)} %pad_add_fusion.1.info_ref, bf16[512,1024]{1,0:T(8,128)(2,1)} %collective-permute-done.6.refs_0_, bf16[512,1024]{1,0:T(8,128)(2,1)S(1)} %collective-permute-done.7.refs_1_, bf16[512,1024]{1,0:T(8,128)(2,1)S(1)} %bitcast.294, ...), custom_call_target="tpu_custom_call" | custom-call | flops 1 | bytes 1 | tf_op jit(solution)/shard_map/norm_window/pallas_call | solution.py:813
  73.1 7.2 %collective-permute-start.15 = (bf16[256,512]{1,0:T(8,128)(2,1)S(1)}, bf16[256,512]{1,0:T(8,128)(2,1)S(1)}, u32[]{:S(2)}, u32[]{:S(2)}) collective-permute-start(bf16[256,512]{1,0:T(8,128)(2,1)S(1)} %copy-done.113), channel_id=1, source_target_pairs={{0,2},{1,3},{2,4},{3,5},{4,6},{5,7},{6,0},{7,1},{8,10},{9,11},{10,... | collective-permute-start | bytes 786440 | tf_op jit(solution)/shard_map/ppermute | solution.py:66
  89.5 8.0 %project.1 = (bf16[3072,512]{1,0:T(8,128)(2,1)S(1)}, bf16[3072,512]{1,0:T(8,128)(2,1)S(1)}, bf16[3072,512]{1,0:T(8,128)(2,1)S(1)}) custom-call(s32[12]{0:T(128)S(1)} %and_convert_fusion.need_ref, bf16[3072,1024]{1,0:T(8,128)(2,1)S(1)} %norm_window.1.n_ref, bf16[1024,1536]{1,0:T(8,128)(2,1)S(1)} %get-tuple-element.342.w_ref, f32[1,1536]{1,0:T(1,128)S(1)} %fusion.71.b_ref), custom_call_target="tpu_custom_call" | custom-call | flops 1 | bytes 1 | tf_op jit(solution)/shard_map/project/pallas_call | solution.py:765
  100.5 13.1 %attend.4 = (bf16[1024,128]{1,0:T(8,128)(2,1)S(1)}, f32[1,2,1024]{2,1,0:T(2,128)S(1)}) custom-call(s32[4]{0:T(128)S(1)} %slice.878.lo_ref, s32[4]{0:T(128)S(1)} %slice.906.hi_ref, s32[12]{0:T(128)S(1)} %convert_element_type.262.first_ref, s32[12]{0:T(128)S(1)} %convert_element_type.263.last_ref, bf16[3072,512]{1,0:T(8,128)(2,1)S(1)} %get-tuple-element.345.q_ref, ...), custom_call_target="tpu_custom_call" | custom-call | flops 1 | bytes 1 | tf_op jit(solution)/shard_map/attend/pallas_call | solution.py:900
  114.3 3.5 collective-permute-start.19
  117.8 13.1 %attend.5 = (bf16[1024,128]{1,0:T(8,128)(2,1)S(1)}, f32[1,2,1024]{2,1,0:T(2,128)S(1)}) custom-call(s32[4]{0:T(128)S(1)} %slice.878.lo_ref, s32[4]{0:T(128)S(1)} %slice.906.hi_ref, s32[12]{0:T(128)S(1)} %convert_element_type.262.first_ref, s32[12]{0:T(128)S(1)} %convert_element_type.263.last_ref, bf16[3072,512]{1,0:T(8,128)(2,1)S(1)} %get-tuple-element.345.q_ref, ...), custom_call_target="tpu_custom_call" | custom-call | flops 1 | bytes 1 | tf_op jit(solution)/shard_map/attend/pallas_call | solution.py:900
  133.0 11.5 %collective-permute-start.22 = (bf16[512,256]{1,0:T(8,128)(2,1)S(1)}, bf16[512,256]{1,0:T(8,128)(2,1)S(1)}, u32[]{:S(2)}, u32[]{:S(2)}) collective-permute-start(bf16[512,256]{1,0:T(8,128)(2,1)S(1)} %copy-done.112), channel_id=1, source_target_pairs={{0,2},{1,3},{2,4},{3,5},{4,6},{5,7},{6,0},{7,1},{8,10},{9,11},{10,... | collective-permute-start | bytes 786440 | tf_op jit(solution)/shard_map/ppermute | solution.py:66
  147.3 13.1 %attend.6 = (bf16[1024,128]{1,0:T(8,128)(2,1)S(1)}, f32[1,2,1024]{2,1,0:T(2,128)S(1)}) custom-call(s32[4]{0:T(128)S(1)} %slice.878.lo_ref, s32[4]{0:T(128)S(1)} %slice.906.hi_ref, s32[12]{0:T(128)S(1)} %convert_element_type.262.first_ref, s32[12]{0:T(128)S(1)} %convert_element_type.263.last_ref, bf16[3072,512]{1,0:T(8,128)(2,1)S(1)} %get-tuple-element.345.q_ref, ...), custom_call_target="tpu_custom_call" | custom-call | flops 1 | bytes 1 | tf_op jit(solution)/shard_map/attend/pallas_call | solution.py:900
  170.7 13.1 %attend.7 = (bf16[1024,128]{1,0:T(8,128)(2,1)S(1)}, f32[1,2,1024]{2,1,0:T(2,128)S(1)}) custom-call(s32[4]{0:T(128)S(1)} %slice.878.lo_ref, s32[4]{0:T(128)S(1)} %slice.906.hi_ref, s32[12]{0:T(128)S(1)} %convert_element_type.262.first_ref, s32[12]{0:T(128)S(1)} %convert_element_type.263.last_ref, bf16[3072,512]{1,0:T(8,128)(2,1)S(1)} %get-tuple-element.345.q_ref, ...), custom_call_target="tpu_custom_call" | custom-call | flops 1 | bytes 1 | tf_op jit(solution)/shard_map/attend/pallas_call | solution.py:900
  191.5 4.0 collective-permute-done.27
  195.5 4.6 fusion.76
  207.6 10.5 %fusion.3 = (f32[1024,2048]{1,0:T(8,128)}, bf16[1024,2048]{1,0:T(8,128)(2,1)S(1)}) fusion(f32[2048]{0:T(1024)S(1)} %bitcast.321, bf16[1024,2048]{1,0:T(8,128)(2,1)S(1)} %gather2.1.w_ref, bf16[512,1024]{1,0:T(8,128)(2,1)S(1)} %collective-permute-done.28, bf16[512,1024]{1,0:T(8,128)(2,1)S(1)} %add_convert_fusion.4), kind=kOutput, calls=%fused_computation.4 | convolution fusion | flops 4322230272 | bytes 18882560 | tf_op jit(solution)/shard_map/dot_general | solution.py:48
  218.1 13.1 %collective-permute-done.29.refs_1_ = bf16[2,4,256,256]{3,2,1,0:T(8,128)(2,1)S(1)} collective-permute-done((bf16[2,4,256,256]{3,2,1,0:T(8,128)(2,1)S(1)}, bf16[2,4,256,256]{3,2,1,0:T(8,128)(2,1)S(1)}, u32[]{:S(2)}, u32[]{:S(2)}) %collective-permute-start.29) | collective-permute-done | bytes 1048608 | tf_op jit(solution)/shard_map/ppermute | solution.py:77
  233.2 7.0 %fc2_grad.1 = (bf16[2,4,256,256]{3,2,1,0:T(8,128)(2,1)S(1)}, bf16[2,4,256,256]{3,2,1,0:T(8,128)(2,1)}, bf16[2,4,256,256]{3,2,1,0:T(8,128)(2,1)S(1)}, bf16[2,4,256,256]{3,2,1,0:T(8,128)(2,1)}) custom-call(s32[1]{0:T(128)} %bitcast.3.index_ref, bf16[1024,2048]{1,0:T(8,128)(2,1)S(1)} %get-tuple-element.554.a_ref.first_ref.second_ref, ...), custom_call_target="tpu_custom_call" | custom-call | flops 1 | bytes 1 | tf_op jit(solution)/shard_map/fc2_grad/pallas_call | solution.py:528
  243.8 10.3 %pre_grad.1 = (bf16[1024,2048]{1,0:T(8,128)(2,1)S(1)}, f32[1,2048]{1,0:T(1,128)S(1)}) custom-call(bf16[1024,1024]{1,0:T(8,128)(2,1)S(1)} %multiply_convert_fusion.1.b_ref.g_ref, bf16[2048,1024]{1,0:T(8,128)(2,1)S(1)} %gather3.1.w_ref, f32[1024,2048]{1,0:T(8,128)} %get-tuple-element.633.slope_ref), custom_call_target="tpu_custom_call" | custom-call | flops 1 | bytes 1 | tf_op jit(solution)/shard_map/pre_grad/pallas_call | solution.py:557
  254.7 6.3 %fc1_grad.1 = (bf16[2,4,128,512]{3,2,1,0:T(8,128)(2,1)S(1)}, bf16[2,4,128,512]{3,2,1,0:T(8,128)(2,1)S(1)}, bf16[2,4,128,512]{3,2,1,0:T(8,128)(2,1)S(1)}, bf16[2,4,128,512]{3,2,1,0:T(8,128)(2,1)S(1)}) custom-call(s32[1]{0:T(128)} %bitcast.3.index_ref, bf16[1024,1024]{1,0:T(8,128)(2,1)S(1)} %pad_maximum_fusion.a_ref, ...), custom_call_target="tpu_custom_call" | custom-call | flops 1 | bytes 1 | tf_op jit(solution)/shard_map/fc1_grad/pallas_call | solution.py:528
  262.0 11.5 %mlp_in_grad.1 = (f32[512,1024]{1,0:T(8,128)S(1)}, f32[512,1024]{1,0:T(8,128)S(1)}) custom-call(s32[1]{0:T(128)} %constant.162.clone.1.half_ref, bf16[1024,2048]{1,0:T(8,128)(2,1)S(1)} %get-tuple-element.412.b_ref.first_ref.second_ref, bf16[1024,2048]{1,0:T(8,128)(2,1)S(1)} %get-tuple-element.412.b_ref.first_ref.second_ref, bf16[1024,2048]{1,0:T(8,128)(2,1)S(1)} %copy-done.19), custom_call_target="tpu_custom_call" | custom-call | flops 1 | bytes 1 | tf_op jit(solution)/shard_map/mlp_in_grad/pallas_call | solution.py:582
  278.7 4.2 collective-permute-done.33.sent_ref
  282.8 6.6 %norm_grad.1 = (f32[512,1024]{1,0:T(8,128)S(1)}, bf16[512,1024]{1,0:T(8,128)(2,1)}, f32[8,1024]{1,0:T(8,128)S(1)}) custom-call(f32[512,1024]{1,0:T(8,128)S(1)} %get-tuple-element.423.own_ref, f32[512,1024]{1,0:T(8,128)S(1)} %collective-permute-done.33.sent_ref, f32[512,1024]{1,0:T(8,128)S(1)} %get-tuple-element.632.resid_ref, ...), custom_call_target="tpu_custom_call" | custom-call | flops 1 | bytes 1 | tf_op jit(solution)/shard_map/norm_grad/pallas_call | solution.py:657
  293.8 3.3 maximum_select_fusion.g_ref
  300.3 10.4 %collective-permute-start.37 = (f32[16,1024]{1,0:T(8,128)S(1)}, f32[16,1024]{1,0:T(8,128)S(1)}, u32[]{:S(2)}, u32[]{:S(2)}) collective-permute-start(f32[16,1024]{1,0:T(8,128)S(1)} %pad_maximum_fusion.21), channel_id=1, source_target_pairs={{0,2},{1,3},{2,4},{3,5},{4,6},{5,7},{8,10},{9,11},{10,12},{11,13},... | collective-permute-start | bytes 196616 | tf_op jit(solution)/shard_map/ppermute | solution.py:72
  313.1 5.3 collective-permute-start.35
  321.4 7.4 %collective-permute-done.35 = bf16[1024,256]{1,0:T(8,128)(2,1)} collective-permute-done((bf16[1024,256]{1,0:T(8,128)(2,1)}, bf16[1024,256]{1,0:T(8,128)(2,1)}, u32[]{:S(2)}, u32[]{:S(2)}) %collective-permute-start.35) | collective-permute-done | bytes 524320 | tf_op jit(solution)/shard_map/ppermute | solution.py:72
  328.8 4.9 collective-permute-done.36
  341.5 19.2 %attend_back.4 = (bf16[1024,128]{1,0:T(8,128)(2,1)S(1)}, bf16[1024,128]{1,0:T(8,128)(2,1)S(1)}, bf16[1024,128]{1,0:T(8,128)(2,1)S(1)}, f32[1,8,128]{2,1,0:T(8,128)S(1)}) custom-call(s32[12]{0:T(128)S(1)} %get-tuple-element.521.lo_ref, s32[12]{0:T(128)S(1)} %get-tuple-element.835.hi_ref, bf16[3072,512]{1,0:T(8,128)(2,1)S(1)} %get-tuple-element.345.q_ref, ...), custom_call_target="tpu_custom_call" | custom-call | flops 1 | bytes 1 | tf_op jit(solution)/shard_map/attend_back/pallas_call | solution.py:1009
  369.4 4.1 collective-permute-start.44
  373.5 4.3 collective-permute-start.45
  381.5 19.2 %attend_back.5 = (bf16[1024,128]{1,0:T(8,128)(2,1)S(1)}, bf16[1024,128]{1,0:T(8,128)(2,1)S(1)}, bf16[1024,128]{1,0:T(8,128)(2,1)S(1)}, f32[1,8,128]{2,1,0:T(8,128)S(1)}) custom-call(s32[12]{0:T(128)S(1)} %get-tuple-element.521.lo_ref, s32[12]{0:T(128)S(1)} %get-tuple-element.835.hi_ref, bf16[3072,512]{1,0:T(8,128)(2,1)S(1)} %get-tuple-element.345.q_ref, ...), custom_call_target="tpu_custom_call" | custom-call | flops 1 | bytes 1 | tf_op jit(solution)/shard_map/attend_back/pallas_call | solution.py:1009
  403.0 5.2 collective-permute-start.48
  413.1 3.3 collective-permute-start.54
  419.3 11.2 %collective-permute-done.49 = bf16[1024,256]{1,0:T(8,128)(2,1)S(1)} collective-permute-done((bf16[1024,256]{1,0:T(8,128)(2,1)S(1)}, bf16[1024,256]{1,0:T(8,128)(2,1)S(1)}, u32[]{:S(2)}, u32[]{:S(2)}) %collective-permute-start.49) | collective-permute-done | bytes 524320 | tf_op jit(solution)/shard_map/ppermute | solution.py:72
  432.5 19.2 %attend_back.6 = (bf16[1024,128]{1,0:T(8,128)(2,1)S(1)}, bf16[1024,128]{1,0:T(8,128)(2,1)S(1)}, bf16[1024,128]{1,0:T(8,128)(2,1)S(1)}, f32[1,8,128]{2,1,0:T(8,128)S(1)}) custom-call(s32[12]{0:T(128)S(1)} %get-tuple-element.521.lo_ref, s32[12]{0:T(128)S(1)} %get-tuple-element.835.hi_ref, bf16[3072,512]{1,0:T(8,128)(2,1)S(1)} %get-tuple-element.345.q_ref, ...), custom_call_target="tpu_custom_call" | custom-call | flops 1 | bytes 1 | tf_op jit(solution)/shard_map/attend_back/pallas_call | solution.py:1009
  454.7 5.0 collective-permute-start.55
  463.1 19.2 %attend_back.7 = (bf16[1024,128]{1,0:T(8,128)(2,1)S(1)}, bf16[1024,128]{1,0:T(8,128)(2,1)S(1)}, bf16[1024,128]{1,0:T(8,128)(2,1)S(1)}, f32[1,8,128]{2,1,0:T(8,128)S(1)}) custom-call(s32[12]{0:T(128)S(1)} %get-tuple-element.521.lo_ref, s32[12]{0:T(128)S(1)} %get-tuple-element.835.hi_ref, bf16[3072,512]{1,0:T(8,128)(2,1)S(1)} %get-tuple-element.345.q_ref, ...), custom_call_target="tpu_custom_call" | custom-call | flops 1 | bytes 1 | tf_op jit(solution)/shard_map/attend_back/pallas_call | solution.py:1009
  491.3 4.3 collective-permute-start.60
  495.6 14.6 %collective-permute-start.61 = (bf16[256,256]{1,0:T(8,128)(2,1)S(1)}, bf16[256,256]{1,0:T(8,128)(2,1)S(1)}, u32[]{:S(2)}, u32[]{:S(2)}) collective-permute-start(bf16[256,256]{1,0:T(8,128)(2,1)S(1)} %get-tuple-element.560), channel_id=1, source_target_pairs={{0,2},{1,3},{2,4},{3,5},{4,6},{5,7},{6,0},{7,1},{8,10},{9,11},{10,... | collective-permute-start | bytes 393224 | tf_op jit(solution)/shard_map/ppermute | solution.py:66
  515.5 6.1 mlp_out.1
  521.5 9.2 %attn_in_grad.1 = (f32[512,1024]{1,0:T(8,128)S(1)}, f32[512,1024]{1,0:T(8,128)}) custom-call(s32[1]{0:T(128)} %bitcast.half_ref.index_ref, bf16[1024,1536]{1,0:T(8,128)(2,1)S(1)} %constant_dynamic-update-slice_fusion.first_ref.second_ref, bf16[1024,1536]{1,0:T(8,128)(2,1)S(1)} %constant_dynamic-update-slice_fusion.first_ref.second_ref, ...), custom_call_target="tpu_custom_call" | custom-call | flops 1 | bytes 1 | tf_op jit(solution)/shard_map/attn_in_grad/pallas_call | solution.py:582
  540.4 8.1 %collective-permute-done.75 = bf16[2,128,1024]{2,1,0:T(8,128)(2,1)S(1)} collective-permute-done((bf16[2,128,1024]{2,1,0:T(8,128)(2,1)}, bf16[2,128,1024]{2,1,0:T(8,128)(2,1)S(1)}, u32[]{:S(2)}, u32[]{:S(2)}) %collective-permute-start.75) | collective-permute-done | bytes 524320 | tf_op jit(solution)/shard_map/ppermute | solution.py:77
  557.1 7.7 %finish.1 = (f32[512,1024]{1,0:T(8,128)}, bf16[512,1024]{1,0:T(8,128)(2,1)}, f32[8,1024]{1,0:T(8,128)S(1)}) custom-call(f32[512,1024]{1,0:T(8,128)S(1)} %copy-done.47, f32[512,1024]{1,0:T(8,128)} %collective-permute-done.64.sent1_ref, bf16[512,1024]{1,0:T(8,128)(2,1)S(1)} %bitcast.295, f32[512,1024]{1,0:T(8,128)S(1)} %copy-done.43, ...), custom_call_target="tpu_custom_call" | custom-call | flops 1 | bytes 1 | tf_op jit(solution)/shard_map/finish/pallas_call | solution.py:623
  569.9 3.2 collective-permute-start.70
  579.5 3.2 collective-permute-done.71
  582.7 3.2 collective-permute-done.72
  594.3 9.4 %convert_multiply_fusion = f32[512,1024]{1,0:T(8,128)} fusion(bf16[128,256]{1,0:T(8,128)(2,1)S(1)} %get-tuple-element.650, bf16[128,256]{1,0:T(8,128)(2,1)S(1)} %get-tuple-element.648, bf16[128,256]{1,0:T(8,128)(2,1)S(1)} %get-tuple-element.644, bf16[128,256]{1,0:T(8,128)(2,1)S(1)} %get-tuple-element.647, bf16[128,256]{1,0:T(8,128)(2,1)S(1)} %get-tuple-element.642, ...), kind=kLoop, calls=%fused_computation.10 | loop fusion | flops 17301504 | bytes 3145728 | tf_op jit(solution)/shard_map/mul | solution.py:1359
  605.5 6.9 %collective-permute-done.81 = bf16[2,128,512]{2,1,0:T(8,128)(2,1)S(1)} collective-permute-done((bf16[2,128,512]{2,1,0:T(8,128)(2,1)S(1)}, bf16[2,128,512]{2,1,0:T(8,128)(2,1)S(1)}, u32[]{:S(2)}, u32[]{:S(2)}) %collective-permute-start.81) | collective-permute-done | bytes 262176 | tf_op jit(solution)/shard_map/ppermute | solution.py:77
  (626 shorter events, 204.1 us)
Async XLA Ops:
  13.8 52.3 %collective-permute-start.8 = (bf16[512,1024]{1,0:T(8,128)(2,1)S(1)}, bf16[512,1024]{1,0:T(8,128)(2,1)S(1)}, u32[]{:S(2)}, u32[]{:S(2)}) collective-permute-start(bf16[512,1024]{1,0:T(8,128)(2,1)S(1)} %bitcast.291), channel_id=1, source_target_pairs={{0,1},{1,0},{2,3},{3,2},{4,5},{5,4},{6,7},{7,6},{8,9},{9,8},{10,11... | collective-permute-start | bytes 3145736 | tf_op jit(solution)/shard_map/ppermute | solution.py:61
  13.8 26.0 %collective-permute-start.4 = (bf16[272,512]{1,0:T(8,128)(2,1)S(1)}, bf16[272,512]{1,0:T(8,128)(2,1)S(1)}, u32[]{:S(2)}, u32[]{:S(2)}) collective-permute-start(bf16[272,512]{1,0:T(8,128)(2,1)S(1)} %pad_maximum_fusion.15.refs_0_), channel_id=1, source_target_pairs={{0,4},{1,5},{2,6},{3,7},{4,0},{5,1},{6,2},{7,3},{8,12},{9,13},{10,... | collective-permute-start | bytes 835592 | tf_op jit(solution)/shard_map/ppermute | solution.py:66
  16.4 23.5 %collective-permute-start.5 = (bf16[272,512]{1,0:T(8,128)(2,1)S(1)}, bf16[272,512]{1,0:T(8,128)(2,1)S(1)}, u32[]{:S(2)}, u32[]{:S(2)}) collective-permute-start(bf16[272,512]{1,0:T(8,128)(2,1)S(1)} %pad_maximum_fusion.15.refs_0_), channel_id=1, source_target_pairs={{0,6},{1,7},{2,0},{3,1},{4,2},{5,3},{6,4},{7,5},{8,14},{9,15},{10,... | collective-permute-start | bytes 835592 | tf_op jit(solution)/shard_map/ppermute | solution.py:66
  23.6 33.5 %collective-permute-start.9 = (bf16[512,1024]{1,0:T(8,128)(2,1)S(1)}, bf16[512,1024]{1,0:T(8,128)(2,1)S(1)}, u32[]{:S(2)}, u32[]{:S(2)}) collective-permute-start(bf16[512,1024]{1,0:T(8,128)(2,1)S(1)} %bitcast.292), channel_id=1, source_target_pairs={{2,0},{3,1},{4,2},{5,3},{6,4},{7,5},{10,8},{11,9},{12,10},{13,11},... | collective-permute-start | bytes 3145736 | tf_op jit(solution)/shard_map/ppermute | solution.py:72
  24.8 32.2 %collective-permute-start.6 = (bf16[512,1024]{1,0:T(8,128)(2,1)S(1)}, bf16[512,1024]{1,0:T(8,128)(2,1)}, u32[]{:S(2)}, u32[]{:S(2)}) collective-permute-start(bf16[512,1024]{1,0:T(8,128)(2,1)S(1)} %bitcast.293), channel_id=1, source_target_pairs={{0,2},{1,3},{2,4},{3,5},{4,6},{5,7},{8,10},{9,11},{10,12},{11,13},... | collective-permute-start | bytes 3145736 | tf_op jit(solution)/shard_map/ppermute | solution.py:72
  60.2 25.1 %collective-permute-start.13 = (bf16[2,4,128,512]{3,2,1,0:T(8,128)(2,1)S(1)}, bf16[2,4,128,512]{3,2,1,0:T(8,128)(2,1)S(1)}, u32[]{:S(2)}, u32[]{:S(2)}) collective-permute-start(bf16[2,4,128,512]{3,2,1,0:T(8,128)(2,1)S(1)} %pad_maximum_fusion.3.refs_0_), channel_id=1, source_target_pairs={{0,16},{8,24},{16,0},{24,8},{1,17},{9,25},{17,1},{25,9},{2,18},{10... | collective-permute-start | bytes 3145736 | tf_op jit(solution)/shard_map/ppermute | solution.py:77
  61.8 24.8 %collective-permute-start.14 = (bf16[2,4,128,512]{3,2,1,0:T(8,128)(2,1)S(1)}, bf16[2,4,128,512]{3,2,1,0:T(8,128)(2,1)S(1)}, u32[]{:S(2)}, u32[]{:S(2)}) collective-permute-start(bf16[2,4,128,512]{3,2,1,0:T(8,128)(2,1)S(1)} %pad_maximum_fusion.4.refs_2_), channel_id=1, source_target_pairs={{0,8},{8,0},{16,24},{24,16},{1,9},{9,1},{17,25},{25,17},{2,10},{10... | collective-permute-start | bytes 3145736 | tf_op jit(solution)/shard_map/ppermute | solution.py:77
  73.1 40.5 %collective-permute-start.15 = (bf16[256,512]{1,0:T(8,128)(2,1)S(1)}, bf16[256,512]{1,0:T(8,128)(2,1)S(1)}, u32[]{:S(2)}, u32[]{:S(2)}) collective-permute-start(bf16[256,512]{1,0:T(8,128)(2,1)S(1)} %copy-done.113), channel_id=1, source_target_pairs={{0,2},{1,3},{2,4},{3,5},{4,6},{5,7},{6,0},{7,1},{8,10},{9,11},{10,... | collective-permute-start | bytes 786440 | tf_op jit(solution)/shard_map/ppermute | solution.py:66
  80.3 33.3 %collective-permute-start.16 = (bf16[256,512]{1,0:T(8,128)(2,1)S(1)}, bf16[256,512]{1,0:T(8,128)(2,1)S(1)}, u32[]{:S(2)}, u32[]{:S(2)}) collective-permute-start(bf16[256,512]{1,0:T(8,128)(2,1)S(1)} %copy-done.113), channel_id=1, source_target_pairs={{0,4},{1,5},{2,6},{3,7},{4,0},{5,1},{6,2},{7,3},{8,12},{9,13},{10,... | collective-permute-start | bytes 786440 | tf_op jit(solution)/shard_map/ppermute | solution.py:66
  80.3 33.3 %collective-permute-start.17 = (bf16[256,512]{1,0:T(8,128)(2,1)S(1)}, bf16[256,512]{1,0:T(8,128)(2,1)S(1)}, u32[]{:S(2)}, u32[]{:S(2)}) collective-permute-start(bf16[256,512]{1,0:T(8,128)(2,1)S(1)} %copy-done.113), channel_id=1, source_target_pairs={{0,6},{1,7},{2,0},{3,1},{4,2},{5,3},{6,4},{7,5},{8,14},{9,15},{10,... | collective-permute-start | bytes 786440 | tf_op jit(solution)/shard_map/ppermute | solution.py:66
  131.8 28.6 %collective-permute-start.20 = (bf16[2,4,128,512]{3,2,1,0:T(8,128)(2,1)S(1)}, bf16[2,4,128,512]{3,2,1,0:T(8,128)(2,1)S(1)}, u32[]{:S(2)}, u32[]{:S(2)}) collective-permute-start(bf16[2,4,128,512]{3,2,1,0:T(8,128)(2,1)S(1)} %pad_maximum_fusion.5.refs_0_), channel_id=1, source_target_pairs={{0,16},{8,24},{16,0},{24,8},{1,17},{9,25},{17,1},{25,9},{2,18},{10... | collective-permute-start | bytes 3145736 | tf_op jit(solution)/shard_map/ppermute | solution.py:77
  131.9 28.5 %collective-permute-start.21 = (bf16[2,4,128,512]{3,2,1,0:T(8,128)(2,1)S(1)}, bf16[2,4,128,512]{3,2,1,0:T(8,128)(2,1)S(1)}, u32[]{:S(2)}, u32[]{:S(2)}) collective-permute-start(bf16[2,4,128,512]{3,2,1,0:T(8,128)(2,1)S(1)} %pad_maximum_fusion.6.refs_2_), channel_id=1, source_target_pairs={{0,8},{8,0},{16,24},{24,16},{1,9},{9,1},{17,25},{25,17},{2,10},{10... | collective-permute-start | bytes 3145736 | tf_op jit(solution)/shard_map/ppermute | solution.py:77
  133.0 27.4 %collective-permute-start.22 = (bf16[512,256]{1,0:T(8,128)(2,1)S(1)}, bf16[512,256]{1,0:T(8,128)(2,1)S(1)}, u32[]{:S(2)}, u32[]{:S(2)}) collective-permute-start(bf16[512,256]{1,0:T(8,128)(2,1)S(1)} %copy-done.112), channel_id=1, source_target_pairs={{0,2},{1,3},{2,4},{3,5},{4,6},{5,7},{6,0},{7,1},{8,10},{9,11},{10,... | collective-permute-start | bytes 786440 | tf_op jit(solution)/shard_map/ppermute | solution.py:66
  162.5 21.5 %collective-permute-start.25 = (bf16[1,4,256,256]{3,2,1,0:T(8,128)(2,1)}, bf16[1,4,256,256]{3,2,1,0:T(8,128)(2,1)}, u32[]{:S(2)}, u32[]{:S(2)}) collective-permute-start(bf16[1,4,256,256]{3,2,1,0:T(8,128)(2,1)} %maximum_bitcast_fusion.4), channel_id=1, source_target_pairs={{0,8},{8,0},{16,24},{24,16},{1,9},{9,1},{17,25},{25,17},{2,10},{10... | collective-permute-start | bytes 1572872 | tf_op jit(solution)/shard_map/ppermute | solution.py:77
  163.7 20.3 %collective-permute-start.26 = (bf16[1,4,256,256]{3,2,1,0:T(8,128)(2,1)}, bf16[1,4,256,256]{3,2,1,0:T(8,128)(2,1)}, u32[]{:S(2)}, u32[]{:S(2)}) collective-permute-start(bf16[1,4,256,256]{3,2,1,0:T(8,128)(2,1)} %maximum_bitcast_fusion.5), channel_id=1, source_target_pairs={{0,16},{8,24},{16,0},{24,8},{1,17},{9,25},{17,1},{25,9},{2,18},{10... | collective-permute-start | bytes 1572872 | tf_op jit(solution)/shard_map/ppermute | solution.py:77
  205.9 25.3 %collective-permute-start.29 = (bf16[2,4,256,256]{3,2,1,0:T(8,128)(2,1)S(1)}, bf16[2,4,256,256]{3,2,1,0:T(8,128)(2,1)S(1)}, u32[]{:S(2)}, u32[]{:S(2)}) collective-permute-start(bf16[2,4,256,256]{3,2,1,0:T(8,128)(2,1)S(1)} %copy-done.37), channel_id=1, source_target_pairs={{0,16},{8,24},{16,0},{24,8},{1,17},{9,25},{17,1},{25,9},{2,18},{10... | collective-permute-start | bytes 3145736 | tf_op jit(solution)/shard_map/ppermute | solution.py:77
  205.9 26.2 %collective-permute-start.30 = (bf16[2,4,256,256]{3,2,1,0:T(8,128)(2,1)S(1)}, bf16[2,4,256,256]{3,2,1,0:T(8,128)(2,1)S(1)}, u32[]{:S(2)}, u32[]{:S(2)}) collective-permute-start(bf16[2,4,256,256]{3,2,1,0:T(8,128)(2,1)S(1)} %copy-done.35), channel_id=1, source_target_pairs={{0,8},{8,0},{16,24},{24,16},{1,9},{9,1},{17,25},{25,17},{2,10},{10... | collective-permute-start | bytes 3145736 | tf_op jit(solution)/shard_map/ppermute | solution.py:77
  240.2 33.3 %collective-permute-start.31 = (bf16[2,4,256,256]{3,2,1,0:T(8,128)(2,1)}, bf16[2,4,256,256]{3,2,1,0:T(8,128)(2,1)}, u32[]{:S(2)}, u32[]{:S(2)}) collective-permute-start(bf16[2,4,256,256]{3,2,1,0:T(8,128)(2,1)} %get-tuple-element.415), channel_id=1, source_target_pairs={{0,8},{8,0},{16,24},{24,16},{1,9},{9,1},{17,25},{25,17},{2,10},{10... | collective-permute-start | bytes 3145736 | tf_op jit(solution)/shard_map/ppermute | solution.py:77
  240.7 32.9 %collective-permute-start.32 = (bf16[2,4,256,256]{3,2,1,0:T(8,128)(2,1)}, bf16[2,4,256,256]{3,2,1,0:T(8,128)(2,1)}, u32[]{:S(2)}, u32[]{:S(2)}) collective-permute-start(bf16[2,4,256,256]{3,2,1,0:T(8,128)(2,1)} %get-tuple-element.416), channel_id=1, source_target_pairs={{0,16},{8,24},{16,0},{24,8},{1,17},{9,25},{17,1},{25,9},{2,18},{10... | collective-permute-start | bytes 3145736 | tf_op jit(solution)/shard_map/ppermute | solution.py:77
  291.0 30.4 %collective-permute-start.39 = (bf16[1,4,256,256]{3,2,1,0:T(8,128)(2,1)}, bf16[1,4,256,256]{3,2,1,0:T(8,128)(2,1)}, u32[]{:S(2)}, u32[]{:S(2)}) collective-permute-start(bf16[1,4,256,256]{3,2,1,0:T(8,128)(2,1)} %slice.1073), channel_id=1, source_target_pairs={{0,16},{8,24},{16,0},{24,8},{1,17},{9,25},{17,1},{25,9},{2,18},{10... | collective-permute-start | bytes 1572872 | tf_op jit(solution)/shard_map/ppermute | solution.py:77
  291.8 29.6 %collective-permute-start.40 = (bf16[1,4,256,256]{3,2,1,0:T(8,128)(2,1)}, bf16[1,4,256,256]{3,2,1,0:T(8,128)(2,1)}, u32[]{:S(2)}, u32[]{:S(2)}) collective-permute-start(bf16[1,4,256,256]{3,2,1,0:T(8,128)(2,1)} %slice.1074), channel_id=1, source_target_pairs={{0,8},{8,0},{16,24},{24,16},{1,9},{9,1},{17,25},{25,17},{2,10},{10... | collective-permute-start | bytes 1572872 | tf_op jit(solution)/shard_map/ppermute | solution.py:77
  333.7 30.5 %collective-permute-start.41 = (bf16[2,4,128,512]{3,2,1,0:T(8,128)(2,1)}, bf16[2,4,128,512]{3,2,1,0:T(8,128)(2,1)}, u32[]{:S(2)}, u32[]{:S(2)}) collective-permute-start(bf16[2,4,128,512]{3,2,1,0:T(8,128)(2,1)} %copy-done.93), channel_id=1, source_target_pairs={{0,8},{8,0},{16,24},{24,16},{1,9},{9,1},{17,25},{25,17},{2,10},{10... | collective-permute-start | bytes 3145736 | tf_op jit(solution)/shard_map/ppermute | solution.py:77
  334.1 30.2 %collective-permute-start.42 = (bf16[2,4,128,512]{3,2,1,0:T(8,128)(2,1)}, bf16[2,4,128,512]{3,2,1,0:T(8,128)(2,1)}, u32[]{:S(2)}, u32[]{:S(2)}) collective-permute-start(bf16[2,4,128,512]{3,2,1,0:T(8,128)(2,1)} %copy-done.92), channel_id=1, source_target_pairs={{0,16},{8,24},{16,0},{24,8},{1,17},{9,25},{17,1},{25,9},{2,18},{10... | collective-permute-start | bytes 3145736 | tf_op jit(solution)/shard_map/ppermute | solution.py:77
  369.4 40.1 %collective-permute-start.43 = (bf16[1,4,128,512]{3,2,1,0:T(8,128)(2,1)}, bf16[1,4,128,512]{3,2,1,0:T(8,128)(2,1)}, u32[]{:S(2)}, u32[]{:S(2)}) collective-permute-start(bf16[1,4,128,512]{3,2,1,0:T(8,128)(2,1)} %slice.1079), channel_id=1, source_target_pairs={{0,16},{8,24},{16,0},{24,8},{1,17},{9,25},{17,1},{25,9},{2,18},{10... | collective-permute-start | bytes 1572872 | tf_op jit(solution)/shard_map/ppermute | solution.py:77
  369.4 40.2 %collective-permute-start.44 = (bf16[1,4,128,512]{3,2,1,0:T(8,128)(2,1)}, bf16[1,4,128,512]{3,2,1,0:T(8,128)(2,1)}, u32[]{:S(2)}, u32[]{:S(2)}) collective-permute-start(bf16[1,4,128,512]{3,2,1,0:T(8,128)(2,1)} %slice.1080), channel_id=1, source_target_pairs={{0,8},{8,0},{16,24},{24,16},{1,9},{9,1},{17,25},{25,17},{2,10},{10... | collective-permute-start | bytes 1572872 | tf_op jit(solution)/shard_map/ppermute | solution.py:77
  373.5 29.5 %collective-permute-start.45 = (bf16[512,256]{1,0:T(8,128)(2,1)}, bf16[512,256]{1,0:T(8,128)(2,1)}, u32[]{:S(2)}, u32[]{:S(2)}) collective-permute-start(bf16[512,256]{1,0:T(8,128)(2,1)} %get-tuple-element.465), channel_id=1, source_target_pairs={{0,2},{1,3},{2,4},{3,5},{4,6},{5,7},{6,0},{7,1},{8,10},{9,11},{10,... | collective-permute-start | bytes 786440 | tf_op jit(solution)/shard_map/ppermute | solution.py:66
  377.8 30.4 %collective-permute-start.46 = (bf16[512,256]{1,0:T(8,128)(2,1)}, bf16[512,256]{1,0:T(8,128)(2,1)}, u32[]{:S(2)}, u32[]{:S(2)}) collective-permute-start(bf16[512,256]{1,0:T(8,128)(2,1)} %get-tuple-element.466), channel_id=1, source_target_pairs={{0,4},{1,5},{2,6},{3,7},{4,0},{5,1},{6,2},{7,3},{8,12},{9,13},{10,... | collective-permute-start | bytes 786440 | tf_op jit(solution)/shard_map/ppermute | solution.py:66
  377.8 31.7 %collective-permute-start.47 = (bf16[512,256]{1,0:T(8,128)(2,1)}, bf16[512,256]{1,0:T(8,128)(2,1)}, u32[]{:S(2)}, u32[]{:S(2)}) collective-permute-start(bf16[512,256]{1,0:T(8,128)(2,1)} %get-tuple-element.467), channel_id=1, source_target_pairs={{0,6},{1,7},{2,0},{3,1},{4,2},{5,3},{6,4},{7,5},{8,14},{9,15},{10,... | collective-permute-start | bytes 786440 | tf_op jit(solution)/shard_map/ppermute | solution.py:66
  408.2 22.3 %collective-permute-start.49 = (bf16[1024,256]{1,0:T(8,128)(2,1)S(1)}, bf16[1024,256]{1,0:T(8,128)(2,1)S(1)}, u32[]{:S(2)}, u32[]{:S(2)}) collective-permute-start(bf16[1024,256]{1,0:T(8,128)(2,1)S(1)} %copy-done.108), channel_id=1, source_target_pairs={{2,0},{3,1},{4,2},{5,3},{6,4},{7,5},{10,8},{11,9},{12,10},{13,11},... | collective-permute-start | bytes 1572872 | tf_op jit(solution)/shard_map/ppermute | solution.py:72
  413.1 38.6 %collective-permute-start.53 = (bf16[2,4,128,256]{3,2,1,0:T(8,128)(2,1)S(1)}, bf16[2,4,128,256]{3,2,1,0:T(8,128)(2,1)}, u32[]{:S(2)}, u32[]{:S(2)}) collective-permute-start(bf16[2,4,128,256]{3,2,1,0:T(8,128)(2,1)S(1)} %get-tuple-element.492), channel_id=1, source_target_pairs={{0,8},{8,0},{16,24},{24,16},{1,9},{9,1},{17,25},{25,17},{2,10},{10... | collective-permute-start | bytes 1572872 | tf_op jit(solution)/shard_map/ppermute | solution.py:77
  413.1 38.6 %collective-permute-start.54 = (bf16[2,4,128,256]{3,2,1,0:T(8,128)(2,1)S(1)}, bf16[2,4,128,256]{3,2,1,0:T(8,128)(2,1)}, u32[]{:S(2)}, u32[]{:S(2)}) collective-permute-start(bf16[2,4,128,256]{3,2,1,0:T(8,128)(2,1)S(1)} %get-tuple-element.493), channel_id=1, source_target_pairs={{0,16},{8,24},{16,0},{24,8},{1,17},{9,25},{17,1},{25,9},{2,18},{10... | collective-permute-start | bytes 1572872 | tf_op jit(solution)/shard_map/ppermute | solution.py:77
  416.4 35.3 %collective-permute-start.50 = (bf16[256,512]{1,0:T(8,128)(2,1)}, bf16[256,512]{1,0:T(8,128)(2,1)}, u32[]{:S(2)}, u32[]{:S(2)}) collective-permute-start(bf16[256,512]{1,0:T(8,128)(2,1)} %get-tuple-element.489), channel_id=1, source_target_pairs={{0,2},{1,3},{2,4},{3,5},{4,6},{5,7},{6,0},{7,1},{8,10},{9,11},{10,... | collective-permute-start | bytes 786440 | tf_op jit(solution)/shard_map/ppermute | solution.py:66
  419.1 32.6 %collective-permute-start.51 = (bf16[256,512]{1,0:T(8,128)(2,1)}, bf16[256,512]{1,0:T(8,128)(2,1)}, u32[]{:S(2)}, u32[]{:S(2)}) collective-permute-start(bf16[256,512]{1,0:T(8,128)(2,1)} %get-tuple-element.490), channel_id=1, source_target_pairs={{0,4},{1,5},{2,6},{3,7},{4,0},{5,1},{6,2},{7,3},{8,12},{9,13},{10,... | collective-permute-start | bytes 786440 | tf_op jit(solution)/shard_map/ppermute | solution.py:66
  430.5 21.2 %collective-permute-start.52 = (bf16[256,512]{1,0:T(8,128)(2,1)}, bf16[256,512]{1,0:T(8,128)(2,1)}, u32[]{:S(2)}, u32[]{:S(2)}) collective-permute-start(bf16[256,512]{1,0:T(8,128)(2,1)} %get-tuple-element.491), channel_id=1, source_target_pairs={{0,6},{1,7},{2,0},{3,1},{4,2},{5,3},{6,4},{7,5},{8,14},{9,15},{10,... | collective-permute-start | bytes 786440 | tf_op jit(solution)/shard_map/ppermute | solution.py:66
  454.6 27.7 %collective-permute-start.56 = (bf16[1,128,1024]{2,1,0:T(8,128)(2,1)S(1)}, bf16[1,128,1024]{2,1,0:T(8,128)(2,1)S(1)}, u32[]{:S(2)}, u32[]{:S(2)}) collective-permute-start(bf16[1,128,1024]{2,1,0:T(8,128)(2,1)S(1)} %get-tuple-element.530), channel_id=1, source_target_pairs={{0,16},{8,24},{16,0},{24,8},{1,17},{9,25},{17,1},{25,9},{2,18},{10... | collective-permute-start | bytes 786440 | tf_op jit(solution)/shard_map/ppermute | solution.py:77
  454.7 28.6 %collective-permute-start.55 = (bf16[1,128,1024]{2,1,0:T(8,128)(2,1)S(1)}, bf16[1,128,1024]{2,1,0:T(8,128)(2,1)S(1)}, u32[]{:S(2)}, u32[]{:S(2)}) collective-permute-start(bf16[1,128,1024]{2,1,0:T(8,128)(2,1)S(1)} %get-tuple-element.529), channel_id=1, source_target_pairs={{0,8},{8,0},{16,24},{24,16},{1,9},{9,1},{17,25},{25,17},{2,10},{10... | collective-permute-start | bytes 786440 | tf_op jit(solution)/shard_map/ppermute | solution.py:77
  462.2 21.9 %collective-permute-start.57 = (bf16[1,4,128,256]{3,2,1,0:T(8,128)(2,1)S(1)}, bf16[1,4,128,256]{3,2,1,0:T(8,128)(2,1)S(1)}, u32[]{:S(2)}, u32[]{:S(2)}) collective-permute-start(bf16[1,4,128,256]{3,2,1,0:T(8,128)(2,1)S(1)} %slice.1085), channel_id=1, source_target_pairs={{0,16},{8,24},{16,0},{24,8},{1,17},{9,25},{17,1},{25,9},{2,18},{10... | collective-permute-start | bytes 786440 | tf_op jit(solution)/shard_map/ppermute | solution.py:77
  462.3 21.8 %collective-permute-start.58 = (bf16[1,4,128,256]{3,2,1,0:T(8,128)(2,1)S(1)}, bf16[1,4,128,256]{3,2,1,0:T(8,128)(2,1)S(1)}, u32[]{:S(2)}, u32[]{:S(2)}) collective-permute-start(bf16[1,4,128,256]{3,2,1,0:T(8,128)(2,1)S(1)} %slice.1086), channel_id=1, source_target_pairs={{0,8},{8,0},{16,24},{24,16},{1,9},{9,1},{17,25},{25,17},{2,10},{10... | collective-permute-start | bytes 786440 | tf_op jit(solution)/shard_map/ppermute | solution.py:77
  490.4 40.4 %collective-permute-start.59 = (bf16[2,4,128,256]{3,2,1,0:T(8,128)(2,1)S(1)}, bf16[2,4,128,256]{3,2,1,0:T(8,128)(2,1)S(1)}, u32[]{:S(2)}, u32[]{:S(2)}) collective-permute-start(bf16[2,4,128,256]{3,2,1,0:T(8,128)(2,1)S(1)} %get-tuple-element.557), channel_id=1, source_target_pairs={{0,8},{8,0},{16,24},{24,16},{1,9},{9,1},{17,25},{25,17},{2,10},{10... | collective-permute-start | bytes 1572872 | tf_op jit(solution)/shard_map/ppermute | solution.py:77
  491.3 39.6 %collective-permute-start.60 = (bf16[2,4,128,256]{3,2,1,0:T(8,128)(2,1)S(1)}, bf16[2,4,128,256]{3,2,1,0:T(8,128)(2,1)S(1)}, u32[]{:S(2)}, u32[]{:S(2)}) collective-permute-start(bf16[2,4,128,256]{3,2,1,0:T(8,128)(2,1)S(1)} %get-tuple-element.558), channel_id=1, source_target_pairs={{0,16},{8,24},{16,0},{24,8},{1,17},{9,25},{17,1},{25,9},{2,18},{10... | collective-permute-start | bytes 1572872 | tf_op jit(solution)/shard_map/ppermute | solution.py:77
  495.6 35.2 %collective-permute-start.61 = (bf16[256,256]{1,0:T(8,128)(2,1)S(1)}, bf16[256,256]{1,0:T(8,128)(2,1)S(1)}, u32[]{:S(2)}, u32[]{:S(2)}) collective-permute-start(bf16[256,256]{1,0:T(8,128)(2,1)S(1)} %get-tuple-element.560), channel_id=1, source_target_pairs={{0,2},{1,3},{2,4},{3,5},{4,6},{5,7},{6,0},{7,1},{8,10},{9,11},{10,... | collective-permute-start | bytes 393224 | tf_op jit(solution)/shard_map/ppermute | solution.py:66
  510.2 20.6 %collective-permute-start.62 = (bf16[256,256]{1,0:T(8,128)(2,1)S(1)}, bf16[256,256]{1,0:T(8,128)(2,1)S(1)}, u32[]{:S(2)}, u32[]{:S(2)}) collective-permute-start(bf16[256,256]{1,0:T(8,128)(2,1)S(1)} %get-tuple-element.561), channel_id=1, source_target_pairs={{0,4},{1,5},{2,6},{3,7},{4,0},{5,1},{6,2},{7,3},{8,12},{9,13},{10,... | collective-permute-start | bytes 393224 | tf_op jit(solution)/shard_map/ppermute | solution.py:66
  512.1 18.7 %collective-permute-start.63 = (bf16[256,256]{1,0:T(8,128)(2,1)S(1)}, bf16[256,256]{1,0:T(8,128)(2,1)S(1)}, u32[]{:S(2)}, u32[]{:S(2)}) collective-permute-start(bf16[256,256]{1,0:T(8,128)(2,1)S(1)} %get-tuple-element.562), channel_id=1, source_target_pairs={{0,6},{1,7},{2,0},{3,1},{4,2},{5,3},{6,4},{7,5},{8,14},{9,15},{10,... | collective-permute-start | bytes 393224 | tf_op jit(solution)/shard_map/ppermute | solution.py:66
  532.9 19.5 %collective-permute-start.64 = (f32[512,1024]{1,0:T(8,128)}, f32[512,1024]{1,0:T(8,128)}, u32[]{:S(2)}, u32[]{:S(2)}) collective-permute-start(f32[512,1024]{1,0:T(8,128)} %get-tuple-element.584), channel_id=1, source_target_pairs={{0,1},{1,0},{2,3},{3,2},{4,5},{5,4},{6,7},{7,6},{8,9},{9,8},{10,11... | collective-permute-start | bytes 6291464 | tf_op jit(solution)/shard_map/ppermute | solution.py:61
  533.0 19.3 %collective-permute-start.65 = (f32[512,1024]{1,0:T(8,128)}, f32[512,1024]{1,0:T(8,128)}, u32[]{:S(2)}, u32[]{:S(2)}) collective-permute-start(f32[512,1024]{1,0:T(8,128)} %get-tuple-element.587), channel_id=1, source_target_pairs={{0,1},{1,0},{2,3},{3,2},{4,5},{5,4},{6,7},{7,6},{8,9},{9,8},{10,11... | collective-permute-start | bytes 6291464 | tf_op jit(solution)/shard_map/ppermute | solution.py:61
  537.2 35.9 %collective-permute-start.74 = (bf16[2,128,1024]{2,1,0:T(8,128)(2,1)}, bf16[2,128,1024]{2,1,0:T(8,128)(2,1)}, u32[]{:S(2)}, u32[]{:S(2)}) collective-permute-start(bf16[2,128,1024]{2,1,0:T(8,128)(2,1)} %pad_maximum_fusion.13), channel_id=1, source_target_pairs={{0,16},{8,24},{16,0},{24,8},{1,17},{9,25},{17,1},{25,9},{2,18},{10... | collective-permute-start | bytes 1572872 | tf_op jit(solution)/shard_map/ppermute | solution.py:77
  537.2 29.7 %collective-permute-start.66 = (bf16[1,4,128,256]{3,2,1,0:T(8,128)(2,1)}, bf16[1,4,128,256]{3,2,1,0:T(8,128)(2,1)}, u32[]{:S(2)}, u32[]{:S(2)}) collective-permute-start(bf16[1,4,128,256]{3,2,1,0:T(8,128)(2,1)} %slice.1089), channel_id=1, source_target_pairs={{0,16},{8,24},{16,0},{24,8},{1,17},{9,25},{17,1},{25,9},{2,18},{10... | collective-permute-start | bytes 786440 | tf_op jit(solution)/shard_map/ppermute | solution.py:77
  586.6 28.4 %collective-permute-start.84 = (bf16[128,2048]{1,0:T(8,128)(2,1)S(1)}, bf16[128,2048]{1,0:T(8,128)(2,1)S(1)}, u32[]{:S(2)}, u32[]{:S(2)}) collective-permute-start(bf16[128,2048]{1,0:T(8,128)(2,1)S(1)} %constant_dynamic-slice_fusion), channel_id=1, source_target_pairs={{0,1},{1,0},{2,3},{3,2},{4,5},{5,4},{6,7},{7,6},{8,9},{9,8},{10,11... | collective-permute-start | bytes 1572872 | tf_op jit(solution)/shard_map/ppermute | solution.py:61
  (163 other events, 1547.4 us)

commit v4 on v3

--- a/solution.py
+++ b/solution.py
@@ -570,17 +570,26 @@
     )(mlp_grad, fc2_matrix, slope)
 
 
-def product_kernel(multiply, half_ref, first_ref, second_ref, w_ref, out1_ref, out2_ref):
-    out1_ref[...] = multiply(first_ref[...], w_ref[...])
-    out2_ref[...] = multiply(second_ref[...], w_ref[...])
-
-
-def product(a, weight, multiply, half, name):
+def product_kernel(half_ref, first_ref, second_ref, w_ref, out1_ref, out2_ref):
+    out1_ref[...] = dot(first_ref[...], w_ref[...])
+    out2_ref[...] = dot(second_ref[...], w_ref[...])
+
+
+def product_nt_kernel(half_ref, first_ref, second_ref, w_ref, out1_ref, out2_ref, held):
+    @pl.when(pl.program_id(0) == 0)
+    def _():
+        held[...] = w_ref[...].T
+
+    out1_ref[...] = dot(first_ref[...], held[...])
+    out2_ref[...] = dot(second_ref[...], held[...])
+
+
+def product(a, weight, flipped, half, name):
     rows, tile = a.shape[0] // 2, 128
     count = rows // tile
     out = pl.BlockSpec((tile, D), lambda i, h: (i, 0))
     return pl.pallas_call(
-        functools.partial(product_kernel, multiply),
+        product_nt_kernel if flipped else product_kernel,
         out_shape=[jax.ShapeDtypeStruct((rows, D), f32)] * 2,
         grid_spec=pltpu.PrefetchScalarGridSpec(
             num_scalar_prefetch=1,
@@ -591,6 +600,7 @@
                 pl.BlockSpec(weight.shape, lambda i, h: (0, 0)),
             ],
             out_specs=[out, out],
+            scratch_shapes=[pltpu.VMEM(weight.shape[::-1], bf16)] if flipped else [],
         ),
         compiler_params=pltpu.CompilerParams(vmem_limit_bytes=32 << 20),
         cost_estimate=SHORT,
@@ -825,7 +835,7 @@
     )(need, info, *sources, vecs)
 
 
-def attend_kernel(lo_ref, hi_ref, first_ref, last_ref, q_ref, k_ref, v_ref, qt_ref, kt_ref, o_ref, lse_ref, s_ref, m_ref):
+def attend_kernel(lo_ref, hi_ref, first_ref, last_ref, q_ref, k_ref, v_ref, qt_ref, kt_ref, o_ref, lse_ref, s_ref, m_ref, acc_ref):
     i = pl.program_id(0)
     left = lax.broadcasted_iota(jnp.int32, (1, LANES), 1) < HEAD_DIM
     lo, hi = lo_ref[i], hi_ref[i]
@@ -866,28 +876,20 @@
     lax.fori_loop(lo, hi, scores, 0)
     tops = [jnp.max(m_ref[h], axis=1, keepdims=True) for h in range(2)]
     m_ref[...] = jnp.zeros_like(m_ref)
-
-    def powers(j, carry):
-        for h in range(2):
-            e = jnp.exp(s_ref[h, j] - tops[h])
-            s_ref[h, j] = e
-            m_ref[h] += fold(e, jnp.add)
-        return carry
-
-    lax.fori_loop(lo, hi, powers, 0)
-    sums = [jnp.sum(m_ref[h], axis=1, keepdims=True) for h in range(2)]
-    shares = [1.0 / s for s in sums]
-    m_ref[...] = jnp.zeros_like(m_ref)
+    acc_ref[...] = jnp.zeros_like(acc_ref)
 
     def mix(j, carry):
         at = pl.multiple_of(j * BLOCK, BLOCK)
         v = v_ref[pl.ds(at, BLOCK), :]
         for h in range(2):
-            m_ref[h] += dot((s_ref[h, j] * shares[h]).astype(bf16), v)
+            e = jnp.exp(s_ref[h, j] - tops[h])
+            m_ref[h] += fold(e, jnp.add)
+            acc_ref[h] += dot(e.astype(bf16), v)
         return carry
 
     lax.fori_loop(lo, hi, mix, 0)
-    o_ref[...] = jnp.where(left, m_ref[0], m_ref[1]).astype(bf16)
+    sums = [jnp.sum(m_ref[h], axis=1, keepdims=True) for h in range(2)]
+    o_ref[...] = jnp.where(left, acc_ref[0] / sums[0], acc_ref[1] / sums[1]).astype(bf16)
     for h in range(2):
         lse = jnp.broadcast_to(tops[h] + jnp.log(sums[h]), (BLOCK, LANES))
         lse_ref[0, h : h + 1, :] = lse.T[0:1, :]
@@ -920,6 +922,7 @@
             scratch_shapes=[
                 pltpu.VMEM((2, window // BLOCK, BLOCK, BLOCK), f32),
                 pltpu.VMEM((2, BLOCK, LANES), f32),
+                pltpu.VMEM((2, BLOCK, LANES), f32),
             ],
         ),
         compiler_params=pltpu.CompilerParams(vmem_limit_bytes=32 << 20),
@@ -941,57 +944,57 @@
         zero = jnp.zeros_like(value)
         return jnp.where(first, value, zero), jnp.where(first, zero, value)
 
-    def query_block(i, carry):
+    def visit(i, j, qs, gs, of_key, of_query):
+        at_q, at_k = pl.multiple_of(i * BLOCK, BLOCK), pl.multiple_of(j * BLOCK, BLOCK)
+        k = k_ref[pl.ds(at_k, BLOCK), :]
+        v = v_ref[pl.ds(at_k, BLOCK), :]
+        same = spread_lanes(tc_ref[pl.ds(at_k, BLOCK), :], BLOCK) == tr_ref[:, pl.ds(at_q, BLOCK)]
+        ps, ds = [], []
+        for h in range(2):
+            s = dot_nt(k, qs[h])
+            dp = dot_nt(v, gs[h])
+            p = jnp.where(same, jnp.exp(s - lse_ref[0, h : h + 1, pl.ds(at_q, BLOCK)]), 0.0)
+            d = p * (dp - delta_ref[0, h : h + 1, pl.ds(at_q, BLOCK)])
+            ps.append(p.astype(bf16))
+            ds.append(d.astype(bf16))
+        if of_key:
+            at = pl.multiple_of((j - start) * BLOCK, BLOCK)
+            dv_acc[pl.ds(at, BLOCK), :] += dot(ps[0], gs[0]) + dot(ps[1], gs[1])
+            dk_acc[pl.ds(at, BLOCK), :] += dot(ds[0], qs[0]) + dot(ds[1], qs[1])
+        if of_query:
+            ks = split(k)
+            dq_acc[...] += dot_tn(ds[0], ks[0]) + dot_tn(ds[1], ks[1])
+
+    def query_block(own_q, i, carry):
         at_q = pl.multiple_of(i * BLOCK, BLOCK)
-        own_q = jnp.logical_and(i >= start, i < stop)
-        lo = jnp.where(own_q, lo_ref[i], jnp.maximum(lo_ref[i], start))
-        hi = jnp.where(own_q, hi_ref[i], jnp.minimum(hi_ref[i], stop))
-
-        @pl.when(own_q)
-        def _():
+        qs = split(q_ref[pl.ds(at_q, BLOCK), :])
+        gs = split(g_ref[pl.ds(at_q, BLOCK), :])
+        lo, hi = lo_ref[i], hi_ref[i]
+
+        def keys(first_key, last_key, of_key):
+            def body(j, carry):
+                visit(i, j, qs, gs, of_key, own_q)
+                return carry
+
+            lax.fori_loop(first_key, last_key, body, 0)
+
+        if own_q:
             dq_acc[...] = jnp.zeros_like(dq_acc)
-
-        def key_block(j, carry):
-            at_k = pl.multiple_of(j * BLOCK, BLOCK)
-            k = k_ref[pl.ds(at_k, BLOCK), :]
-            v = v_ref[pl.ds(at_k, BLOCK), :]
-            qs = split(q_ref[pl.ds(at_q, BLOCK), :])
-            gs = split(g_ref[pl.ds(at_q, BLOCK), :])
-            same = spread_lanes(tc_ref[pl.ds(at_k, BLOCK), :], BLOCK) == tr_ref[:, pl.ds(at_q, BLOCK)]
-            ps, ds = [], []
-            for h in range(2):
-                s = dot_nt(k, qs[h])
-                p = jnp.where(same, jnp.exp(s - lse_ref[0, h : h + 1, pl.ds(at_q, BLOCK)]), 0.0)
-                dp = dot_nt(v, gs[h])
-                d = p * (dp - delta_ref[0, h : h + 1, pl.ds(at_q, BLOCK)])
-                ps.append(p.astype(bf16))
-                ds.append(d.astype(bf16))
-
-            @pl.when(jnp.logical_and(j >= start, j < stop))
-            def _():
-                at = pl.multiple_of((j - start) * BLOCK, BLOCK)
-                dv_acc[pl.ds(at, BLOCK), :] += dot(ps[0], gs[0]) + dot(ps[1], gs[1])
-                dk_acc[pl.ds(at, BLOCK), :] += dot(ds[0], qs[0]) + dot(ds[1], qs[1])
-
-            @pl.when(own_q)
-            def _():
-                ks = split(k)
-                dq_acc[...] += dot_tn(ds[0], ks[0]) + dot_tn(ds[1], ks[1])
-
-            return carry
-
-        lax.fori_loop(lo, hi, key_block, 0)
-
-        @pl.when(own_q)
-        def _():
+            keys(lo, jnp.minimum(hi, start), False)
+            keys(jnp.maximum(lo, stop), hi, False)
+        keys(jnp.maximum(lo, start), jnp.minimum(hi, stop), True)
+        if own_q:
             at = pl.multiple_of((i - start) * BLOCK, BLOCK)
             dq = dq_acc[...] * HEAD_DIM ** (-0.5)
             dq_ref[pl.ds(at, BLOCK), :] = dq.astype(bf16)
             sum_ref[0, 0:1, :] += jnp.sum(dq, axis=0, keepdims=True)
-
         return carry
 
-    lax.fori_loop(0, q_ref.shape[0] // BLOCK, query_block, 0)
+    before = jnp.where(lo_ref[start] < start, lo_ref[start], start)
+    after = jnp.maximum(hi_ref[stop - 1], stop)
+    lax.fori_loop(before, start, functools.partial(query_block, False), 0)
+    lax.fori_loop(start, stop, functools.partial(query_block, True), 0)
+    lax.fori_loop(stop, after, functools.partial(query_block, False), 0)
     dk_ref[...] = dk_acc[...].astype(bf16)
     dv_ref[...] = dv_acc[...].astype(bf16)
     sum_ref[0, 1:2, :] = jnp.sum(dv_acc[...], axis=0, keepdims=True)
@@ -1226,7 +1229,7 @@
     pre_grad, fc1_bias_part = pre_grads(mlp_grad, fc2_matrix, slope)
     reduce2 = Reduce(grad_blocks(mlp_input, pre_grad, rank, both, "fc1_grad"), here, both)
     pre_grad, _ = tie(pre_grad, [give for _, _, give in reduce2.held])
-    own, given = product(pre_grad, fc1_matrix, dot_nt, 0, "mlp_in_grad")
+    own, given = product(pre_grad, fc1_matrix, True, 0, "mlp_in_grad")
     own, given = reduce3.arrive(own, given)
     for _ in bits[2:]:
         own, given = reduce3.arrive(*reduce3.send(own, given))
@@ -1315,15 +1318,14 @@
 
     factor = 1.0 / math.sqrt(count * devices * ranks)
     in_own, in_given = product(
-        jnp.concatenate(every, axis=1), qkv_matrix, dot_nt, core, "attn_in_grad"
+        jnp.concatenate(every, axis=1), qkv_matrix, True, core, "attn_in_grad"
     )
-    out_own, out_given = product(activated, fc2_matrix, dot, 0, "mlp_out")
+    out_own, out_given = product(activated, fc2_matrix, False, 0, "mlp_out")
     tail = (in_own, in_given, out_own, out_given)
     tail = settle(tail, (reduce1b, "received"), (reduce1a, "pieces"))
     for _ in bits[1:]:
         tail = reduce1b.arrive(tail)
         tail = reduce1b.send(tail)
-        tail = mlp_spread.send(tail)
     in_own, in_given, out_own, out_given = tail
     input_rows, output_rows, end_sums = finish(
         in_own, swap_cores(in_given), tok, resid_grad, out_own, swap_cores(out_given), resid, cot, vec_rows
@@ -1339,6 +1341,8 @@
     partial = pack_grads(vectors, list(zip(sizes, of_core)), core, depth)
     partial = reduce1b.arrive(partial)
     partial = reduce1b.send_z(partial)
+    for _ in bits[1:]:
+        partial = mlp_spread.send(partial)
 
     vec_total = pick(partial, here, 0)
     for k in range(1, depth):
@@ -1356,9 +1360,8 @@
     mlp_cols = fc1_part.shape[1]
     fc1_full = mlp_spread.blocks(rank, 0, mlp_cols)
     fc2_width = fc2_part.shape[1]
-    grad_fc2 = jnp.concatenate(
-        [mlp_spread.blocks(rank, mlp_cols + n * fc2_width, fc2_width) for n in range(split)]
-    ).astype(f32) * factor
+    fc2_full = tie(*[mlp_spread.blocks(rank, mlp_cols + n * fc2_width, fc2_width) for n in range(split)])
+    grad_fc2 = jnp.concatenate(fc2_full).astype(f32) * factor
     vec_width = D // ranks
     first_a = first_spread.blocks(rank, 0, vec_width)
     first_b = first_spread.blocks(rank, vec_width, vec_width)

time: 630 us -> 579 us (0.919)
  Pallas kernels: 227 us -> 194 us
  other arithmetic: 69.6 us -> 57.1 us
  waiting for transfers between devices: 88.8 us -> 82 us
    pallas_call x4, Pallas kernels: 76.7 us -> 57.7 us  [attend_back(): pl.pallas_call(functools.partial(attend_back_kernel, start, stop), out_sh...]
    ppermute x38, waiting for transfers between devices: 37.1 us -> 26.6 us  [across_rep(): return lax.ppermute(value, 'rep', [(i, i ^ 1 << bit) for i in range(size)])]
    pallas_call x3, Pallas kernels: 26.8 us -> 18.5 us  [product(): pl.pallas_call(product_nt_kernel if flipped else product_kernel, out_shap...]
    mul x1, other arithmetic: 9.36 us -> 1.59 us  [on_device(): grad_fc2 = jnp.concatenate(fc2_full).astype(f32) * factor]
    pallas_call x4, Pallas kernels: 52.3 us -> 45.5 us  [attend(): pl.pallas_call(attend_kernel, out_shape=[jax.ShapeDtypeStruct((own_rows,...]
    unnamed x301 -> x307, local copies, waits for them, and re-layouts: 32.9 us -> 34 us
  transfers between devices with their start and end apart: 85 -> 85, of which waited for: 18 -> 23; matrix products, arithmetic and copies ran while one was open for 13% -> 12% of each run, Pallas kernels for 34% -> 31%
where the time goes in v4:
time: 579 us; the launch traced here: 568 us
  Pallas kernels  194 us (34%)
  starting transfers between devices  161 us (28%)
  waiting for transfers between devices  82 us (14%)
  other arithmetic  57.1 us (10%)
  local copies, waits for them, and re-layouts  50.9 us (9%)
  matrix products  19.7 us (3%)
    ppermute x24, starting transfers between devices, along_z(): lax.ppermute(value, 'fsdp', [(i, (i + 2 * by) % size) for i in range(size)])  69.9 us
    pallas_call x4, Pallas kernels, attend_back(): pl.pallas_call(functools.partial(attend_back_kernel, start, stop), out_sh...  57.7 us
    ppermute x38, starting transfers between devices, across_rep(): return lax.ppermute(value, 'rep', [(i, i ^ 1 << bit) for i in range(size)])  51 us
    pallas_call x4, Pallas kernels, attend(): pl.pallas_call(attend_kernel, out_shape=[jax.ShapeDtypeStruct((own_rows,...  45.5 us
    ppermute x8, starting transfers between devices, from_chip(): return lax.ppermute(value, 'fsdp', pairs)  37.6 us
    unnamed x307, local copies, waits for them, and re-layouts  34 us
    ppermute x8, waiting for transfers between devices, from_chip(): return lax.ppermute(value, 'fsdp', pairs)  29.1 us
    ppermute x38, waiting for transfers between devices, across_rep(): return lax.ppermute(value, 'rep', [(i, i ^ 1 << bit) for i in range(size)])  26.6 us
  transfers between devices with their start and end apart: 85, of which 23 were waited for; matrix products, arithmetic and copies ran while one was open for 12% of the time, Pallas kernels for 31%

profile of v4, /device:TPU:0, one launch (start us, length us, event | category | flops | bytes accessed | tf_op | source)
XLA Modules:
  0.0 568.1 jit_solution(2526876605021962714)
XLA Ops:
  10.7 3.1 collective-permute-start.3
  17.8 5.8 %collective-permute-done.3.refs_1_ = bf16[272,512]{1,0:T(8,128)(2,1)} collective-permute-done((bf16[272,512]{1,0:T(8,128)(2,1)S(1)}, bf16[272,512]{1,0:T(8,128)(2,1)}, u32[]{:S(2)}, u32[]{:S(2)}) %collective-permute-start.3) | collective-permute-done | bytes 278560 | tf_op jit(solution)/shard_map/ppermute | solution.py:66
  24.9 13.9 %collective-permute-start.6 = (bf16[512,1024]{1,0:T(8,128)(2,1)S(1)}, bf16[512,1024]{1,0:T(8,128)(2,1)}, u32[]{:S(2)}, u32[]{:S(2)}) collective-permute-start(bf16[512,1024]{1,0:T(8,128)(2,1)S(1)} %bitcast.293), channel_id=1, source_target_pairs={{0,2},{1,3},{2,4},{3,5},{4,6},{5,7},{8,10},{9,11},{10,12},{11,13},... | collective-permute-start | bytes 3145736 | tf_op jit(solution)/shard_map/ppermute | solution.py:72
  49.7 7.4 %collective-permute-done.9.refs_4_ = bf16[512,1024]{1,0:T(8,128)(2,1)S(1)} collective-permute-done((bf16[512,1024]{1,0:T(8,128)(2,1)S(1)}, bf16[512,1024]{1,0:T(8,128)(2,1)S(1)}, u32[]{:S(2)}, u32[]{:S(2)}) %collective-permute-start.9) | collective-permute-done | bytes 1048608 | tf_op jit(solution)/shard_map/ppermute | solution.py:72
  66.1 7.0 %norm_window.1.n_ref = bf16[3072,1024]{1,0:T(8,128)(2,1)S(1)} custom-call(s32[12]{0:T(128)S(1)} %and_convert_fusion.need_ref, s32[2]{0:T(128)S(1)} %pad_add_fusion.1.info_ref, bf16[512,1024]{1,0:T(8,128)(2,1)} %collective-permute-done.6.refs_0_, bf16[512,1024]{1,0:T(8,128)(2,1)S(1)} %collective-permute-done.7.refs_1_, bf16[512,1024]{1,0:T(8,128)(2,1)S(1)} %bitcast.294, ...), custom_call_target="tpu_custom_call" | custom-call | flops 1 | bytes 1 | tf_op jit(solution)/shard_map/norm_window/pallas_call | solution.py:823
  73.2 6.7 %collective-permute-start.15 = (bf16[256,512]{1,0:T(8,128)(2,1)S(1)}, bf16[256,512]{1,0:T(8,128)(2,1)S(1)}, u32[]{:S(2)}, u32[]{:S(2)}) collective-permute-start(bf16[256,512]{1,0:T(8,128)(2,1)S(1)} %copy-done.113), channel_id=1, source_target_pairs={{0,2},{1,3},{2,4},{3,5},{4,6},{5,7},{6,0},{7,1},{8,10},{9,11},{10,... | collective-permute-start | bytes 786440 | tf_op jit(solution)/shard_map/ppermute | solution.py:66
  89.5 8.0 %project.1 = (bf16[3072,512]{1,0:T(8,128)(2,1)S(1)}, bf16[3072,512]{1,0:T(8,128)(2,1)S(1)}, bf16[3072,512]{1,0:T(8,128)(2,1)S(1)}) custom-call(s32[12]{0:T(128)S(1)} %and_convert_fusion.need_ref, bf16[3072,1024]{1,0:T(8,128)(2,1)S(1)} %norm_window.1.n_ref, bf16[1024,1536]{1,0:T(8,128)(2,1)S(1)} %get-tuple-element.341.w_ref, f32[1,1536]{1,0:T(1,128)S(1)} %fusion.71.b_ref), custom_call_target="tpu_custom_call" | custom-call | flops 1 | bytes 1 | tf_op jit(solution)/shard_map/project/pallas_call | solution.py:775
  100.5 11.4 %attend.4 = (bf16[1024,128]{1,0:T(8,128)(2,1)S(1)}, f32[1,2,1024]{2,1,0:T(2,128)S(1)}) custom-call(s32[4]{0:T(128)S(1)} %slice.878.lo_ref, s32[4]{0:T(128)S(1)} %slice.906.hi_ref, s32[12]{0:T(128)S(1)} %convert_element_type.262.first_ref, s32[12]{0:T(128)S(1)} %convert_element_type.263.last_ref, bf16[3072,512]{1,0:T(8,128)(2,1)S(1)} %get-tuple-element.344.q_ref, ...), custom_call_target="tpu_custom_call" | custom-call | flops 1 | bytes 1 | tf_op jit(solution)/shard_map/attend/pallas_call | solution.py:902
  113.2 11.4 %attend.5 = (bf16[1024,128]{1,0:T(8,128)(2,1)S(1)}, f32[1,2,1024]{2,1,0:T(2,128)S(1)}) custom-call(s32[4]{0:T(128)S(1)} %slice.878.lo_ref, s32[4]{0:T(128)S(1)} %slice.906.hi_ref, s32[12]{0:T(128)S(1)} %convert_element_type.262.first_ref, s32[12]{0:T(128)S(1)} %convert_element_type.263.last_ref, bf16[3072,512]{1,0:T(8,128)(2,1)S(1)} %get-tuple-element.344.q_ref, ...), custom_call_target="tpu_custom_call" | custom-call | flops 1 | bytes 1 | tf_op jit(solution)/shard_map/attend/pallas_call | solution.py:902
  128.6 8.1 %collective-permute-start.22 = (bf16[512,256]{1,0:T(8,128)(2,1)S(1)}, bf16[512,256]{1,0:T(8,128)(2,1)S(1)}, u32[]{:S(2)}, u32[]{:S(2)}) collective-permute-start(bf16[512,256]{1,0:T(8,128)(2,1)S(1)} %copy-done.112), channel_id=1, source_target_pairs={{0,2},{1,3},{2,4},{3,5},{4,6},{5,7},{6,0},{7,1},{8,10},{9,11},{10,... | collective-permute-start | bytes 786440 | tf_op jit(solution)/shard_map/ppermute | solution.py:66
  136.7 4.8 collective-permute-start.23
  141.5 3.1 collective-permute-start.24
  144.6 11.4 %attend.6 = (bf16[1024,128]{1,0:T(8,128)(2,1)S(1)}, f32[1,2,1024]{2,1,0:T(2,128)S(1)}) custom-call(s32[4]{0:T(128)S(1)} %slice.878.lo_ref, s32[4]{0:T(128)S(1)} %slice.906.hi_ref, s32[12]{0:T(128)S(1)} %convert_element_type.262.first_ref, s32[12]{0:T(128)S(1)} %convert_element_type.263.last_ref, bf16[3072,512]{1,0:T(8,128)(2,1)S(1)} %get-tuple-element.344.q_ref, ...), custom_call_target="tpu_custom_call" | custom-call | flops 1 | bytes 1 | tf_op jit(solution)/shard_map/attend/pallas_call | solution.py:902
  163.9 11.4 %attend.7 = (bf16[1024,128]{1,0:T(8,128)(2,1)S(1)}, f32[1,2,1024]{2,1,0:T(2,128)S(1)}) custom-call(s32[4]{0:T(128)S(1)} %slice.878.lo_ref, s32[4]{0:T(128)S(1)} %slice.906.hi_ref, s32[12]{0:T(128)S(1)} %convert_element_type.262.first_ref, s32[12]{0:T(128)S(1)} %convert_element_type.263.last_ref, bf16[3072,512]{1,0:T(8,128)(2,1)S(1)} %get-tuple-element.344.q_ref, ...), custom_call_target="tpu_custom_call" | custom-call | flops 1 | bytes 1 | tf_op jit(solution)/shard_map/attend/pallas_call | solution.py:902
  183.0 4.0 collective-permute-done.27
  187.0 4.6 fusion.76
  200.5 10.5 %fusion.3 = (f32[1024,2048]{1,0:T(8,128)}, bf16[1024,2048]{1,0:T(8,128)(2,1)S(1)}) fusion(f32[2048]{0:T(1024)S(1)} %bitcast.321, bf16[1024,2048]{1,0:T(8,128)(2,1)S(1)} %gather2.1.w_ref, bf16[512,1024]{1,0:T(8,128)(2,1)S(1)} %collective-permute-done.28, bf16[512,1024]{1,0:T(8,128)(2,1)S(1)} %add_convert_fusion.4), kind=kOutput, calls=%fused_computation.4 | convolution fusion | flops 4322230272 | bytes 18882560 | tf_op jit(solution)/shard_map/dot_general | solution.py:48
  211.1 11.6 %collective-permute-done.29.refs_1_ = bf16[2,4,256,256]{3,2,1,0:T(8,128)(2,1)S(1)} collective-permute-done((bf16[2,4,256,256]{3,2,1,0:T(8,128)(2,1)S(1)}, bf16[2,4,256,256]{3,2,1,0:T(8,128)(2,1)S(1)}, u32[]{:S(2)}, u32[]{:S(2)}) %collective-permute-start.29) | collective-permute-done | bytes 1048608 | tf_op jit(solution)/shard_map/ppermute | solution.py:77
  224.7 7.0 %fc2_grad.1 = (bf16[2,4,256,256]{3,2,1,0:T(8,128)(2,1)S(1)}, bf16[2,4,256,256]{3,2,1,0:T(8,128)(2,1)}, bf16[2,4,256,256]{3,2,1,0:T(8,128)(2,1)S(1)}, bf16[2,4,256,256]{3,2,1,0:T(8,128)(2,1)}) custom-call(s32[1]{0:T(128)} %bitcast.3.index_ref, bf16[1024,2048]{1,0:T(8,128)(2,1)S(1)} %get-tuple-element.553.a_ref.first_ref.second_ref, ...), custom_call_target="tpu_custom_call" | custom-call | flops 1 | bytes 1 | tf_op jit(solution)/shard_map/fc2_grad/pallas_call | solution.py:528
  236.7 10.3 %pre_grad.1 = (bf16[1024,2048]{1,0:T(8,128)(2,1)S(1)}, f32[1,2048]{1,0:T(1,128)S(1)}) custom-call(bf16[1024,1024]{1,0:T(8,128)(2,1)S(1)} %multiply_convert_fusion.1.b_ref.g_ref, bf16[2048,1024]{1,0:T(8,128)(2,1)S(1)} %gather3.1.w_ref, f32[1024,2048]{1,0:T(8,128)} %get-tuple-element.631.slope_ref), custom_call_target="tpu_custom_call" | custom-call | flops 1 | bytes 1 | tf_op jit(solution)/shard_map/pre_grad/pallas_call | solution.py:557
  247.6 6.5 %fc1_grad.1 = (bf16[2,4,128,512]{3,2,1,0:T(8,128)(2,1)S(1)}, bf16[2,4,128,512]{3,2,1,0:T(8,128)(2,1)S(1)}, bf16[2,4,128,512]{3,2,1,0:T(8,128)(2,1)S(1)}, bf16[2,4,128,512]{3,2,1,0:T(8,128)(2,1)S(1)}) custom-call(s32[1]{0:T(128)} %bitcast.3.index_ref, bf16[1024,1024]{1,0:T(8,128)(2,1)S(1)} %pad_maximum_fusion.a_ref, ...), custom_call_target="tpu_custom_call" | custom-call | flops 1 | bytes 1 | tf_op jit(solution)/shard_map/fc1_grad/pallas_call | solution.py:528
  255.2 6.4 %mlp_in_grad.1 = (f32[512,1024]{1,0:T(8,128)S(1)}, f32[512,1024]{1,0:T(8,128)S(1)}) custom-call(s32[1]{0:T(128)} %constant.162.clone.1.half_ref, bf16[1024,2048]{1,0:T(8,128)(2,1)S(1)} %get-tuple-element.411.b_ref.first_ref.second_ref, bf16[1024,2048]{1,0:T(8,128)(2,1)S(1)} %get-tuple-element.411.b_ref.first_ref.second_ref, bf16[1024,2048]{1,0:T(8,128)(2,1)S(1)} %copy-done.19), custom_call_target="tpu_custom_call" | custom-call | flops 1 | bytes 1 | tf_op jit(solution)/shard_map/mlp_in_grad/pallas_call | solution.py:591
  266.7 4.2 collective-permute-done.33.sent_ref
  270.9 6.6 %norm_grad.1 = (f32[512,1024]{1,0:T(8,128)S(1)}, bf16[512,1024]{1,0:T(8,128)(2,1)}, f32[8,1024]{1,0:T(8,128)S(1)}) custom-call(f32[512,1024]{1,0:T(8,128)S(1)} %get-tuple-element.422.own_ref, f32[512,1024]{1,0:T(8,128)S(1)} %collective-permute-done.33.sent_ref, f32[512,1024]{1,0:T(8,128)S(1)} %get-tuple-element.630.resid_ref, ...), custom_call_target="tpu_custom_call" | custom-call | flops 1 | bytes 1 | tf_op jit(solution)/shard_map/norm_grad/pallas_call | solution.py:667
  281.8 3.3 maximum_select_fusion.g_ref
  288.4 10.1 %collective-permute-start.37 = (f32[16,1024]{1,0:T(8,128)S(1)}, f32[16,1024]{1,0:T(8,128)S(1)}, u32[]{:S(2)}, u32[]{:S(2)}) collective-permute-start(f32[16,1024]{1,0:T(8,128)S(1)} %pad_maximum_fusion.21), channel_id=1, source_target_pairs={{0,2},{1,3},{2,4},{3,5},{4,6},{5,7},{8,10},{9,11},{10,12},{11,13},... | collective-permute-start | bytes 196616 | tf_op jit(solution)/shard_map/ppermute | solution.py:72
  300.9 5.5 collective-permute-start.35
  309.4 7.7 %collective-permute-done.35 = bf16[1024,256]{1,0:T(8,128)(2,1)} collective-permute-done((bf16[1024,256]{1,0:T(8,128)(2,1)}, bf16[1024,256]{1,0:T(8,128)(2,1)}, u32[]{:S(2)}, u32[]{:S(2)}) %collective-permute-start.35) | collective-permute-done | bytes 524320 | tf_op jit(solution)/shard_map/ppermute | solution.py:72
  317.1 4.9 collective-permute-done.36
  330.0 14.5 %attend_back.4 = (bf16[1024,128]{1,0:T(8,128)(2,1)S(1)}, bf16[1024,128]{1,0:T(8,128)(2,1)S(1)}, bf16[1024,128]{1,0:T(8,128)(2,1)S(1)}, f32[1,8,128]{2,1,0:T(8,128)S(1)}) custom-call(s32[12]{0:T(128)S(1)} %get-tuple-element.520.lo_ref, s32[12]{0:T(128)S(1)} %get-tuple-element.833.hi_ref, bf16[3072,512]{1,0:T(8,128)(2,1)S(1)} %get-tuple-element.344.q_ref, ...), custom_call_target="tpu_custom_call" | custom-call | flops 1 | bytes 1 | tf_op jit(solution)/shard_map/attend_back/pallas_call | solution.py:1012
  353.2 3.5 collective-permute-start.44
  356.7 4.2 collective-permute-start.45
  366.1 14.3 %attend_back.5 = (bf16[1024,128]{1,0:T(8,128)(2,1)S(1)}, bf16[1024,128]{1,0:T(8,128)(2,1)S(1)}, bf16[1024,128]{1,0:T(8,128)(2,1)S(1)}, f32[1,8,128]{2,1,0:T(8,128)S(1)}) custom-call(s32[12]{0:T(128)S(1)} %get-tuple-element.520.lo_ref, s32[12]{0:T(128)S(1)} %get-tuple-element.833.hi_ref, bf16[3072,512]{1,0:T(8,128)(2,1)S(1)} %get-tuple-element.344.q_ref, ...), custom_call_target="tpu_custom_call" | custom-call | flops 1 | bytes 1 | tf_op jit(solution)/shard_map/attend_back/pallas_call | solution.py:1012
  390.8 3.9 collective-permute-start.54
  397.5 9.1 %collective-permute-done.49 = bf16[1024,256]{1,0:T(8,128)(2,1)S(1)} collective-permute-done((bf16[1024,256]{1,0:T(8,128)(2,1)S(1)}, bf16[1024,256]{1,0:T(8,128)(2,1)S(1)}, u32[]{:S(2)}, u32[]{:S(2)}) %collective-permute-start.49) | collective-permute-done | bytes 524320 | tf_op jit(solution)/shard_map/ppermute | solution.py:72
  408.2 14.5 %attend_back.6 = (bf16[1024,128]{1,0:T(8,128)(2,1)S(1)}, bf16[1024,128]{1,0:T(8,128)(2,1)S(1)}, bf16[1024,128]{1,0:T(8,128)(2,1)S(1)}, f32[1,8,128]{2,1,0:T(8,128)S(1)}) custom-call(s32[12]{0:T(128)S(1)} %get-tuple-element.520.lo_ref, s32[12]{0:T(128)S(1)} %get-tuple-element.833.hi_ref, bf16[3072,512]{1,0:T(8,128)(2,1)S(1)} %get-tuple-element.344.q_ref, ...), custom_call_target="tpu_custom_call" | custom-call | flops 1 | bytes 1 | tf_op jit(solution)/shard_map/attend_back/pallas_call | solution.py:1012
  425.7 4.0 collective-permute-start.56
  429.7 3.7 collective-permute-start.55
  436.8 14.3 %attend_back.7 = (bf16[1024,128]{1,0:T(8,128)(2,1)S(1)}, bf16[1024,128]{1,0:T(8,128)(2,1)S(1)}, bf16[1024,128]{1,0:T(8,128)(2,1)S(1)}, f32[1,8,128]{2,1,0:T(8,128)S(1)}) custom-call(s32[12]{0:T(128)S(1)} %get-tuple-element.520.lo_ref, s32[12]{0:T(128)S(1)} %get-tuple-element.833.hi_ref, bf16[3072,512]{1,0:T(8,128)(2,1)S(1)} %get-tuple-element.344.q_ref, ...), custom_call_target="tpu_custom_call" | custom-call | flops 1 | bytes 1 | tf_op jit(solution)/shard_map/attend_back/pallas_call | solution.py:1012
  458.9 4.7 collective-permute-start.60
  463.6 11.5 %collective-permute-start.61 = (bf16[256,256]{1,0:T(8,128)(2,1)S(1)}, bf16[256,256]{1,0:T(8,128)(2,1)S(1)}, u32[]{:S(2)}, u32[]{:S(2)}) collective-permute-start(bf16[256,256]{1,0:T(8,128)(2,1)S(1)} %get-tuple-element.559), channel_id=1, source_target_pairs={{0,2},{1,3},{2,4},{3,5},{4,6},{5,7},{6,0},{7,1},{8,10},{9,11},{10,... | collective-permute-start | bytes 393224 | tf_op jit(solution)/shard_map/ppermute | solution.py:66
  475.1 3.3 collective-permute-start.62
  481.8 6.0 %mlp_out.1 = (f32[512,1024]{1,0:T(8,128)S(1)}, f32[512,1024]{1,0:T(8,128)}) custom-call(s32[1]{0:T(128)} %constant.162.clone.1.half_ref, bf16[1024,2048]{1,0:T(8,128)(2,1)S(1)} %copy-done.17, bf16[1024,2048]{1,0:T(8,128)(2,1)S(1)} %copy-done.17, bf16[2048,1024]{1,0:T(8,128)(2,1)S(1)} %copy-done.15), custom_call_target="tpu_custom_call" | custom-call | flops 1 | bytes 1 | tf_op jit(solution)/shard_map/mlp_out/pallas_call | solution.py:591
  487.8 6.1 %attn_in_grad.1 = (f32[512,1024]{1,0:T(8,128)S(1)}, f32[512,1024]{1,0:T(8,128)}) custom-call(s32[1]{0:T(128)} %bitcast.half_ref.index_ref, bf16[1024,1536]{1,0:T(8,128)(2,1)S(1)} %constant_dynamic-update-slice_fusion.first_ref.second_ref, bf16[1024,1536]{1,0:T(8,128)(2,1)S(1)} %constant_dynamic-update-slice_fusion.first_ref.second_ref, ...), custom_call_target="tpu_custom_call" | custom-call | flops 1 | bytes 1 | tf_op jit(solution)/shard_map/attn_in_grad/pallas_call | solution.py:591
  508.7 7.7 %finish.1 = (f32[512,1024]{1,0:T(8,128)}, bf16[512,1024]{1,0:T(8,128)(2,1)}, f32[8,1024]{1,0:T(8,128)S(1)}) custom-call(f32[512,1024]{1,0:T(8,128)S(1)} %copy-done.47, f32[512,1024]{1,0:T(8,128)} %collective-permute-done.64.sent1_ref, bf16[512,1024]{1,0:T(8,128)(2,1)S(1)} %bitcast.295, f32[512,1024]{1,0:T(8,128)S(1)} %copy-done.43, ...), custom_call_target="tpu_custom_call" | custom-call | flops 1 | bytes 1 | tf_op jit(solution)/shard_map/finish/pallas_call | solution.py:633
  521.7 3.3 collective-permute-start.70
  532.2 3.2 collective-permute-done.71
  535.4 4.0 collective-permute-done.72
  (634 shorter events, 211.8 us)
Async XLA Ops:
  13.8 52.3 %collective-permute-start.8 = (bf16[512,1024]{1,0:T(8,128)(2,1)S(1)}, bf16[512,1024]{1,0:T(8,128)(2,1)S(1)}, u32[]{:S(2)}, u32[]{:S(2)}) collective-permute-start(bf16[512,1024]{1,0:T(8,128)(2,1)S(1)} %bitcast.291), channel_id=1, source_target_pairs={{0,1},{1,0},{2,3},{3,2},{4,5},{5,4},{6,7},{7,6},{8,9},{9,8},{10,11... | collective-permute-start | bytes 3145736 | tf_op jit(solution)/shard_map/ppermute | solution.py:61
  13.8 26.0 %collective-permute-start.4 = (bf16[272,512]{1,0:T(8,128)(2,1)S(1)}, bf16[272,512]{1,0:T(8,128)(2,1)S(1)}, u32[]{:S(2)}, u32[]{:S(2)}) collective-permute-start(bf16[272,512]{1,0:T(8,128)(2,1)S(1)} %pad_maximum_fusion.15.refs_0_), channel_id=1, source_target_pairs={{0,4},{1,5},{2,6},{3,7},{4,0},{5,1},{6,2},{7,3},{8,12},{9,13},{10,... | collective-permute-start | bytes 835592 | tf_op jit(solution)/shard_map/ppermute | solution.py:66
  16.4 23.4 %collective-permute-start.5 = (bf16[272,512]{1,0:T(8,128)(2,1)S(1)}, bf16[272,512]{1,0:T(8,128)(2,1)S(1)}, u32[]{:S(2)}, u32[]{:S(2)}) collective-permute-start(bf16[272,512]{1,0:T(8,128)(2,1)S(1)} %pad_maximum_fusion.15.refs_0_), channel_id=1, source_target_pairs={{0,6},{1,7},{2,0},{3,1},{4,2},{5,3},{6,4},{7,5},{8,14},{9,15},{10,... | collective-permute-start | bytes 835592 | tf_op jit(solution)/shard_map/ppermute | solution.py:66
  23.6 33.5 %collective-permute-start.9 = (bf16[512,1024]{1,0:T(8,128)(2,1)S(1)}, bf16[512,1024]{1,0:T(8,128)(2,1)S(1)}, u32[]{:S(2)}, u32[]{:S(2)}) collective-permute-start(bf16[512,1024]{1,0:T(8,128)(2,1)S(1)} %bitcast.292), channel_id=1, source_target_pairs={{2,0},{3,1},{4,2},{5,3},{6,4},{7,5},{10,8},{11,9},{12,10},{13,11},... | collective-permute-start | bytes 3145736 | tf_op jit(solution)/shard_map/ppermute | solution.py:72
  24.9 32.2 %collective-permute-start.6 = (bf16[512,1024]{1,0:T(8,128)(2,1)S(1)}, bf16[512,1024]{1,0:T(8,128)(2,1)}, u32[]{:S(2)}, u32[]{:S(2)}) collective-permute-start(bf16[512,1024]{1,0:T(8,128)(2,1)S(1)} %bitcast.293), channel_id=1, source_target_pairs={{0,2},{1,3},{2,4},{3,5},{4,6},{5,7},{8,10},{9,11},{10,12},{11,13},... | collective-permute-start | bytes 3145736 | tf_op jit(solution)/shard_map/ppermute | solution.py:72
  60.2 25.1 %collective-permute-start.13 = (bf16[2,4,128,512]{3,2,1,0:T(8,128)(2,1)S(1)}, bf16[2,4,128,512]{3,2,1,0:T(8,128)(2,1)S(1)}, u32[]{:S(2)}, u32[]{:S(2)}) collective-permute-start(bf16[2,4,128,512]{3,2,1,0:T(8,128)(2,1)S(1)} %pad_maximum_fusion.3.refs_0_), channel_id=1, source_target_pairs={{0,16},{8,24},{16,0},{24,8},{1,17},{9,25},{17,1},{25,9},{2,18},{10... | collective-permute-start | bytes 3145736 | tf_op jit(solution)/shard_map/ppermute | solution.py:77
  61.8 24.8 %collective-permute-start.14 = (bf16[2,4,128,512]{3,2,1,0:T(8,128)(2,1)S(1)}, bf16[2,4,128,512]{3,2,1,0:T(8,128)(2,1)S(1)}, u32[]{:S(2)}, u32[]{:S(2)}) collective-permute-start(bf16[2,4,128,512]{3,2,1,0:T(8,128)(2,1)S(1)} %pad_maximum_fusion.4.refs_2_), channel_id=1, source_target_pairs={{0,8},{8,0},{16,24},{24,16},{1,9},{9,1},{17,25},{25,17},{2,10},{10... | collective-permute-start | bytes 3145736 | tf_op jit(solution)/shard_map/ppermute | solution.py:77
  73.2 38.8 %collective-permute-start.15 = (bf16[256,512]{1,0:T(8,128)(2,1)S(1)}, bf16[256,512]{1,0:T(8,128)(2,1)S(1)}, u32[]{:S(2)}, u32[]{:S(2)}) collective-permute-start(bf16[256,512]{1,0:T(8,128)(2,1)S(1)} %copy-done.113), channel_id=1, source_target_pairs={{0,2},{1,3},{2,4},{3,5},{4,6},{5,7},{6,0},{7,1},{8,10},{9,11},{10,... | collective-permute-start | bytes 786440 | tf_op jit(solution)/shard_map/ppermute | solution.py:66
  79.8 32.1 %collective-permute-start.16 = (bf16[256,512]{1,0:T(8,128)(2,1)S(1)}, bf16[256,512]{1,0:T(8,128)(2,1)S(1)}, u32[]{:S(2)}, u32[]{:S(2)}) collective-permute-start(bf16[256,512]{1,0:T(8,128)(2,1)S(1)} %copy-done.113), channel_id=1, source_target_pairs={{0,4},{1,5},{2,6},{3,7},{4,0},{5,1},{6,2},{7,3},{8,12},{9,13},{10,... | collective-permute-start | bytes 786440 | tf_op jit(solution)/shard_map/ppermute | solution.py:66
  79.8 32.1 %collective-permute-start.17 = (bf16[256,512]{1,0:T(8,128)(2,1)S(1)}, bf16[256,512]{1,0:T(8,128)(2,1)S(1)}, u32[]{:S(2)}, u32[]{:S(2)}) collective-permute-start(bf16[256,512]{1,0:T(8,128)(2,1)S(1)} %copy-done.113), channel_id=1, source_target_pairs={{0,6},{1,7},{2,0},{3,1},{4,2},{5,3},{6,4},{7,5},{8,14},{9,15},{10,... | collective-permute-start | bytes 786440 | tf_op jit(solution)/shard_map/ppermute | solution.py:66
  125.6 30.5 %collective-permute-start.20 = (bf16[2,4,128,512]{3,2,1,0:T(8,128)(2,1)S(1)}, bf16[2,4,128,512]{3,2,1,0:T(8,128)(2,1)S(1)}, u32[]{:S(2)}, u32[]{:S(2)}) collective-permute-start(bf16[2,4,128,512]{3,2,1,0:T(8,128)(2,1)S(1)} %pad_maximum_fusion.5.refs_0_), channel_id=1, source_target_pairs={{0,16},{8,24},{16,0},{24,8},{1,17},{9,25},{17,1},{25,9},{2,18},{10... | collective-permute-start | bytes 3145736 | tf_op jit(solution)/shard_map/ppermute | solution.py:77
  126.6 29.5 %collective-permute-start.21 = (bf16[2,4,128,512]{3,2,1,0:T(8,128)(2,1)S(1)}, bf16[2,4,128,512]{3,2,1,0:T(8,128)(2,1)S(1)}, u32[]{:S(2)}, u32[]{:S(2)}) collective-permute-start(bf16[2,4,128,512]{3,2,1,0:T(8,128)(2,1)S(1)} %pad_maximum_fusion.6.refs_2_), channel_id=1, source_target_pairs={{0,8},{8,0},{16,24},{24,16},{1,9},{9,1},{17,25},{25,17},{2,10},{10... | collective-permute-start | bytes 3145736 | tf_op jit(solution)/shard_map/ppermute | solution.py:77
  128.6 27.5 %collective-permute-start.22 = (bf16[512,256]{1,0:T(8,128)(2,1)S(1)}, bf16[512,256]{1,0:T(8,128)(2,1)S(1)}, u32[]{:S(2)}, u32[]{:S(2)}) collective-permute-start(bf16[512,256]{1,0:T(8,128)(2,1)S(1)} %copy-done.112), channel_id=1, source_target_pairs={{0,2},{1,3},{2,4},{3,5},{4,6},{5,7},{6,0},{7,1},{8,10},{9,11},{10,... | collective-permute-start | bytes 786440 | tf_op jit(solution)/shard_map/ppermute | solution.py:66
  136.7 19.4 %collective-permute-start.23 = (bf16[512,256]{1,0:T(8,128)(2,1)S(1)}, bf16[512,256]{1,0:T(8,128)(2,1)S(1)}, u32[]{:S(2)}, u32[]{:S(2)}) collective-permute-start(bf16[512,256]{1,0:T(8,128)(2,1)S(1)} %copy-done.112), channel_id=1, source_target_pairs={{0,4},{1,5},{2,6},{3,7},{4,0},{5,1},{6,2},{7,3},{8,12},{9,13},{10,... | collective-permute-start | bytes 786440 | tf_op jit(solution)/shard_map/ppermute | solution.py:66
  158.2 17.3 %collective-permute-start.25 = (bf16[1,4,256,256]{3,2,1,0:T(8,128)(2,1)}, bf16[1,4,256,256]{3,2,1,0:T(8,128)(2,1)}, u32[]{:S(2)}, u32[]{:S(2)}) collective-permute-start(bf16[1,4,256,256]{3,2,1,0:T(8,128)(2,1)} %maximum_bitcast_fusion.4), channel_id=1, source_target_pairs={{0,8},{8,0},{16,24},{24,16},{1,9},{9,1},{17,25},{25,17},{2,10},{10... | collective-permute-start | bytes 1572872 | tf_op jit(solution)/shard_map/ppermute | solution.py:77
  158.3 17.2 %collective-permute-start.26 = (bf16[1,4,256,256]{3,2,1,0:T(8,128)(2,1)}, bf16[1,4,256,256]{3,2,1,0:T(8,128)(2,1)}, u32[]{:S(2)}, u32[]{:S(2)}) collective-permute-start(bf16[1,4,256,256]{3,2,1,0:T(8,128)(2,1)} %maximum_bitcast_fusion.5), channel_id=1, source_target_pairs={{0,16},{8,24},{16,0},{24,8},{1,17},{9,25},{17,1},{25,9},{2,18},{10... | collective-permute-start | bytes 1572872 | tf_op jit(solution)/shard_map/ppermute | solution.py:77
  197.4 25.3 %collective-permute-start.29 = (bf16[2,4,256,256]{3,2,1,0:T(8,128)(2,1)S(1)}, bf16[2,4,256,256]{3,2,1,0:T(8,128)(2,1)S(1)}, u32[]{:S(2)}, u32[]{:S(2)}) collective-permute-start(bf16[2,4,256,256]{3,2,1,0:T(8,128)(2,1)S(1)} %copy-done.37), channel_id=1, source_target_pairs={{0,16},{8,24},{16,0},{24,8},{1,17},{9,25},{17,1},{25,9},{2,18},{10... | collective-permute-start | bytes 3145736 | tf_op jit(solution)/shard_map/ppermute | solution.py:77
  198.6 25.2 %collective-permute-start.30 = (bf16[2,4,256,256]{3,2,1,0:T(8,128)(2,1)S(1)}, bf16[2,4,256,256]{3,2,1,0:T(8,128)(2,1)S(1)}, u32[]{:S(2)}, u32[]{:S(2)}) collective-permute-start(bf16[2,4,256,256]{3,2,1,0:T(8,128)(2,1)S(1)} %copy-done.35), channel_id=1, source_target_pairs={{0,8},{8,0},{16,24},{24,16},{1,9},{9,1},{17,25},{25,17},{2,10},{10... | collective-permute-start | bytes 3145736 | tf_op jit(solution)/shard_map/ppermute | solution.py:77
  231.8 29.8 %collective-permute-start.31 = (bf16[2,4,256,256]{3,2,1,0:T(8,128)(2,1)}, bf16[2,4,256,256]{3,2,1,0:T(8,128)(2,1)}, u32[]{:S(2)}, u32[]{:S(2)}) collective-permute-start(bf16[2,4,256,256]{3,2,1,0:T(8,128)(2,1)} %get-tuple-element.414), channel_id=1, source_target_pairs={{0,8},{8,0},{16,24},{24,16},{1,9},{9,1},{17,25},{25,17},{2,10},{10... | collective-permute-start | bytes 3145736 | tf_op jit(solution)/shard_map/ppermute | solution.py:77
  233.6 28.0 %collective-permute-start.32 = (bf16[2,4,256,256]{3,2,1,0:T(8,128)(2,1)}, bf16[2,4,256,256]{3,2,1,0:T(8,128)(2,1)}, u32[]{:S(2)}, u32[]{:S(2)}) collective-permute-start(bf16[2,4,256,256]{3,2,1,0:T(8,128)(2,1)} %get-tuple-element.415), channel_id=1, source_target_pairs={{0,16},{8,24},{16,0},{24,8},{1,17},{9,25},{17,1},{25,9},{2,18},{10... | collective-permute-start | bytes 3145736 | tf_op jit(solution)/shard_map/ppermute | solution.py:77
  279.0 30.3 %collective-permute-start.39 = (bf16[1,4,256,256]{3,2,1,0:T(8,128)(2,1)}, bf16[1,4,256,256]{3,2,1,0:T(8,128)(2,1)}, u32[]{:S(2)}, u32[]{:S(2)}) collective-permute-start(bf16[1,4,256,256]{3,2,1,0:T(8,128)(2,1)} %slice.1073), channel_id=1, source_target_pairs={{0,16},{8,24},{16,0},{24,8},{1,17},{9,25},{17,1},{25,9},{2,18},{10... | collective-permute-start | bytes 1572872 | tf_op jit(solution)/shard_map/ppermute | solution.py:77
  279.9 29.5 %collective-permute-start.40 = (bf16[1,4,256,256]{3,2,1,0:T(8,128)(2,1)}, bf16[1,4,256,256]{3,2,1,0:T(8,128)(2,1)}, u32[]{:S(2)}, u32[]{:S(2)}) collective-permute-start(bf16[1,4,256,256]{3,2,1,0:T(8,128)(2,1)} %slice.1074), channel_id=1, source_target_pairs={{0,8},{8,0},{16,24},{24,16},{1,9},{9,1},{17,25},{25,17},{2,10},{10... | collective-permute-start | bytes 1572872 | tf_op jit(solution)/shard_map/ppermute | solution.py:77
  288.4 17.9 %collective-permute-start.37 = (f32[16,1024]{1,0:T(8,128)S(1)}, f32[16,1024]{1,0:T(8,128)S(1)}, u32[]{:S(2)}, u32[]{:S(2)}) collective-permute-start(f32[16,1024]{1,0:T(8,128)S(1)} %pad_maximum_fusion.21), channel_id=1, source_target_pairs={{0,2},{1,3},{2,4},{3,5},{4,6},{5,7},{8,10},{9,11},{10,12},{11,13},... | collective-permute-start | bytes 196616 | tf_op jit(solution)/shard_map/ppermute | solution.py:72
  322.0 26.1 %collective-permute-start.41 = (bf16[2,4,128,512]{3,2,1,0:T(8,128)(2,1)}, bf16[2,4,128,512]{3,2,1,0:T(8,128)(2,1)}, u32[]{:S(2)}, u32[]{:S(2)}) collective-permute-start(bf16[2,4,128,512]{3,2,1,0:T(8,128)(2,1)} %copy-done.93), channel_id=1, source_target_pairs={{0,8},{8,0},{16,24},{24,16},{1,9},{9,1},{17,25},{25,17},{2,10},{10... | collective-permute-start | bytes 3145736 | tf_op jit(solution)/shard_map/ppermute | solution.py:77
  322.3 25.8 %collective-permute-start.42 = (bf16[2,4,128,512]{3,2,1,0:T(8,128)(2,1)}, bf16[2,4,128,512]{3,2,1,0:T(8,128)(2,1)}, u32[]{:S(2)}, u32[]{:S(2)}) collective-permute-start(bf16[2,4,128,512]{3,2,1,0:T(8,128)(2,1)} %copy-done.92), channel_id=1, source_target_pairs={{0,16},{8,24},{16,0},{24,8},{1,17},{9,25},{17,1},{25,9},{2,18},{10... | collective-permute-start | bytes 3145736 | tf_op jit(solution)/shard_map/ppermute | solution.py:77
  353.2 33.9 %collective-permute-start.43 = (bf16[1,4,128,512]{3,2,1,0:T(8,128)(2,1)}, bf16[1,4,128,512]{3,2,1,0:T(8,128)(2,1)}, u32[]{:S(2)}, u32[]{:S(2)}) collective-permute-start(bf16[1,4,128,512]{3,2,1,0:T(8,128)(2,1)} %slice.1079), channel_id=1, source_target_pairs={{0,16},{8,24},{16,0},{24,8},{1,17},{9,25},{17,1},{25,9},{2,18},{10... | collective-permute-start | bytes 1572872 | tf_op jit(solution)/shard_map/ppermute | solution.py:77
  353.2 33.9 %collective-permute-start.44 = (bf16[1,4,128,512]{3,2,1,0:T(8,128)(2,1)}, bf16[1,4,128,512]{3,2,1,0:T(8,128)(2,1)}, u32[]{:S(2)}, u32[]{:S(2)}) collective-permute-start(bf16[1,4,128,512]{3,2,1,0:T(8,128)(2,1)} %slice.1080), channel_id=1, source_target_pairs={{0,8},{8,0},{16,24},{24,16},{1,9},{9,1},{17,25},{25,17},{2,10},{10... | collective-permute-start | bytes 1572872 | tf_op jit(solution)/shard_map/ppermute | solution.py:77
  356.7 26.1 %collective-permute-start.45 = (bf16[512,256]{1,0:T(8,128)(2,1)}, bf16[512,256]{1,0:T(8,128)(2,1)}, u32[]{:S(2)}, u32[]{:S(2)}) collective-permute-start(bf16[512,256]{1,0:T(8,128)(2,1)} %get-tuple-element.464), channel_id=1, source_target_pairs={{0,2},{1,3},{2,4},{3,5},{4,6},{5,7},{6,0},{7,1},{8,10},{9,11},{10,... | collective-permute-start | bytes 786440 | tf_op jit(solution)/shard_map/ppermute | solution.py:66
  360.9 24.8 %collective-permute-start.46 = (bf16[512,256]{1,0:T(8,128)(2,1)}, bf16[512,256]{1,0:T(8,128)(2,1)}, u32[]{:S(2)}, u32[]{:S(2)}) collective-permute-start(bf16[512,256]{1,0:T(8,128)(2,1)} %get-tuple-element.465), channel_id=1, source_target_pairs={{0,4},{1,5},{2,6},{3,7},{4,0},{5,1},{6,2},{7,3},{8,12},{9,13},{10,... | collective-permute-start | bytes 786440 | tf_op jit(solution)/shard_map/ppermute | solution.py:66
  361.9 25.2 %collective-permute-start.47 = (bf16[512,256]{1,0:T(8,128)(2,1)}, bf16[512,256]{1,0:T(8,128)(2,1)}, u32[]{:S(2)}, u32[]{:S(2)}) collective-permute-start(bf16[512,256]{1,0:T(8,128)(2,1)} %get-tuple-element.466), channel_id=1, source_target_pairs={{0,6},{1,7},{2,0},{3,1},{4,2},{5,3},{6,4},{7,5},{8,14},{9,15},{10,... | collective-permute-start | bytes 786440 | tf_op jit(solution)/shard_map/ppermute | solution.py:66
  385.7 20.9 %collective-permute-start.49 = (bf16[1024,256]{1,0:T(8,128)(2,1)S(1)}, bf16[1024,256]{1,0:T(8,128)(2,1)S(1)}, u32[]{:S(2)}, u32[]{:S(2)}) collective-permute-start(bf16[1024,256]{1,0:T(8,128)(2,1)S(1)} %copy-done.108), channel_id=1, source_target_pairs={{2,0},{3,1},{4,2},{5,3},{6,4},{7,5},{10,8},{11,9},{12,10},{13,11},... | collective-permute-start | bytes 1572872 | tf_op jit(solution)/shard_map/ppermute | solution.py:72
  390.6 32.2 %collective-permute-start.53 = (bf16[2,4,128,256]{3,2,1,0:T(8,128)(2,1)S(1)}, bf16[2,4,128,256]{3,2,1,0:T(8,128)(2,1)}, u32[]{:S(2)}, u32[]{:S(2)}) collective-permute-start(bf16[2,4,128,256]{3,2,1,0:T(8,128)(2,1)S(1)} %get-tuple-element.491), channel_id=1, source_target_pairs={{0,8},{8,0},{16,24},{24,16},{1,9},{9,1},{17,25},{25,17},{2,10},{10... | collective-permute-start | bytes 1572872 | tf_op jit(solution)/shard_map/ppermute | solution.py:77
  390.8 32.0 %collective-permute-start.54 = (bf16[2,4,128,256]{3,2,1,0:T(8,128)(2,1)S(1)}, bf16[2,4,128,256]{3,2,1,0:T(8,128)(2,1)}, u32[]{:S(2)}, u32[]{:S(2)}) collective-permute-start(bf16[2,4,128,256]{3,2,1,0:T(8,128)(2,1)S(1)} %get-tuple-element.492), channel_id=1, source_target_pairs={{0,16},{8,24},{16,0},{24,8},{1,17},{9,25},{17,1},{25,9},{2,18},{10... | collective-permute-start | bytes 1572872 | tf_op jit(solution)/shard_map/ppermute | solution.py:77
  394.6 28.1 %collective-permute-start.50 = (bf16[256,512]{1,0:T(8,128)(2,1)}, bf16[256,512]{1,0:T(8,128)(2,1)}, u32[]{:S(2)}, u32[]{:S(2)}) collective-permute-start(bf16[256,512]{1,0:T(8,128)(2,1)} %get-tuple-element.488), channel_id=1, source_target_pairs={{0,2},{1,3},{2,4},{3,5},{4,6},{5,7},{6,0},{7,1},{8,10},{9,11},{10,... | collective-permute-start | bytes 786440 | tf_op jit(solution)/shard_map/ppermute | solution.py:66
  397.3 25.5 %collective-permute-start.51 = (bf16[256,512]{1,0:T(8,128)(2,1)}, bf16[256,512]{1,0:T(8,128)(2,1)}, u32[]{:S(2)}, u32[]{:S(2)}) collective-permute-start(bf16[256,512]{1,0:T(8,128)(2,1)} %get-tuple-element.489), channel_id=1, source_target_pairs={{0,4},{1,5},{2,6},{3,7},{4,0},{5,1},{6,2},{7,3},{8,12},{9,13},{10,... | collective-permute-start | bytes 786440 | tf_op jit(solution)/shard_map/ppermute | solution.py:66
  425.7 25.5 %collective-permute-start.56 = (bf16[1,128,1024]{2,1,0:T(8,128)(2,1)S(1)}, bf16[1,128,1024]{2,1,0:T(8,128)(2,1)S(1)}, u32[]{:S(2)}, u32[]{:S(2)}) collective-permute-start(bf16[1,128,1024]{2,1,0:T(8,128)(2,1)S(1)} %get-tuple-element.529), channel_id=1, source_target_pairs={{0,16},{8,24},{16,0},{24,8},{1,17},{9,25},{17,1},{25,9},{2,18},{10... | collective-permute-start | bytes 786440 | tf_op jit(solution)/shard_map/ppermute | solution.py:77
  429.7 22.4 %collective-permute-start.55 = (bf16[1,128,1024]{2,1,0:T(8,128)(2,1)S(1)}, bf16[1,128,1024]{2,1,0:T(8,128)(2,1)S(1)}, u32[]{:S(2)}, u32[]{:S(2)}) collective-permute-start(bf16[1,128,1024]{2,1,0:T(8,128)(2,1)S(1)} %get-tuple-element.528), channel_id=1, source_target_pairs={{0,8},{8,0},{16,24},{24,16},{1,9},{9,1},{17,25},{25,17},{2,10},{10... | collective-permute-start | bytes 786440 | tf_op jit(solution)/shard_map/ppermute | solution.py:77
  435.9 17.1 %collective-permute-start.57 = (bf16[1,4,128,256]{3,2,1,0:T(8,128)(2,1)S(1)}, bf16[1,4,128,256]{3,2,1,0:T(8,128)(2,1)S(1)}, u32[]{:S(2)}, u32[]{:S(2)}) collective-permute-start(bf16[1,4,128,256]{3,2,1,0:T(8,128)(2,1)S(1)} %slice.1085), channel_id=1, source_target_pairs={{0,16},{8,24},{16,0},{24,8},{1,17},{9,25},{17,1},{25,9},{2,18},{10... | collective-permute-start | bytes 786440 | tf_op jit(solution)/shard_map/ppermute | solution.py:77
  436.0 17.0 %collective-permute-start.58 = (bf16[1,4,128,256]{3,2,1,0:T(8,128)(2,1)S(1)}, bf16[1,4,128,256]{3,2,1,0:T(8,128)(2,1)S(1)}, u32[]{:S(2)}, u32[]{:S(2)}) collective-permute-start(bf16[1,4,128,256]{3,2,1,0:T(8,128)(2,1)S(1)} %slice.1086), channel_id=1, source_target_pairs={{0,8},{8,0},{16,24},{24,16},{1,9},{9,1},{17,25},{25,17},{2,10},{10... | collective-permute-start | bytes 786440 | tf_op jit(solution)/shard_map/ppermute | solution.py:77
  458.8 35.1 %collective-permute-start.59 = (bf16[2,4,128,256]{3,2,1,0:T(8,128)(2,1)S(1)}, bf16[2,4,128,256]{3,2,1,0:T(8,128)(2,1)S(1)}, u32[]{:S(2)}, u32[]{:S(2)}) collective-permute-start(bf16[2,4,128,256]{3,2,1,0:T(8,128)(2,1)S(1)} %get-tuple-element.556), channel_id=1, source_target_pairs={{0,8},{8,0},{16,24},{24,16},{1,9},{9,1},{17,25},{25,17},{2,10},{10... | collective-permute-start | bytes 1572872 | tf_op jit(solution)/shard_map/ppermute | solution.py:77
  458.9 35.0 %collective-permute-start.60 = (bf16[2,4,128,256]{3,2,1,0:T(8,128)(2,1)S(1)}, bf16[2,4,128,256]{3,2,1,0:T(8,128)(2,1)S(1)}, u32[]{:S(2)}, u32[]{:S(2)}) collective-permute-start(bf16[2,4,128,256]{3,2,1,0:T(8,128)(2,1)S(1)} %get-tuple-element.557), channel_id=1, source_target_pairs={{0,16},{8,24},{16,0},{24,8},{1,17},{9,25},{17,1},{25,9},{2,18},{10... | collective-permute-start | bytes 1572872 | tf_op jit(solution)/shard_map/ppermute | solution.py:77
  463.6 30.2 %collective-permute-start.61 = (bf16[256,256]{1,0:T(8,128)(2,1)S(1)}, bf16[256,256]{1,0:T(8,128)(2,1)S(1)}, u32[]{:S(2)}, u32[]{:S(2)}) collective-permute-start(bf16[256,256]{1,0:T(8,128)(2,1)S(1)} %get-tuple-element.559), channel_id=1, source_target_pairs={{0,2},{1,3},{2,4},{3,5},{4,6},{5,7},{6,0},{7,1},{8,10},{9,11},{10,... | collective-permute-start | bytes 393224 | tf_op jit(solution)/shard_map/ppermute | solution.py:66
  475.1 18.8 %collective-permute-start.62 = (bf16[256,256]{1,0:T(8,128)(2,1)S(1)}, bf16[256,256]{1,0:T(8,128)(2,1)S(1)}, u32[]{:S(2)}, u32[]{:S(2)}) collective-permute-start(bf16[256,256]{1,0:T(8,128)(2,1)S(1)} %get-tuple-element.560), channel_id=1, source_target_pairs={{0,4},{1,5},{2,6},{3,7},{4,0},{5,1},{6,2},{7,3},{8,12},{9,13},{10,... | collective-permute-start | bytes 393224 | tf_op jit(solution)/shard_map/ppermute | solution.py:66
  498.1 20.4 %collective-permute-start.66 = (bf16[1,4,128,256]{3,2,1,0:T(8,128)(2,1)}, bf16[1,4,128,256]{3,2,1,0:T(8,128)(2,1)}, u32[]{:S(2)}, u32[]{:S(2)}) collective-permute-start(bf16[1,4,128,256]{3,2,1,0:T(8,128)(2,1)} %slice.1089), channel_id=1, source_target_pairs={{0,16},{8,24},{16,0},{24,8},{1,17},{9,25},{17,1},{25,9},{2,18},{10... | collective-permute-start | bytes 786440 | tf_op jit(solution)/shard_map/ppermute | solution.py:77
  500.2 18.4 %collective-permute-start.67 = (bf16[1,4,128,256]{3,2,1,0:T(8,128)(2,1)}, bf16[1,4,128,256]{3,2,1,0:T(8,128)(2,1)}, u32[]{:S(2)}, u32[]{:S(2)}) collective-permute-start(bf16[1,4,128,256]{3,2,1,0:T(8,128)(2,1)} %slice.1090), channel_id=1, source_target_pairs={{0,8},{8,0},{16,24},{24,16},{1,9},{9,1},{17,25},{25,17},{2,10},{10... | collective-permute-start | bytes 786440 | tf_op jit(solution)/shard_map/ppermute | solution.py:77
  525.1 23.3 %collective-permute-start.75 = (bf16[2,128,1024]{2,1,0:T(8,128)(2,1)S(1)}, bf16[2,128,1024]{2,1,0:T(8,128)(2,1)S(1)}, u32[]{:S(2)}, u32[]{:S(2)}) collective-permute-start(bf16[2,128,1024]{2,1,0:T(8,128)(2,1)S(1)} %copy-done.106), channel_id=1, source_target_pairs={{0,8},{8,0},{16,24},{24,16},{1,9},{9,1},{17,25},{25,17},{2,10},{10... | collective-permute-start | bytes 1572872 | tf_op jit(solution)/shard_map/ppermute | solution.py:77
  525.3 23.2 %collective-permute-start.74 = (bf16[2,128,1024]{2,1,0:T(8,128)(2,1)S(1)}, bf16[2,128,1024]{2,1,0:T(8,128)(2,1)S(1)}, u32[]{:S(2)}, u32[]{:S(2)}) collective-permute-start(bf16[2,128,1024]{2,1,0:T(8,128)(2,1)S(1)} %copy-done.107), channel_id=1, source_target_pairs={{0,16},{8,24},{16,0},{24,8},{1,17},{9,25},{17,1},{25,9},{2,18},{10... | collective-permute-start | bytes 1572872 | tf_op jit(solution)/shard_map/ppermute | solution.py:77
  549.4 16.3 %collective-permute-start.84 = (bf16[128,2048]{1,0:T(8,128)(2,1)S(1)}, bf16[128,2048]{1,0:T(8,128)(2,1)S(1)}, u32[]{:S(2)}, u32[]{:S(2)}) collective-permute-start(bf16[128,2048]{1,0:T(8,128)(2,1)S(1)} %constant_dynamic-slice_fusion), channel_id=1, source_target_pairs={{0,1},{1,0},{2,3},{3,2},{4,5},{5,4},{6,7},{7,6},{8,9},{9,8},{10,11... | collective-permute-start | bytes 1572872 | tf_op jit(solution)/shard_map/ppermute | solution.py:61
  (166 other events, 1418.7 us)
